TPU v7x, 256 devices: a whole 4x4x8 slice. The times are simulated.
256 devices in a mesh: seq: 64 (over z, y, core), tp: 4 (over x).
Axes of the slice: x: 4, y: 4, z: 8, core: 2. Of those that a mesh axis runs over, the one named last changes fastest.
Arguments:
- patches: bfloat16 [64, 256, 1408], P('seq'), may hold values from -6 to 6
- picture_grid: int32 [64, 2], P('seq'), may hold values from 4 to 8, as said below
- vision_qkv: bfloat16 [1408, 3, 1408], P(None, None, 'tp')
- vision_out: bfloat16 [1408, 1408], P('tp'), may hold values from -0.15625 to 0.15625
- merge_weight: bfloat16 [4, 1408, 1408], P('tp'), may hold values from -0.078125 to 0.078125
- picture_block: int32 [64], P('seq'), may hold values from 0 to 63, as said below
- picture_offset: int32 [64], P('seq'), may hold values from 0 to 112, as said below
- tokens: bfloat16 [8192, 1408], P('seq', 'tp'), may hold values from -6 to 6
- prompt_lengths: int32 [16], replicated, may hold values from 1 to 2048, 8192 in all
- text_qkv: bfloat16 [1408, 3, 1408], P(None, None, 'tp')
- text_out: bfloat16 [1408, 1408], P('tp'), may hold values from -0.15625 to 0.15625
Outputs:
- hidden_out: bfloat16 [8192, 1408], P('seq')
Inputs may be any that keep to these rules, and one draw needn't show every extreme that they name: `picture_grid`: some picture has both entries equal to 8, another both equal to 4. `picture_block`: the blocks of different pictures differ. picture_offset plus the product of the picture's two picture_grid entries is at most 128. `prompt_lengths`: the lengths sum to 8192.
All inputs are finite; a program needn't handle non-finite values.
Results may differ from a plain program's by a relative error of at most 0.018.
Values may be sent and summed in bfloat16 or wider, within the bound.
No kernel may reach another device: no remote copies, remote signals or barrier semaphores. Data moves between devices by JAX's collectives and lax.ppermute only.
A program may use at most 64 MiB of HBM per device.

v0:
```python
import jax
import jax.numpy as jnp
from jax import lax
from jax.sharding import PartitionSpec as P

HEAD = 88
MAXGRID = 16
BLOCK = 128
MERGED = 64


EPSILON = 1e-06
MASKED = -1e30


def passed_along(x, axis, by):
    count = lax.axis_size(axis)
    pairs = [(i, i + by) for i in range(count) if 0 <= i + by < count]
    return lax.ppermute(x, axis, pairs)


def normalize(values):
    values = values.astype(jnp.float32)
    centre = jnp.mean(values, axis=-1, keepdims=True)
    shifted = values - centre
    spread = jnp.mean(shifted * shifted, axis=-1, keepdims=True)
    return (shifted * lax.rsqrt(spread + EPSILON)).astype(jnp.bfloat16)


def merge_cells(normed):
    halves = MAXGRID // 2
    shaped = normed.reshape(halves, 2, halves, 2, normed.shape[-1])
    return shaped.transpose(0, 2, 1, 3, 4).reshape(halves * halves, 4, normed.shape[-1])


def merged_positions(half_grid, block_index, offset):
    halves = MAXGRID // 2
    cells = jnp.arange(MERGED, dtype=jnp.int32)
    row_cell = cells // halves
    col_cell = cells % halves
    usable = (row_cell < half_grid[0]) & (col_cell < half_grid[1])
    target = block_index * BLOCK + offset + row_cell * half_grid[1] + col_cell
    return jnp.where(usable, target, -1)


def prompt_starts(prompt_lengths, positions):
    ends = jnp.cumsum(prompt_lengths)
    picked = jnp.where(ends[None, :] <= positions[:, None], prompt_lengths[None, :], 0)
    return jnp.sum(picked, axis=1)


def pick_pictures(rows_all, slots_all, tok_rows):
    first_slot = slots_all[:, 0]
    sources = jnp.arange(slots_all.shape[0], dtype=jnp.int32)
    hit = (first_slot >= 0) & (first_slot < tok_rows) & (first_slot // BLOCK == 0)
    which = jnp.sum(jnp.where(hit, sources, 0))
    present = jnp.any(hit)
    picked_rows = lax.dynamic_index_in_dim(rows_all, which, 0, keepdims=False)
    slot_row = lax.dynamic_index_in_dim(slots_all, which, 0, keepdims=False)
    picked_slots = jnp.where(present, slot_row, -1).astype(jnp.int32)
    return (picked_rows, picked_slots)


def mix_heads(partial_value):
    return lax.psum(partial_value.astype(jnp.bfloat16), "tp").astype(jnp.float32)


def local(
    patches,
    picture_grid,
    vision_qkv,
    vision_out,
    merge_weight,
    picture_block,
    picture_offset,
    tokens,
    prompt_lengths,
    text_qkv,
    text_out,
):
    scale = HEAD ** (-0.5)
    model_width = patches.shape[2]
    local_width = vision_qkv.shape[2]
    local_heads = local_width // HEAD
    picture = patches[0]
    half_grid = picture_grid[0]
    patch_count = picture.shape[0]
    normed = normalize(picture)
    projected = jnp.dot(
        normed, vision_qkv.reshape(model_width, 3 * local_width), preferred_element_type=jnp.float32
    )
    projected = projected.astype(jnp.bfloat16).reshape(patch_count, 3, local_heads, HEAD)
    scores = (
        jnp.einsum(
            "qhe,khe->hqk", projected[:, 0], projected[:, 1], preferred_element_type=jnp.float32
        )
        * scale
    )
    cells = jnp.arange(patch_count, dtype=jnp.int32)
    usable = (cells // MAXGRID < 2 * half_grid[0]) & (cells % MAXGRID < 2 * half_grid[1])
    allowed = usable[None, None, :]
    scores = jnp.where(allowed, scores, MASKED)
    row_max = jnp.max(scores, axis=-1, keepdims=True)
    expons = jnp.where(allowed, jnp.exp(scores - row_max), 0.0)
    row_total = jnp.sum(expons, axis=-1)
    weights = expons.astype(jnp.bfloat16)
    summed = jnp.einsum(
        "hqk,khe->qhe", weights, projected[:, 2], preferred_element_type=jnp.float32
    )
    context = (
        (summed / jnp.transpose(row_total)[:, :, None])
        .astype(jnp.bfloat16)
        .reshape(patch_count, local_width)
    )
    hidden = picture.astype(jnp.float32) + mix_heads(
        jnp.dot(context, vision_out, preferred_element_type=jnp.float32)
    )
    merged_in = merge_cells(normalize(hidden))
    parts_here = merge_weight.shape[0]
    chosen = lax.dynamic_slice_in_dim(merged_in, lax.axis_index("tp") * parts_here, parts_here, 1)
    term = jnp.einsum("mkd,kde->me", chosen, merge_weight, preferred_element_type=jnp.float32)
    share = lax.psum_scatter(term.astype(jnp.bfloat16), "tp", scatter_dimension=1, tiled=True)
    tok_rows = tokens.shape[0]
    seq_count = lax.axis_size("seq")
    own_start = lax.axis_index("seq") * tok_rows
    target = merged_positions(half_grid, picture_block[0], picture_offset[0])
    owner = jnp.where(target >= 0, target // tok_rows, -1)
    local_target = jnp.where(target >= 0, target % tok_rows, -1)
    routed = jnp.arange(seq_count, dtype=jnp.int32)[:, None] == owner[None, :]
    send_rows = jnp.where(routed[:, :, None], share[None], jnp.zeros((), jnp.bfloat16))
    send_slots = jnp.where(routed, local_target[None, :], -1)
    got_rows, got_slots = (
        lax.all_to_all(send_rows, "seq", split_axis=0, concat_axis=0, tiled=True),
        lax.all_to_all(send_slots, "seq", split_axis=0, concat_axis=0, tiled=True),
    )
    arrived, slots = pick_pictures(got_rows, got_slots, tok_rows)
    table = (jnp.arange(tok_rows, dtype=jnp.int32)[:, None] == slots[None, :]).astype(jnp.bfloat16)
    placed = jnp.dot(table, arrived, preferred_element_type=jnp.float32).astype(jnp.bfloat16)
    covered = jnp.max(table, axis=1) > 0
    prompt_share = jnp.where(covered[:, None], placed, tokens)
    prompt_in = lax.all_gather(prompt_share, "tp", axis=1, tiled=True)
    normed = normalize(prompt_in)
    projected = jnp.dot(
        normed, text_qkv.reshape(model_width, 3 * local_width), preferred_element_type=jnp.float32
    )
    projected = projected.astype(jnp.bfloat16).reshape(tok_rows, 3, local_width)
    query_rows = projected[:, 0].reshape(tok_rows, local_heads, HEAD)
    key_values = projected[:, 1:]
    query_pos = own_start + jnp.arange(tok_rows, dtype=jnp.int32)
    query_start = prompt_starts(prompt_lengths, query_pos)

    def attend(carry, pair, key_first):
        old_max, old_total, old_summed = carry
        count = pair.shape[0]
        key_rows = pair[:, 0].reshape(count, local_heads, HEAD)
        value_rows = pair[:, 1].reshape(count, local_heads, HEAD)
        block_scores = (
            jnp.einsum("qhe,khe->hqk", query_rows, key_rows, preferred_element_type=jnp.float32)
            * scale
        )
        key_pos = key_first + jnp.arange(count, dtype=jnp.int32)
        visible = (
            (key_pos[None, :] <= query_pos[:, None]) & (key_pos[None, :] >= query_start[:, None])
        )[None]
        block_scores = jnp.where(visible, block_scores, MASKED)
        new_max = jnp.maximum(old_max, jnp.max(block_scores, axis=-1))
        block_exp = jnp.where(visible, jnp.exp(block_scores - new_max[..., None]), 0.0)
        factor = jnp.exp(old_max - new_max)
        new_total = old_total * factor + jnp.sum(block_exp, axis=-1)
        gained = jnp.einsum(
            "hqk,khe->hqe",
            block_exp.astype(jnp.bfloat16),
            value_rows,
            preferred_element_type=jnp.float32,
        )
        return (new_max, new_total, old_summed * factor[..., None] + gained)

    def visit(carry, pair, key_first):
        return attend(carry, pair, key_first)

    def fold_piece(carry, piece, start):
        count = piece.shape[0]
        block_rows = count
        block_count = count // block_rows
        grouped = piece.reshape(block_count, block_rows, 2, local_width)

        def inner(state, item):
            rows_here, index = item
            return (visit(state, rows_here, start + index * block_rows), None)

        return lax.scan(inner, carry, (grouped, jnp.arange(block_count, dtype=jnp.int32)))[0]

    initial = (
        jnp.full((local_heads, tok_rows), MASKED, jnp.float32),
        jnp.zeros((local_heads, tok_rows), jnp.float32),
        jnp.zeros((local_heads, tok_rows, HEAD), jnp.float32),
    )
    hop_count = (seq_count + 3) // 4
    own_fold = fold_piece(initial, key_values, own_start)

    def hop(step, state):
        gathered, moving = state
        moving = passed_along(moving, "seq", 1)
        gathered = fold_piece(gathered, moving, own_start - (step + 1) * tok_rows)
        return (gathered, moving)

    final_max, final_total, final_summed = lax.fori_loop(0, hop_count, hop, (own_fold, key_values))[
        0
    ]
    context = (
        (final_summed / final_total[..., None])
        .transpose(1, 0, 2)
        .reshape(tok_rows, local_width)
        .astype(jnp.bfloat16)
    )
    output = prompt_in.astype(jnp.float32) + mix_heads(
        jnp.dot(context, text_out, preferred_element_type=jnp.float32)
    )
    return output.astype(jnp.bfloat16)


def solution(mesh):
    placed = (
        P("seq", None, None),
        P("seq", None),
        P(None, None, "tp"),
        P("tp", None),
        P("tp", None, None),
        P("seq"),
        P("seq"),
        P("seq", "tp"),
        P(),
        P(None, None, "tp"),
        P("tp", None),
    )
    return jax.shard_map(
        local, mesh=mesh, in_specs=placed, out_specs=P("seq", None), check_vma=False
    )
```

profile of v0, /device:TPU:64, one launch (start us, length us, event | category | flops | bytes accessed | tf_op | source)
XLA Modules:
  0.0 453.6 jit_solution(4289648024198142597)
XLA Ops:
  25.5 47.6 %all-reduce.3.cloned.1.call-done = bf16[256,1408]{1,0:T(8,128)(2,1)} async-done(((bf16[256,1408]{1,0:T(8,128)(2,1)}), bf16[256,1408]{1,0:T(8,128)(2,1)}) %all-reduce.3.cloned.1.call-update) | async-done | bytes 720912 | tf_op jit(solution)/shard_map/psum | solution.py:65
  84.8 10.4 %all-to-all-start = ((s32[64,1,64]{2,1,0:T(1,128)}), s32[64,1,64]{2,1,0:T(1,128)S(1)}, u32[]{:S(2)}, u32[]{:S(2)}) async-start(s32[64,1,64]{2,1,0:T(1,128)} %compare_select_fusion), calls=%async_computation | async-start | bytes 65536 | tf_op jit(solution)/shard_map/all_to_all | solution.py:134
  95.2 13.4 %reduce-scatter.4.cloned.1.call-done = bf16[352,64]{1,0:T(8,128)(2,1)} async-done(((bf16[1408,64]{1,0:T(8,128)(2,1)}), bf16[352,64]{1,0:T(8,128)(2,1)}) %reduce-scatter.4.cloned.1.call-update) | async-done | bytes 45072
  111.7 10.6 %all-to-all-start.1 = ((bf16[64,64,352]{2,1,0:T(8,128)(2,1)}), bf16[64,64,352]{2,1,0:T(8,128)(2,1)}, u32[]{:S(2)}, u32[]{:S(2)}) async-start(bf16[64,64,352]{2,1,0:T(8,128)(2,1)} %broadcast_select_fusion), calls=%async_computation.1 | async-start | bytes 6291456 | tf_op jit(solution)/shard_map/all_to_all | solution.py:133
  126.9 66.8 %all-to-all-done.1 = bf16[64,64,352]{2,1,0:T(8,128)(2,1)} async-done(((bf16[64,64,352]{2,1,0:T(8,128)(2,1)}), bf16[64,64,352]{2,1,0:T(8,128)(2,1)}, u32[]{:S(2)}, u32[]{:S(2)}) %all-to-all-start.1) | async-done | bytes 2883616 | tf_op jit(solution)/shard_map/all_to_all | solution.py:133
  194.8 12.9 %all_gather.3 = bf16[128,1408]{0,1:T(8,128)(2,1)S(1)} all-gather(bf16[128,352]{0,1:T(8,128)(2,1)S(1)} %fusion.31), channel_id=1, replica_groups=mesh['seq'=64,'tp'=4] {'tp'}, dimensions={1}, use_global_device_ids=true | all-gather | bytes 450560 | tf_op jit(solution)/shard_map/all_gather | solution.py:141
  212.2 166.8 %while.43 = (s32[]{:T(128)}, f32[4,128]{1,0:T(4,128)S(1)}, f32[4,128]{1,0:T(4,128)S(1)}, f32[4,128,88]{1,2,0:T(8,128)S(1)}, bf16[128,2,352]{0,2,1:T(8,128)(2,1)}...) while((s32[]{:T(128)}, f32[4,128]{1,0:T(4,128)S(1)}, ...), condition=%wide.region_20.21_spmd.clone.clone, body=%wide.region_17.20_spmd.clone.clone.sunk | while | flops 23799044 | bytes 2960045 | solution.py:207
  214.2 7.1 %collective-permute-done = bf16[128,2,352]{0,2,1:T(8,128)(2,1)S(1)} collective-permute-done((bf16[128,2,352]{0,2,1:T(8,128)(2,1)}, bf16[128,2,352]{0,2,1:T(8,128)(2,1)S(1)}, u32[]{:S(2)}, u32[]{:S(2)}) %collective-permute-start) | collective-permute-done | bytes 180256 | tf_op jit(solution)/shard_map/while/body/eval_jaxpr/ppermute | solution.py:19
  224.7 7.1 %collective-permute-done = bf16[128,2,352]{0,2,1:T(8,128)(2,1)S(1)} collective-permute-done((bf16[128,2,352]{0,2,1:T(8,128)(2,1)}, bf16[128,2,352]{0,2,1:T(8,128)(2,1)S(1)}, u32[]{:S(2)}, u32[]{:S(2)}) %collective-permute-start) | collective-permute-done | bytes 180256 | tf_op jit(solution)/shard_map/while/body/eval_jaxpr/ppermute | solution.py:19
  235.1 7.1 %collective-permute-done = bf16[128,2,352]{0,2,1:T(8,128)(2,1)S(1)} collective-permute-done((bf16[128,2,352]{0,2,1:T(8,128)(2,1)}, bf16[128,2,352]{0,2,1:T(8,128)(2,1)S(1)}, u32[]{:S(2)}, u32[]{:S(2)}) %collective-permute-start) | collective-permute-done | bytes 180256 | tf_op jit(solution)/shard_map/while/body/eval_jaxpr/ppermute | solution.py:19
  245.5 7.1 %collective-permute-done = bf16[128,2,352]{0,2,1:T(8,128)(2,1)S(1)} collective-permute-done((bf16[128,2,352]{0,2,1:T(8,128)(2,1)}, bf16[128,2,352]{0,2,1:T(8,128)(2,1)S(1)}, u32[]{:S(2)}, u32[]{:S(2)}) %collective-permute-start) | collective-permute-done | bytes 180256 | tf_op jit(solution)/shard_map/while/body/eval_jaxpr/ppermute | solution.py:19
  255.9 7.1 %collective-permute-done = bf16[128,2,352]{0,2,1:T(8,128)(2,1)S(1)} collective-permute-done((bf16[128,2,352]{0,2,1:T(8,128)(2,1)}, bf16[128,2,352]{0,2,1:T(8,128)(2,1)S(1)}, u32[]{:S(2)}, u32[]{:S(2)}) %collective-permute-start) | collective-permute-done | bytes 180256 | tf_op jit(solution)/shard_map/while/body/eval_jaxpr/ppermute | solution.py:19
  266.3 7.1 %collective-permute-done = bf16[128,2,352]{0,2,1:T(8,128)(2,1)S(1)} collective-permute-done((bf16[128,2,352]{0,2,1:T(8,128)(2,1)}, bf16[128,2,352]{0,2,1:T(8,128)(2,1)S(1)}, u32[]{:S(2)}, u32[]{:S(2)}) %collective-permute-start) | collective-permute-done | bytes 180256 | tf_op jit(solution)/shard_map/while/body/eval_jaxpr/ppermute | solution.py:19
  276.8 7.1 %collective-permute-done = bf16[128,2,352]{0,2,1:T(8,128)(2,1)S(1)} collective-permute-done((bf16[128,2,352]{0,2,1:T(8,128)(2,1)}, bf16[128,2,352]{0,2,1:T(8,128)(2,1)S(1)}, u32[]{:S(2)}, u32[]{:S(2)}) %collective-permute-start) | collective-permute-done | bytes 180256 | tf_op jit(solution)/shard_map/while/body/eval_jaxpr/ppermute | solution.py:19
  287.2 7.1 %collective-permute-done = bf16[128,2,352]{0,2,1:T(8,128)(2,1)S(1)} collective-permute-done((bf16[128,2,352]{0,2,1:T(8,128)(2,1)}, bf16[128,2,352]{0,2,1:T(8,128)(2,1)S(1)}, u32[]{:S(2)}, u32[]{:S(2)}) %collective-permute-start) | collective-permute-done | bytes 180256 | tf_op jit(solution)/shard_map/while/body/eval_jaxpr/ppermute | solution.py:19
  297.6 7.1 %collective-permute-done = bf16[128,2,352]{0,2,1:T(8,128)(2,1)S(1)} collective-permute-done((bf16[128,2,352]{0,2,1:T(8,128)(2,1)}, bf16[128,2,352]{0,2,1:T(8,128)(2,1)S(1)}, u32[]{:S(2)}, u32[]{:S(2)}) %collective-permute-start) | collective-permute-done | bytes 180256 | tf_op jit(solution)/shard_map/while/body/eval_jaxpr/ppermute | solution.py:19
  308.0 7.1 %collective-permute-done = bf16[128,2,352]{0,2,1:T(8,128)(2,1)S(1)} collective-permute-done((bf16[128,2,352]{0,2,1:T(8,128)(2,1)}, bf16[128,2,352]{0,2,1:T(8,128)(2,1)S(1)}, u32[]{:S(2)}, u32[]{:S(2)}) %collective-permute-start) | collective-permute-done | bytes 180256 | tf_op jit(solution)/shard_map/while/body/eval_jaxpr/ppermute | solution.py:19
  318.5 7.1 %collective-permute-done = bf16[128,2,352]{0,2,1:T(8,128)(2,1)S(1)} collective-permute-done((bf16[128,2,352]{0,2,1:T(8,128)(2,1)}, bf16[128,2,352]{0,2,1:T(8,128)(2,1)S(1)}, u32[]{:S(2)}, u32[]{:S(2)}) %collective-permute-start) | collective-permute-done | bytes 180256 | tf_op jit(solution)/shard_map/while/body/eval_jaxpr/ppermute | solution.py:19
  328.9 7.1 %collective-permute-done = bf16[128,2,352]{0,2,1:T(8,128)(2,1)S(1)} collective-permute-done((bf16[128,2,352]{0,2,1:T(8,128)(2,1)}, bf16[128,2,352]{0,2,1:T(8,128)(2,1)S(1)}, u32[]{:S(2)}, u32[]{:S(2)}) %collective-permute-start) | collective-permute-done | bytes 180256 | tf_op jit(solution)/shard_map/while/body/eval_jaxpr/ppermute | solution.py:19
  339.3 7.1 %collective-permute-done = bf16[128,2,352]{0,2,1:T(8,128)(2,1)S(1)} collective-permute-done((bf16[128,2,352]{0,2,1:T(8,128)(2,1)}, bf16[128,2,352]{0,2,1:T(8,128)(2,1)S(1)}, u32[]{:S(2)}, u32[]{:S(2)}) %collective-permute-start) | collective-permute-done | bytes 180256 | tf_op jit(solution)/shard_map/while/body/eval_jaxpr/ppermute | solution.py:19
  349.7 7.1 %collective-permute-done = bf16[128,2,352]{0,2,1:T(8,128)(2,1)S(1)} collective-permute-done((bf16[128,2,352]{0,2,1:T(8,128)(2,1)}, bf16[128,2,352]{0,2,1:T(8,128)(2,1)S(1)}, u32[]{:S(2)}, u32[]{:S(2)}) %collective-permute-start) | collective-permute-done | bytes 180256 | tf_op jit(solution)/shard_map/while/body/eval_jaxpr/ppermute | solution.py:19
  360.1 7.1 %collective-permute-done = bf16[128,2,352]{0,2,1:T(8,128)(2,1)S(1)} collective-permute-done((bf16[128,2,352]{0,2,1:T(8,128)(2,1)}, bf16[128,2,352]{0,2,1:T(8,128)(2,1)S(1)}, u32[]{:S(2)}, u32[]{:S(2)}) %collective-permute-start) | collective-permute-done | bytes 180256 | tf_op jit(solution)/shard_map/while/body/eval_jaxpr/ppermute | solution.py:19
  370.6 7.1 %collective-permute-done = bf16[128,2,352]{0,2,1:T(8,128)(2,1)S(1)} collective-permute-done((bf16[128,2,352]{0,2,1:T(8,128)(2,1)}, bf16[128,2,352]{0,2,1:T(8,128)(2,1)S(1)}, u32[]{:S(2)}, u32[]{:S(2)}) %collective-permute-start) | collective-permute-done | bytes 180256 | tf_op jit(solution)/shard_map/while/body/eval_jaxpr/ppermute | solution.py:19
  381.6 61.8 %all-reduce.5.cloned.1.call-done = bf16[128,1408]{0,1:T(8,128)(2,1)} async-done(((bf16[128,1408]{0,1:T(8,128)(2,1)}), bf16[128,1408]{0,1:T(8,128)(2,1)}) %all-reduce.5.cloned.1.call-update) | async-done | bytes 360464 | tf_op jit(solution)/shard_map/psum | solution.py:65
  (252 shorter events, 97.9 us)
Async XLA Ops:
  6.5 66.6 %all-reduce.3.cloned.1.call-start = ((), (), s32[]{:S(2)}) async-start(), calls=%async_computation.3 | async-start | bytes 1441792 | tf_op jit(solution)/shard_map/psum | solution.py:65
  21.6 86.9 %reduce-scatter.4.cloned.1.call-start = ((), (), s32[]{:S(2)}) async-start(), calls=%async_computation.5 | async-start | bytes 450560
  84.8 26.9 %all-to-all-start = ((s32[64,1,64]{2,1,0:T(1,128)}), s32[64,1,64]{2,1,0:T(1,128)S(1)}, u32[]{:S(2)}, u32[]{:S(2)}) async-start(s32[64,1,64]{2,1,0:T(1,128)} %compare_select_fusion), calls=%async_computation | async-start | bytes 65536 | tf_op jit(solution)/shard_map/all_to_all | solution.py:134
  111.6 10.7 %copy-start.6 = (s32[16]{0:T(128)S(1)}, s32[16]{0:T(128)}, u32[]{:S(2)}) copy-start(s32[16]{0:T(128)} %param.21) | copy-start | bytes 196
  111.7 82.1 %copy-start.5 = (bf16[128,352]{0,1:T(8,128)(2,1)S(1)}, bf16[128,352]{0,1:T(8,128)(2,1)}, u32[]{:S(2)}) copy-start(bf16[128,352]{0,1:T(8,128)(2,1)} %param.20) | copy-start | bytes 270340
  111.7 82.0 %all-to-all-start.1 = ((bf16[64,64,352]{2,1,0:T(8,128)(2,1)}), bf16[64,64,352]{2,1,0:T(8,128)(2,1)}, u32[]{:S(2)}, u32[]{:S(2)}) async-start(bf16[64,64,352]{2,1,0:T(8,128)(2,1)} %broadcast_select_fusion), calls=%async_computation.1 | async-start | bytes 6291456 | tf_op jit(solution)/shard_map/all_to_all | solution.py:133
  122.3 321.1 %all-reduce.5.cloned.1.call-start = ((), (), s32[]{:S(2)}) async-start(), calls=%async_computation.4 | async-start | bytes 720896 | tf_op jit(solution)/shard_map/psum | solution.py:65
  212.2 9.1 %collective-permute-start = (bf16[128,2,352]{0,2,1:T(8,128)(2,1)}, bf16[128,2,352]{0,2,1:T(8,128)(2,1)S(1)}, u32[]{:S(2)}, u32[]{:S(2)}) collective-permute-start(bf16[128,2,352]{0,2,1:T(8,128)(2,1)} %get-tuple-element.455), channel_id=1, source_target_pairs={{0,4},{4,8},{8,12},{12,16},{16,20},{20,24},{24,28},{28,32},{32,36}... | collective-permute-start | bytes 540680 | tf_op jit(solution)/shard_map/while/body/eval_jaxpr/ppermute | solution.py:19
  222.6 9.1 %collective-permute-start = (bf16[128,2,352]{0,2,1:T(8,128)(2,1)}, bf16[128,2,352]{0,2,1:T(8,128)(2,1)S(1)}, u32[]{:S(2)}, u32[]{:S(2)}) collective-permute-start(bf16[128,2,352]{0,2,1:T(8,128)(2,1)} %get-tuple-element.455), channel_id=1, source_target_pairs={{0,4},{4,8},{8,12},{12,16},{16,20},{20,24},{24,28},{28,32},{32,36}... | collective-permute-start | bytes 540680 | tf_op jit(solution)/shard_map/while/body/eval_jaxpr/ppermute | solution.py:19
  233.1 9.1 %collective-permute-start = (bf16[128,2,352]{0,2,1:T(8,128)(2,1)}, bf16[128,2,352]{0,2,1:T(8,128)(2,1)S(1)}, u32[]{:S(2)}, u32[]{:S(2)}) collective-permute-start(bf16[128,2,352]{0,2,1:T(8,128)(2,1)} %get-tuple-element.455), channel_id=1, source_target_pairs={{0,4},{4,8},{8,12},{12,16},{16,20},{20,24},{24,28},{28,32},{32,36}... | collective-permute-start | bytes 540680 | tf_op jit(solution)/shard_map/while/body/eval_jaxpr/ppermute | solution.py:19
  243.5 9.1 %collective-permute-start = (bf16[128,2,352]{0,2,1:T(8,128)(2,1)}, bf16[128,2,352]{0,2,1:T(8,128)(2,1)S(1)}, u32[]{:S(2)}, u32[]{:S(2)}) collective-permute-start(bf16[128,2,352]{0,2,1:T(8,128)(2,1)} %get-tuple-element.455), channel_id=1, source_target_pairs={{0,4},{4,8},{8,12},{12,16},{16,20},{20,24},{24,28},{28,32},{32,36}... | collective-permute-start | bytes 540680 | tf_op jit(solution)/shard_map/while/body/eval_jaxpr/ppermute | solution.py:19
  253.9 9.1 %collective-permute-start = (bf16[128,2,352]{0,2,1:T(8,128)(2,1)}, bf16[128,2,352]{0,2,1:T(8,128)(2,1)S(1)}, u32[]{:S(2)}, u32[]{:S(2)}) collective-permute-start(bf16[128,2,352]{0,2,1:T(8,128)(2,1)} %get-tuple-element.455), channel_id=1, source_target_pairs={{0,4},{4,8},{8,12},{12,16},{16,20},{20,24},{24,28},{28,32},{32,36}... | collective-permute-start | bytes 540680 | tf_op jit(solution)/shard_map/while/body/eval_jaxpr/ppermute | solution.py:19
  264.3 9.1 %collective-permute-start = (bf16[128,2,352]{0,2,1:T(8,128)(2,1)}, bf16[128,2,352]{0,2,1:T(8,128)(2,1)S(1)}, u32[]{:S(2)}, u32[]{:S(2)}) collective-permute-start(bf16[128,2,352]{0,2,1:T(8,128)(2,1)} %get-tuple-element.455), channel_id=1, source_target_pairs={{0,4},{4,8},{8,12},{12,16},{16,20},{20,24},{24,28},{28,32},{32,36}... | collective-permute-start | bytes 540680 | tf_op jit(solution)/shard_map/while/body/eval_jaxpr/ppermute | solution.py:19
  274.7 9.1 %collective-permute-start = (bf16[128,2,352]{0,2,1:T(8,128)(2,1)}, bf16[128,2,352]{0,2,1:T(8,128)(2,1)S(1)}, u32[]{:S(2)}, u32[]{:S(2)}) collective-permute-start(bf16[128,2,352]{0,2,1:T(8,128)(2,1)} %get-tuple-element.455), channel_id=1, source_target_pairs={{0,4},{4,8},{8,12},{12,16},{16,20},{20,24},{24,28},{28,32},{32,36}... | collective-permute-start | bytes 540680 | tf_op jit(solution)/shard_map/while/body/eval_jaxpr/ppermute | solution.py:19
  285.2 9.1 %collective-permute-start = (bf16[128,2,352]{0,2,1:T(8,128)(2,1)}, bf16[128,2,352]{0,2,1:T(8,128)(2,1)S(1)}, u32[]{:S(2)}, u32[]{:S(2)}) collective-permute-start(bf16[128,2,352]{0,2,1:T(8,128)(2,1)} %get-tuple-element.455), channel_id=1, source_target_pairs={{0,4},{4,8},{8,12},{12,16},{16,20},{20,24},{24,28},{28,32},{32,36}... | collective-permute-start | bytes 540680 | tf_op jit(solution)/shard_map/while/body/eval_jaxpr/ppermute | solution.py:19
  295.6 9.1 %collective-permute-start = (bf16[128,2,352]{0,2,1:T(8,128)(2,1)}, bf16[128,2,352]{0,2,1:T(8,128)(2,1)S(1)}, u32[]{:S(2)}, u32[]{:S(2)}) collective-permute-start(bf16[128,2,352]{0,2,1:T(8,128)(2,1)} %get-tuple-element.455), channel_id=1, source_target_pairs={{0,4},{4,8},{8,12},{12,16},{16,20},{20,24},{24,28},{28,32},{32,36}... | collective-permute-start | bytes 540680 | tf_op jit(solution)/shard_map/while/body/eval_jaxpr/ppermute | solution.py:19
  306.0 9.1 %collective-permute-start = (bf16[128,2,352]{0,2,1:T(8,128)(2,1)}, bf16[128,2,352]{0,2,1:T(8,128)(2,1)S(1)}, u32[]{:S(2)}, u32[]{:S(2)}) collective-permute-start(bf16[128,2,352]{0,2,1:T(8,128)(2,1)} %get-tuple-element.455), channel_id=1, source_target_pairs={{0,4},{4,8},{8,12},{12,16},{16,20},{20,24},{24,28},{28,32},{32,36}... | collective-permute-start | bytes 540680 | tf_op jit(solution)/shard_map/while/body/eval_jaxpr/ppermute | solution.py:19
  316.4 9.1 %collective-permute-start = (bf16[128,2,352]{0,2,1:T(8,128)(2,1)}, bf16[128,2,352]{0,2,1:T(8,128)(2,1)S(1)}, u32[]{:S(2)}, u32[]{:S(2)}) collective-permute-start(bf16[128,2,352]{0,2,1:T(8,128)(2,1)} %get-tuple-element.455), channel_id=1, source_target_pairs={{0,4},{4,8},{8,12},{12,16},{16,20},{20,24},{24,28},{28,32},{32,36}... | collective-permute-start | bytes 540680 | tf_op jit(solution)/shard_map/while/body/eval_jaxpr/ppermute | solution.py:19
  326.8 9.1 %collective-permute-start = (bf16[128,2,352]{0,2,1:T(8,128)(2,1)}, bf16[128,2,352]{0,2,1:T(8,128)(2,1)S(1)}, u32[]{:S(2)}, u32[]{:S(2)}) collective-permute-start(bf16[128,2,352]{0,2,1:T(8,128)(2,1)} %get-tuple-element.455), channel_id=1, source_target_pairs={{0,4},{4,8},{8,12},{12,16},{16,20},{20,24},{24,28},{28,32},{32,36}... | collective-permute-start | bytes 540680 | tf_op jit(solution)/shard_map/while/body/eval_jaxpr/ppermute | solution.py:19
  337.3 9.1 %collective-permute-start = (bf16[128,2,352]{0,2,1:T(8,128)(2,1)}, bf16[128,2,352]{0,2,1:T(8,128)(2,1)S(1)}, u32[]{:S(2)}, u32[]{:S(2)}) collective-permute-start(bf16[128,2,352]{0,2,1:T(8,128)(2,1)} %get-tuple-element.455), channel_id=1, source_target_pairs={{0,4},{4,8},{8,12},{12,16},{16,20},{20,24},{24,28},{28,32},{32,36}... | collective-permute-start | bytes 540680 | tf_op jit(solution)/shard_map/while/body/eval_jaxpr/ppermute | solution.py:19
  347.7 9.1 %collective-permute-start = (bf16[128,2,352]{0,2,1:T(8,128)(2,1)}, bf16[128,2,352]{0,2,1:T(8,128)(2,1)S(1)}, u32[]{:S(2)}, u32[]{:S(2)}) collective-permute-start(bf16[128,2,352]{0,2,1:T(8,128)(2,1)} %get-tuple-element.455), channel_id=1, source_target_pairs={{0,4},{4,8},{8,12},{12,16},{16,20},{20,24},{24,28},{28,32},{32,36}... | collective-permute-start | bytes 540680 | tf_op jit(solution)/shard_map/while/body/eval_jaxpr/ppermute | solution.py:19
  358.1 9.1 %collective-permute-start = (bf16[128,2,352]{0,2,1:T(8,128)(2,1)}, bf16[128,2,352]{0,2,1:T(8,128)(2,1)S(1)}, u32[]{:S(2)}, u32[]{:S(2)}) collective-permute-start(bf16[128,2,352]{0,2,1:T(8,128)(2,1)} %get-tuple-element.455), channel_id=1, source_target_pairs={{0,4},{4,8},{8,12},{12,16},{16,20},{20,24},{24,28},{28,32},{32,36}... | collective-permute-start | bytes 540680 | tf_op jit(solution)/shard_map/while/body/eval_jaxpr/ppermute | solution.py:19
  368.5 9.1 %collective-permute-start = (bf16[128,2,352]{0,2,1:T(8,128)(2,1)}, bf16[128,2,352]{0,2,1:T(8,128)(2,1)S(1)}, u32[]{:S(2)}, u32[]{:S(2)}) collective-permute-start(bf16[128,2,352]{0,2,1:T(8,128)(2,1)} %get-tuple-element.455), channel_id=1, source_target_pairs={{0,4},{4,8},{8,12},{12,16},{16,20},{20,24},{24,28},{28,32},{32,36}... | collective-permute-start | bytes 540680 | tf_op jit(solution)/shard_map/while/body/eval_jaxpr/ppermute | solution.py:19
  379.0 64.4 %copy-start.4 = (bf16[128,1408]{0,1:T(8,128)(2,1)S(1)}, bf16[128,1408]{0,1:T(8,128)(2,1)}, u32[]{:S(2)}) copy-start(bf16[128,1408]{0,1:T(8,128)(2,1)} %copy-done.3) | copy-start | bytes 1081348
  (4 other events, 12.2 us)
Sparse Core Ops, SparseCore 0:
  21.7 51.3 all-reduce.2
  84.2 24.2 reduce-scatter.3
  381.7 61.6 all-reduce.4
where the time goes:
time: 456 us; the launch traced here: 454 us
  waiting for transfers between devices  303 us (66%)
  starting transfers between devices  51.6 us (11%)
  matrix products  27.3 us (6%)
  local copies, waits for them, and re-layouts  21 us (5%)
  other arithmetic  19 us (4%)
  between operations  17.8 us (4%)
  blocking collectives  12.9 us (3%)
    ppermute x16, waiting for transfers between devices, passed_along(): return lax.ppermute(x, axis, pairs)  114 us
    psum x2, waiting for transfers between devices, mix_heads(): lax.psum(partial_value.astype(jnp.bfloat16), 'tp').astype(jnp.float32)  109 us
    all_to_all x1, waiting for transfers between devices, local(): lax.all_to_all(send_rows, 'seq', split_axis=0, concat_axis=0, tiled=True)  66.8 us
    ppermute x16, starting transfers between devices, passed_along(): return lax.ppermute(x, axis, pairs)  30.5 us
    unnamed x4, waiting for transfers between devices  13.4 us
    all_gather x1, blocking collectives, local(): prompt_in = lax.all_gather(prompt_share, 'tp', axis=1, tiled=True)  12.9 us
    while x32, local copies, waits for them, and re-layouts  10.7 us
    all_to_all x1, starting transfers between devices, local(): lax.all_to_all(send_rows, 'seq', split_axis=0, concat_axis=0, tiled=True)  10.6 us
  transfers between devices with their start and end apart: 21, of which 20 were waited for; matrix products, arithmetic and copies ran while one was open for 2% of the time, Pallas kernels for 0%

commit v1 on v0

v1 whole, which is shorter than its diff:
```python
import jax
import jax.numpy as jnp
import numpy as np
from jax import lax
from jax.sharding import Mesh
from jax.sharding import PartitionSpec as P

HEAD = 88
MAXGRID = 16
BLOCK = 128
MERGED = 64
EPSILON = 1e-06
MASKED = -1e30
SCALE = HEAD ** (-0.5)
BF = jnp.bfloat16
F32 = jnp.float32


def ahead(x, axis, by):
    count = lax.axis_size(axis)
    return lax.ppermute(x, axis, [(i, i + by) for i in range(count - by)])


def around(x, axis, by):
    count = lax.axis_size(axis)
    return lax.ppermute(x, axis, [(i, (i + by) % count) for i in range(count)])


def gather_ring(x, axis):
    count = lax.axis_size(axis)
    me = lax.axis_index(axis)
    out = jnp.zeros((count,) + x.shape, x.dtype)
    out = lax.dynamic_update_index_in_dim(out, x, me, 0)
    for by in range(1, count):
        got = around(x, axis, by)
        out = lax.dynamic_update_index_in_dim(out, got, (me - by) % count, 0)
    return out


def normalize(values, axis=-1):
    values = values.astype(F32)
    centre = jnp.mean(values, axis=axis, keepdims=True)
    shifted = values - centre
    spread = jnp.mean(shifted * shifted, axis=axis, keepdims=True)
    return (shifted * lax.rsqrt(spread + EPSILON)).astype(BF)


def vision_share(picture, half_grid, vision_qkv, vision_out):
    width, _, local_width = vision_qkv.shape
    heads = local_width // HEAD
    count = picture.shape[0]
    normed = normalize(picture)
    projected = jnp.dot(
        normed, vision_qkv.reshape(width, 3 * local_width), preferred_element_type=F32
    )
    projected = projected.astype(BF).reshape(count, 3, heads, HEAD)
    scores = (
        jnp.einsum("qhe,khe->hqk", projected[:, 0], projected[:, 1], preferred_element_type=F32)
        * SCALE
    )
    cells = jnp.arange(count, dtype=jnp.int32)
    usable = (cells // MAXGRID < 2 * half_grid[0]) & (cells % MAXGRID < 2 * half_grid[1])
    allowed = usable[None, None, :]
    scores = jnp.where(allowed, scores, MASKED)
    row_max = jnp.max(scores, axis=-1, keepdims=True)
    expons = jnp.where(allowed, jnp.exp(scores - row_max), 0.0)
    row_total = jnp.sum(expons, axis=-1)
    summed = jnp.einsum(
        "hqk,khe->qhe", expons.astype(BF), projected[:, 2], preferred_element_type=F32
    )
    context = (summed / jnp.transpose(row_total)[:, :, None]).astype(BF)
    context = context.reshape(8, 2, 8, 2, local_width).transpose(1, 3, 0, 2, 4)
    context = context.reshape(count, local_width)
    share = jnp.dot(context, vision_out, preferred_element_type=F32).astype(BF)
    return share.reshape(4, MERGED, width)


def local(
    patches,
    picture_grid,
    vision_qkv,
    vision_out,
    merge_weight,
    picture_block,
    picture_offset,
    tokens,
    prompt_lengths,
    text_qkv,
    text_out,
):
    width = patches.shape[2]
    local_width = vision_qkv.shape[2]
    heads = local_width // HEAD
    z = lax.axis_index("z")
    c = lax.axis_index("c")
    t = lax.axis_index("t")
    half_grid = picture_grid[0]
    block = picture_block[0]
    offset = picture_offset[0]
    picture = patches[0]

    token_parts = gather_ring(tokens, "t")
    out_full = gather_ring(text_out, "t")

    shares = vision_share(picture, half_grid, vision_qkv, vision_out)
    shares = lax.all_to_all(shares, "t", 0, 0, tiled=True)
    own = picture.reshape(8, 2, 8, 2, width).transpose(1, 3, 0, 2, 4).reshape(4, MERGED, width)
    own = lax.dynamic_index_in_dim(own, t, 0, keepdims=False)
    hidden = own.astype(F32) + jnp.sum(shares.astype(F32), axis=0)
    merged = jnp.dot(normalize(hidden), merge_weight[0], preferred_element_type=F32).astype(BF)

    facts = jnp.stack([block, offset, half_grid[0], half_grid[1], jnp.int32(1)])
    facts = jnp.where(t == 0, facts, 0).astype(BF)
    facts = jnp.pad(facts, (0, 123))
    rows = jnp.concatenate([merged, jnp.broadcast_to(facts, (MERGED, 128))], axis=1)
    wide = width + 128
    rows = rows.reshape(1, 4, 16, wide)
    to_y = (block % 8) // 2
    routed = jnp.where(jnp.arange(4)[:, None, None, None] == to_y, rows, jnp.zeros((), BF))
    got = lax.all_to_all(routed.reshape(16, 16, wide), ("y", "t"), 0, 0, tiled=True)
    got = jnp.sum(got.reshape(4, 4, 16, wide).astype(F32), axis=1).astype(BF)
    got = lax.all_gather(got, "c", axis=0, tiled=True)
    to = got[:, 0, width].astype(F32).astype(jnp.int32)
    there = got[:, 0, width + 4] > 0
    pick = there & (to % 2 == c)
    pick = pick[None, :] & (to[None, :] // 8 == jnp.arange(8)[:, None])
    routed = jnp.einsum("zk,krd->zrd", pick.astype(BF), got, preferred_element_type=F32).astype(BF)
    got = lax.all_to_all(routed, "z", 0, 0, tiled=True)
    got = jnp.sum(got.astype(F32), axis=0).astype(BF)
    got = gather_ring(got, "t").reshape(MERGED, wide)

    facts = got[0, width:].astype(F32).astype(jnp.int32)
    cells = jnp.arange(MERGED, dtype=jnp.int32)
    target = facts[1] + (cells // 8) * facts[3] + cells % 8
    usable = (cells // 8 < facts[2]) & (cells % 8 < facts[3]) & (facts[4] > 0)
    target = jnp.where(usable, target, -1)
    table = jnp.arange(BLOCK, dtype=jnp.int32)[:, None] == target[None, :]
    placed = jnp.dot(table.astype(BF), got[:, :width], preferred_element_type=F32).astype(BF)
    covered = jnp.any(table, axis=1)
    own_tokens = token_parts.transpose(1, 0, 2).reshape(BLOCK, width)
    prompt_in = jnp.where(covered[:, None], placed, own_tokens)

    normed = normalize(prompt_in)
    projected = jnp.einsum("td,dce->cet", normed, text_qkv, preferred_element_type=F32).astype(BF)
    projected = projected.reshape(3, heads, HEAD, BLOCK).transpose(1, 0, 2, 3)
    projected = lax.all_to_all(projected, "y", 0, 0, tiled=True)
    queries = projected[:, 0]
    pairs = projected[:, 1:]
    pairs = jnp.stack([pairs, ahead(pairs, "z", 1), ahead(pairs, "z", 2)])
    pairs = lax.all_gather(pairs, "c", axis=0, tiled=False)
    keys = pairs[:, :, :, 0].transpose(3, 0, 1, 2, 4).reshape(HEAD, -1)
    values = pairs[:, :, :, 1].transpose(3, 0, 1, 2, 4).reshape(HEAD, -1)
    lanes = jnp.arange(BLOCK, dtype=jnp.int32)
    planes = jnp.arange(3, dtype=jnp.int32)[None, :, None, None]
    rows_y = jnp.arange(4, dtype=jnp.int32)
    cores = jnp.arange(2, dtype=jnp.int32)[:, None, None, None]
    key_pos = (z - planes) * 1024 + rows_y[None, None, :, None] * 256 + cores * 128 + lanes
    key_pos = key_pos.reshape(-1)
    query_pos = (z * 1024 + rows_y[:, None] * 256 + c * 128 + lanes[None, :]).reshape(-1)
    ends = jnp.cumsum(prompt_lengths)
    starts = jnp.max(jnp.where(ends[None, :] <= query_pos[:, None], ends[None, :], 0), axis=1)
    visible = (key_pos[None, :] <= query_pos[:, None]) & (key_pos[None, :] >= starts[:, None])
    queries = queries.transpose(0, 2, 1).reshape(4 * BLOCK, HEAD)
    scores = jnp.dot(queries, keys, preferred_element_type=F32) * SCALE
    scores = jnp.where(visible, scores, MASKED)
    top = jnp.max(scores, axis=1, keepdims=True)
    expons = jnp.where(visible, jnp.exp(scores - top), 0.0)
    total = jnp.sum(expons, axis=1, keepdims=True)
    summed = lax.dot_general(
        expons.astype(BF), values, (((1,), (1,)), ((), ())), preferred_element_type=F32
    )
    context = (summed / total).astype(BF).reshape(4, BLOCK, HEAD).transpose(0, 2, 1)
    sent = jnp.broadcast_to(context[None], (4, 4, HEAD, BLOCK)).reshape(16, HEAD, BLOCK)
    context = lax.all_to_all(sent, ("t", "y"), 0, 0, tiled=True).reshape(width, BLOCK)
    gained = lax.dot_general(
        context, out_full.reshape(width, width), (((0,), (0,)), ((), ())), preferred_element_type=F32
    )
    return (prompt_in.astype(F32) + gained).astype(BF)


def solution(mesh):
    split = Mesh(np.asarray(mesh.devices).reshape(8, 4, 2, 4), ("z", "y", "c", "t"))
    seq = ("z", "y", "c")
    placed = (
        P(seq, None, None),
        P(seq, None),
        P(None, None, "t"),
        P("t", None),
        P("t", None, None),
        P(seq),
        P(seq),
        P(seq, "t"),
        P(),
        P(None, None, "t"),
        P("t", None),
    )
    return jax.shard_map(
        local, mesh=split, in_specs=placed, out_specs=P(seq, None), check_vma=False
    )
```

time: 456 us -> 230 us (0.50)
  waiting for transfers between devices: 303 us -> 79.3 us
  local copies, waits for them, and re-layouts: 21 us -> 39.7 us
  blocking collectives: 12.9 us -> 2.09 us
  starting transfers between devices: 51.6 us -> 45.7 us
    psum x2 -> x0, waiting for transfers between devices: 109 us -> none  [mix_heads(): lax.psum(partial_value.astype(jnp.bfloat16), 'tp').astype(jnp.float32)]
    ppermute x16 -> x11, waiting for transfers between devices: 114 us -> 16.4 us  [the longest x9 12.5 us: around(): return lax.ppermute(x, axis, [(i, (i + by) % count) for i in range(count)])]
    all_to_all x2 -> x5, waiting for transfers between devices: 66.8 us -> 51.2 us  [the longest x1 22.6 us: local(): shares = lax.all_to_all(shares, 't', 0, 0, tiled=True)]
    unnamed x4 -> x1, waiting for transfers between devices: 13.4 us -> 0.02 us
    dynamic_update_slice x0 -> x12, local copies, waits for them, and re-layouts: none -> 13.1 us  [the longest x9 11.4 us: gather_ring(): out = lax.dynamic_update_index_in_dim(out, got, (me - by) % count, 0)]
    ppermute x16 -> x11, starting transfers between devices: 30.5 us -> 17.8 us  [the longest x9 9.87 us: around(): return lax.ppermute(x, axis, [(i, (i + by) % count) for i in range(count)])]
    all_gather x0 -> x1, waiting for transfers between devices: none -> 11.7 us  [local(): pairs = lax.all_gather(pairs, 'c', axis=0, tiled=False)]
    all_gather x1, blocking collectives: 12.9 us -> 2.09 us  [local(): got = lax.all_gather(got, 'c', axis=0, tiled=True)]
  transfers between devices with their start and end apart: 21 -> 17, of which waited for: 20 -> 10; matrix products, arithmetic and copies ran while one was open for 2% -> 34% of each run, Pallas kernels for 0% -> 0%
where the time goes in v1:
time: 230 us; the launch traced here: 228 us
  waiting for transfers between devices  79.3 us (34%)
  starting transfers between devices  45.7 us (20%)
  local copies, waits for them, and re-layouts  39.7 us (17%)
  matrix products  28.6 us (12%)
  between operations  16.9 us (7%)
  other arithmetic  15.2 us (7%)
    all_to_all x1, waiting for transfers between devices, local(): shares = lax.all_to_all(shares, 't', 0, 0, tiled=True)  22.6 us
    ppermute x9, waiting for transfers between devices, around(): return lax.ppermute(x, axis, [(i, (i + by) % count) for i in range(count)])  12.5 us
    all_gather x1, waiting for transfers between devices, local(): pairs = lax.all_gather(pairs, 'c', axis=0, tiled=False)  11.7 us
    dynamic_update_slice x9, local copies, waits for them, and re-layouts, gather_ring(): out = lax.dynamic_update_index_in_dim(out, got, (me - by) % count, 0)  11.4 us
    all_to_all x1, waiting for transfers between devices, local(): lax.all_to_all(routed.reshape(16, 16, wide), ('y', 't'), 0, 0, tiled=True)  10.2 us
    ppermute x9, starting transfers between devices, around(): return lax.ppermute(x, axis, [(i, (i + by) % count) for i in range(count)])  9.87 us
    all_to_all x1, starting transfers between devices, local(): got = lax.all_to_all(routed, 'z', 0, 0, tiled=True)  8.11 us
    ppermute x2, starting transfers between devices, ahead(): return lax.ppermute(x, axis, [(i, i + by) for i in range(count - by)])  7.95 us
  transfers between devices with their start and end apart: 17, of which 10 were waited for; matrix products, arithmetic and copies ran while one was open for 34% of the time, Pallas kernels for 0%

profile of v1, /device:TPU:64, one launch (start us, length us, event | category | flops | bytes accessed | tf_op | source)
XLA Modules:
  0.0 227.5 jit_solution(9898050453339494297)
XLA Ops:
  8.0 2.7 %collective-permute-start.4 = (bf16[128,352]{0,1:T(8,128)(2,1)}, bf16[128,352]{0,1:T(8,128)(2,1)}, u32[]{:S(2)}, u32[]{:S(2)}) collective-permute-start(bf16[128,352]{0,1:T(8,128)(2,1)} %param.18), channel_id=1, source_target_pairs={{0,2},{1,3},{2,0},{3,1},{4,6},{5,7},{6,4},{7,5},{8,10},{9,11},{10,... | collective-permute-start | bytes 270344 | tf_op jit(solution)/shard_map/ppermute | solution.py:26
  30.1 4.2 %all-to-all-start = ((bf16[4,64,1408]{2,1,0:T(8,128)(2,1)}), bf16[4,64,1408]{2,1,0:T(8,128)(2,1)}, u32[]{:S(2)}, u32[]{:S(2)}) async-start(bf16[4,64,1408]{2,1,0:T(8,128)(2,1)} %bitcast.166), calls=%async_computation | async-start | bytes 1441792 | tf_op jit(solution)/shard_map/all_to_all | solution.py:106
  35.0 2.8 %reshape_squeeze.3 = bf16[8,2,8,2,1408]{4,3,2,1,0:T(2,128)(2,1)} reshape(bf16[1,256,1408]{2,1,0:T(8,128)(2,1)} %param.11) | data formatting | bytes 1441792 | tf_op jit(solution)/shard_map/reshape;squeeze | solution.py:107
  43.5 22.6 %all-to-all-done = bf16[4,64,1408]{2,1,0:T(8,128)(2,1)} async-done(((bf16[4,64,1408]{2,1,0:T(8,128)(2,1)}), bf16[4,64,1408]{2,1,0:T(8,128)(2,1)}, u32[]{:S(2)}, u32[]{:S(2)}) %all-to-all-start) | async-done | bytes 720928 | tf_op jit(solution)/shard_map/all_to_all | solution.py:106
  69.6 3.0 %fusion.11 = bf16[64,1408]{1,0:T(8,128)(2,1)S(1)} fusion(bf16[1,1408,1408]{2,1,0:T(8,128)(2,1)} %param.15, f32[64,1408]{1,0:T(8,128)S(1)} %convert_reduce_fusion.1, f32[64]{0:T(128)S(1)} %add_rsqrt_fusion.2, f32[64]{0:T(128)S(1)} %broadcast_multiply_fusion.2, bf16[4,64,1408]{2,1,0:T(8,128)(2,1)} %bitcast.169, s32[]{:T(128)S(6)} %select_n.171), kind=kOutput, calls=%fused_computation.18 | convolution fusion | flops 254296064 | bytes 4686340 | tf_op jit(solution)/shard_map/dot_general | solution.py:110
  73.7 5.3 %all-to-all-start.1 = ((bf16[16,16,1536]{2,1,0:T(8,128)(2,1)}), bf16[16,16,1536]{2,1,0:T(8,128)(2,1)}, u32[]{:S(2)}, u32[]{:S(2)}) async-start(bf16[16,16,1536]{2,1,0:T(8,128)(2,1)} %bitcast_select_fusion), calls=%async_computation.1 | async-start | bytes 1572864 | tf_op jit(solution)/shard_map/all_to_all | solution.py:120
  82.4 10.2 %all-to-all-done.1 = bf16[16,16,1536]{2,1,0:T(8,128)(2,1)} async-done(((bf16[16,16,1536]{2,1,0:T(8,128)(2,1)}), bf16[16,16,1536]{2,1,0:T(8,128)(2,1)}, u32[]{:S(2)}, u32[]{:S(2)}) %all-to-all-start.1) | async-done | bytes 786464 | tf_op jit(solution)/shard_map/all_to_all | solution.py:120
  97.7 8.1 %all-to-all-start.2 = ((bf16[8,16,1536]{2,1,0:T(8,128)(2,1)}), bf16[8,16,1536]{2,1,0:T(8,128)(2,1)S(1)}, u32[]{:S(2)}, u32[]{:S(2)}) async-start(bf16[8,16,1536]{2,1,0:T(8,128)(2,1)} %copy.54), calls=%async_computation.2 | async-start | bytes 786432 | tf_op jit(solution)/shard_map/all_to_all | solution.py:128
  113.3 4.1 %all-to-all-done.2 = bf16[8,16,1536]{2,1,0:T(8,128)(2,1)S(1)} async-done(((bf16[8,16,1536]{2,1,0:T(8,128)(2,1)}), bf16[8,16,1536]{2,1,0:T(8,128)(2,1)S(1)}, u32[]{:S(2)}, u32[]{:S(2)}) %all-to-all-start.2) | async-done | bytes 393248 | tf_op jit(solution)/shard_map/all_to_all | solution.py:128
  119.5 3.3 %collective-permute-done = bf16[16,1536]{1,0:T(8,128)(2,1)S(1)} collective-permute-done((bf16[16,1536]{1,0:T(8,128)(2,1)S(1)}, bf16[16,1536]{1,0:T(8,128)(2,1)S(1)}, u32[]{:S(2)}, u32[]{:S(2)}) %collective-permute-start) | collective-permute-done | bytes 49184 | tf_op jit(solution)/shard_map/ppermute | solution.py:26
  123.7 8.3 %collective-permute-done.2 = bf16[16,1536]{1,0:T(8,128)(2,1)S(1)} collective-permute-done((bf16[16,1536]{1,0:T(8,128)(2,1)S(1)}, bf16[16,1536]{1,0:T(8,128)(2,1)S(1)}, u32[]{:S(2)}, u32[]{:S(2)}) %collective-permute-start.2) | collective-permute-done | bytes 49184 | tf_op jit(solution)/shard_map/ppermute | solution.py:26
  137.7 2.8 %convolution_convert_fusion.4 = bf16[128,3,352]{0,2,1:T(8,128)(2,1)S(1)} fusion(bf16[1408,3,352]{0,2,1:T(8,128)(2,1)} %param.20, f32[128,1408]{1,0:T(8,128)S(1)} %get-tuple-element.16, f32[128]{0:T(128)S(1)} %add_rsqrt_fusion.1, f32[128]{0:T(128)S(1)} %broadcast_multiply_fusion.1), kind=kOutput, calls=%fused_computation.33 | convolution fusion | flops 381308928 | bytes 3965952 | tf_op jit(solution)/shard_map/td,dce->cet/dot_general | solution.py:144
  141.2 3.4 %all-to-all-start.3 = ((bf16[4,3,88,128]{3,2,1,0:T(8,128)(2,1)}), bf16[4,3,88,128]{3,2,1,0:T(8,128)(2,1)S(1)}, u32[]{:S(2)}, u32[]{:S(2)}) async-start(bf16[4,3,88,128]{3,2,1,0:T(8,128)(2,1)} %bitcast.160), calls=%async_computation.3 | async-start | bytes 540672 | tf_op jit(solution)/shard_map/all_to_all | solution.py:146
  144.8 6.6 %all-to-all-done.3 = bf16[4,3,88,128]{3,2,1,0:T(8,128)(2,1)S(1)} async-done(((bf16[4,3,88,128]{3,2,1,0:T(8,128)(2,1)}), bf16[4,3,88,128]{3,2,1,0:T(8,128)(2,1)S(1)}, u32[]{:S(2)}, u32[]{:S(2)}) %all-to-all-start.3) | async-done | bytes 270368 | tf_op jit(solution)/shard_map/all_to_all | solution.py:146
  151.4 3.4 %collective-permute-start.6 = (bf16[4,2,88,128]{3,2,1,0:T(8,128)(2,1)S(1)}, bf16[4,2,88,128]{3,2,1,0:T(8,128)(2,1)S(1)}, u32[]{:S(2)}, u32[]{:S(2)}) collective-permute-start(bf16[4,2,88,128]{3,2,1,0:T(8,128)(2,1)S(1)} %get-tuple-element.8), channel_id=1, source_target_pairs={{0,32},{32,64},{64,96},{96,128},{128,160},{160,192},{192,224},{1,3... | collective-permute-start | bytes 540680 | tf_op jit(solution)/shard_map/ppermute | solution.py:21
  154.8 4.6 %collective-permute-start.7 = (bf16[4,2,88,128]{3,2,1,0:T(8,128)(2,1)S(1)}, bf16[4,2,88,128]{3,2,1,0:T(8,128)(2,1)S(1)}, u32[]{:S(2)}, u32[]{:S(2)}) collective-permute-start(bf16[4,2,88,128]{3,2,1,0:T(8,128)(2,1)S(1)} %get-tuple-element.8), channel_id=1, source_target_pairs={{0,64},{32,96},{64,128},{96,160},{128,192},{160,224},{1,65},{33,97... | collective-permute-start | bytes 540680 | tf_op jit(solution)/shard_map/ppermute | solution.py:21
  159.5 3.8 %collective-permute-done.6 = bf16[4,2,88,128]{3,2,1,0:T(8,128)(2,1)S(1)} collective-permute-done((bf16[4,2,88,128]{3,2,1,0:T(8,128)(2,1)S(1)}, bf16[4,2,88,128]{3,2,1,0:T(8,128)(2,1)S(1)}, u32[]{:S(2)}, u32[]{:S(2)}) %collective-permute-start.6) | collective-permute-done | bytes 180256 | tf_op jit(solution)/shard_map/ppermute | solution.py:21
  168.8 11.7 %all-gather.3.cloned.1.call-done = bf16[6,4,2,88,128]{4,3,2,1,0:T(8,128)(2,1)} async-done(((bf16[3,4,2,88,128]{4,3,2,1,0:T(8,128)(2,1)}), bf16[6,4,2,88,128]{4,3,2,1,0:T(8,128)(2,1)}) %all-gather.3.cloned.1.call-update) | async-done | bytes 1081360 | tf_op jit(solution)/shard_map/all_gather | solution.py:150
  185.3 2.9 %fusion.1 = (f32[512]{0:T(512)S(1)}, f32[512,3072]{1,0:T(8,128)S(1)}) fusion(s32[3072]{0:T(1024)S(1)} %bitcast.184, s32[512]{0:T(512)S(1)} %select_reduce_fusion, s32[512]{0:T(512)S(1)} %add_bitcast_fusion, bf16[88,3072]{1,0:T(8,128)(2,1)} %reshape.408, bf16[4,3,88,128]{3,2,1,0:T(8,128)(2,1)} %copy-done.4), kind=kOutput, calls=%fused_computation.4 | convolution fusion | flops 286260736 | bytes 6940672 | tf_op jit(solution)/shard_map/dot_general | solution.py:164
  188.2 2.7 %copy-done.2 = f32[512,3072]{1,0:T(8,128)} copy-done((f32[512,3072]{1,0:T(8,128)}, f32[512,3072]{1,0:T(8,128)S(1)}, u32[]{:S(2)}) %copy-start.2) | copy-done | bytes 6291480
  194.4 4.8 %fusion.28 = bf16[512,88]{0,1:T(8,128)(2,1)S(1)} fusion(bf16[88,3072]{1,0:T(8,128)(2,1)} %reshape.409, f32[512,3072]{1,0:T(8,128)} %copy-done.2, f32[512]{0:T(512)S(1)} %get-tuple-element.17, s32[3072]{0:T(1024)S(1)} %bitcast.186, s32[512]{0:T(512)S(1)} %select_reduce_fusion, s32[512]{0:T(512)S(1)} %add_bitcast_fusion, f32[512]{0:T(512)S(1)} %fusion.4), kind=kOutput, calls=%fused_computation.38 | convolution fusion | flops 289497088 | bytes 6942720 | tf_op jit(solution)/shard_map/dot_general | solution.py:169
  200.1 6.8 %all-to-all-start.4 = ((bf16[16,88,128]{2,1,0:T(8,128)(2,1)}), bf16[16,88,128]{2,1,0:T(8,128)(2,1)S(1)}, u32[]{:S(2)}, u32[]{:S(2)}) async-start(bf16[16,88,128]{2,1,0:T(8,128)(2,1)} %bitcast.60), calls=%async_computation.4 | async-start | bytes 720896 | tf_op jit(solution)/shard_map/all_to_all | solution.py:174
  209.1 7.7 %all-to-all-done.4 = bf16[16,88,128]{2,1,0:T(8,128)(2,1)S(1)} async-done(((bf16[16,88,128]{2,1,0:T(8,128)(2,1)}), bf16[16,88,128]{2,1,0:T(8,128)(2,1)S(1)}, u32[]{:S(2)}, u32[]{:S(2)}) %all-to-all-start.4) | async-done | bytes 360480 | tf_op jit(solution)/shard_map/all_to_all | solution.py:174
  216.8 3.9 %fusion.8 = bf16[128,1408]{1,0:T(8,128)(2,1)} fusion(f32[128,1408]{1,0:T(8,128)} %copy-done.1, bf16[1408,128]{1,0:T(8,128)(2,1)S(1)} %bitcast.170, bf16[1408,1408]{1,0:T(8,128)(2,1)} %bitcast.66), kind=kOutput, calls=%fused_computation.13 | convolution fusion | flops 507871232 | bytes 5406720 | tf_op jit(solution)/shard_map/dot_general | solution.py:175
  (115 shorter events, 70.8 us)
Async XLA Ops:
  6.5 12.5 %copy-start = (bf16[1408,3,352]{0,2,1:T(8,128)(2,1)S(1)}, bf16[1408,3,352]{0,2,1:T(8,128)(2,1)}, u32[]{:S(2)}) copy-start(bf16[1408,3,352]{0,2,1:T(8,128)(2,1)} %param.13) | copy-start | bytes 8921092
  6.5 99.5 %collective-permute-start.3 = (bf16[128,352]{0,1:T(8,128)(2,1)}, bf16[128,352]{0,1:T(8,128)(2,1)}, u32[]{:S(2)}, u32[]{:S(2)}) collective-permute-start(bf16[128,352]{0,1:T(8,128)(2,1)} %param.18), channel_id=1, source_target_pairs={{0,1},{1,2},{2,3},{3,0},{4,5},{5,6},{6,7},{7,4},{8,9},{9,10},{10,1... | collective-permute-start | bytes 270344 | tf_op jit(solution)/shard_map/ppermute | solution.py:26
  8.0 100.3 %collective-permute-start.4 = (bf16[128,352]{0,1:T(8,128)(2,1)}, bf16[128,352]{0,1:T(8,128)(2,1)}, u32[]{:S(2)}, u32[]{:S(2)}) collective-permute-start(bf16[128,352]{0,1:T(8,128)(2,1)} %param.18), channel_id=1, source_target_pairs={{0,2},{1,3},{2,0},{3,1},{4,6},{5,7},{6,4},{7,5},{8,10},{9,11},{10,... | collective-permute-start | bytes 270344 | tf_op jit(solution)/shard_map/ppermute | solution.py:26
  10.8 99.1 %collective-permute-start.5 = (bf16[128,352]{0,1:T(8,128)(2,1)}, bf16[128,352]{0,1:T(8,128)(2,1)}, u32[]{:S(2)}, u32[]{:S(2)}) collective-permute-start(bf16[128,352]{0,1:T(8,128)(2,1)} %param.18), channel_id=1, source_target_pairs={{0,3},{1,0},{2,1},{3,2},{4,7},{5,4},{6,5},{7,6},{8,11},{9,8},{10,9... | collective-permute-start | bytes 270344 | tf_op jit(solution)/shard_map/ppermute | solution.py:26
  12.2 152.1 %collective-permute-start.8 = (bf16[352,1408]{1,0:T(8,128)(2,1)}, bf16[352,1408]{1,0:T(8,128)(2,1)}, u32[]{:S(2)}, u32[]{:S(2)}) collective-permute-start(bf16[352,1408]{1,0:T(8,128)(2,1)} %param.21), channel_id=1, source_target_pairs={{0,1},{1,2},{2,3},{3,0},{4,5},{5,6},{6,7},{7,4},{8,9},{9,10},{10,1... | collective-permute-start | bytes 2973704 | tf_op jit(solution)/shard_map/ppermute | solution.py:26
  12.8 153.8 %collective-permute-start.9 = (bf16[352,1408]{1,0:T(8,128)(2,1)}, bf16[352,1408]{1,0:T(8,128)(2,1)}, u32[]{:S(2)}, u32[]{:S(2)}) collective-permute-start(bf16[352,1408]{1,0:T(8,128)(2,1)} %param.21), channel_id=1, source_target_pairs={{0,2},{1,3},{2,0},{3,1},{4,6},{5,7},{6,4},{7,5},{8,10},{9,11},{10,... | collective-permute-start | bytes 2973704 | tf_op jit(solution)/shard_map/ppermute | solution.py:26
  25.8 17.1 %copy-start.5 = (bf16[128,352]{0,1:T(8,128)(2,1)S(1)}, bf16[128,352]{0,1:T(8,128)(2,1)}, u32[]{:S(2)}) copy-start(bf16[128,352]{0,1:T(8,128)(2,1)} %param.18) | copy-start | bytes 270340
  30.1 36.0 %all-to-all-start = ((bf16[4,64,1408]{2,1,0:T(8,128)(2,1)}), bf16[4,64,1408]{2,1,0:T(8,128)(2,1)}, u32[]{:S(2)}, u32[]{:S(2)}) async-start(bf16[4,64,1408]{2,1,0:T(8,128)(2,1)} %bitcast.166), calls=%async_computation | async-start | bytes 1441792 | tf_op jit(solution)/shard_map/all_to_all | solution.py:106
  73.7 18.9 %all-to-all-start.1 = ((bf16[16,16,1536]{2,1,0:T(8,128)(2,1)}), bf16[16,16,1536]{2,1,0:T(8,128)(2,1)}, u32[]{:S(2)}, u32[]{:S(2)}) async-start(bf16[16,16,1536]{2,1,0:T(8,128)(2,1)} %bitcast_select_fusion), calls=%async_computation.1 | async-start | bytes 1572864 | tf_op jit(solution)/shard_map/all_to_all | solution.py:120
  79.0 2.3 %copy-start.3 = (bf16[352,1408]{1,0:T(8,128)(2,1)S(1)}, bf16[352,1408]{1,0:T(8,128)(2,1)}, u32[]{:S(2)}) copy-start(bf16[352,1408]{1,0:T(8,128)(2,1)} %param.21) | copy-start | bytes 2973700
  81.3 24.5 %copy-start.6 = (s32[16]{0:T(128)S(1)}, s32[16]{0:T(128)}, u32[]{:S(2)}) copy-start(s32[16]{0:T(128)} %param.19) | copy-start | bytes 196
  97.7 19.7 %all-to-all-start.2 = ((bf16[8,16,1536]{2,1,0:T(8,128)(2,1)}), bf16[8,16,1536]{2,1,0:T(8,128)(2,1)S(1)}, u32[]{:S(2)}, u32[]{:S(2)}) async-start(bf16[8,16,1536]{2,1,0:T(8,128)(2,1)} %copy.54), calls=%async_computation.2 | async-start | bytes 786432 | tf_op jit(solution)/shard_map/all_to_all | solution.py:128
  106.1 100.8 %collective-permute-start.10 = (bf16[352,1408]{1,0:T(8,128)(2,1)}, bf16[352,1408]{1,0:T(8,128)(2,1)}, u32[]{:S(2)}, u32[]{:S(2)}) collective-permute-start(bf16[352,1408]{1,0:T(8,128)(2,1)} %param.21), channel_id=1, source_target_pairs={{0,3},{1,0},{2,1},{3,2},{4,7},{5,4},{6,5},{7,6},{8,11},{9,8},{10,9... | collective-permute-start | bytes 2973704 | tf_op jit(solution)/shard_map/ppermute | solution.py:26
  117.5 5.4 %collective-permute-start = (bf16[16,1536]{1,0:T(8,128)(2,1)S(1)}, bf16[16,1536]{1,0:T(8,128)(2,1)S(1)}, u32[]{:S(2)}, u32[]{:S(2)}) collective-permute-start(bf16[16,1536]{1,0:T(8,128)(2,1)S(1)} %reduce_sum.115), channel_id=1, source_target_pairs={{0,1},{1,2},{2,3},{3,0},{4,5},{5,6},{6,7},{7,4},{8,9},{9,10},{10,1... | collective-permute-start | bytes 147464 | tf_op jit(solution)/shard_map/ppermute | solution.py:26
  118.1 5.6 %collective-permute-start.1 = (bf16[16,1536]{1,0:T(8,128)(2,1)S(1)}, bf16[16,1536]{1,0:T(8,128)(2,1)S(1)}, u32[]{:S(2)}, u32[]{:S(2)}) collective-permute-start(bf16[16,1536]{1,0:T(8,128)(2,1)S(1)} %reduce_sum.115), channel_id=1, source_target_pairs={{0,2},{1,3},{2,0},{3,1},{4,6},{5,7},{6,4},{7,5},{8,10},{9,11},{10,... | collective-permute-start | bytes 147464 | tf_op jit(solution)/shard_map/ppermute | solution.py:26
  122.9 9.2 %collective-permute-start.2 = (bf16[16,1536]{1,0:T(8,128)(2,1)S(1)}, bf16[16,1536]{1,0:T(8,128)(2,1)S(1)}, u32[]{:S(2)}, u32[]{:S(2)}) collective-permute-start(bf16[16,1536]{1,0:T(8,128)(2,1)S(1)} %reduce_sum.115), channel_id=1, source_target_pairs={{0,3},{1,0},{2,1},{3,2},{4,7},{5,4},{6,5},{7,6},{8,11},{9,8},{10,9... | collective-permute-start | bytes 147464 | tf_op jit(solution)/shard_map/ppermute | solution.py:26
  136.8 0.9 copy-start.1
  141.2 10.1 %all-to-all-start.3 = ((bf16[4,3,88,128]{3,2,1,0:T(8,128)(2,1)}), bf16[4,3,88,128]{3,2,1,0:T(8,128)(2,1)S(1)}, u32[]{:S(2)}, u32[]{:S(2)}) async-start(bf16[4,3,88,128]{3,2,1,0:T(8,128)(2,1)} %bitcast.160), calls=%async_computation.3 | async-start | bytes 540672 | tf_op jit(solution)/shard_map/all_to_all | solution.py:146
  144.7 35.8 %all-gather.3.cloned.1.call-start = ((), (), s32[]{:S(2)}) async-start(), calls=%async_computation.5 | async-start | bytes 1622016 | tf_op jit(solution)/shard_map/all_gather | solution.py:150
  151.4 30.4 %copy-start.4 = (bf16[4,3,88,128]{3,2,1,0:T(8,128)(2,1)}, bf16[4,3,88,128]{3,2,1,0:T(8,128)(2,1)S(1)}, u32[]{:S(2)}) copy-start(bf16[4,3,88,128]{3,2,1,0:T(8,128)(2,1)S(1)} %all-to-all-done.3) | copy-start | bytes 811012
  151.4 11.9 %collective-permute-start.6 = (bf16[4,2,88,128]{3,2,1,0:T(8,128)(2,1)S(1)}, bf16[4,2,88,128]{3,2,1,0:T(8,128)(2,1)S(1)}, u32[]{:S(2)}, u32[]{:S(2)}) collective-permute-start(bf16[4,2,88,128]{3,2,1,0:T(8,128)(2,1)S(1)} %get-tuple-element.8), channel_id=1, source_target_pairs={{0,32},{32,64},{64,96},{96,128},{128,160},{160,192},{192,224},{1,3... | collective-permute-start | bytes 540680 | tf_op jit(solution)/shard_map/ppermute | solution.py:21
  154.8 8.5 %collective-permute-start.7 = (bf16[4,2,88,128]{3,2,1,0:T(8,128)(2,1)S(1)}, bf16[4,2,88,128]{3,2,1,0:T(8,128)(2,1)S(1)}, u32[]{:S(2)}, u32[]{:S(2)}) collective-permute-start(bf16[4,2,88,128]{3,2,1,0:T(8,128)(2,1)S(1)} %get-tuple-element.8), channel_id=1, source_target_pairs={{0,64},{32,96},{64,128},{96,160},{128,192},{160,224},{1,65},{33,97... | collective-permute-start | bytes 540680 | tf_op jit(solution)/shard_map/ppermute | solution.py:21
  188.2 2.7 %copy-start.2 = (f32[512,3072]{1,0:T(8,128)}, f32[512,3072]{1,0:T(8,128)S(1)}, u32[]{:S(2)}) copy-start(f32[512,3072]{1,0:T(8,128)S(1)} %get-tuple-element.18) | copy-start | bytes 18874372
  200.1 16.8 %all-to-all-start.4 = ((bf16[16,88,128]{2,1,0:T(8,128)(2,1)}), bf16[16,88,128]{2,1,0:T(8,128)(2,1)S(1)}, u32[]{:S(2)}, u32[]{:S(2)}) async-start(bf16[16,88,128]{2,1,0:T(8,128)(2,1)} %bitcast.60), calls=%async_computation.4 | async-start | bytes 720896 | tf_op jit(solution)/shard_map/all_to_all | solution.py:174
Sparse Core Ops, SparseCore 0:
  164.3 16.1 all-gather.2

commit v2 on v1

v2 whole, which is shorter than its diff:
```python
import jax
import jax.numpy as jnp
import numpy as np
from jax import lax
from jax.experimental import pallas as pl
from jax.experimental.pallas import tpu as pltpu
from jax.sharding import Mesh
from jax.sharding import PartitionSpec as P

HEAD = 88
MAXGRID = 16
BLOCK = 128
MERGED = 64
EPSILON = 1e-06
SCALE = HEAD ** (-0.5)
BF = jnp.bfloat16
F32 = jnp.float32
I32 = jnp.int32
VMEM = pltpu.VMEM
SMEM = pltpu.SMEM
FACTS = 128
WINDOW = 18 * BLOCK


def ahead(x, axis, by):
    count = lax.axis_size(axis)
    return lax.ppermute(x, axis, [(i, i + by) for i in range(count - by)])


def around(x, axis, by):
    count = lax.axis_size(axis)
    return lax.ppermute(x, axis, [(i, (i + by) % count) for i in range(count)])


def call(kernel, out_shape, spaces, scratch=()):
    single = not isinstance(out_shape, (list, tuple))
    outs = pl.BlockSpec(memory_space=VMEM)
    return pl.pallas_call(
        kernel,
        out_shape=out_shape,
        in_specs=[pl.BlockSpec(memory_space=s) for s in spaces],
        out_specs=outs if single else [outs] * len(out_shape),
        scratch_shapes=scratch,
        compiler_params=pltpu.CompilerParams(vmem_limit_bytes=48 << 20),
    )


def shape(dims, dtype=BF):
    return jax.ShapeDtypeStruct(dims, dtype)


def iota(dims, axis):
    return lax.broadcasted_iota(I32, dims, axis)


def dot(a, b, over):
    return lax.dot_general(
        a, b, (((over[0],), (over[1],)), ((), ())), preferred_element_type=F32
    )


def normalize(values):
    centre = jnp.mean(values, axis=-1, keepdims=True)
    shifted = values - centre
    spread = jnp.mean(shifted * shifted, axis=-1, keepdims=True)
    return (shifted * lax.rsqrt(spread + EPSILON)).astype(BF)


def slot_of(row):
    i, j = row // 128, (row // 64) % 2
    a, b = (row // 8) % 8, row % 8
    return (2 * a + i) * MAXGRID + 2 * b + j


def vision_kernel(grid_ref, picture_ref, qkv_ref, out_ref, share_ref):
    count = picture_ref.shape[0]
    local_width = qkv_ref.shape[1]
    normed = normalize(picture_ref[...].astype(F32))
    queries = dot(qkv_ref[0], normed, (1, 1))
    keys = dot(qkv_ref[1], normed, (1, 1))
    values = dot(qkv_ref[2], normed, (1, 1))
    slots = iota((count, 1), 0)
    usable = (slots // MAXGRID < 2 * grid_ref[0, 0]) & (slots % MAXGRID < 2 * grid_ref[0, 1])
    contexts = []
    for first in range(0, local_width, HEAD):
        q, k, v = (x[first : first + HEAD].astype(BF) for x in (queries, keys, values))
        scores = dot(k, q, (0, 0)) * SCALE
        scores = jnp.where(usable, scores, -jnp.inf)
        expons = jnp.exp(scores - jnp.max(scores, axis=0, keepdims=True))
        total = jnp.sum(expons, axis=0, keepdims=True)
        contexts.append(dot(v, expons.astype(BF), (1, 0)) / total)
    context = jnp.concatenate(contexts, axis=0).astype(BF)
    order = slot_of(iota((count, count), 0)) == iota((count, count), 1)
    context = dot(order.astype(BF), context, (1, 1)).astype(BF)
    share_ref[...] = dot(context, out_ref[...], (1, 0)).astype(BF)


def merge_kernel(facts_ref, own_ref, shares_ref, weight_ref, rows_ref):
    width = own_ref.shape[1]
    hidden = own_ref[...].astype(F32)
    gained = shares_ref[0].astype(F32)
    for other in range(1, 4):
        gained = gained + shares_ref[other].astype(F32)
    merged = dot(normalize(hidden + gained), weight_ref[...], (1, 0)).astype(BF)
    lane = iota((MERGED, FACTS), 1)
    facts = jnp.zeros((MERGED, FACTS), I32)
    for index in range(5):
        facts = jnp.where(lane == index, facts_ref[index], facts)
    facts = facts.astype(F32).astype(BF)
    for y in range(4):
        here = facts_ref[5] == y
        rows_ref[y, :, :width] = jnp.where(here, merged, jnp.zeros_like(merged))
        rows_ref[y, :, width:] = jnp.where(here, facts, jnp.zeros_like(facts))


def project_kernel(rows_ref, tokens_ref, qkv_ref, prompt_ref, heads_ref):
    width = tokens_ref.shape[1]
    facts = rows_ref[:, width:].astype(F32)
    cell = iota((MERGED, 1), 0)
    a, b = (cell // 8).astype(F32), (cell % 8).astype(F32)
    offset, high, wide, there = (facts[:, i : i + 1] for i in (1, 2, 3, 4))
    target = offset + a * wide + b
    usable = (a < high) & (b < wide) & (there > 0.0)
    target = jnp.where(usable, target, -1.0)
    table = (target == iota((MERGED, BLOCK), 1).astype(F32)).astype(BF)
    placed = dot(table, rows_ref[...], (0, 0))
    covered = placed[:, width + 4 : width + 5] > 0.0
    prompt = jnp.where(covered, placed[:, :width], tokens_ref[...].astype(F32))
    prompt_ref[...] = prompt.astype(BF)
    normed = normalize(prompt)
    for part in range(3):
        projected = dot(qkv_ref[part], normed, (1, 1)).astype(F32)
        for head in range(4):
            heads_ref[head, part] = projected[head * HEAD : (head + 1) * HEAD].astype(BF)


def attend_kernel(facts_ref, lengths_ref, own_ref, near_ref, far_ref,
                  own2_ref, near2_ref, far2_ref, sent_ref, keys_ref, values_ref):
    z, c = facts_ref[0], facts_ref[1]
    for plane, (mine, other) in enumerate(
        ((far_ref, far2_ref), (near_ref, near2_ref), (own_ref, own2_ref))
    ):
        skip = 1 if plane == 2 else 0
        for y in range(4):
            at = (plane * 8 + 2 * y) * BLOCK
            for half in range(2):
                lanes = pl.ds(at + half * BLOCK, BLOCK)
                for part, store in ((0, keys_ref), (1, values_ref)):
                    picked = jnp.where(
                        c == half, mine[y, skip + part], other[y, part]
                    )
                    store[:, lanes] = picked
    row = iota((BLOCK, 1), 0)
    column = iota((BLOCK, WINDOW), 1)
    for j in range(4):
        base = (z - 2) * 1024 + j * 256
        here = 2048 + c * BLOCK + row
        start = jnp.zeros((BLOCK, 1), I32)
        end = jnp.int32(0)
        for prompt in range(16):
            end = end + lengths_ref[prompt]
            start = jnp.where(end <= here + base, end, start)
        query = own_ref[j, 0]
        window = pl.ds(j * 256, WINDOW)
        scores = dot(query, keys_ref[:, window], (0, 0)) * SCALE
        visible = (column <= here) & (column >= start - base)
        scores = jnp.where(visible, scores, -jnp.inf)
        expons = jnp.exp(scores - jnp.max(scores, axis=1, keepdims=True))
        total = jnp.sum(expons, axis=1, keepdims=True)
        summed = dot(values_ref[:, window], expons.astype(BF), (1, 1))
        total = jnp.transpose(jnp.broadcast_to(total, (BLOCK, BLOCK)))
        context = (summed / total[:HEAD]).astype(BF)
        for t in range(4):
            sent_ref[t, j] = context


def output_kernel(facts_ref, context_ref, w0_ref, w1_ref, w2_ref, w3_ref, prompt_ref, out_ref):
    total = prompt_ref[...].astype(F32)
    for by, weight in enumerate((w0_ref, w1_ref, w2_ref, w3_ref)):
        piece = context_ref[lax.rem(facts_ref[2] + 4 - by, 4)]
        total = total + dot(piece, weight[...], (0, 0))
    out_ref[...] = total.astype(BF)


def local(
    patches,
    picture_grid,
    vision_qkv,
    vision_out,
    merge_weight,
    picture_block,
    picture_offset,
    tokens,
    prompt_lengths,
    text_qkv,
    text_out,
):
    count, width = patches.shape[1:]
    local_width = vision_qkv.shape[2]
    wide = width + FACTS
    z = lax.axis_index("z")
    c = lax.axis_index("c")
    t = lax.axis_index("t")
    picture = patches[0]
    block = picture_block[0]

    share = call(vision_kernel, shape((count, width)), [SMEM, VMEM, VMEM, VMEM])(
        picture_grid, picture, vision_qkv.transpose(1, 2, 0), vision_out
    )
    shares = lax.all_to_all(share.reshape(4, MERGED, width), "t", 0, 0, tiled=True)
    chosen = slot_of(t * MERGED + jnp.arange(MERGED))[:, None] == jnp.arange(count)[None, :]
    own = jnp.dot(chosen.astype(BF), picture, preferred_element_type=F32).astype(BF)
    facts = jnp.stack([block, picture_offset[0], picture_grid[0, 0], picture_grid[0, 1], 1])
    facts = jnp.where(t == 0, facts, 0)
    facts = jnp.concatenate([facts, (block % 8 // 2)[None]]).astype(I32)
    routed = call(merge_kernel, shape((4, MERGED, wide)), [SMEM, VMEM, VMEM, VMEM])(
        facts, own, shares, merge_weight[0]
    )

    got = lax.all_to_all(routed.reshape(16, 16, wide), ("y", "t"), 0, 0, tiled=True)
    got, tokens = lax.optimization_barrier((got, tokens))
    pieces = [tokens] + [around(tokens, "t", by) for by in range(1, 4)]
    got = jnp.sum(got.reshape(4, 4, 16, wide).astype(F32), axis=1).astype(BF)
    got = jnp.concatenate([got, around(got, "c", 1)])
    to = got[:, 0, width].astype(F32).astype(I32)
    pick = (got[:, 0, width + 4] > 0) & (to % 2 == c)
    pick = pick[None, :] & (to[None, :] // 8 == jnp.arange(8)[:, None])
    routed = jnp.einsum("zk,krd->zrd", pick.astype(BF), got, preferred_element_type=F32).astype(BF)
    got = lax.all_to_all(routed, "z", 0, 0, tiled=True)
    got = jnp.sum(got.astype(F32), axis=0).astype(BF)
    got = jnp.broadcast_to(got[None], (4, 16, wide))
    got = lax.all_to_all(got, "t", 0, 0, tiled=True).reshape(MERGED, wide)
    own_tokens = jnp.zeros((4, BLOCK, local_width), BF)
    for by, piece in enumerate(pieces):
        own_tokens = lax.dynamic_update_index_in_dim(own_tokens, piece, (t - by) % 4, 0)
    own_tokens = own_tokens.transpose(1, 0, 2).reshape(BLOCK, width)

    prompt_in, heads = call(
        project_kernel, [shape((BLOCK, width)), shape((4, 3, HEAD, BLOCK))], [VMEM] * 3
    )(got, own_tokens, text_qkv.transpose(1, 2, 0))
    heads, text_out = lax.optimization_barrier((heads, text_out))
    weights = [text_out] + [around(text_out, "t", by) for by in range(1, 4)]
    mine = lax.all_to_all(heads, "y", 0, 0, tiled=True)
    pair = mine[:, 1:]
    near, far = ahead(pair, "z", 1), ahead(pair, "z", 2)
    facts = jnp.stack([z, c, t]).astype(I32)
    sent = call(
        attend_kernel,
        shape((4, 4, HEAD, BLOCK)),
        [SMEM, SMEM] + [VMEM] * 6,
        [pltpu.VMEM((HEAD, 24 * BLOCK), BF)] * 2,
    )(facts, prompt_lengths, mine, near, far, *(around(x, "c", 1) for x in (pair, near, far)))
    context = lax.all_to_all(sent.reshape(16, HEAD, BLOCK), ("t", "y"), 0, 0, tiled=True)
    return call(output_kernel, shape((BLOCK, width)), [SMEM] + [VMEM] * 6)(
        facts, context.reshape(4, local_width, BLOCK), *weights, prompt_in
    )


def solution(mesh):
    split = Mesh(np.asarray(mesh.devices).reshape(8, 4, 2, 4), ("z", "y", "c", "t"))
    seq = ("z", "y", "c")
    placed = (
        P(seq, None, None),
        P(seq, None),
        P(None, None, "t"),
        P("t", None),
        P("t", None, None),
        P(seq),
        P(seq),
        P(seq, "t"),
        P(),
        P(None, None, "t"),
        P("t", None),
    )
    return jax.shard_map(
        local, mesh=split, in_specs=placed, out_specs=P(seq, None), check_vma=False
    )
```

time: 230 us -> 150 us (0.65)
  the two profiles are of different devices: /device:TPU:64 before, /device:TPU:1 now
where the time goes in v2:
time: 150 us; the launch traced here: 149 us
  blocking collectives  47.8 us (32%)
  starting transfers between devices  37.3 us (25%)
  waiting for transfers between devices  27.4 us (18%)
  local copies, waits for them, and re-layouts  18.6 us (12%)
  Pallas kernels  15.6 us (10%)
  between operations  1.54 us (1%)
    all_to_all x1, blocking collectives, local(): lax.all_to_all(sent.reshape(16, HEAD, BLOCK), ('t', 'y'), 0, 0, tiled=True)  29.6 us
    all_to_all x1, blocking collectives, local(): lax.all_to_all(routed.reshape(16, 16, wide), ('y', 't'), 0, 0, tiled=True)  18.2 us
    ppermute x10, starting transfers between devices, around(): return lax.ppermute(x, axis, [(i, (i + by) % count) for i in range(count)])  12 us
    unnamed x28, local copies, waits for them, and re-layouts  9.37 us
    all_to_all x1, starting transfers between devices, local(): got = lax.all_to_all(routed, 'z', 0, 0, tiled=True)  8.22 us
    ppermute x10, waiting for transfers between devices, around(): return lax.ppermute(x, axis, [(i, (i + by) % count) for i in range(count)])  6.93 us
    all_to_all x1, waiting for transfers between devices, local(): got = lax.all_to_all(routed, 'z', 0, 0, tiled=True)  5.73 us
    all_to_all x1, waiting for transfers between devices, local(): lax.all_to_all(share.reshape(4, MERGED, width), 't', 0, 0, tiled=True)  5.65 us
  transfers between devices with their start and end apart: 16, of which 9 were waited for; matrix products, arithmetic and copies ran while one was open for 6% of the time, Pallas kernels for 3%

profile of v2, /device:TPU:1, one launch (start us, length us, event | category | flops | bytes accessed | tf_op | source)
XLA Modules:
  0.0 149.5 jit_solution(2802937476001277501)
XLA Ops:
  0.0 1.8 %copy-done.2 = bf16[1408,3,352]{0,2,1:T(8,128)(2,1)S(1)} copy-done((bf16[1408,3,352]{0,2,1:T(8,128)(2,1)S(1)}, bf16[1408,3,352]{0,2,1:T(8,128)(2,1)}, u32[]{:S(2)}) %copy-start.2) | copy-done | bytes 2973720
  4.8 4.6 %shard_map.109 = bf16[256,1408]{1,0:T(8,128)(2,1)} custom-call(s32[1,2]{1,0:T(1,128)S(1)} %copy-done.10, bf16[256,1408]{1,0:T(8,128)(2,1)S(1)} %bitcast.41, bf16[3,352,1408]{2,1,0:T(8,128)(2,1)S(1)} %bitcast.40, bf16[352,1408]{1,0:T(8,128)(2,1)S(1)} %copy-done.5), custom_call_target="tpu_custom_call" | custom-call | tf_op jit(solution)/shard_map/pallas_call | solution.py:207
  9.4 4.8 %all-to-all-start = ((bf16[4,64,1408]{2,1,0:T(8,128)(2,1)}), bf16[4,64,1408]{2,1,0:T(8,128)(2,1)S(1)}, u32[]{:S(2)}, u32[]{:S(2)}) async-start(bf16[4,64,1408]{2,1,0:T(8,128)(2,1)} %bitcast.9), calls=%async_computation | async-start | bytes 1441792 | tf_op jit(solution)/shard_map/all_to_all | solution.py:210
  18.1 5.7 %all-to-all-done.shares_ref = bf16[4,64,1408]{2,1,0:T(8,128)(2,1)S(1)} async-done(((bf16[4,64,1408]{2,1,0:T(8,128)(2,1)}), bf16[4,64,1408]{2,1,0:T(8,128)(2,1)S(1)}, u32[]{:S(2)}, u32[]{:S(2)}) %all-to-all-start) | async-done | bytes 720928 | tf_op jit(solution)/shard_map/all_to_all | solution.py:210
  23.7 2.1 %copy-done = bf16[1,1408,1408]{2,1,0:T(8,128)(2,1)S(1)} copy-done((bf16[1,1408,1408]{2,1,0:T(8,128)(2,1)S(1)}, bf16[1,1408,1408]{2,1,0:T(8,128)(2,1)}, u32[]{:S(2)}) %copy-start) | copy-done | bytes 3964952
  25.8 1.6 %shard_map.110 = bf16[4,64,1536]{2,1,0:T(8,128)(2,1)S(1)} custom-call(s32[6]{0:T(128)S(1)} %pad_add_fusion.1.facts_ref, bf16[64,1408]{1,0:T(8,128)(2,1)S(1)} %convolution_convert_fusion.1.own_ref, bf16[4,64,1408]{2,1,0:T(8,128)(2,1)S(1)} %all-to-all-done.shares_ref, bf16[1408,1408]{1,0:T(8,128)(2,1)S(1)} %bitcast.37), custom_call_target="tpu_custom_call" | custom-call | tf_op jit(solution)/shard_map/pallas_call | solution.py:216
  27.4 18.2 %all_to_all.30 = bf16[16,16,1536]{2,1,0:T(8,128)(2,1)S(1)} all-to-all(bf16[16,16,1536]{2,1,0:T(8,128)(2,1)S(1)} %bitcast.38), channel_id=1, replica_groups=mesh['z'=8,'y'=4,'c'=2,'t'=4] {'y','t'}, dimensions={0} | all-to-all | bytes 1572864 | tf_op jit(solution)/shard_map/all_to_all | solution.py:220
  45.9 3.2 %collective-permute-start = (bf16[4,16,1536]{2,0,1:T(4,128)(2,1)S(1)}, bf16[4,16,1536]{2,0,1:T(4,128)(2,1)S(1)}, u32[]{:S(2)}, u32[]{:S(2)}) collective-permute-start(bf16[4,16,1536]{2,0,1:T(4,128)(2,1)S(1)} %copy.18), channel_id=1, source_target_pairs={{0,4},{4,0},{1,5},{5,1},{2,6},{6,2},{3,7},{7,3},{8,12},{12,8},{9,1... | collective-permute-start | bytes 589832 | tf_op jit(solution)/shard_map/ppermute | solution.py:32
  51.7 8.2 %all-to-all-start.2 = ((bf16[8,16,1536]{2,1,0:T(8,128)(2,1)}), bf16[8,16,1536]{2,1,0:T(8,128)(2,1)S(1)}, u32[]{:S(2)}, u32[]{:S(2)}) async-start(bf16[8,16,1536]{2,1,0:T(8,128)(2,1)} %copy.19), calls=%async_computation.2 | async-start | bytes 786432 | tf_op jit(solution)/shard_map/all_to_all | solution.py:229
  60.5 1.6 %collective-permute-start.2 = (bf16[128,352]{0,1:T(8,128)(2,1)S(1)}, bf16[128,352]{0,1:T(8,128)(2,1)S(1)}, u32[]{:S(2)}, u32[]{:S(2)}) collective-permute-start(bf16[128,352]{0,1:T(8,128)(2,1)S(1)} %copy-done.13), channel_id=1, source_target_pairs={{0,2},{1,3},{2,0},{3,1},{4,6},{5,7},{6,4},{7,5},{8,10},{9,11},{10,... | collective-permute-start | bytes 270344 | tf_op jit(solution)/shard_map/ppermute | solution.py:32
  63.5 4.5 %collective-permute-done.1 = bf16[128,352]{0,1:T(8,128)(2,1)S(1)} collective-permute-done((bf16[128,352]{0,1:T(8,128)(2,1)S(1)}, bf16[128,352]{0,1:T(8,128)(2,1)S(1)}, u32[]{:S(2)}, u32[]{:S(2)}) %collective-permute-start.1) | collective-permute-done | bytes 90144 | tf_op jit(solution)/shard_map/ppermute | solution.py:32
  69.4 5.7 %all-to-all-done.2 = bf16[8,16,1536]{2,1,0:T(8,128)(2,1)S(1)} async-done(((bf16[8,16,1536]{2,1,0:T(8,128)(2,1)}), bf16[8,16,1536]{2,1,0:T(8,128)(2,1)S(1)}, u32[]{:S(2)}, u32[]{:S(2)}) %all-to-all-start.2) | async-done | bytes 393248 | tf_op jit(solution)/shard_map/all_to_all | solution.py:229
  75.9 3.4 %all-to-all-start.3 = ((bf16[4,16,1536]{2,1,0:T(8,128)(2,1)}), bf16[4,16,1536]{2,1,0:T(8,128)(2,1)S(1)}, u32[]{:S(2)}, u32[]{:S(2)}) async-start(bf16[4,16,1536]{2,1,0:T(8,128)(2,1)} %broadcast_in_dim.36), calls=%async_computation.3 | async-start | bytes 393216 | tf_op jit(solution)/shard_map/all_to_all | solution.py:232
  82.0 2.5 %all-to-all-done.3 = bf16[4,16,1536]{2,1,0:T(8,128)(2,1)S(1)} async-done(((bf16[4,16,1536]{2,1,0:T(8,128)(2,1)}), bf16[4,16,1536]{2,1,0:T(8,128)(2,1)S(1)}, u32[]{:S(2)}, u32[]{:S(2)}) %all-to-all-start.3) | async-done | bytes 196640 | tf_op jit(solution)/shard_map/all_to_all | solution.py:232
  84.5 1.8 %shard_map.111 = (bf16[128,1408]{1,0:T(8,128)(2,1)S(1)}, bf16[4,3,88,128]{3,2,1,0:T(8,128)(2,1)S(1)}) custom-call(bf16[64,1536]{1,0:T(8,128)(2,1)S(1)} %bitcast.44, bf16[128,1408]{1,0:T(8,128)(2,1)S(1)} %copy.20.tokens_ref, bf16[3,352,1408]{2,1,0:T(8,128)(2,1)S(1)} %bitcast.39), custom_call_target="tpu_custom_call" | custom-call | tf_op jit(solution)/shard_map/pallas_call | solution.py:238
  87.7 3.6 %all-to-all-start.4 = ((bf16[4,3,88,128]{3,2,1,0:T(8,128)(2,1)}), bf16[4,3,88,128]{3,2,1,0:T(8,128)(2,1)S(1)}, u32[]{:S(2)}, u32[]{:S(2)}) async-start(bf16[4,3,88,128]{3,2,1,0:T(8,128)(2,1)} %copy-done.9), calls=%async_computation.4 | async-start | bytes 540672 | tf_op jit(solution)/shard_map/all_to_all | solution.py:243
  93.4 3.4 %all-to-all-done.4.own_ref = bf16[4,3,88,128]{3,2,1,0:T(8,128)(2,1)S(1)} async-done(((bf16[4,3,88,128]{3,2,1,0:T(8,128)(2,1)}), bf16[4,3,88,128]{3,2,1,0:T(8,128)(2,1)S(1)}, u32[]{:S(2)}, u32[]{:S(2)}) %all-to-all-start.4) | async-done | bytes 270368 | tf_op jit(solution)/shard_map/all_to_all | solution.py:243
  96.8 2.9 %collective-permute-start.6 = (bf16[4,2,88,128]{3,2,1,0:T(8,128)(2,1)S(1)}, bf16[4,2,88,128]{3,2,1,0:T(8,128)(2,1)S(1)}, u32[]{:S(2)}, u32[]{:S(2)}) collective-permute-start(bf16[4,2,88,128]{3,2,1,0:T(8,128)(2,1)S(1)} %slice.20), channel_id=1, source_target_pairs={{0,4},{4,0},{1,5},{5,1},{2,6},{6,2},{3,7},{7,3},{8,12},{12,8},{9,1... | collective-permute-start | bytes 540680 | tf_op jit(solution)/shard_map/ppermute | solution.py:32
  99.7 2.1 %collective-permute-start.5 = (bf16[4,2,88,128]{3,2,1,0:T(8,128)(2,1)S(1)}, bf16[4,2,88,128]{3,2,1,0:T(8,128)(2,1)}, u32[]{:S(2)}, u32[]{:S(2)}) collective-permute-start(bf16[4,2,88,128]{3,2,1,0:T(8,128)(2,1)S(1)} %slice.20), channel_id=1, source_target_pairs={{0,64},{32,96},{64,128},{96,160},{128,192},{160,224},{1,65},{33,97... | collective-permute-start | bytes 540680 | tf_op jit(solution)/shard_map/ppermute | solution.py:27
  101.9 3.1 %collective-permute-start.4 = (bf16[4,2,88,128]{3,2,1,0:T(8,128)(2,1)S(1)}, bf16[4,2,88,128]{3,2,1,0:T(8,128)(2,1)}, u32[]{:S(2)}, u32[]{:S(2)}) collective-permute-start(bf16[4,2,88,128]{3,2,1,0:T(8,128)(2,1)S(1)} %slice.20), channel_id=1, source_target_pairs={{0,32},{32,64},{64,96},{96,128},{128,160},{160,192},{192,224},{1,3... | collective-permute-start | bytes 540680 | tf_op jit(solution)/shard_map/ppermute | solution.py:27
  106.3 2.9 %collective-permute-done.4.near_ref = bf16[4,2,88,128]{3,2,1,0:T(8,128)(2,1)} collective-permute-done((bf16[4,2,88,128]{3,2,1,0:T(8,128)(2,1)S(1)}, bf16[4,2,88,128]{3,2,1,0:T(8,128)(2,1)}, u32[]{:S(2)}, u32[]{:S(2)}) %collective-permute-start.4) | collective-permute-done | bytes 180256 | tf_op jit(solution)/shard_map/ppermute | solution.py:27
  111.2 4.7 %shard_map.112 = bf16[4,4,88,128]{3,2,1,0:T(8,128)(2,1)S(1)} custom-call(s32[3]{0:T(128)S(1)} %pad_add_fusion.facts_ref, s32[16]{0:T(128)S(1)} %copy-done.12, bf16[4,3,88,128]{3,2,1,0:T(8,128)(2,1)S(1)} %all-to-all-done.4.own_ref, bf16[4,2,88,128]{3,2,1,0:T(8,128)(2,1)} %collective-permute-done.4.near_ref, ...), custom_call_target="tpu_custom_call" | custom-call | tf_op jit(solution)/shard_map/pallas_call | solution.py:247
  115.9 29.6 %all_to_all.31 = bf16[16,88,128]{2,1,0:T(8,128)(2,1)S(1)} all-to-all(bf16[16,88,128]{2,1,0:T(8,128)(2,1)S(1)} %bitcast.42), channel_id=1, replica_groups=mesh['z'=8,'y'=4,'c'=2,'t'=4] {'t','y'}, dimensions={0} | all-to-all | bytes 720896 | tf_op jit(solution)/shard_map/all_to_all | solution.py:253
  146.5 3.0 %shard_map.113 = bf16[128,1408]{1,0:T(8,128)(2,1)} custom-call(s32[3]{0:T(128)S(1)} %pad_add_fusion.facts_ref, bf16[4,352,128]{2,1,0:T(8,128)(2,1)S(1)} %bitcast.43, bf16[352,1408]{1,0:T(8,128)(2,1)S(1)} %copy-done.6, bf16[352,1408]{1,0:T(8,128)(2,1)} %collective-permute-done.9.w1_ref, bf16[352,1408]{1,0:T(8,128)(2,1)S(1)} %collective-permute-done.10.w2_ref, ...), custom_call_target="tpu_custom_call" | custom-call | tf_op jit(solution)/shard_map/pallas_call | solution.py:254
  (67 shorter events, 22.9 us)
Async XLA Ops:
  0.0 1.8 %copy-start.2 = (bf16[1408,3,352]{0,2,1:T(8,128)(2,1)S(1)}, bf16[1408,3,352]{0,2,1:T(8,128)(2,1)}, u32[]{:S(2)}) copy-start(bf16[1408,3,352]{0,2,1:T(8,128)(2,1)} %param.13) | copy-start | bytes 8921092
  4.8 10.1 %copy-start.11 = (s32[1,2]{1,0:T(1,128)S(1)}, s32[1,2]{1,0:T(1,128)}, u32[]{:S(2)}) copy-start(s32[1,2]{1,0:T(1,128)} %grid_ref.1) | copy-start | bytes 28
  4.8 13.0 %copy-start.4 = (bf16[1,256,1408]{2,1,0:T(8,128)(2,1)S(1)}, bf16[1,256,1408]{2,1,0:T(8,128)(2,1)}, u32[]{:S(2)}) copy-start(bf16[1,256,1408]{2,1,0:T(8,128)(2,1)} %param.11) | copy-start | bytes 2162692
  9.4 14.3 %all-to-all-start = ((bf16[4,64,1408]{2,1,0:T(8,128)(2,1)}), bf16[4,64,1408]{2,1,0:T(8,128)(2,1)S(1)}, u32[]{:S(2)}, u32[]{:S(2)}) async-start(bf16[4,64,1408]{2,1,0:T(8,128)(2,1)} %bitcast.9), calls=%async_computation | async-start | bytes 1441792 | tf_op jit(solution)/shard_map/all_to_all | solution.py:210
  23.7 2.1 %copy-start = (bf16[1,1408,1408]{2,1,0:T(8,128)(2,1)S(1)}, bf16[1,1408,1408]{2,1,0:T(8,128)(2,1)}, u32[]{:S(2)}) copy-start(bf16[1,1408,1408]{2,1,0:T(8,128)(2,1)} %param.15) | copy-start | bytes 11894788
  27.4 32.5 %copy-start.13 = (bf16[128,352]{0,1:T(8,128)(2,1)S(1)}, bf16[128,352]{0,1:T(8,128)(2,1)}, u32[]{:S(2)}) copy-start(bf16[128,352]{0,1:T(8,128)(2,1)} %param.18) | copy-start | bytes 270340
  45.9 4.3 %collective-permute-start = (bf16[4,16,1536]{2,0,1:T(4,128)(2,1)S(1)}, bf16[4,16,1536]{2,0,1:T(4,128)(2,1)S(1)}, u32[]{:S(2)}, u32[]{:S(2)}) collective-permute-start(bf16[4,16,1536]{2,0,1:T(4,128)(2,1)S(1)} %copy.18), channel_id=1, source_target_pairs={{0,4},{4,0},{1,5},{5,1},{2,6},{6,2},{3,7},{7,3},{8,12},{12,8},{9,1... | collective-permute-start | bytes 589832 | tf_op jit(solution)/shard_map/ppermute | solution.py:32
  49.1 35.4 %copy-start.1 = (bf16[1408,3,352]{0,2,1:T(8,128)(2,1)S(1)}, bf16[1408,3,352]{0,2,1:T(8,128)(2,1)}, u32[]{:S(2)}) copy-start(bf16[1408,3,352]{0,2,1:T(8,128)(2,1)} %param.20) | copy-start | bytes 8921092
  51.7 23.4 %all-to-all-start.2 = ((bf16[8,16,1536]{2,1,0:T(8,128)(2,1)}), bf16[8,16,1536]{2,1,0:T(8,128)(2,1)S(1)}, u32[]{:S(2)}, u32[]{:S(2)}) async-start(bf16[8,16,1536]{2,1,0:T(8,128)(2,1)} %copy.19), calls=%async_computation.2 | async-start | bytes 786432 | tf_op jit(solution)/shard_map/all_to_all | solution.py:229
  59.9 19.3 %collective-permute-start.3 = (bf16[128,352]{0,1:T(8,128)(2,1)S(1)}, bf16[128,352]{0,1:T(8,128)(2,1)}, u32[]{:S(2)}, u32[]{:S(2)}) collective-permute-start(bf16[128,352]{0,1:T(8,128)(2,1)S(1)} %copy-done.13), channel_id=1, source_target_pairs={{0,3},{1,0},{2,1},{3,2},{4,7},{5,4},{6,5},{7,6},{8,11},{9,8},{10,9... | collective-permute-start | bytes 270344 | tf_op jit(solution)/shard_map/ppermute | solution.py:32
  60.5 8.2 %collective-permute-start.2 = (bf16[128,352]{0,1:T(8,128)(2,1)S(1)}, bf16[128,352]{0,1:T(8,128)(2,1)S(1)}, u32[]{:S(2)}, u32[]{:S(2)}) collective-permute-start(bf16[128,352]{0,1:T(8,128)(2,1)S(1)} %copy-done.13), channel_id=1, source_target_pairs={{0,2},{1,3},{2,0},{3,1},{4,6},{5,7},{6,4},{7,5},{8,10},{9,11},{10,... | collective-permute-start | bytes 270344 | tf_op jit(solution)/shard_map/ppermute | solution.py:32
  62.1 6.0 %collective-permute-start.1 = (bf16[128,352]{0,1:T(8,128)(2,1)S(1)}, bf16[128,352]{0,1:T(8,128)(2,1)S(1)}, u32[]{:S(2)}, u32[]{:S(2)}) collective-permute-start(bf16[128,352]{0,1:T(8,128)(2,1)S(1)} %copy-done.13), channel_id=1, source_target_pairs={{0,1},{1,2},{2,3},{3,0},{4,5},{5,6},{6,7},{7,4},{8,9},{9,10},{10,1... | collective-permute-start | bytes 270344 | tf_op jit(solution)/shard_map/ppermute | solution.py:32
  75.1 36.1 %copy-start.12 = (s32[16]{0:T(128)S(1)}, s32[16]{0:T(128)}, u32[]{:S(2)}) copy-start(s32[16]{0:T(128)} %lengths_ref.1) | copy-start | bytes 196
  75.9 8.6 %all-to-all-start.3 = ((bf16[4,16,1536]{2,1,0:T(8,128)(2,1)}), bf16[4,16,1536]{2,1,0:T(8,128)(2,1)S(1)}, u32[]{:S(2)}, u32[]{:S(2)}) async-start(bf16[4,16,1536]{2,1,0:T(8,128)(2,1)} %broadcast_in_dim.36), calls=%async_computation.3 | async-start | bytes 393216 | tf_op jit(solution)/shard_map/all_to_all | solution.py:232
  87.7 57.8 %copy-start.6 = (bf16[352,1408]{1,0:T(8,128)(2,1)S(1)}, bf16[352,1408]{1,0:T(8,128)(2,1)}, u32[]{:S(2)}) copy-start(bf16[352,1408]{1,0:T(8,128)(2,1)} %w0_ref) | copy-start | bytes 2973700
  87.7 9.1 %all-to-all-start.4 = ((bf16[4,3,88,128]{3,2,1,0:T(8,128)(2,1)}), bf16[4,3,88,128]{3,2,1,0:T(8,128)(2,1)S(1)}, u32[]{:S(2)}, u32[]{:S(2)}) async-start(bf16[4,3,88,128]{3,2,1,0:T(8,128)(2,1)} %copy-done.9), calls=%async_computation.4 | async-start | bytes 540672 | tf_op jit(solution)/shard_map/all_to_all | solution.py:243
  91.3 54.2 %collective-permute-start.11 = (bf16[352,1408]{1,0:T(8,128)(2,1)}, bf16[352,1408]{1,0:T(8,128)(2,1)S(1)}, u32[]{:S(2)}, u32[]{:S(2)}) collective-permute-start(bf16[352,1408]{1,0:T(8,128)(2,1)} %w0_ref), channel_id=1, source_target_pairs={{0,3},{1,0},{2,1},{3,2},{4,7},{5,4},{6,5},{7,6},{8,11},{9,8},{10,9... | collective-permute-start | bytes 2973704 | tf_op jit(solution)/shard_map/ppermute | solution.py:32
  92.3 53.2 %collective-permute-start.10 = (bf16[352,1408]{1,0:T(8,128)(2,1)}, bf16[352,1408]{1,0:T(8,128)(2,1)S(1)}, u32[]{:S(2)}, u32[]{:S(2)}) collective-permute-start(bf16[352,1408]{1,0:T(8,128)(2,1)} %w0_ref), channel_id=1, source_target_pairs={{0,2},{1,3},{2,0},{3,1},{4,6},{5,7},{6,4},{7,5},{8,10},{9,11},{10,... | collective-permute-start | bytes 2973704 | tf_op jit(solution)/shard_map/ppermute | solution.py:32
  93.4 52.1 %collective-permute-start.9 = (bf16[352,1408]{1,0:T(8,128)(2,1)}, bf16[352,1408]{1,0:T(8,128)(2,1)}, u32[]{:S(2)}, u32[]{:S(2)}) collective-permute-start(bf16[352,1408]{1,0:T(8,128)(2,1)} %w0_ref), channel_id=1, source_target_pairs={{0,1},{1,2},{2,3},{3,0},{4,5},{5,6},{6,7},{7,4},{8,9},{9,10},{10,1... | collective-permute-start | bytes 2973704 | tf_op jit(solution)/shard_map/ppermute | solution.py:32
  96.8 5.0 %collective-permute-start.6 = (bf16[4,2,88,128]{3,2,1,0:T(8,128)(2,1)S(1)}, bf16[4,2,88,128]{3,2,1,0:T(8,128)(2,1)S(1)}, u32[]{:S(2)}, u32[]{:S(2)}) collective-permute-start(bf16[4,2,88,128]{3,2,1,0:T(8,128)(2,1)S(1)} %slice.20), channel_id=1, source_target_pairs={{0,4},{4,0},{1,5},{5,1},{2,6},{6,2},{3,7},{7,3},{8,12},{12,8},{9,1... | collective-permute-start | bytes 540680 | tf_op jit(solution)/shard_map/ppermute | solution.py:32
  99.7 5.6 %collective-permute-start.5 = (bf16[4,2,88,128]{3,2,1,0:T(8,128)(2,1)S(1)}, bf16[4,2,88,128]{3,2,1,0:T(8,128)(2,1)}, u32[]{:S(2)}, u32[]{:S(2)}) collective-permute-start(bf16[4,2,88,128]{3,2,1,0:T(8,128)(2,1)S(1)} %slice.20), channel_id=1, source_target_pairs={{0,64},{32,96},{64,128},{96,160},{128,192},{160,224},{1,65},{33,97... | collective-permute-start | bytes 540680 | tf_op jit(solution)/shard_map/ppermute | solution.py:27
  101.9 7.3 %collective-permute-start.4 = (bf16[4,2,88,128]{3,2,1,0:T(8,128)(2,1)S(1)}, bf16[4,2,88,128]{3,2,1,0:T(8,128)(2,1)}, u32[]{:S(2)}, u32[]{:S(2)}) collective-permute-start(bf16[4,2,88,128]{3,2,1,0:T(8,128)(2,1)S(1)} %slice.20), channel_id=1, source_target_pairs={{0,32},{32,64},{64,96},{96,128},{128,160},{160,192},{192,224},{1,3... | collective-permute-start | bytes 540680 | tf_op jit(solution)/shard_map/ppermute | solution.py:27
  105.3 4.6 %collective-permute-start.8 = (bf16[4,2,88,128]{3,2,1,0:T(8,128)(2,1)}, bf16[4,2,88,128]{3,2,1,0:T(8,128)(2,1)}, u32[]{:S(2)}, u32[]{:S(2)}) collective-permute-start(bf16[4,2,88,128]{3,2,1,0:T(8,128)(2,1)} %collective-permute-done.5.far_ref), channel_id=1, source_target_pairs={{0,4},{4,0},{1,5},{5,1},{2,6},{6,2},{3,7},{7,3},{8,12},{12,8},{9,1... | collective-permute-start | bytes 540680 | tf_op jit(solution)/shard_map/ppermute | solution.py:32
  109.2 2.1 %collective-permute-start.7 = (bf16[4,2,88,128]{3,2,1,0:T(8,128)(2,1)}, bf16[4,2,88,128]{3,2,1,0:T(8,128)(2,1)}, u32[]{:S(2)}, u32[]{:S(2)}) collective-permute-start(bf16[4,2,88,128]{3,2,1,0:T(8,128)(2,1)} %collective-permute-done.4.near_ref), channel_id=1, source_target_pairs={{0,4},{4,0},{1,5},{5,1},{2,6},{6,2},{3,7},{7,3},{8,12},{12,8},{9,1... | collective-permute-start | bytes 540680 | tf_op jit(solution)/shard_map/ppermute | solution.py:32
  (6 other events, 5.4 us)

commit v3 on v2

--- a/solution.py
+++ b/solution.py
@@ -32,7 +32,7 @@
     return lax.ppermute(x, axis, [(i, (i + by) % count) for i in range(count)])
 
 
-def call(kernel, out_shape, spaces, scratch=()):
+def call(kernel, out_shape, spaces, scratch=(), limit=8):
     single = not isinstance(out_shape, (list, tuple))
     outs = pl.BlockSpec(memory_space=VMEM)
     return pl.pallas_call(
@@ -41,7 +41,7 @@
         in_specs=[pl.BlockSpec(memory_space=s) for s in spaces],
         out_specs=outs if single else [outs] * len(out_shape),
         scratch_shapes=scratch,
-        compiler_params=pltpu.CompilerParams(vmem_limit_bytes=48 << 20),
+        compiler_params=pltpu.CompilerParams(vmem_limit_bytes=limit << 20),
     )
 
 
@@ -72,18 +72,30 @@
     return (2 * a + i) * MAXGRID + 2 * b + j
 
 
-def vision_kernel(grid_ref, picture_ref, qkv_ref, out_ref, share_ref):
+def vision_kernel(
+    grid_ref, picture_hbm, qkv_hbm, out_hbm, share_ref, picture_ref, qkv_ref, out_ref, arrived
+):
+    copies = [pltpu.make_async_copy(picture_hbm, picture_ref, arrived.at[0])]
+    for part in range(3):
+        copies.append(
+            pltpu.make_async_copy(qkv_hbm.at[part], qkv_ref.at[part], arrived.at[1 + part])
+        )
+    copies.append(pltpu.make_async_copy(out_hbm, out_ref, arrived.at[4]))
+    for copy in copies:
+        copy.start()
     count = picture_ref.shape[0]
     local_width = qkv_ref.shape[1]
+    copies[0].wait()
     normed = normalize(picture_ref[...].astype(F32))
-    queries = dot(qkv_ref[0], normed, (1, 1))
-    keys = dot(qkv_ref[1], normed, (1, 1))
-    values = dot(qkv_ref[2], normed, (1, 1))
+    parts = []
+    for part in range(3):
+        copies[1 + part].wait()
+        parts.append(dot(qkv_ref[part], normed, (1, 1)))
     slots = iota((count, 1), 0)
     usable = (slots // MAXGRID < 2 * grid_ref[0, 0]) & (slots % MAXGRID < 2 * grid_ref[0, 1])
     contexts = []
     for first in range(0, local_width, HEAD):
-        q, k, v = (x[first : first + HEAD].astype(BF) for x in (queries, keys, values))
+        q, k, v = (x[first : first + HEAD].astype(BF) for x in parts)
         scores = dot(k, q, (0, 0)) * SCALE
         scores = jnp.where(usable, scores, -jnp.inf)
         expons = jnp.exp(scores - jnp.max(scores, axis=0, keepdims=True))
@@ -92,7 +104,33 @@
     context = jnp.concatenate(contexts, axis=0).astype(BF)
     order = slot_of(iota((count, count), 0)) == iota((count, count), 1)
     context = dot(order.astype(BF), context, (1, 1)).astype(BF)
+    copies[4].wait()
     share_ref[...] = dot(context, out_ref[...], (1, 0)).astype(BF)
+
+
+def sum_kernel(parts_ref, rows_ref):
+    for y in range(4):
+        total = parts_ref[y, 0].astype(F32)
+        for t in range(1, 4):
+            total = total + parts_ref[y, t].astype(F32)
+        rows_ref[y] = total.astype(BF)
+
+
+def select_kernel(place_ref, mine_ref, other_ref, routed_ref):
+    width = mine_ref.shape[2] - FACTS
+    chosen = []
+    for rows_ref in (mine_ref, other_ref):
+        for y in range(4):
+            facts = rows_ref[y, 0:1, width:].astype(F32)
+            block, there = facts[:, 0:1], facts[:, 4:5]
+            same_core = block - 2.0 * jnp.floor(block * 0.5) == place_ref[1].astype(F32)
+            to = jnp.where(same_core & (there > 0.0), jnp.floor(block * 0.125), -1.0)
+            chosen.append((to, rows_ref, y))
+    for z in range(8):
+        rows = jnp.zeros(mine_ref.shape[1:], F32)
+        for to, rows_ref, y in chosen:
+            rows = jnp.where(to == float(z), rows_ref[y].astype(F32), rows)
+        routed_ref[z] = rows.astype(BF)
 
 
 def merge_kernel(facts_ref, own_ref, shares_ref, weight_ref, rows_ref):
@@ -113,23 +151,30 @@
         rows_ref[y, :, width:] = jnp.where(here, facts, jnp.zeros_like(facts))
 
 
-def project_kernel(rows_ref, tokens_ref, qkv_ref, prompt_ref, heads_ref):
+def project_kernel(
+    place_ref, r0_ref, r1_ref, r2_ref, r3_ref, tokens_ref, qkv_ref, prompt_ref, heads_ref
+):
     width = tokens_ref.shape[1]
-    facts = rows_ref[:, width:].astype(F32)
-    cell = iota((MERGED, 1), 0)
+    pieces, firsts = [], []
+    for by, piece in enumerate((r0_ref, r1_ref, r2_ref, r3_ref)):
+        pieces.append(piece[...])
+        firsts.append(jnp.full((16, 1), 16 * lax.rem(place_ref[2] + 4 - by, 4), I32))
+    rows = jnp.concatenate(pieces, axis=0)
+    cell = jnp.concatenate(firsts, axis=0) + iota((MERGED, 1), 0) % 16
+    facts = rows[:, width:].astype(F32)
     a, b = (cell // 8).astype(F32), (cell % 8).astype(F32)
     offset, high, wide, there = (facts[:, i : i + 1] for i in (1, 2, 3, 4))
     target = offset + a * wide + b
     usable = (a < high) & (b < wide) & (there > 0.0)
     target = jnp.where(usable, target, -1.0)
     table = (target == iota((MERGED, BLOCK), 1).astype(F32)).astype(BF)
-    placed = dot(table, rows_ref[...], (0, 0))
+    placed = dot(table, rows, (0, 0))
     covered = placed[:, width + 4 : width + 5] > 0.0
     prompt = jnp.where(covered, placed[:, :width], tokens_ref[...].astype(F32))
     prompt_ref[...] = prompt.astype(BF)
     normed = normalize(prompt)
     for part in range(3):
-        projected = dot(qkv_ref[part], normed, (1, 1)).astype(F32)
+        projected = dot(qkv_ref[part], normed, (1, 1))
         for head in range(4):
             heads_ref[head, part] = projected[head * HEAD : (head + 1) * HEAD].astype(BF)
 
@@ -174,11 +219,19 @@
             sent_ref[t, j] = context
 
 
-def output_kernel(facts_ref, context_ref, w0_ref, w1_ref, w2_ref, w3_ref, prompt_ref, out_ref):
+def output_kernel(
+    place_ref, context_ref, w0_ref, m1_ref, m2_ref, m3_ref, o1_ref, o2_ref, o3_ref,
+    prompt_ref, out_ref,
+):
+    c, t = place_ref[1], place_ref[2]
+    half = w0_ref.shape[0] // 2
     total = prompt_ref[...].astype(F32)
-    for by, weight in enumerate((w0_ref, w1_ref, w2_ref, w3_ref)):
-        piece = context_ref[lax.rem(facts_ref[2] + 4 - by, 4)]
-        total = total + dot(piece, weight[...], (0, 0))
+    for part in range(2):
+        total = total + dot(context_ref[t, part], w0_ref[part * half : (part + 1) * half], (0, 0))
+    for by, mine, other in ((1, m1_ref, o1_ref), (2, m2_ref, o2_ref), (3, m3_ref, o3_ref)):
+        source = lax.rem(t + 4 - by, 4)
+        total = total + dot(context_ref[source, c], mine[...], (0, 0))
+        total = total + dot(context_ref[source, 1 - c], other[...], (0, 0))
     out_ref[...] = total.astype(BF)
 
 
@@ -204,9 +257,19 @@
     picture = patches[0]
     block = picture_block[0]
 
-    share = call(vision_kernel, shape((count, width)), [SMEM, VMEM, VMEM, VMEM])(
-        picture_grid, picture, vision_qkv.transpose(1, 2, 0), vision_out
-    )
+    place = jnp.stack([z, c, t]).astype(I32)
+    share = call(
+        vision_kernel,
+        shape((count, width)),
+        [SMEM, pl.ANY, pl.ANY, pl.ANY],
+        [
+            VMEM((count, width), BF),
+            VMEM((3, local_width, width), BF),
+            VMEM((local_width, width), BF),
+            pltpu.SemaphoreType.DMA((5,)),
+        ],
+        limit=20,
+    )(picture_grid, picture, vision_qkv.transpose(1, 2, 0), vision_out)
     shares = lax.all_to_all(share.reshape(4, MERGED, width), "t", 0, 0, tiled=True)
     chosen = slot_of(t * MERGED + jnp.arange(MERGED))[:, None] == jnp.arange(count)[None, :]
     own = jnp.dot(chosen.astype(BF), picture, preferred_element_type=F32).astype(BF)
@@ -218,41 +281,48 @@
     )
 
     got = lax.all_to_all(routed.reshape(16, 16, wide), ("y", "t"), 0, 0, tiled=True)
-    got, tokens = lax.optimization_barrier((got, tokens))
+    got = call(sum_kernel, shape((4, 16, wide)), [VMEM])(got.reshape(4, 4, 16, wide))
+    other = around(got, "c", 1)
+    routed = call(select_kernel, shape((8, 16, wide)), [SMEM, VMEM, VMEM])(place, got, other)
+    routed, tokens, text_out = lax.optimization_barrier((routed, tokens, text_out))
+    half = local_width // 2
+    near_half = lax.dynamic_slice_in_dim(text_out, c * half, half, 0)
+    from_left, from_right = around(near_half, "t", 1), around(near_half, "t", -1)
     pieces = [tokens] + [around(tokens, "t", by) for by in range(1, 4)]
-    got = jnp.sum(got.reshape(4, 4, 16, wide).astype(F32), axis=1).astype(BF)
-    got = jnp.concatenate([got, around(got, "c", 1)])
-    to = got[:, 0, width].astype(F32).astype(I32)
-    pick = (got[:, 0, width + 4] > 0) & (to % 2 == c)
-    pick = pick[None, :] & (to[None, :] // 8 == jnp.arange(8)[:, None])
-    routed = jnp.einsum("zk,krd->zrd", pick.astype(BF), got, preferred_element_type=F32).astype(BF)
     got = lax.all_to_all(routed, "z", 0, 0, tiled=True)
     got = jnp.sum(got.astype(F32), axis=0).astype(BF)
-    got = jnp.broadcast_to(got[None], (4, 16, wide))
-    got = lax.all_to_all(got, "t", 0, 0, tiled=True).reshape(MERGED, wide)
+    rows = [got] + [around(got, "t", by) for by in range(1, 4)]
     own_tokens = jnp.zeros((4, BLOCK, local_width), BF)
     for by, piece in enumerate(pieces):
         own_tokens = lax.dynamic_update_index_in_dim(own_tokens, piece, (t - by) % 4, 0)
     own_tokens = own_tokens.transpose(1, 0, 2).reshape(BLOCK, width)
 
     prompt_in, heads = call(
-        project_kernel, [shape((BLOCK, width)), shape((4, 3, HEAD, BLOCK))], [VMEM] * 3
-    )(got, own_tokens, text_qkv.transpose(1, 2, 0))
-    heads, text_out = lax.optimization_barrier((heads, text_out))
-    weights = [text_out] + [around(text_out, "t", by) for by in range(1, 4)]
+        project_kernel,
+        [shape((BLOCK, width)), shape((4, 3, HEAD, BLOCK))],
+        [SMEM] + [VMEM] * 6,
+    )(place, *rows, own_tokens, text_qkv.transpose(1, 2, 0))
+    heads, from_left, from_right = lax.optimization_barrier((heads, from_left, from_right))
+    far_halves = (
+        around(from_left[: half // 2], "t", 1),
+        around(from_right[half // 2 :], "t", -1),
+    )
     mine = lax.all_to_all(heads, "y", 0, 0, tiled=True)
     pair = mine[:, 1:]
     near, far = ahead(pair, "z", 1), ahead(pair, "z", 2)
-    facts = jnp.stack([z, c, t]).astype(I32)
+    others = [around(x, "c", 1) for x in (pair, near, far)]
+    weights = [from_left, jnp.concatenate(far_halves), from_right]
+    weights = weights + [around(x, "c", 1) for x in weights]
     sent = call(
         attend_kernel,
         shape((4, 4, HEAD, BLOCK)),
         [SMEM, SMEM] + [VMEM] * 6,
         [pltpu.VMEM((HEAD, 24 * BLOCK), BF)] * 2,
-    )(facts, prompt_lengths, mine, near, far, *(around(x, "c", 1) for x in (pair, near, far)))
+        limit=16,
+    )(place, prompt_lengths, mine, near, far, *others)
     context = lax.all_to_all(sent.reshape(16, HEAD, BLOCK), ("t", "y"), 0, 0, tiled=True)
-    return call(output_kernel, shape((BLOCK, width)), [SMEM] + [VMEM] * 6)(
-        facts, context.reshape(4, local_width, BLOCK), *weights, prompt_in
+    return call(output_kernel, shape((BLOCK, width)), [SMEM] + [VMEM] * 9)(
+        place, context.reshape(4, 2, half, BLOCK), text_out, *weights, prompt_in
     )
 
 

time: 150 us -> 142 us (0.947)
  the two profiles are of different devices: /device:TPU:1 before, /device:TPU:64 now
where the time goes in v3:
time: 142 us; the launch traced here: 141 us
  starting transfers between devices  42.6 us (30%)
  waiting for transfers between devices  34.8 us (25%)
  local copies, waits for them, and re-layouts  21.3 us (15%)
  Pallas kernels  20.8 us (15%)
  blocking collectives  18.2 us (13%)
  between operations  1.67 us (1%)
    all_to_all x1, blocking collectives, local(): lax.all_to_all(routed.reshape(16, 16, wide), ('y', 't'), 0, 0, tiled=True)  18.2 us
    ppermute x17, starting transfers between devices, around(): return lax.ppermute(x, axis, [(i, (i + by) % count) for i in range(count)])  15.4 us
    all_to_all x1, waiting for transfers between devices, local(): lax.all_to_all(sent.reshape(16, HEAD, BLOCK), ('t', 'y'), 0, 0, tiled=True)  9.77 us
    unnamed x27, local copies, waits for them, and re-layouts  9.39 us
    ppermute x2, waiting for transfers between devices, ahead(): return lax.ppermute(x, axis, [(i, i + by) for i in range(count - by)])  8.34 us
    all_to_all x1, starting transfers between devices, local(): got = lax.all_to_all(routed, 'z', 0, 0, tiled=True)  8.13 us
    all_to_all x1, waiting for transfers between devices, local(): lax.all_to_all(share.reshape(4, MERGED, width), 't', 0, 0, tiled=True)  7.93 us
    pallas_call x1, Pallas kernels, local(): call(vision_kernel, shape((count, width)), [SMEM, pl.ANY, pl.ANY, pl.ANY]...  7.26 us
  transfers between devices with their start and end apart: 23, of which 10 were waited for; matrix products, arithmetic and copies ran while one was open for 9% of the time, Pallas kernels for 5%

profile of v3, /device:TPU:64, one launch (start us, length us, event | category | flops | bytes accessed | tf_op | source)
XLA Modules:
  0.0 140.8 jit_solution(16640825576042923591)
XLA Ops:
  0.0 1.8 %copy-done.1 = bf16[1408,3,352]{0,2,1:T(8,128)(2,1)S(1)} copy-done((bf16[1408,3,352]{0,2,1:T(8,128)(2,1)S(1)}, bf16[1408,3,352]{0,2,1:T(8,128)(2,1)}, u32[]{:S(2)}) %copy-start.1) | copy-done | bytes 2973720
  4.8 7.3 %shard_map.109 = bf16[256,1408]{1,0:T(8,128)(2,1)} custom-call(s32[1,2]{1,0:T(1,128)S(1)} %copy-done.10, bf16[256,1408]{1,0:T(8,128)(2,1)S(1)} %bitcast.37, bf16[3,352,1408]{2,1,0:T(8,128)(2,1)S(1)} %bitcast.35, bf16[352,1408]{1,0:T(8,128)(2,1)S(1)} %copy-done.6), custom_call_target="tpu_custom_call" | custom-call | tf_op jit(solution)/shard_map/pallas_call | solution.py:261
  12.1 4.3 %all-to-all-start = ((bf16[4,64,1408]{2,1,0:T(8,128)(2,1)}), bf16[4,64,1408]{2,1,0:T(8,128)(2,1)S(1)}, u32[]{:S(2)}, u32[]{:S(2)}) async-start(bf16[4,64,1408]{2,1,0:T(8,128)(2,1)} %bitcast.9), calls=%async_computation | async-start | bytes 1441792 | tf_op jit(solution)/shard_map/all_to_all | solution.py:273
  20.0 7.9 %all-to-all-done.shares_ref = bf16[4,64,1408]{2,1,0:T(8,128)(2,1)S(1)} async-done(((bf16[4,64,1408]{2,1,0:T(8,128)(2,1)}), bf16[4,64,1408]{2,1,0:T(8,128)(2,1)S(1)}, u32[]{:S(2)}, u32[]{:S(2)}) %all-to-all-start) | async-done | bytes 720928 | tf_op jit(solution)/shard_map/all_to_all | solution.py:273
  28.0 2.1 %copy-done = bf16[1,1408,1408]{2,1,0:T(8,128)(2,1)S(1)} copy-done((bf16[1,1408,1408]{2,1,0:T(8,128)(2,1)S(1)}, bf16[1,1408,1408]{2,1,0:T(8,128)(2,1)}, u32[]{:S(2)}) %copy-start) | copy-done | bytes 3964952
  31.7 18.2 %all_to_all.25 = bf16[16,16,1536]{2,1,0:T(8,128)(2,1)S(1)} all-to-all(bf16[16,16,1536]{2,1,0:T(8,128)(2,1)S(1)} %bitcast.34), channel_id=1, replica_groups=mesh['z'=8,'y'=4,'c'=2,'t'=4] {'y','t'}, dimensions={0} | all-to-all | bytes 1572864 | tf_op jit(solution)/shard_map/all_to_all | solution.py:283
  54.0 1.9 %collective-permute-start.5 = (bf16[128,352]{0,1:T(8,128)(2,1)}, bf16[128,352]{0,1:T(8,128)(2,1)S(1)}, u32[]{:S(2)}, u32[]{:S(2)}) collective-permute-start(bf16[128,352]{0,1:T(8,128)(2,1)} %param.18), channel_id=1, source_target_pairs={{0,2},{1,3},{2,0},{3,1},{4,6},{5,7},{6,4},{7,5},{8,10},{9,11},{10,... | collective-permute-start | bytes 270344 | tf_op jit(solution)/shard_map/ppermute | solution.py:32
  55.9 8.1 %all-to-all-start.2 = ((bf16[8,16,1536]{2,1,0:T(8,128)(2,1)}), bf16[8,16,1536]{2,1,0:T(8,128)(2,1)}, u32[]{:S(2)}, u32[]{:S(2)}) async-start(bf16[8,16,1536]{2,1,0:T(8,128)(2,1)} %shard_map.112), calls=%async_computation.2 | async-start | bytes 786432 | tf_op jit(solution)/shard_map/all_to_all | solution.py:292
  64.0 1.8 %constant_dynamic-slice_fusion = bf16[176,1408]{1,0:T(8,128)(2,1)} fusion(bf16[352,1408]{1,0:T(8,128)(2,1)} %w0_ref, s32[]{:T(128)S(6)} %select_n.118), kind=kLoop, calls=%fused_computation.19 | loop fusion | bytes 991236 | tf_op jit(solution)/shard_map/dynamic_slice | solution.py:289
  65.9 3.2 %collective-permute-start.8 = (bf16[176,1408]{1,0:T(8,128)(2,1)}, bf16[176,1408]{1,0:T(8,128)(2,1)}, u32[]{:S(2)}, u32[]{:S(2)}) collective-permute-start(bf16[176,1408]{1,0:T(8,128)(2,1)} %constant_dynamic-slice_fusion), channel_id=1, source_target_pairs={{0,3},{1,0},{2,1},{3,2},{4,7},{5,4},{6,5},{7,6},{8,11},{9,8},{10,9... | collective-permute-start | bytes 1486856 | tf_op jit(solution)/shard_map/ppermute | solution.py:32
  72.7 2.8 %all-to-all-done.2 = bf16[8,16,1536]{2,1,0:T(8,128)(2,1)} async-done(((bf16[8,16,1536]{2,1,0:T(8,128)(2,1)}), bf16[8,16,1536]{2,1,0:T(8,128)(2,1)}, u32[]{:S(2)}, u32[]{:S(2)}) %all-to-all-start.2) | async-done | bytes 393248 | tf_op jit(solution)/shard_map/all_to_all | solution.py:292
  76.6 3.2 %collective-permute-start.3 = (bf16[16,1536]{1,0:T(8,128)(2,1)S(1)}, bf16[16,1536]{1,0:T(8,128)(2,1)S(1)}, u32[]{:S(2)}, u32[]{:S(2)}) collective-permute-start(bf16[16,1536]{1,0:T(8,128)(2,1)S(1)} %reduce_sum.12.r0_ref), channel_id=1, source_target_pairs={{0,3},{1,0},{2,1},{3,2},{4,7},{5,4},{6,5},{7,6},{8,11},{9,8},{10,9... | collective-permute-start | bytes 147464 | tf_op jit(solution)/shard_map/ppermute | solution.py:32
  83.3 2.1 %collective-permute-done.2.r2_ref = bf16[16,1536]{1,0:T(8,128)(2,1)S(1)} collective-permute-done((bf16[16,1536]{1,0:T(8,128)(2,1)S(1)}, bf16[16,1536]{1,0:T(8,128)(2,1)S(1)}, u32[]{:S(2)}, u32[]{:S(2)}) %collective-permute-start.2) | collective-permute-done | bytes 49184 | tf_op jit(solution)/shard_map/ppermute | solution.py:32
  85.9 2.4 %shard_map.113 = (bf16[128,1408]{1,0:T(8,128)(2,1)S(1)}, bf16[4,3,88,128]{3,2,1,0:T(8,128)(2,1)S(1)}) custom-call(s32[3]{0:T(128)S(1)} %pad_add_fusion.place_ref.facts_ref, bf16[16,1536]{1,0:T(8,128)(2,1)S(1)} %reduce_sum.12.r0_ref, bf16[16,1536]{1,0:T(8,128)(2,1)S(1)} %collective-permute-done.1.r1_ref, bf16[16,1536]{1,0:T(8,128)(2,1)S(1)} %collective-permute-done.2.r2_ref, ...), custom_call_target="tpu_custom_call" | custom-call | tf_op jit(solution)/shard_map/pallas_call | solution.py:300
  90.9 3.5 %all-to-all-start.3 = ((bf16[4,3,88,128]{3,2,1,0:T(8,128)(2,1)}), bf16[4,3,88,128]{3,2,1,0:T(8,128)(2,1)S(1)}, u32[]{:S(2)}, u32[]{:S(2)}) async-start(bf16[4,3,88,128]{3,2,1,0:T(8,128)(2,1)} %copy-done.9), calls=%async_computation.3 | async-start | bytes 540672 | tf_op jit(solution)/shard_map/all_to_all | solution.py:310
  96.0 3.2 %collective-permute-start.15 = (bf16[88,1408]{1,0:T(8,128)(2,1)}, bf16[88,1408]{1,0:T(8,128)(2,1)S(1)}, u32[]{:S(2)}, u32[]{:S(2)}) collective-permute-start(bf16[88,1408]{1,0:T(8,128)(2,1)} %slice.19), channel_id=1, source_target_pairs={{0,3},{1,0},{2,1},{3,2},{4,7},{5,4},{6,5},{7,6},{8,11},{9,8},{10,9... | collective-permute-start | bytes 743432 | tf_op jit(solution)/shard_map/ppermute | solution.py:32
  101.1 3.9 %collective-permute-start.10 = (bf16[4,2,88,128]{3,2,1,0:T(8,128)(2,1)S(1)}, bf16[4,2,88,128]{3,2,1,0:T(8,128)(2,1)S(1)}, u32[]{:S(2)}, u32[]{:S(2)}) collective-permute-start(bf16[4,2,88,128]{3,2,1,0:T(8,128)(2,1)S(1)} %slice.20), channel_id=1, source_target_pairs={{0,64},{32,96},{64,128},{96,160},{128,192},{160,224},{1,65},{33,97... | collective-permute-start | bytes 540680 | tf_op jit(solution)/shard_map/ppermute | solution.py:27
  105.0 2.5 %collective-permute-start.9 = (bf16[4,2,88,128]{3,2,1,0:T(8,128)(2,1)S(1)}, bf16[4,2,88,128]{3,2,1,0:T(8,128)(2,1)S(1)}, u32[]{:S(2)}, u32[]{:S(2)}) collective-permute-start(bf16[4,2,88,128]{3,2,1,0:T(8,128)(2,1)S(1)} %slice.20), channel_id=1, source_target_pairs={{0,32},{32,64},{64,96},{96,128},{128,160},{160,192},{192,224},{1,3... | collective-permute-start | bytes 540680 | tf_op jit(solution)/shard_map/ppermute | solution.py:27
  107.6 5.3 %collective-permute-done.10.far_ref = bf16[4,2,88,128]{3,2,1,0:T(8,128)(2,1)S(1)} collective-permute-done((bf16[4,2,88,128]{3,2,1,0:T(8,128)(2,1)S(1)}, bf16[4,2,88,128]{3,2,1,0:T(8,128)(2,1)S(1)}, u32[]{:S(2)}, u32[]{:S(2)}) %collective-permute-start.10) | collective-permute-done | bytes 180256 | tf_op jit(solution)/shard_map/ppermute | solution.py:27
  112.9 3.0 %collective-permute-done.9.near_ref = bf16[4,2,88,128]{3,2,1,0:T(8,128)(2,1)S(1)} collective-permute-done((bf16[4,2,88,128]{3,2,1,0:T(8,128)(2,1)S(1)}, bf16[4,2,88,128]{3,2,1,0:T(8,128)(2,1)S(1)}, u32[]{:S(2)}, u32[]{:S(2)}) %collective-permute-start.9) | collective-permute-done | bytes 180256 | tf_op jit(solution)/shard_map/ppermute | solution.py:27
  117.4 4.8 %shard_map.114 = bf16[4,4,88,128]{3,2,1,0:T(8,128)(2,1)} custom-call(s32[3]{0:T(128)S(1)} %pad_add_fusion.place_ref.facts_ref, s32[16]{0:T(128)S(1)} %copy-done.12, bf16[4,3,88,128]{3,2,1,0:T(8,128)(2,1)S(1)} %all-to-all-done.3.own_ref, bf16[4,2,88,128]{3,2,1,0:T(8,128)(2,1)S(1)} %collective-permute-done.9.near_ref, ...), custom_call_target="tpu_custom_call" | custom-call | tf_op jit(solution)/shard_map/pallas_call | solution.py:316
  122.1 4.9 %all-to-all-start.4 = ((bf16[16,88,128]{2,1,0:T(8,128)(2,1)}), bf16[16,88,128]{2,1,0:T(8,128)(2,1)S(1)}, u32[]{:S(2)}, u32[]{:S(2)}) async-start(bf16[16,88,128]{2,1,0:T(8,128)(2,1)} %bitcast.20), calls=%async_computation.4 | async-start | bytes 720896 | tf_op jit(solution)/shard_map/all_to_all | solution.py:323
  127.1 9.8 %all-to-all-done.4 = bf16[16,88,128]{2,1,0:T(8,128)(2,1)S(1)} async-done(((bf16[16,88,128]{2,1,0:T(8,128)(2,1)}), bf16[16,88,128]{2,1,0:T(8,128)(2,1)S(1)}, u32[]{:S(2)}, u32[]{:S(2)}) %all-to-all-start.4) | async-done | bytes 360480 | tf_op jit(solution)/shard_map/all_to_all | solution.py:323
  137.9 2.9 %shard_map.115 = bf16[128,1408]{1,0:T(8,128)(2,1)} custom-call(s32[3]{0:T(128)S(1)} %pad_add_fusion.place_ref.facts_ref, bf16[4,2,176,128]{3,2,1,0:T(8,128)(2,1)S(1)} %bitcast.38, bf16[352,1408]{1,0:T(8,128)(2,1)S(1)} %copy-done.5, bf16[176,1408]{1,0:T(8,128)(2,1)} %collective-permute-done.7.m1_ref, ...), custom_call_target="tpu_custom_call" | custom-call | tf_op jit(solution)/shard_map/pallas_call | solution.py:324
  (76 shorter events, 28.2 us)
Async XLA Ops:
  12.1 15.9 %all-to-all-start = ((bf16[4,64,1408]{2,1,0:T(8,128)(2,1)}), bf16[4,64,1408]{2,1,0:T(8,128)(2,1)S(1)}, u32[]{:S(2)}, u32[]{:S(2)}) async-start(bf16[4,64,1408]{2,1,0:T(8,128)(2,1)} %bitcast.9), calls=%async_computation | async-start | bytes 1441792 | tf_op jit(solution)/shard_map/all_to_all | solution.py:273
  49.9 1.5 %collective-permute-start = (bf16[4,16,1536]{2,1,0:T(8,128)(2,1)S(1)}, bf16[4,16,1536]{2,1,0:T(8,128)(2,1)S(1)}, u32[]{:S(2)}, u32[]{:S(2)}) collective-permute-start(bf16[4,16,1536]{2,1,0:T(8,128)(2,1)S(1)} %shard_map.111.mine_ref), channel_id=1, source_target_pairs={{0,4},{4,0},{1,5},{5,1},{2,6},{6,2},{3,7},{7,3},{8,12},{12,8},{9,1... | collective-permute-start | bytes 589832 | tf_op jit(solution)/shard_map/ppermute | solution.py:32
  53.3 27.0 %collective-permute-start.6 = (bf16[128,352]{0,1:T(8,128)(2,1)}, bf16[128,352]{0,1:T(8,128)(2,1)S(1)}, u32[]{:S(2)}, u32[]{:S(2)}) collective-permute-start(bf16[128,352]{0,1:T(8,128)(2,1)} %param.18), channel_id=1, source_target_pairs={{0,3},{1,0},{2,1},{3,2},{4,7},{5,4},{6,5},{7,6},{8,11},{9,8},{10,9... | collective-permute-start | bytes 270344 | tf_op jit(solution)/shard_map/ppermute | solution.py:32
  54.0 18.1 %collective-permute-start.5 = (bf16[128,352]{0,1:T(8,128)(2,1)}, bf16[128,352]{0,1:T(8,128)(2,1)S(1)}, u32[]{:S(2)}, u32[]{:S(2)}) collective-permute-start(bf16[128,352]{0,1:T(8,128)(2,1)} %param.18), channel_id=1, source_target_pairs={{0,2},{1,3},{2,0},{3,1},{4,6},{5,7},{6,4},{7,5},{8,10},{9,11},{10,... | collective-permute-start | bytes 270344 | tf_op jit(solution)/shard_map/ppermute | solution.py:32
  55.9 15.5 %collective-permute-start.4 = (bf16[128,352]{0,1:T(8,128)(2,1)}, bf16[128,352]{0,1:T(8,128)(2,1)S(1)}, u32[]{:S(2)}, u32[]{:S(2)}) collective-permute-start(bf16[128,352]{0,1:T(8,128)(2,1)} %param.18), channel_id=1, source_target_pairs={{0,1},{1,2},{2,3},{3,0},{4,5},{5,6},{6,7},{7,4},{8,9},{9,10},{10,1... | collective-permute-start | bytes 270344 | tf_op jit(solution)/shard_map/ppermute | solution.py:32
  55.9 19.6 %all-to-all-start.2 = ((bf16[8,16,1536]{2,1,0:T(8,128)(2,1)}), bf16[8,16,1536]{2,1,0:T(8,128)(2,1)}, u32[]{:S(2)}, u32[]{:S(2)}) async-start(bf16[8,16,1536]{2,1,0:T(8,128)(2,1)} %shard_map.112), calls=%async_computation.2 | async-start | bytes 786432 | tf_op jit(solution)/shard_map/all_to_all | solution.py:292
  65.9 23.9 %collective-permute-start.8 = (bf16[176,1408]{1,0:T(8,128)(2,1)}, bf16[176,1408]{1,0:T(8,128)(2,1)}, u32[]{:S(2)}, u32[]{:S(2)}) collective-permute-start(bf16[176,1408]{1,0:T(8,128)(2,1)} %constant_dynamic-slice_fusion), channel_id=1, source_target_pairs={{0,3},{1,0},{2,1},{3,2},{4,7},{5,4},{6,5},{7,6},{8,11},{9,8},{10,9... | collective-permute-start | bytes 1486856 | tf_op jit(solution)/shard_map/ppermute | solution.py:32
  69.1 20.6 %collective-permute-start.7 = (bf16[176,1408]{1,0:T(8,128)(2,1)}, bf16[176,1408]{1,0:T(8,128)(2,1)}, u32[]{:S(2)}, u32[]{:S(2)}) collective-permute-start(bf16[176,1408]{1,0:T(8,128)(2,1)} %constant_dynamic-slice_fusion), channel_id=1, source_target_pairs={{0,1},{1,2},{2,3},{3,0},{4,5},{5,6},{6,7},{7,4},{8,9},{9,10},{10,1... | collective-permute-start | bytes 1486856 | tf_op jit(solution)/shard_map/ppermute | solution.py:32
  76.6 6.8 %collective-permute-start.3 = (bf16[16,1536]{1,0:T(8,128)(2,1)S(1)}, bf16[16,1536]{1,0:T(8,128)(2,1)S(1)}, u32[]{:S(2)}, u32[]{:S(2)}) collective-permute-start(bf16[16,1536]{1,0:T(8,128)(2,1)S(1)} %reduce_sum.12.r0_ref), channel_id=1, source_target_pairs={{0,3},{1,0},{2,1},{3,2},{4,7},{5,4},{6,5},{7,6},{8,11},{9,8},{10,9... | collective-permute-start | bytes 147464 | tf_op jit(solution)/shard_map/ppermute | solution.py:32
  79.8 5.6 %collective-permute-start.2 = (bf16[16,1536]{1,0:T(8,128)(2,1)S(1)}, bf16[16,1536]{1,0:T(8,128)(2,1)S(1)}, u32[]{:S(2)}, u32[]{:S(2)}) collective-permute-start(bf16[16,1536]{1,0:T(8,128)(2,1)S(1)} %reduce_sum.12.r0_ref), channel_id=1, source_target_pairs={{0,2},{1,3},{2,0},{3,1},{4,6},{5,7},{6,4},{7,5},{8,10},{9,11},{10,... | collective-permute-start | bytes 147464 | tf_op jit(solution)/shard_map/ppermute | solution.py:32
  80.2 5.7 %collective-permute-start.1 = (bf16[16,1536]{1,0:T(8,128)(2,1)S(1)}, bf16[16,1536]{1,0:T(8,128)(2,1)S(1)}, u32[]{:S(2)}, u32[]{:S(2)}) collective-permute-start(bf16[16,1536]{1,0:T(8,128)(2,1)S(1)} %reduce_sum.12.r0_ref), channel_id=1, source_target_pairs={{0,1},{1,2},{2,3},{3,0},{4,5},{5,6},{6,7},{7,4},{8,9},{9,10},{10,1... | collective-permute-start | bytes 147464 | tf_op jit(solution)/shard_map/ppermute | solution.py:32
  89.8 47.1 %copy-start.5 = (bf16[352,1408]{1,0:T(8,128)(2,1)S(1)}, bf16[352,1408]{1,0:T(8,128)(2,1)}, u32[]{:S(2)}) copy-start(bf16[352,1408]{1,0:T(8,128)(2,1)} %w0_ref) | copy-start | bytes 2973700
  90.8 14.2 %collective-permute-start.14 = (bf16[88,1408]{1,0:T(8,128)(2,1)S(1)}, bf16[88,1408]{1,0:T(8,128)(2,1)S(1)}, u32[]{:S(2)}, u32[]{:S(2)}) collective-permute-start(bf16[88,1408]{1,0:T(8,128)(2,1)S(1)} %slice.18), channel_id=1, source_target_pairs={{0,1},{1,2},{2,3},{3,0},{4,5},{5,6},{6,7},{7,4},{8,9},{9,10},{10,1... | collective-permute-start | bytes 743432 | tf_op jit(solution)/shard_map/ppermute | solution.py:32
  90.9 10.2 %all-to-all-start.3 = ((bf16[4,3,88,128]{3,2,1,0:T(8,128)(2,1)}), bf16[4,3,88,128]{3,2,1,0:T(8,128)(2,1)S(1)}, u32[]{:S(2)}, u32[]{:S(2)}) async-start(bf16[4,3,88,128]{3,2,1,0:T(8,128)(2,1)} %copy-done.9), calls=%async_computation.3 | async-start | bytes 540672 | tf_op jit(solution)/shard_map/all_to_all | solution.py:310
  96.0 11.5 %collective-permute-start.15 = (bf16[88,1408]{1,0:T(8,128)(2,1)}, bf16[88,1408]{1,0:T(8,128)(2,1)S(1)}, u32[]{:S(2)}, u32[]{:S(2)}) collective-permute-start(bf16[88,1408]{1,0:T(8,128)(2,1)} %slice.19), channel_id=1, source_target_pairs={{0,3},{1,0},{2,1},{3,2},{4,7},{5,4},{6,5},{7,6},{8,11},{9,8},{10,9... | collective-permute-start | bytes 743432 | tf_op jit(solution)/shard_map/ppermute | solution.py:32
  99.2 27.8 %collective-permute-start.16 = (bf16[176,1408]{1,0:T(8,128)(2,1)}, bf16[176,1408]{1,0:T(8,128)(2,1)S(1)}, u32[]{:S(2)}, u32[]{:S(2)}) collective-permute-start(bf16[176,1408]{1,0:T(8,128)(2,1)} %collective-permute-done.7.m1_ref), channel_id=1, source_target_pairs={{0,4},{4,0},{1,5},{5,1},{2,6},{6,2},{3,7},{7,3},{8,12},{12,8},{9,1... | collective-permute-start | bytes 1486856 | tf_op jit(solution)/shard_map/ppermute | solution.py:32
  99.3 27.8 %collective-permute-start.18 = (bf16[176,1408]{1,0:T(8,128)(2,1)}, bf16[176,1408]{1,0:T(8,128)(2,1)S(1)}, u32[]{:S(2)}, u32[]{:S(2)}) collective-permute-start(bf16[176,1408]{1,0:T(8,128)(2,1)} %collective-permute-done.8.m3_ref), channel_id=1, source_target_pairs={{0,4},{4,0},{1,5},{5,1},{2,6},{6,2},{3,7},{7,3},{8,12},{12,8},{9,1... | collective-permute-start | bytes 1486856 | tf_op jit(solution)/shard_map/ppermute | solution.py:32
  101.1 11.8 %collective-permute-start.10 = (bf16[4,2,88,128]{3,2,1,0:T(8,128)(2,1)S(1)}, bf16[4,2,88,128]{3,2,1,0:T(8,128)(2,1)S(1)}, u32[]{:S(2)}, u32[]{:S(2)}) collective-permute-start(bf16[4,2,88,128]{3,2,1,0:T(8,128)(2,1)S(1)} %slice.20), channel_id=1, source_target_pairs={{0,64},{32,96},{64,128},{96,160},{128,192},{160,224},{1,65},{33,97... | collective-permute-start | bytes 540680 | tf_op jit(solution)/shard_map/ppermute | solution.py:27
  105.0 11.0 %collective-permute-start.9 = (bf16[4,2,88,128]{3,2,1,0:T(8,128)(2,1)S(1)}, bf16[4,2,88,128]{3,2,1,0:T(8,128)(2,1)S(1)}, u32[]{:S(2)}, u32[]{:S(2)}) collective-permute-start(bf16[4,2,88,128]{3,2,1,0:T(8,128)(2,1)S(1)} %slice.20), channel_id=1, source_target_pairs={{0,32},{32,64},{64,96},{96,128},{128,160},{160,192},{192,224},{1,3... | collective-permute-start | bytes 540680 | tf_op jit(solution)/shard_map/ppermute | solution.py:27
  107.5 8.5 %collective-permute-start.11 = (bf16[4,2,88,128]{3,2,1,0:T(8,128)(2,1)S(1)}, bf16[4,2,88,128]{3,2,1,0:T(8,128)(2,1)S(1)}, u32[]{:S(2)}, u32[]{:S(2)}) collective-permute-start(bf16[4,2,88,128]{3,2,1,0:T(8,128)(2,1)S(1)} %slice.20), channel_id=1, source_target_pairs={{0,4},{4,0},{1,5},{5,1},{2,6},{6,2},{3,7},{7,3},{8,12},{12,8},{9,1... | collective-permute-start | bytes 540680 | tf_op jit(solution)/shard_map/ppermute | solution.py:32
  112.9 3.7 %collective-permute-start.13 = (bf16[4,2,88,128]{3,2,1,0:T(8,128)(2,1)S(1)}, bf16[4,2,88,128]{3,2,1,0:T(8,128)(2,1)S(1)}, u32[]{:S(2)}, u32[]{:S(2)}) collective-permute-start(bf16[4,2,88,128]{3,2,1,0:T(8,128)(2,1)S(1)} %collective-permute-done.10.far_ref), channel_id=1, source_target_pairs={{0,4},{4,0},{1,5},{5,1},{2,6},{6,2},{3,7},{7,3},{8,12},{12,8},{9,1... | collective-permute-start | bytes 540680 | tf_op jit(solution)/shard_map/ppermute | solution.py:32
  116.0 1.4 %collective-permute-start.12 = (bf16[4,2,88,128]{3,2,1,0:T(8,128)(2,1)S(1)}, bf16[4,2,88,128]{3,2,1,0:T(8,128)(2,1)S(1)}, u32[]{:S(2)}, u32[]{:S(2)}) collective-permute-start(bf16[4,2,88,128]{3,2,1,0:T(8,128)(2,1)S(1)} %collective-permute-done.9.near_ref), channel_id=1, source_target_pairs={{0,4},{4,0},{1,5},{5,1},{2,6},{6,2},{3,7},{7,3},{8,12},{12,8},{9,1... | collective-permute-start | bytes 540680 | tf_op jit(solution)/shard_map/ppermute | solution.py:32
  116.0 11.1 %collective-permute-start.17 = (bf16[176,1408]{1,0:T(8,128)(2,1)S(1)}, bf16[176,1408]{1,0:T(8,128)(2,1)S(1)}, u32[]{:S(2)}, u32[]{:S(2)}) collective-permute-start(bf16[176,1408]{1,0:T(8,128)(2,1)S(1)} %constant_dynamic-update-slice_fusion.m2_ref), channel_id=1, source_target_pairs={{0,4},{4,0},{1,5},{5,1},{2,6},{6,2},{3,7},{7,3},{8,12},{12,8},{9,1... | collective-permute-start | bytes 1486856 | tf_op jit(solution)/shard_map/ppermute | solution.py:32
  122.1 14.7 %all-to-all-start.4 = ((bf16[16,88,128]{2,1,0:T(8,128)(2,1)}), bf16[16,88,128]{2,1,0:T(8,128)(2,1)S(1)}, u32[]{:S(2)}, u32[]{:S(2)}) async-start(bf16[16,88,128]{2,1,0:T(8,128)(2,1)} %bitcast.20), calls=%async_computation.4 | async-start | bytes 720896 | tf_op jit(solution)/shard_map/all_to_all | solution.py:323
  (12 other events, 104.1 us)

commit v4 on v3

--- a/solution.py
+++ b/solution.py
@@ -18,6 +18,7 @@
 I32 = jnp.int32
 VMEM = pltpu.VMEM
 SMEM = pltpu.SMEM
+HBM = pltpu.HBM
 FACTS = 128
 WINDOW = 18 * BLOCK
 
@@ -118,19 +119,15 @@
 
 def select_kernel(place_ref, mine_ref, other_ref, routed_ref):
     width = mine_ref.shape[2] - FACTS
-    chosen = []
+    routed_ref[...] = jnp.zeros(routed_ref.shape, BF)
     for rows_ref in (mine_ref, other_ref):
         for y in range(4):
             facts = rows_ref[y, 0:1, width:].astype(F32)
-            block, there = facts[:, 0:1], facts[:, 4:5]
-            same_core = block - 2.0 * jnp.floor(block * 0.5) == place_ref[1].astype(F32)
-            to = jnp.where(same_core & (there > 0.0), jnp.floor(block * 0.125), -1.0)
-            chosen.append((to, rows_ref, y))
-    for z in range(8):
-        rows = jnp.zeros(mine_ref.shape[1:], F32)
-        for to, rows_ref, y in chosen:
-            rows = jnp.where(to == float(z), rows_ref[y].astype(F32), rows)
-        routed_ref[z] = rows.astype(BF)
+            block = facts[0, 0].astype(I32)
+
+            @pl.when((facts[0, 4] > 0.0) & (block % 2 == place_ref[1]))
+            def _():
+                routed_ref[block // 8] = rows_ref[y]
 
 
 def merge_kernel(facts_ref, own_ref, shares_ref, weight_ref, rows_ref):
@@ -151,12 +148,10 @@
         rows_ref[y, :, width:] = jnp.where(here, facts, jnp.zeros_like(facts))
 
 
-def project_kernel(
-    place_ref, r0_ref, r1_ref, r2_ref, r3_ref, tokens_ref, qkv_ref, prompt_ref, heads_ref
-):
+def placed_rows(place_ref, pieces_refs, tokens_ref):
     width = tokens_ref.shape[1]
     pieces, firsts = [], []
-    for by, piece in enumerate((r0_ref, r1_ref, r2_ref, r3_ref)):
+    for by, piece in enumerate(pieces_refs):
         pieces.append(piece[...])
         firsts.append(jnp.full((16, 1), 16 * lax.rem(place_ref[2] + 4 - by, 4), I32))
     rows = jnp.concatenate(pieces, axis=0)
@@ -170,9 +165,19 @@
     table = (target == iota((MERGED, BLOCK), 1).astype(F32)).astype(BF)
     placed = dot(table, rows, (0, 0))
     covered = placed[:, width + 4 : width + 5] > 0.0
-    prompt = jnp.where(covered, placed[:, :width], tokens_ref[...].astype(F32))
-    prompt_ref[...] = prompt.astype(BF)
-    normed = normalize(prompt)
+    return jnp.where(covered, placed[:, :width], tokens_ref[...].astype(F32))
+
+
+def place_kernel(place_ref, r0_ref, r1_ref, r2_ref, r3_ref, tokens_ref, prompt_ref):
+    pieces = (r0_ref, r1_ref, r2_ref, r3_ref)
+    prompt_ref[...] = placed_rows(place_ref, pieces, tokens_ref).astype(BF)
+
+
+def project_kernel(
+    place_ref, r0_ref, r1_ref, r2_ref, r3_ref, tokens_ref, qkv_ref, heads_ref
+):
+    pieces = (r0_ref, r1_ref, r2_ref, r3_ref)
+    normed = normalize(placed_rows(place_ref, pieces, tokens_ref))
     for part in range(3):
         projected = dot(qkv_ref[part], normed, (1, 1))
         for head in range(4):
@@ -224,15 +229,19 @@
     prompt_ref, out_ref,
 ):
     c, t = place_ref[1], place_ref[2]
-    half = w0_ref.shape[0] // 2
-    total = prompt_ref[...].astype(F32)
-    for part in range(2):
-        total = total + dot(context_ref[t, part], w0_ref[part * half : (part + 1) * half], (0, 0))
+    half = m1_ref.shape[0]
+    width = out_ref.shape[1]
+    pairs = [(context_ref[t, part].T, w0_ref.at[part * half : (part + 1) * half]) for part in (0, 1)]
     for by, mine, other in ((1, m1_ref, o1_ref), (2, m2_ref, o2_ref), (3, m3_ref, o3_ref)):
         source = lax.rem(t + 4 - by, 4)
-        total = total + dot(context_ref[source, c], mine[...], (0, 0))
-        total = total + dot(context_ref[source, 1 - c], other[...], (0, 0))
-    out_ref[...] = total.astype(BF)
+        pairs.append((context_ref[source, c].T, mine))
+        pairs.append((context_ref[source, 1 - c].T, other))
+    for first in range(0, width, 256):
+        strip = slice(first, min(first + 256, width))
+        total = prompt_ref[:, strip].astype(F32)
+        for context, weight in pairs:
+            total = total + dot(context, weight[:, strip], (1, 0))
+        out_ref[:, strip] = total.astype(BF)
 
 
 def local(
@@ -261,18 +270,20 @@
     share = call(
         vision_kernel,
         shape((count, width)),
-        [SMEM, pl.ANY, pl.ANY, pl.ANY],
+        [SMEM, HBM, HBM, HBM],
         [
             VMEM((count, width), BF),
             VMEM((3, local_width, width), BF),
             VMEM((local_width, width), BF),
             pltpu.SemaphoreType.DMA((5,)),
         ],
-        limit=20,
+        limit=60,
     )(picture_grid, picture, vision_qkv.transpose(1, 2, 0), vision_out)
     shares = lax.all_to_all(share.reshape(4, MERGED, width), "t", 0, 0, tiled=True)
     chosen = slot_of(t * MERGED + jnp.arange(MERGED))[:, None] == jnp.arange(count)[None, :]
     own = jnp.dot(chosen.astype(BF), picture, preferred_element_type=F32).astype(BF)
+    own, tokens = lax.optimization_barrier((own, tokens))
+    pieces = [tokens] + [around(tokens, "t", by) for by in range(1, 4)]
     facts = jnp.stack([block, picture_offset[0], picture_grid[0, 0], picture_grid[0, 1], 1])
     facts = jnp.where(t == 0, facts, 0)
     facts = jnp.concatenate([facts, (block % 8 // 2)[None]]).astype(I32)
@@ -284,11 +295,10 @@
     got = call(sum_kernel, shape((4, 16, wide)), [VMEM])(got.reshape(4, 4, 16, wide))
     other = around(got, "c", 1)
     routed = call(select_kernel, shape((8, 16, wide)), [SMEM, VMEM, VMEM])(place, got, other)
-    routed, tokens, text_out = lax.optimization_barrier((routed, tokens, text_out))
+    routed, text_out = lax.optimization_barrier((routed, text_out))
     half = local_width // 2
     near_half = lax.dynamic_slice_in_dim(text_out, c * half, half, 0)
     from_left, from_right = around(near_half, "t", 1), around(near_half, "t", -1)
-    pieces = [tokens] + [around(tokens, "t", by) for by in range(1, 4)]
     got = lax.all_to_all(routed, "z", 0, 0, tiled=True)
     got = jnp.sum(got.astype(F32), axis=0).astype(BF)
     rows = [got] + [around(got, "t", by) for by in range(1, 4)]
@@ -297,17 +307,21 @@
         own_tokens = lax.dynamic_update_index_in_dim(own_tokens, piece, (t - by) % 4, 0)
     own_tokens = own_tokens.transpose(1, 0, 2).reshape(BLOCK, width)
 
-    prompt_in, heads = call(
+    heads = call(
         project_kernel,
-        [shape((BLOCK, width)), shape((4, 3, HEAD, BLOCK))],
+        shape((4, 3, HEAD, BLOCK)),
         [SMEM] + [VMEM] * 6,
     )(place, *rows, own_tokens, text_qkv.transpose(1, 2, 0))
-    heads, from_left, from_right = lax.optimization_barrier((heads, from_left, from_right))
+    mine = lax.all_to_all(heads, "y", 0, 0, tiled=True)
+    mine, from_left, from_right = lax.optimization_barrier((mine, from_left, from_right))
+    mine, own_tokens = lax.optimization_barrier((mine, own_tokens))
+    prompt_in = call(place_kernel, shape((BLOCK, width)), [SMEM] + [VMEM] * 5)(
+        place, *rows, own_tokens
+    )
     far_halves = (
         around(from_left[: half // 2], "t", 1),
         around(from_right[half // 2 :], "t", -1),
     )
-    mine = lax.all_to_all(heads, "y", 0, 0, tiled=True)
     pair = mine[:, 1:]
     near, far = ahead(pair, "z", 1), ahead(pair, "z", 2)
     others = [around(x, "c", 1) for x in (pair, near, far)]

time: 142 us -> 141 us (level)
  blocking collectives: 18.2 us -> 0 us
  waiting for transfers between devices: 34.8 us -> 51 us
  local copies, waits for them, and re-layouts: 21.3 us -> 17.2 us
  starting transfers between devices: 42.6 us -> 45.9 us
  Pallas kernels: 20.8 us -> 23.4 us
    all_to_all x1 -> x0, blocking collectives: 18.2 us -> none  [local(): lax.all_to_all(routed.reshape(16, 16, wide), ('y', 't'), 0, 0, tiled=True)]
    all_to_all x0 -> x1, waiting for transfers between devices: none -> 10.2 us  [local(): lax.all_to_all(routed.reshape(16, 16, wide), ('y', 't'), 0, 0, tiled=True)]
    unnamed x27 -> x17, local copies, waits for them, and re-layouts: 9.39 us -> 2.9 us
    all_to_all x1, waiting for transfers between devices: 1.3 us -> 6.67 us  [local(): mine = lax.all_to_all(heads, 'y', 0, 0, tiled=True)]
    all_to_all x0 -> x1, starting transfers between devices: none -> 5.18 us  [local(): lax.all_to_all(routed.reshape(16, 16, wide), ('y', 't'), 0, 0, tiled=True)]
    all_to_all x1, waiting for transfers between devices: 2.77 us -> 5.5 us  [local(): got = lax.all_to_all(routed, 'z', 0, 0, tiled=True)]
    all_to_all x1, waiting for transfers between devices: 9.77 us -> 7.68 us  [local(): lax.all_to_all(sent.reshape(16, HEAD, BLOCK), ('t', 'y'), 0, 0, tiled=True)]
    dynamic_update_slice x4, local copies, waits for them, and re-layouts: 3.46 us -> 5.24 us  [local(): lax.dynamic_update_index_in_dim(own_tokens, piece, (t - by) % 4, 0)]
  transfers between devices with their start and end apart: 23 -> 24, of which waited for: 10 -> 12; matrix products, arithmetic and copies ran while one was open for 9% -> 10% of each run, Pallas kernels for 5% -> 8%
where the time goes in v4:
time: 141 us; the launch traced here: 140 us
  waiting for transfers between devices  51 us (36%)
  starting transfers between devices  45.9 us (33%)
  Pallas kernels  23.4 us (17%)
  local copies, waits for them, and re-layouts  17.2 us (12%)
  between operations  1.61 us (1%)
    ppermute x17, starting transfers between devices, around(): return lax.ppermute(x, axis, [(i, (i + by) % count) for i in range(count)])  13.9 us
    all_to_all x1, waiting for transfers between devices, local(): lax.all_to_all(routed.reshape(16, 16, wide), ('y', 't'), 0, 0, tiled=True)  10.2 us
    ppermute x2, waiting for transfers between devices, ahead(): return lax.ppermute(x, axis, [(i, i + by) for i in range(count - by)])  9.39 us
    all_to_all x1, starting transfers between devices, local(): got = lax.all_to_all(routed, 'z', 0, 0, tiled=True)  8.08 us
    all_to_all x1, waiting for transfers between devices, local(): lax.all_to_all(share.reshape(4, MERGED, width), 't', 0, 0, tiled=True)  7.85 us
    all_to_all x1, waiting for transfers between devices, local(): lax.all_to_all(sent.reshape(16, HEAD, BLOCK), ('t', 'y'), 0, 0, tiled=True)  7.68 us
    ppermute x2, starting transfers between devices, ahead(): return lax.ppermute(x, axis, [(i, i + by) for i in range(count - by)])  7.45 us
    pallas_call x1, Pallas kernels, local(): call(vision_kernel, shape((count, width)), [SMEM, HBM, HBM, HBM], [VMEM((...  7.07 us
  transfers between devices with their start and end apart: 24, of which 12 were waited for; matrix products, arithmetic and copies ran while one was open for 10% of the time, Pallas kernels for 8%

profile of v4, /device:TPU:64, one launch (start us, length us, event | category | flops | bytes accessed | tf_op | source)
XLA Modules:
  0.0 139.6 jit_solution(4490518863391269516)
XLA Ops:
  0.0 7.1 %shard_map.109 = bf16[256,1408]{1,0:T(8,128)(2,1)} custom-call(s32[1,2]{1,0:T(1,128)} %grid_ref.1, bf16[256,1408]{1,0:T(8,128)(2,1)} %bitcast.37, bf16[3,352,1408]{2,1,0:T(8,128)(2,1)} %bitcast.36, bf16[352,1408]{1,0:T(8,128)(2,1)} %out_hbm.1), custom_call_target="tpu_custom_call" | custom-call | tf_op jit(solution)/shard_map/pallas_call | solution.py:270
  7.1 4.3 %all-to-all-start = ((bf16[4,64,1408]{2,1,0:T(8,128)(2,1)}), bf16[4,64,1408]{2,1,0:T(8,128)(2,1)S(1)}, u32[]{:S(2)}, u32[]{:S(2)}) async-start(bf16[4,64,1408]{2,1,0:T(8,128)(2,1)} %bitcast.38), calls=%async_computation | async-start | bytes 1441792 | tf_op jit(solution)/shard_map/all_to_all | solution.py:282
  15.1 7.8 %all-to-all-done.shares_ref = bf16[4,64,1408]{2,1,0:T(8,128)(2,1)S(1)} async-done(((bf16[4,64,1408]{2,1,0:T(8,128)(2,1)}), bf16[4,64,1408]{2,1,0:T(8,128)(2,1)S(1)}, u32[]{:S(2)}, u32[]{:S(2)}) %all-to-all-start) | async-done | bytes 720928 | tf_op jit(solution)/shard_map/all_to_all | solution.py:282
  23.0 2.1 %copy-done = bf16[1,1408,1408]{2,1,0:T(8,128)(2,1)S(1)} copy-done((bf16[1,1408,1408]{2,1,0:T(8,128)(2,1)S(1)}, bf16[1,1408,1408]{2,1,0:T(8,128)(2,1)}, u32[]{:S(2)}) %copy-start) | copy-done | bytes 3964952
  25.1 2.5 %shard_map.110 = bf16[4,64,1536]{2,1,0:T(8,128)(2,1)} custom-call(s32[6]{0:T(128)S(1)} %pad_add_fusion.1.facts_ref, bf16[64,1408]{1,0:T(8,128)(2,1)S(1)} %convolution_convert_fusion.own_ref, bf16[4,64,1408]{2,1,0:T(8,128)(2,1)S(1)} %all-to-all-done.shares_ref, bf16[1408,1408]{1,0:T(8,128)(2,1)S(1)} %bitcast.32), custom_call_target="tpu_custom_call" | custom-call | tf_op jit(solution)/shard_map/pallas_call | solution.py:290
  27.5 5.2 %all-to-all-start.1 = ((bf16[16,16,1536]{2,1,0:T(8,128)(2,1)}), bf16[16,16,1536]{2,1,0:T(8,128)(2,1)S(1)}, u32[]{:S(2)}, u32[]{:S(2)}) async-start(bf16[16,16,1536]{2,1,0:T(8,128)(2,1)} %bitcast.11), calls=%async_computation.1 | async-start | bytes 1572864 | tf_op jit(solution)/shard_map/all_to_all | solution.py:294
  32.7 3.2 %collective-permute-start.6 = (bf16[128,352]{0,1:T(8,128)(2,1)S(1)}, bf16[128,352]{0,1:T(8,128)(2,1)}, u32[]{:S(2)}, u32[]{:S(2)}) collective-permute-start(bf16[128,352]{0,1:T(8,128)(2,1)S(1)} %copy-done.6), channel_id=1, source_target_pairs={{0,3},{1,0},{2,1},{3,2},{4,7},{5,4},{6,5},{7,6},{8,11},{9,8},{10,9... | collective-permute-start | bytes 270344 | tf_op jit(solution)/shard_map/ppermute | solution.py:33
  37.7 10.2 %all-to-all-done.1 = bf16[16,16,1536]{2,1,0:T(8,128)(2,1)S(1)} async-done(((bf16[16,16,1536]{2,1,0:T(8,128)(2,1)}), bf16[16,16,1536]{2,1,0:T(8,128)(2,1)S(1)}, u32[]{:S(2)}, u32[]{:S(2)}) %all-to-all-start.1) | async-done | bytes 786464 | tf_op jit(solution)/shard_map/all_to_all | solution.py:294
  49.6 2.2 %shard_map.112 = bf16[8,16,1536]{2,1,0:T(8,128)(2,1)} custom-call(s32[3]{0:T(128)S(1)} %pad_add_fusion.place_ref.facts_ref, bf16[4,16,1536]{2,1,0:T(8,128)(2,1)S(1)} %shard_map.111.mine_ref, bf16[4,16,1536]{2,1,0:T(8,128)(2,1)S(1)} %collective-permute-done.other_ref), custom_call_target="tpu_custom_call" | custom-call | tf_op jit(solution)/shard_map/pallas_call | solution.py:297
  51.8 8.1 %all-to-all-start.2 = ((bf16[8,16,1536]{2,1,0:T(8,128)(2,1)}), bf16[8,16,1536]{2,1,0:T(8,128)(2,1)S(1)}, u32[]{:S(2)}, u32[]{:S(2)}) async-start(bf16[8,16,1536]{2,1,0:T(8,128)(2,1)} %shard_map.112), calls=%async_computation.2 | async-start | bytes 786432 | tf_op jit(solution)/shard_map/all_to_all | solution.py:302
  66.9 5.5 %all-to-all-done.2 = bf16[8,16,1536]{2,1,0:T(8,128)(2,1)S(1)} async-done(((bf16[8,16,1536]{2,1,0:T(8,128)(2,1)}), bf16[8,16,1536]{2,1,0:T(8,128)(2,1)S(1)}, u32[]{:S(2)}, u32[]{:S(2)}) %all-to-all-start.2) | async-done | bytes 393248 | tf_op jit(solution)/shard_map/all_to_all | solution.py:302
  72.5 2.7 %collective-permute-start.2 = (bf16[16,1536]{1,0:T(8,128)(2,1)S(1)}, bf16[16,1536]{1,0:T(8,128)(2,1)S(1)}, u32[]{:S(2)}, u32[]{:S(2)}) collective-permute-start(bf16[16,1536]{1,0:T(8,128)(2,1)S(1)} %reduce_sum.12.r0_ref), channel_id=1, source_target_pairs={{0,2},{1,3},{2,0},{3,1},{4,6},{5,7},{6,4},{7,5},{8,10},{9,11},{10,... | collective-permute-start | bytes 147464 | tf_op jit(solution)/shard_map/ppermute | solution.py:33
  80.5 2.4 %shard_map.113 = bf16[4,3,88,128]{3,2,1,0:T(8,128)(2,1)S(1)} custom-call(s32[3]{0:T(128)S(1)} %pad_add_fusion.place_ref.facts_ref, bf16[16,1536]{1,0:T(8,128)(2,1)S(1)} %reduce_sum.12.r0_ref, bf16[16,1536]{1,0:T(8,128)(2,1)S(1)} %collective-permute-done.1.r1_ref, bf16[16,1536]{1,0:T(8,128)(2,1)S(1)} %collective-permute-done.2.r2_ref, ...), custom_call_target="tpu_custom_call" | custom-call | tf_op jit(solution)/shard_map/pallas_call | solution.py:310
  83.6 3.4 %all-to-all-start.3 = ((bf16[4,3,88,128]{3,2,1,0:T(8,128)(2,1)}), bf16[4,3,88,128]{3,2,1,0:T(8,128)(2,1)S(1)}, u32[]{:S(2)}, u32[]{:S(2)}) async-start(bf16[4,3,88,128]{3,2,1,0:T(8,128)(2,1)} %copy-done.3), calls=%async_computation.3 | async-start | bytes 540672 | tf_op jit(solution)/shard_map/all_to_all | solution.py:315
  87.1 6.7 %all-to-all-done.3.own_ref = bf16[4,3,88,128]{3,2,1,0:T(8,128)(2,1)S(1)} async-done(((bf16[4,3,88,128]{3,2,1,0:T(8,128)(2,1)}), bf16[4,3,88,128]{3,2,1,0:T(8,128)(2,1)S(1)}, u32[]{:S(2)}, u32[]{:S(2)}) %all-to-all-start.3) | async-done | bytes 270368 | tf_op jit(solution)/shard_map/all_to_all | solution.py:315
  95.9 3.2 %collective-permute-start.15 = (bf16[88,1408]{1,0:T(8,128)(2,1)S(1)}, bf16[88,1408]{1,0:T(8,128)(2,1)S(1)}, u32[]{:S(2)}, u32[]{:S(2)}) collective-permute-start(bf16[88,1408]{1,0:T(8,128)(2,1)S(1)} %slice.19), channel_id=1, source_target_pairs={{0,3},{1,0},{2,1},{3,2},{4,7},{5,4},{6,5},{7,6},{8,11},{9,8},{10,9... | collective-permute-start | bytes 743432 | tf_op jit(solution)/shard_map/ppermute | solution.py:33
  99.2 5.0 %collective-permute-start.10 = (bf16[4,2,88,128]{3,2,1,0:T(8,128)(2,1)S(1)}, bf16[4,2,88,128]{3,2,1,0:T(8,128)(2,1)S(1)}, u32[]{:S(2)}, u32[]{:S(2)}) collective-permute-start(bf16[4,2,88,128]{3,2,1,0:T(8,128)(2,1)S(1)} %slice.17), channel_id=1, source_target_pairs={{0,64},{32,96},{64,128},{96,160},{128,192},{160,224},{1,65},{33,97... | collective-permute-start | bytes 540680 | tf_op jit(solution)/shard_map/ppermute | solution.py:28
  104.2 2.5 %collective-permute-start.9 = (bf16[4,2,88,128]{3,2,1,0:T(8,128)(2,1)S(1)}, bf16[4,2,88,128]{3,2,1,0:T(8,128)(2,1)S(1)}, u32[]{:S(2)}, u32[]{:S(2)}) collective-permute-start(bf16[4,2,88,128]{3,2,1,0:T(8,128)(2,1)S(1)} %slice.17), channel_id=1, source_target_pairs={{0,32},{32,64},{64,96},{96,128},{128,160},{160,192},{192,224},{1,3... | collective-permute-start | bytes 540680 | tf_op jit(solution)/shard_map/ppermute | solution.py:28
  106.8 5.4 %collective-permute-done.10.far_ref = bf16[4,2,88,128]{3,2,1,0:T(8,128)(2,1)S(1)} collective-permute-done((bf16[4,2,88,128]{3,2,1,0:T(8,128)(2,1)S(1)}, bf16[4,2,88,128]{3,2,1,0:T(8,128)(2,1)S(1)}, u32[]{:S(2)}, u32[]{:S(2)}) %collective-permute-start.10) | collective-permute-done | bytes 180256 | tf_op jit(solution)/shard_map/ppermute | solution.py:28
  112.2 4.0 %collective-permute-done.9.near_ref = bf16[4,2,88,128]{3,2,1,0:T(8,128)(2,1)S(1)} collective-permute-done((bf16[4,2,88,128]{3,2,1,0:T(8,128)(2,1)S(1)}, bf16[4,2,88,128]{3,2,1,0:T(8,128)(2,1)S(1)}, u32[]{:S(2)}, u32[]{:S(2)}) %collective-permute-start.9) | collective-permute-done | bytes 180256 | tf_op jit(solution)/shard_map/ppermute | solution.py:28
  117.9 4.8 %shard_map.114 = bf16[4,4,88,128]{3,2,1,0:T(8,128)(2,1)} custom-call(s32[3]{0:T(128)S(1)} %pad_add_fusion.place_ref.facts_ref, s32[16]{0:T(128)S(1)} %copy-done.4, bf16[4,3,88,128]{3,2,1,0:T(8,128)(2,1)S(1)} %all-to-all-done.3.own_ref, bf16[4,2,88,128]{3,2,1,0:T(8,128)(2,1)S(1)} %collective-permute-done.9.near_ref, ...), custom_call_target="tpu_custom_call" | custom-call | tf_op jit(solution)/shard_map/pallas_call | solution.py:330
  122.7 3.5 %all-to-all-start.4 = ((bf16[16,88,128]{2,1,0:T(8,128)(2,1)}), bf16[16,88,128]{2,1,0:T(8,128)(2,1)S(1)}, u32[]{:S(2)}, u32[]{:S(2)}) async-start(bf16[16,88,128]{2,1,0:T(8,128)(2,1)} %bitcast.20), calls=%async_computation.4 | async-start | bytes 720896 | tf_op jit(solution)/shard_map/all_to_all | solution.py:337
  128.7 7.7 %all-to-all-done.4 = bf16[16,88,128]{2,1,0:T(8,128)(2,1)S(1)} async-done(((bf16[16,88,128]{2,1,0:T(8,128)(2,1)}), bf16[16,88,128]{2,1,0:T(8,128)(2,1)S(1)}, u32[]{:S(2)}, u32[]{:S(2)}) %all-to-all-start.4) | async-done | bytes 360480 | tf_op jit(solution)/shard_map/all_to_all | solution.py:337
  136.3 3.3 %shard_map.116 = bf16[128,1408]{1,0:T(8,128)(2,1)} custom-call(s32[3]{0:T(128)S(1)} %pad_add_fusion.place_ref.facts_ref, bf16[4,2,176,128]{3,2,1,0:T(8,128)(2,1)S(1)} %bitcast.35, bf16[352,1408]{1,0:T(8,128)(2,1)S(1)} %copy-done.2, bf16[176,1408]{1,0:T(8,128)(2,1)} %collective-permute-done.7.m1_ref, ...), custom_call_target="tpu_custom_call" | custom-call | tf_op jit(solution)/shard_map/pallas_call | solution.py:338
  (69 shorter events, 25.3 us)
Async XLA Ops:
  7.1 15.9 %all-to-all-start = ((bf16[4,64,1408]{2,1,0:T(8,128)(2,1)}), bf16[4,64,1408]{2,1,0:T(8,128)(2,1)S(1)}, u32[]{:S(2)}, u32[]{:S(2)}) async-start(bf16[4,64,1408]{2,1,0:T(8,128)(2,1)} %bitcast.38), calls=%async_computation | async-start | bytes 1441792 | tf_op jit(solution)/shard_map/all_to_all | solution.py:282
  27.5 20.4 %all-to-all-start.1 = ((bf16[16,16,1536]{2,1,0:T(8,128)(2,1)}), bf16[16,16,1536]{2,1,0:T(8,128)(2,1)S(1)}, u32[]{:S(2)}, u32[]{:S(2)}) async-start(bf16[16,16,1536]{2,1,0:T(8,128)(2,1)} %bitcast.11), calls=%async_computation.1 | async-start | bytes 1572864 | tf_op jit(solution)/shard_map/all_to_all | solution.py:294
  32.7 42.5 %collective-permute-start.6 = (bf16[128,352]{0,1:T(8,128)(2,1)S(1)}, bf16[128,352]{0,1:T(8,128)(2,1)}, u32[]{:S(2)}, u32[]{:S(2)}) collective-permute-start(bf16[128,352]{0,1:T(8,128)(2,1)S(1)} %copy-done.6), channel_id=1, source_target_pairs={{0,3},{1,0},{2,1},{3,2},{4,7},{5,4},{6,5},{7,6},{8,11},{9,8},{10,9... | collective-permute-start | bytes 270344 | tf_op jit(solution)/shard_map/ppermute | solution.py:33
  36.0 29.4 %collective-permute-start.5 = (bf16[128,352]{0,1:T(8,128)(2,1)S(1)}, bf16[128,352]{0,1:T(8,128)(2,1)}, u32[]{:S(2)}, u32[]{:S(2)}) collective-permute-start(bf16[128,352]{0,1:T(8,128)(2,1)S(1)} %copy-done.6), channel_id=1, source_target_pairs={{0,2},{1,3},{2,0},{3,1},{4,6},{5,7},{6,4},{7,5},{8,10},{9,11},{10,... | collective-permute-start | bytes 270344 | tf_op jit(solution)/shard_map/ppermute | solution.py:33
  36.8 23.1 %collective-permute-start.4 = (bf16[128,352]{0,1:T(8,128)(2,1)S(1)}, bf16[128,352]{0,1:T(8,128)(2,1)}, u32[]{:S(2)}, u32[]{:S(2)}) collective-permute-start(bf16[128,352]{0,1:T(8,128)(2,1)S(1)} %copy-done.6), channel_id=1, source_target_pairs={{0,1},{1,2},{2,3},{3,0},{4,5},{5,6},{6,7},{7,4},{8,9},{9,10},{10,1... | collective-permute-start | bytes 270344 | tf_op jit(solution)/shard_map/ppermute | solution.py:33
  48.0 1.6 %collective-permute-start = (bf16[4,16,1536]{2,1,0:T(8,128)(2,1)S(1)}, bf16[4,16,1536]{2,1,0:T(8,128)(2,1)S(1)}, u32[]{:S(2)}, u32[]{:S(2)}) collective-permute-start(bf16[4,16,1536]{2,1,0:T(8,128)(2,1)S(1)} %shard_map.111.mine_ref), channel_id=1, source_target_pairs={{0,4},{4,0},{1,5},{5,1},{2,6},{6,2},{3,7},{7,3},{8,12},{12,8},{9,1... | collective-permute-start | bytes 589832 | tf_op jit(solution)/shard_map/ppermute | solution.py:33
  51.8 20.6 %all-to-all-start.2 = ((bf16[8,16,1536]{2,1,0:T(8,128)(2,1)}), bf16[8,16,1536]{2,1,0:T(8,128)(2,1)S(1)}, u32[]{:S(2)}, u32[]{:S(2)}) async-start(bf16[8,16,1536]{2,1,0:T(8,128)(2,1)} %shard_map.112), calls=%async_computation.2 | async-start | bytes 786432 | tf_op jit(solution)/shard_map/all_to_all | solution.py:302
  63.3 23.8 %collective-permute-start.8 = (bf16[176,1408]{1,0:T(8,128)(2,1)}, bf16[176,1408]{1,0:T(8,128)(2,1)}, u32[]{:S(2)}, u32[]{:S(2)}) collective-permute-start(bf16[176,1408]{1,0:T(8,128)(2,1)} %constant_dynamic-slice_fusion), channel_id=1, source_target_pairs={{0,3},{1,0},{2,1},{3,2},{4,7},{5,4},{6,5},{7,6},{8,11},{9,8},{10,9... | collective-permute-start | bytes 1486856 | tf_op jit(solution)/shard_map/ppermute | solution.py:33
  63.3 23.8 %collective-permute-start.7 = (bf16[176,1408]{1,0:T(8,128)(2,1)}, bf16[176,1408]{1,0:T(8,128)(2,1)}, u32[]{:S(2)}, u32[]{:S(2)}) collective-permute-start(bf16[176,1408]{1,0:T(8,128)(2,1)} %constant_dynamic-slice_fusion), channel_id=1, source_target_pairs={{0,1},{1,2},{2,3},{3,0},{4,5},{5,6},{6,7},{7,4},{8,9},{9,10},{10,1... | collective-permute-start | bytes 1486856 | tf_op jit(solution)/shard_map/ppermute | solution.py:33
  72.4 5.8 %collective-permute-start.3 = (bf16[16,1536]{1,0:T(8,128)(2,1)S(1)}, bf16[16,1536]{1,0:T(8,128)(2,1)S(1)}, u32[]{:S(2)}, u32[]{:S(2)}) collective-permute-start(bf16[16,1536]{1,0:T(8,128)(2,1)S(1)} %reduce_sum.12.r0_ref), channel_id=1, source_target_pairs={{0,3},{1,0},{2,1},{3,2},{4,7},{5,4},{6,5},{7,6},{8,11},{9,8},{10,9... | collective-permute-start | bytes 147464 | tf_op jit(solution)/shard_map/ppermute | solution.py:33
  72.5 6.5 %collective-permute-start.2 = (bf16[16,1536]{1,0:T(8,128)(2,1)S(1)}, bf16[16,1536]{1,0:T(8,128)(2,1)S(1)}, u32[]{:S(2)}, u32[]{:S(2)}) collective-permute-start(bf16[16,1536]{1,0:T(8,128)(2,1)S(1)} %reduce_sum.12.r0_ref), channel_id=1, source_target_pairs={{0,2},{1,3},{2,0},{3,1},{4,6},{5,7},{6,4},{7,5},{8,10},{9,11},{10,... | collective-permute-start | bytes 147464 | tf_op jit(solution)/shard_map/ppermute | solution.py:33
  75.2 5.3 %collective-permute-start.1 = (bf16[16,1536]{1,0:T(8,128)(2,1)S(1)}, bf16[16,1536]{1,0:T(8,128)(2,1)S(1)}, u32[]{:S(2)}, u32[]{:S(2)}) collective-permute-start(bf16[16,1536]{1,0:T(8,128)(2,1)S(1)} %reduce_sum.12.r0_ref), channel_id=1, source_target_pairs={{0,1},{1,2},{2,3},{3,0},{4,5},{5,6},{6,7},{7,4},{8,9},{9,10},{10,1... | collective-permute-start | bytes 147464 | tf_op jit(solution)/shard_map/ppermute | solution.py:33
  83.6 10.1 %all-to-all-start.3 = ((bf16[4,3,88,128]{3,2,1,0:T(8,128)(2,1)}), bf16[4,3,88,128]{3,2,1,0:T(8,128)(2,1)S(1)}, u32[]{:S(2)}, u32[]{:S(2)}) async-start(bf16[4,3,88,128]{3,2,1,0:T(8,128)(2,1)} %copy-done.3), calls=%async_computation.3 | async-start | bytes 540672 | tf_op jit(solution)/shard_map/all_to_all | solution.py:315
  94.7 11.9 %collective-permute-start.14 = (bf16[88,1408]{1,0:T(8,128)(2,1)S(1)}, bf16[88,1408]{1,0:T(8,128)(2,1)S(1)}, u32[]{:S(2)}, u32[]{:S(2)}) collective-permute-start(bf16[88,1408]{1,0:T(8,128)(2,1)S(1)} %slice.18), channel_id=1, source_target_pairs={{0,1},{1,2},{2,3},{3,0},{4,5},{5,6},{6,7},{7,4},{8,9},{9,10},{10,1... | collective-permute-start | bytes 743432 | tf_op jit(solution)/shard_map/ppermute | solution.py:33
  95.9 20.3 %collective-permute-start.15 = (bf16[88,1408]{1,0:T(8,128)(2,1)S(1)}, bf16[88,1408]{1,0:T(8,128)(2,1)S(1)}, u32[]{:S(2)}, u32[]{:S(2)}) collective-permute-start(bf16[88,1408]{1,0:T(8,128)(2,1)S(1)} %slice.19), channel_id=1, source_target_pairs={{0,3},{1,0},{2,1},{3,2},{4,7},{5,4},{6,5},{7,6},{8,11},{9,8},{10,9... | collective-permute-start | bytes 743432 | tf_op jit(solution)/shard_map/ppermute | solution.py:33
  99.1 17.6 %collective-permute-start.11 = (bf16[4,2,88,128]{3,2,1,0:T(8,128)(2,1)S(1)}, bf16[4,2,88,128]{3,2,1,0:T(8,128)(2,1)S(1)}, u32[]{:S(2)}, u32[]{:S(2)}) collective-permute-start(bf16[4,2,88,128]{3,2,1,0:T(8,128)(2,1)S(1)} %slice.17), channel_id=1, source_target_pairs={{0,4},{4,0},{1,5},{5,1},{2,6},{6,2},{3,7},{7,3},{8,12},{12,8},{9,1... | collective-permute-start | bytes 540680 | tf_op jit(solution)/shard_map/ppermute | solution.py:33
  99.2 13.0 %collective-permute-start.10 = (bf16[4,2,88,128]{3,2,1,0:T(8,128)(2,1)S(1)}, bf16[4,2,88,128]{3,2,1,0:T(8,128)(2,1)S(1)}, u32[]{:S(2)}, u32[]{:S(2)}) collective-permute-start(bf16[4,2,88,128]{3,2,1,0:T(8,128)(2,1)S(1)} %slice.17), channel_id=1, source_target_pairs={{0,64},{32,96},{64,128},{96,160},{128,192},{160,224},{1,65},{33,97... | collective-permute-start | bytes 540680 | tf_op jit(solution)/shard_map/ppermute | solution.py:28
  104.2 12.0 %collective-permute-start.9 = (bf16[4,2,88,128]{3,2,1,0:T(8,128)(2,1)S(1)}, bf16[4,2,88,128]{3,2,1,0:T(8,128)(2,1)S(1)}, u32[]{:S(2)}, u32[]{:S(2)}) collective-permute-start(bf16[4,2,88,128]{3,2,1,0:T(8,128)(2,1)S(1)} %slice.17), channel_id=1, source_target_pairs={{0,32},{32,64},{64,96},{96,128},{128,160},{160,192},{192,224},{1,3... | collective-permute-start | bytes 540680 | tf_op jit(solution)/shard_map/ppermute | solution.py:28
  106.7 21.9 %collective-permute-start.16 = (bf16[176,1408]{1,0:T(8,128)(2,1)}, bf16[176,1408]{1,0:T(8,128)(2,1)S(1)}, u32[]{:S(2)}, u32[]{:S(2)}) collective-permute-start(bf16[176,1408]{1,0:T(8,128)(2,1)} %collective-permute-done.7.m1_ref), channel_id=1, source_target_pairs={{0,4},{4,0},{1,5},{5,1},{2,6},{6,2},{3,7},{7,3},{8,12},{12,8},{9,1... | collective-permute-start | bytes 1486856 | tf_op jit(solution)/shard_map/ppermute | solution.py:33
  112.2 16.4 %collective-permute-start.18 = (bf16[176,1408]{1,0:T(8,128)(2,1)}, bf16[176,1408]{1,0:T(8,128)(2,1)}, u32[]{:S(2)}, u32[]{:S(2)}) collective-permute-start(bf16[176,1408]{1,0:T(8,128)(2,1)} %collective-permute-done.8.m3_ref), channel_id=1, source_target_pairs={{0,4},{4,0},{1,5},{5,1},{2,6},{6,2},{3,7},{7,3},{8,12},{12,8},{9,1... | collective-permute-start | bytes 1486856 | tf_op jit(solution)/shard_map/ppermute | solution.py:33
  116.2 1.4 %collective-permute-start.13 = (bf16[4,2,88,128]{3,2,1,0:T(8,128)(2,1)S(1)}, bf16[4,2,88,128]{3,2,1,0:T(8,128)(2,1)S(1)}, u32[]{:S(2)}, u32[]{:S(2)}) collective-permute-start(bf16[4,2,88,128]{3,2,1,0:T(8,128)(2,1)S(1)} %collective-permute-done.10.far_ref), channel_id=1, source_target_pairs={{0,4},{4,0},{1,5},{5,1},{2,6},{6,2},{3,7},{7,3},{8,12},{12,8},{9,1... | collective-permute-start | bytes 540680 | tf_op jit(solution)/shard_map/ppermute | solution.py:33
  116.2 1.7 %collective-permute-start.12 = (bf16[4,2,88,128]{3,2,1,0:T(8,128)(2,1)S(1)}, bf16[4,2,88,128]{3,2,1,0:T(8,128)(2,1)S(1)}, u32[]{:S(2)}, u32[]{:S(2)}) collective-permute-start(bf16[4,2,88,128]{3,2,1,0:T(8,128)(2,1)S(1)} %collective-permute-done.9.near_ref), channel_id=1, source_target_pairs={{0,4},{4,0},{1,5},{5,1},{2,6},{6,2},{3,7},{7,3},{8,12},{12,8},{9,1... | collective-permute-start | bytes 540680 | tf_op jit(solution)/shard_map/ppermute | solution.py:33
  116.8 19.6 %collective-permute-start.17 = (bf16[176,1408]{1,0:T(8,128)(2,1)S(1)}, bf16[176,1408]{1,0:T(8,128)(2,1)}, u32[]{:S(2)}, u32[]{:S(2)}) collective-permute-start(bf16[176,1408]{1,0:T(8,128)(2,1)S(1)} %constant_dynamic-update-slice_fusion.m2_ref), channel_id=1, source_target_pairs={{0,4},{4,0},{1,5},{5,1},{2,6},{6,2},{3,7},{7,3},{8,12},{12,8},{9,1... | collective-permute-start | bytes 1486856 | tf_op jit(solution)/shard_map/ppermute | solution.py:33
  122.7 13.7 %all-to-all-start.4 = ((bf16[16,88,128]{2,1,0:T(8,128)(2,1)}), bf16[16,88,128]{2,1,0:T(8,128)(2,1)S(1)}, u32[]{:S(2)}, u32[]{:S(2)}) async-start(bf16[16,88,128]{2,1,0:T(8,128)(2,1)} %bitcast.20), calls=%async_computation.4 | async-start | bytes 720896 | tf_op jit(solution)/shard_map/all_to_all | solution.py:337
  (8 other events, 146.5 us)

commit v5 on v4

--- a/solution.py
+++ b/solution.py
@@ -118,25 +118,40 @@
 
 
 def select_kernel(place_ref, mine_ref, other_ref, routed_ref):
-    width = mine_ref.shape[2] - FACTS
-    routed_ref[...] = jnp.zeros(routed_ref.shape, BF)
-    for rows_ref in (mine_ref, other_ref):
-        for y in range(4):
-            facts = rows_ref[y, 0:1, width:].astype(F32)
-            block = facts[0, 0].astype(I32)
-
-            @pl.when((facts[0, 4] > 0.0) & (block % 2 == place_ref[1]))
-            def _():
-                routed_ref[block // 8] = rows_ref[y]
-
-
-def merge_kernel(facts_ref, own_ref, shares_ref, weight_ref, rows_ref):
+    wide = mine_ref.shape[2]
+    width = wide - FACTS
+    rows = jnp.concatenate(
+        [mine_ref[...].reshape(64, wide), other_ref[...].reshape(64, wide)], axis=0
+    )
+    facts = rows[:, width:].astype(F32)
+    block, there = facts[:, 0:1], facts[:, 4:5]
+    same_core = block - 2.0 * jnp.floor(block * 0.5) == place_ref[1].astype(F32)
+    to = jnp.where(same_core & (there > 0.0), jnp.floor(block * 0.125), -1.0).astype(I32)
+    source, target = iota((128, 128), 0), iota((128, 128), 1)
+    chosen = (to == target // 16) & (source % 16 == target % 16)
+    routed = dot(chosen.astype(BF), rows, (0, 0))
+    routed_ref[...] = routed.astype(BF).reshape(8, 16, wide)
+
+
+def merge_kernel(
+    facts_ref, own_ref, shares_ref, weight_hbm, rows_ref, weight_ref, arrived
+):
     width = own_ref.shape[1]
-    hidden = own_ref[...].astype(F32)
-    gained = shares_ref[0].astype(F32)
-    for other in range(1, 4):
-        gained = gained + shares_ref[other].astype(F32)
-    merged = dot(normalize(hidden + gained), weight_ref[...], (1, 0)).astype(BF)
+    deep = width // 4
+    copies = []
+    for piece in range(4):
+        at = pl.ds(piece * deep, deep)
+        copies.append(
+            pltpu.make_async_copy(weight_hbm.at[at], weight_ref.at[at], arrived.at[piece])
+        )
+        copies[-1].start()
+    total = own_ref[...].astype(F32)
+    for other in range(4):
+        total = total + shares_ref[other].astype(F32)
+    normed = normalize(total)
+    for copy in copies:
+        copy.wait()
+    merged = dot(normed, weight_ref[...], (1, 0)).astype(BF)
     lane = iota((MERGED, FACTS), 1)
     facts = jnp.zeros((MERGED, FACTS), I32)
     for index in range(5):
@@ -225,7 +240,7 @@
 
 
 def output_kernel(
-    place_ref, context_ref, w0_ref, m1_ref, m2_ref, m3_ref, o1_ref, o2_ref, o3_ref,
+    place_ref, context_ref, w0_ref, m2_ref, m1_ref, m3_ref, o2_ref, o1_ref, o3_ref,
     prompt_ref, out_ref,
 ):
     c, t = place_ref[1], place_ref[2]
@@ -282,12 +297,16 @@
     shares = lax.all_to_all(share.reshape(4, MERGED, width), "t", 0, 0, tiled=True)
     chosen = slot_of(t * MERGED + jnp.arange(MERGED))[:, None] == jnp.arange(count)[None, :]
     own = jnp.dot(chosen.astype(BF), picture, preferred_element_type=F32).astype(BF)
-    own, tokens = lax.optimization_barrier((own, tokens))
-    pieces = [tokens] + [around(tokens, "t", by) for by in range(1, 4)]
     facts = jnp.stack([block, picture_offset[0], picture_grid[0, 0], picture_grid[0, 1], 1])
     facts = jnp.where(t == 0, facts, 0)
     facts = jnp.concatenate([facts, (block % 8 // 2)[None]]).astype(I32)
-    routed = call(merge_kernel, shape((4, MERGED, wide)), [SMEM, VMEM, VMEM, VMEM])(
+    routed = call(
+        merge_kernel,
+        shape((4, MERGED, wide)),
+        [SMEM, VMEM, VMEM, HBM],
+        [VMEM((width, width), BF), pltpu.SemaphoreType.DMA((4,))],
+        limit=60,
+    )(
         facts, own, shares, merge_weight[0]
     )
 
@@ -298,7 +317,9 @@
     routed, text_out = lax.optimization_barrier((routed, text_out))
     half = local_width // 2
     near_half = lax.dynamic_slice_in_dim(text_out, c * half, half, 0)
-    from_left, from_right = around(near_half, "t", 1), around(near_half, "t", -1)
+    near_half, tokens = lax.optimization_barrier((near_half, tokens))
+    halves = [around(near_half, "t", by) for by in (2, 1, 3)]
+    pieces = [tokens] + [around(tokens, "t", by) for by in range(1, 4)]
     got = lax.all_to_all(routed, "z", 0, 0, tiled=True)
     got = jnp.sum(got.astype(F32), axis=0).astype(BF)
     rows = [got] + [around(got, "t", by) for by in range(1, 4)]
@@ -306,27 +327,20 @@
     for by, piece in enumerate(pieces):
         own_tokens = lax.dynamic_update_index_in_dim(own_tokens, piece, (t - by) % 4, 0)
     own_tokens = own_tokens.transpose(1, 0, 2).reshape(BLOCK, width)
-
     heads = call(
         project_kernel,
         shape((4, 3, HEAD, BLOCK)),
         [SMEM] + [VMEM] * 6,
     )(place, *rows, own_tokens, text_qkv.transpose(1, 2, 0))
+    heads, late_tokens = lax.optimization_barrier((heads, own_tokens))
     mine = lax.all_to_all(heads, "y", 0, 0, tiled=True)
-    mine, from_left, from_right = lax.optimization_barrier((mine, from_left, from_right))
-    mine, own_tokens = lax.optimization_barrier((mine, own_tokens))
     prompt_in = call(place_kernel, shape((BLOCK, width)), [SMEM] + [VMEM] * 5)(
-        place, *rows, own_tokens
-    )
-    far_halves = (
-        around(from_left[: half // 2], "t", 1),
-        around(from_right[half // 2 :], "t", -1),
+        place, *rows, late_tokens
     )
     pair = mine[:, 1:]
     near, far = ahead(pair, "z", 1), ahead(pair, "z", 2)
     others = [around(x, "c", 1) for x in (pair, near, far)]
-    weights = [from_left, jnp.concatenate(far_halves), from_right]
-    weights = weights + [around(x, "c", 1) for x in weights]
+    halves = halves + [around(x, "c", 1) for x in halves]
     sent = call(
         attend_kernel,
         shape((4, 4, HEAD, BLOCK)),
@@ -336,7 +350,7 @@
     )(place, prompt_lengths, mine, near, far, *others)
     context = lax.all_to_all(sent.reshape(16, HEAD, BLOCK), ("t", "y"), 0, 0, tiled=True)
     return call(output_kernel, shape((BLOCK, width)), [SMEM] + [VMEM] * 9)(
-        place, context.reshape(4, 2, half, BLOCK), text_out, *weights, prompt_in
+        place, context.reshape(4, 2, half, BLOCK), text_out, *halves, prompt_in
     )
 
 

time: 141 us -> 144 us (1.021)
  blocking collectives: 0 us -> 27.8 us
  waiting for transfers between devices: 51 us -> 39.2 us
  starting transfers between devices: 45.9 us -> 36.2 us
  local copies, waits for them, and re-layouts: 17.2 us -> 10.4 us
  Pallas kernels: 23.4 us -> 25.4 us
  other arithmetic: 0.24 us -> 1.82 us
    all_to_all x0 -> x2, blocking collectives: none -> 27.8 us  [the longest x1 18.5 us: local(): lax.all_to_all(routed.reshape(16, 16, wide), ('y', 't'), 0, 0, tiled=True)]
    all_to_all x2 -> x0, waiting for transfers between devices: 16.9 us -> none  [the longest x1 10.2 us: local(): lax.all_to_all(routed.reshape(16, 16, wide), ('y', 't'), 0, 0, tiled=True)]
    ppermute x17 -> x16, waiting for transfers between devices: 3.63 us -> 20.4 us  [around(): return lax.ppermute(x, axis, [(i, (i + by) % count) for i in range(count)])]
    all_to_all x2 -> x0, starting transfers between devices: 8.63 us -> none  [the longest x1 5.18 us: local(): lax.all_to_all(routed.reshape(16, 16, wide), ('y', 't'), 0, 0, tiled=True)]
    all_to_all x1, waiting for transfers between devices: 5.5 us -> 0.01 us  [local(): got = lax.all_to_all(routed, 'z', 0, 0, tiled=True)]
    ppermute x2, waiting for transfers between devices: 9.39 us -> 4.78 us  [ahead(): return lax.ppermute(x, axis, [(i, i + by) for i in range(count - by)])]
    dynamic_update_slice x4, local copies, waits for them, and re-layouts: 5.24 us -> 2.57 us  [local(): lax.dynamic_update_index_in_dim(own_tokens, piece, (t - by) % 4, 0)]
    pallas_call x1, Pallas kernels: 2.45 us -> 4.95 us  [local(): call(merge_kernel, shape((4, MERGED, wide)), [SMEM, VMEM, VMEM, HBM], [VM...]
  transfers between devices with their start and end apart: 24 -> 21, of which waited for: 12 -> 9; matrix products, arithmetic and copies ran while one was open for 10% -> 9% of each run, Pallas kernels for 8% -> 6%
where the time goes in v5:
time: 144 us; the launch traced here: 143 us
  waiting for transfers between devices  39.2 us (27%)
  starting transfers between devices  36.2 us (25%)
  blocking collectives  27.8 us (19%)
  Pallas kernels  25.4 us (18%)
  local copies, waits for them, and re-layouts  10.4 us (7%)
  other arithmetic  1.82 us (1%)
  between operations  1.64 us (1%)
    ppermute x16, waiting for transfers between devices, around(): return lax.ppermute(x, axis, [(i, (i + by) % count) for i in range(count)])  20.4 us
    all_to_all x1, blocking collectives, local(): lax.all_to_all(routed.reshape(16, 16, wide), ('y', 't'), 0, 0, tiled=True)  18.5 us
    ppermute x16, starting transfers between devices, around(): return lax.ppermute(x, axis, [(i, (i + by) % count) for i in range(count)])  11.9 us
    all_to_all x1, blocking collectives, local(): mine = lax.all_to_all(heads, 'y', 0, 0, tiled=True)  9.24 us
    all_to_all x1, starting transfers between devices, local(): got = lax.all_to_all(routed, 'z', 0, 0, tiled=True)  8.09 us
    ppermute x2, starting transfers between devices, ahead(): return lax.ppermute(x, axis, [(i, i + by) for i in range(count - by)])  7.95 us
    all_to_all x1, waiting for transfers between devices, local(): lax.all_to_all(sent.reshape(16, HEAD, BLOCK), ('t', 'y'), 0, 0, tiled=True)  7.36 us
    pallas_call x1, Pallas kernels, local(): call(vision_kernel, shape((count, width)), [SMEM, HBM, HBM, HBM], [VMEM((...  7.05 us
  transfers between devices with their start and end apart: 21, of which 9 were waited for; matrix products, arithmetic and copies ran while one was open for 9% of the time, Pallas kernels for 6%

profile of v5, /device:TPU:64, one launch (start us, length us, event | category | flops | bytes accessed | tf_op | source)
XLA Modules:
  0.0 143.4 jit_solution(13162409483348595058)
XLA Ops:
  0.0 7.1 %shard_map.109 = bf16[256,1408]{1,0:T(8,128)(2,1)} custom-call(s32[1,2]{1,0:T(1,128)} %grid_ref.1, bf16[256,1408]{1,0:T(8,128)(2,1)} %bitcast.38, bf16[3,352,1408]{2,1,0:T(8,128)(2,1)} %bitcast.37, bf16[352,1408]{1,0:T(8,128)(2,1)} %out_hbm.1), custom_call_target="tpu_custom_call" | custom-call | tf_op jit(solution)/shard_map/pallas_call | solution.py:285
  7.1 4.3 %all-to-all-start = ((bf16[4,64,1408]{2,1,0:T(8,128)(2,1)}), bf16[4,64,1408]{2,1,0:T(8,128)(2,1)S(1)}, u32[]{:S(2)}, u32[]{:S(2)}) async-start(bf16[4,64,1408]{2,1,0:T(8,128)(2,1)} %bitcast.39), calls=%async_computation | async-start | bytes 1441792 | tf_op jit(solution)/shard_map/all_to_all | solution.py:297
  16.3 6.7 %all-to-all-done.shares_ref = bf16[4,64,1408]{2,1,0:T(8,128)(2,1)S(1)} async-done(((bf16[4,64,1408]{2,1,0:T(8,128)(2,1)}), bf16[4,64,1408]{2,1,0:T(8,128)(2,1)S(1)}, u32[]{:S(2)}, u32[]{:S(2)}) %all-to-all-start) | async-done | bytes 720928 | tf_op jit(solution)/shard_map/all_to_all | solution.py:297
  23.9 4.9 %shard_map.110 = bf16[4,64,1536]{2,1,0:T(8,128)(2,1)} custom-call(s32[6]{0:T(128)} %pad_add_fusion.1.facts_ref, bf16[64,1408]{1,0:T(8,128)(2,1)} %convolution_convert_fusion.own_ref, bf16[4,64,1408]{2,1,0:T(8,128)(2,1)} %copy-done.4, bf16[1408,1408]{1,0:T(8,128)(2,1)} %bitcast.35), custom_call_target="tpu_custom_call" | custom-call | tf_op jit(solution)/shard_map/pallas_call | solution.py:303
  28.8 18.5 %all_to_all.25 = bf16[16,16,1536]{2,1,0:T(8,128)(2,1)S(1)} all-to-all(bf16[16,16,1536]{2,1,0:T(8,128)(2,1)} %bitcast.36), channel_id=1, replica_groups=mesh['z'=8,'y'=4,'c'=2,'t'=4] {'y','t'}, dimensions={0} | all-to-all | bytes 1572864 | tf_op jit(solution)/shard_map/all_to_all | solution.py:313
  49.0 1.7 %shard_map.112 = bf16[8,16,1536]{2,1,0:T(8,128)(2,1)} custom-call(s32[3]{0:T(128)S(1)} %pad_add_fusion.place_ref.facts_ref, bf16[4,16,1536]{2,1,0:T(8,128)(2,1)S(1)} %shard_map.111.mine_ref, bf16[4,16,1536]{2,1,0:T(8,128)(2,1)S(1)} %collective-permute-done.other_ref), custom_call_target="tpu_custom_call" | custom-call | tf_op jit(solution)/shard_map/pallas_call | solution.py:316
  50.7 8.1 %all-to-all-start.2 = ((bf16[8,16,1536]{2,1,0:T(8,128)(2,1)}), bf16[8,16,1536]{2,1,0:T(8,128)(2,1)}, u32[]{:S(2)}, u32[]{:S(2)}) async-start(bf16[8,16,1536]{2,1,0:T(8,128)(2,1)} %shard_map.112), calls=%async_computation.2 | async-start | bytes 786432 | tf_op jit(solution)/shard_map/all_to_all | solution.py:323
  58.8 1.9 %constant_dynamic-slice_fusion = bf16[176,1408]{1,0:T(8,128)(2,1)} fusion(bf16[352,1408]{1,0:T(8,128)(2,1)} %w0_ref, s32[]{:T(128)S(6)} %select_n.110), kind=kLoop, calls=%fused_computation.17 | loop fusion | bytes 991236 | tf_op jit(solution)/shard_map/dynamic_slice | solution.py:319
  61.4 1.9 %collective-permute-start.5 = (bf16[128,352]{0,1:T(8,128)(2,1)S(1)}, bf16[128,352]{0,1:T(8,128)(2,1)S(1)}, u32[]{:S(2)}, u32[]{:S(2)}) collective-permute-start(bf16[128,352]{0,1:T(8,128)(2,1)S(1)} %copy-done.5), channel_id=1, source_target_pairs={{0,2},{1,3},{2,0},{3,1},{4,6},{5,7},{6,4},{7,5},{8,10},{9,11},{10,... | collective-permute-start | bytes 270344 | tf_op jit(solution)/shard_map/ppermute | solution.py:33
  63.3 3.2 %collective-permute-start.14 = (bf16[176,1408]{1,0:T(8,128)(2,1)}, bf16[176,1408]{1,0:T(8,128)(2,1)}, u32[]{:S(2)}, u32[]{:S(2)}) collective-permute-start(bf16[176,1408]{1,0:T(8,128)(2,1)} %constant_dynamic-slice_fusion), channel_id=1, source_target_pairs={{0,3},{1,0},{2,1},{3,2},{4,7},{5,4},{6,5},{7,6},{8,11},{9,8},{10,9... | collective-permute-start | bytes 1486856 | tf_op jit(solution)/shard_map/ppermute | solution.py:33
  69.4 2.0 %collective-permute-start.12 = (bf16[176,1408]{1,0:T(8,128)(2,1)}, bf16[176,1408]{1,0:T(8,128)(2,1)}, u32[]{:S(2)}, u32[]{:S(2)}) collective-permute-start(bf16[176,1408]{1,0:T(8,128)(2,1)} %constant_dynamic-slice_fusion), channel_id=1, source_target_pairs={{0,2},{1,3},{2,0},{3,1},{4,6},{5,7},{6,4},{7,5},{8,10},{9,11},{10,... | collective-permute-start | bytes 1486856 | tf_op jit(solution)/shard_map/ppermute | solution.py:33
  75.1 1.5 %collective-permute-start.2 = (bf16[16,1536]{1,0:T(8,128)(2,1)S(1)}, bf16[16,1536]{1,0:T(8,128)(2,1)S(1)}, u32[]{:S(2)}, u32[]{:S(2)}) collective-permute-start(bf16[16,1536]{1,0:T(8,128)(2,1)S(1)} %reduce_sum.12.r0_ref), channel_id=1, source_target_pairs={{0,2},{1,3},{2,0},{3,1},{4,6},{5,7},{6,4},{7,5},{8,10},{9,11},{10,... | collective-permute-start | bytes 147464 | tf_op jit(solution)/shard_map/ppermute | solution.py:33
  76.6 13.2 %collective-permute-done.3.r3_ref = bf16[16,1536]{1,0:T(8,128)(2,1)S(1)} collective-permute-done((bf16[16,1536]{1,0:T(8,128)(2,1)S(1)}, bf16[16,1536]{1,0:T(8,128)(2,1)S(1)}, u32[]{:S(2)}, u32[]{:S(2)}) %collective-permute-start.3) | collective-permute-done | bytes 49184 | tf_op jit(solution)/shard_map/ppermute | solution.py:33
  91.6 3.9 %collective-permute-done.1.r1_ref = bf16[16,1536]{1,0:T(8,128)(2,1)S(1)} collective-permute-done((bf16[16,1536]{1,0:T(8,128)(2,1)S(1)}, bf16[16,1536]{1,0:T(8,128)(2,1)S(1)}, u32[]{:S(2)}, u32[]{:S(2)}) %collective-permute-start.1) | collective-permute-done | bytes 49184 | tf_op jit(solution)/shard_map/ppermute | solution.py:33
  95.5 2.4 %shard_map.113 = bf16[4,3,88,128]{3,2,1,0:T(8,128)(2,1)S(1)} custom-call(s32[3]{0:T(128)S(1)} %pad_add_fusion.place_ref.facts_ref, bf16[16,1536]{1,0:T(8,128)(2,1)S(1)} %reduce_sum.12.r0_ref, bf16[16,1536]{1,0:T(8,128)(2,1)S(1)} %collective-permute-done.1.r1_ref, bf16[16,1536]{1,0:T(8,128)(2,1)S(1)} %collective-permute-done.2.r2_ref, ...), custom_call_target="tpu_custom_call" | custom-call | tf_op jit(solution)/shard_map/pallas_call | solution.py:330
  97.9 9.2 %all_to_all.26.own_ref = bf16[4,3,88,128]{3,2,1,0:T(8,128)(2,1)S(1)} all-to-all(bf16[4,3,88,128]{3,2,1,0:T(8,128)(2,1)S(1)} %shard_map.113), channel_id=1, replica_groups=mesh['z'=8,'y'=4,'c'=2,'t'=4] {'y'}, dimensions={0} | all-to-all | bytes 540672 | tf_op jit(solution)/shard_map/all_to_all | solution.py:336
  107.1 5.5 %collective-permute-start.8 = (bf16[4,2,88,128]{3,2,1,0:T(8,128)(2,1)S(1)}, bf16[4,2,88,128]{3,2,1,0:T(8,128)(2,1)S(1)}, u32[]{:S(2)}, u32[]{:S(2)}) collective-permute-start(bf16[4,2,88,128]{3,2,1,0:T(8,128)(2,1)S(1)} %slice.12), channel_id=1, source_target_pairs={{0,64},{32,96},{64,128},{96,160},{128,192},{160,224},{1,65},{33,97... | collective-permute-start | bytes 540680 | tf_op jit(solution)/shard_map/ppermute | solution.py:28
  112.6 2.5 %collective-permute-start.7 = (bf16[4,2,88,128]{3,2,1,0:T(8,128)(2,1)S(1)}, bf16[4,2,88,128]{3,2,1,0:T(8,128)(2,1)S(1)}, u32[]{:S(2)}, u32[]{:S(2)}) collective-permute-start(bf16[4,2,88,128]{3,2,1,0:T(8,128)(2,1)S(1)} %slice.12), channel_id=1, source_target_pairs={{0,32},{32,64},{64,96},{96,128},{128,160},{160,192},{192,224},{1,3... | collective-permute-start | bytes 540680 | tf_op jit(solution)/shard_map/ppermute | solution.py:28
  115.2 2.5 %collective-permute-done.8.far_ref = bf16[4,2,88,128]{3,2,1,0:T(8,128)(2,1)S(1)} collective-permute-done((bf16[4,2,88,128]{3,2,1,0:T(8,128)(2,1)S(1)}, bf16[4,2,88,128]{3,2,1,0:T(8,128)(2,1)S(1)}, u32[]{:S(2)}, u32[]{:S(2)}) %collective-permute-start.8) | collective-permute-done | bytes 180256 | tf_op jit(solution)/shard_map/ppermute | solution.py:28
  117.7 2.3 %collective-permute-done.7.near_ref = bf16[4,2,88,128]{3,2,1,0:T(8,128)(2,1)S(1)} collective-permute-done((bf16[4,2,88,128]{3,2,1,0:T(8,128)(2,1)S(1)}, bf16[4,2,88,128]{3,2,1,0:T(8,128)(2,1)S(1)}, u32[]{:S(2)}, u32[]{:S(2)}) %collective-permute-start.7) | collective-permute-done | bytes 180256 | tf_op jit(solution)/shard_map/ppermute | solution.py:28
  121.6 4.8 %shard_map.114 = bf16[4,4,88,128]{3,2,1,0:T(8,128)(2,1)} custom-call(s32[3]{0:T(128)S(1)} %pad_add_fusion.place_ref.facts_ref, s32[16]{0:T(128)S(1)} %copy-done.2, bf16[4,3,88,128]{3,2,1,0:T(8,128)(2,1)S(1)} %all_to_all.26.own_ref, bf16[4,2,88,128]{3,2,1,0:T(8,128)(2,1)S(1)} %collective-permute-done.7.near_ref, ...), custom_call_target="tpu_custom_call" | custom-call | tf_op jit(solution)/shard_map/pallas_call | solution.py:344
  126.3 4.0 %all-to-all-start.4 = ((bf16[16,88,128]{2,1,0:T(8,128)(2,1)}), bf16[16,88,128]{2,1,0:T(8,128)(2,1)S(1)}, u32[]{:S(2)}, u32[]{:S(2)}) async-start(bf16[16,88,128]{2,1,0:T(8,128)(2,1)} %bitcast.20), calls=%async_computation.4 | async-start | bytes 720896 | tf_op jit(solution)/shard_map/all_to_all | solution.py:351
  132.8 7.4 %all-to-all-done.4 = bf16[16,88,128]{2,1,0:T(8,128)(2,1)S(1)} async-done(((bf16[16,88,128]{2,1,0:T(8,128)(2,1)}), bf16[16,88,128]{2,1,0:T(8,128)(2,1)S(1)}, u32[]{:S(2)}, u32[]{:S(2)}) %all-to-all-start.4) | async-done | bytes 360480 | tf_op jit(solution)/shard_map/all_to_all | solution.py:351
  140.2 3.3 %shard_map.116 = bf16[128,1408]{1,0:T(8,128)(2,1)} custom-call(s32[3]{0:T(128)S(1)} %pad_add_fusion.place_ref.facts_ref, bf16[4,2,176,128]{3,2,1,0:T(8,128)(2,1)S(1)} %bitcast.34, bf16[352,1408]{1,0:T(8,128)(2,1)S(1)} %copy-done.1, bf16[176,1408]{1,0:T(8,128)(2,1)} %collective-permute-done.12.m2_ref, bf16[176,1408]{1,0:T(8,128)(2,1)} %collective-permute-done.13.m1_ref, ...), custom_call_target="tpu_custom_call" | custom-call | tf_op jit(solution)/shard_map/pallas_call | solution.py:352
  (59 shorter events, 19.3 us)
Async XLA Ops:
  7.1 15.9 %all-to-all-start = ((bf16[4,64,1408]{2,1,0:T(8,128)(2,1)}), bf16[4,64,1408]{2,1,0:T(8,128)(2,1)S(1)}, u32[]{:S(2)}, u32[]{:S(2)}) async-start(bf16[4,64,1408]{2,1,0:T(8,128)(2,1)} %bitcast.39), calls=%async_computation | async-start | bytes 1441792 | tf_op jit(solution)/shard_map/all_to_all | solution.py:297
  47.3 48.1 %copy-start = (bf16[1408,3,352]{0,2,1:T(8,128)(2,1)S(1)}, bf16[1408,3,352]{0,2,1:T(8,128)(2,1)}, u32[]{:S(2)}) copy-start(bf16[1408,3,352]{0,2,1:T(8,128)(2,1)} %param.20) | copy-start | bytes 8921092
  47.4 1.5 %collective-permute-start = (bf16[4,16,1536]{2,1,0:T(8,128)(2,1)S(1)}, bf16[4,16,1536]{2,1,0:T(8,128)(2,1)S(1)}, u32[]{:S(2)}, u32[]{:S(2)}) collective-permute-start(bf16[4,16,1536]{2,1,0:T(8,128)(2,1)S(1)} %shard_map.111.mine_ref), channel_id=1, source_target_pairs={{0,4},{4,0},{1,5},{5,1},{2,6},{6,2},{3,7},{7,3},{8,12},{12,8},{9,1... | collective-permute-start | bytes 589832 | tf_op jit(solution)/shard_map/ppermute | solution.py:33
  50.7 21.4 %all-to-all-start.2 = ((bf16[8,16,1536]{2,1,0:T(8,128)(2,1)}), bf16[8,16,1536]{2,1,0:T(8,128)(2,1)}, u32[]{:S(2)}, u32[]{:S(2)}) async-start(bf16[8,16,1536]{2,1,0:T(8,128)(2,1)} %shard_map.112), calls=%async_computation.2 | async-start | bytes 786432 | tf_op jit(solution)/shard_map/all_to_all | solution.py:323
  60.7 14.4 %collective-permute-start.6 = (bf16[128,352]{0,1:T(8,128)(2,1)S(1)}, bf16[128,352]{0,1:T(8,128)(2,1)S(1)}, u32[]{:S(2)}, u32[]{:S(2)}) collective-permute-start(bf16[128,352]{0,1:T(8,128)(2,1)S(1)} %copy-done.5), channel_id=1, source_target_pairs={{0,3},{1,0},{2,1},{3,2},{4,7},{5,4},{6,5},{7,6},{8,11},{9,8},{10,9... | collective-permute-start | bytes 270344 | tf_op jit(solution)/shard_map/ppermute | solution.py:33
  61.4 11.7 %collective-permute-start.5 = (bf16[128,352]{0,1:T(8,128)(2,1)S(1)}, bf16[128,352]{0,1:T(8,128)(2,1)S(1)}, u32[]{:S(2)}, u32[]{:S(2)}) collective-permute-start(bf16[128,352]{0,1:T(8,128)(2,1)S(1)} %copy-done.5), channel_id=1, source_target_pairs={{0,2},{1,3},{2,0},{3,1},{4,6},{5,7},{6,4},{7,5},{8,10},{9,11},{10,... | collective-permute-start | bytes 270344 | tf_op jit(solution)/shard_map/ppermute | solution.py:33
  63.3 6.1 %collective-permute-start.4 = (bf16[128,352]{0,1:T(8,128)(2,1)S(1)}, bf16[128,352]{0,1:T(8,128)(2,1)S(1)}, u32[]{:S(2)}, u32[]{:S(2)}) collective-permute-start(bf16[128,352]{0,1:T(8,128)(2,1)S(1)} %copy-done.5), channel_id=1, source_target_pairs={{0,1},{1,2},{2,3},{3,0},{4,5},{5,6},{6,7},{7,4},{8,9},{9,10},{10,1... | collective-permute-start | bytes 270344 | tf_op jit(solution)/shard_map/ppermute | solution.py:33
  63.3 51.8 %collective-permute-start.14 = (bf16[176,1408]{1,0:T(8,128)(2,1)}, bf16[176,1408]{1,0:T(8,128)(2,1)}, u32[]{:S(2)}, u32[]{:S(2)}) collective-permute-start(bf16[176,1408]{1,0:T(8,128)(2,1)} %constant_dynamic-slice_fusion), channel_id=1, source_target_pairs={{0,3},{1,0},{2,1},{3,2},{4,7},{5,4},{6,5},{7,6},{8,11},{9,8},{10,9... | collective-permute-start | bytes 1486856 | tf_op jit(solution)/shard_map/ppermute | solution.py:33
  66.5 53.5 %collective-permute-start.13 = (bf16[176,1408]{1,0:T(8,128)(2,1)}, bf16[176,1408]{1,0:T(8,128)(2,1)}, u32[]{:S(2)}, u32[]{:S(2)}) collective-permute-start(bf16[176,1408]{1,0:T(8,128)(2,1)} %constant_dynamic-slice_fusion), channel_id=1, source_target_pairs={{0,1},{1,2},{2,3},{3,0},{4,5},{5,6},{6,7},{7,4},{8,9},{9,10},{10,1... | collective-permute-start | bytes 1486856 | tf_op jit(solution)/shard_map/ppermute | solution.py:33
  69.4 51.1 %collective-permute-start.12 = (bf16[176,1408]{1,0:T(8,128)(2,1)}, bf16[176,1408]{1,0:T(8,128)(2,1)}, u32[]{:S(2)}, u32[]{:S(2)}) collective-permute-start(bf16[176,1408]{1,0:T(8,128)(2,1)} %constant_dynamic-slice_fusion), channel_id=1, source_target_pairs={{0,2},{1,3},{2,0},{3,1},{4,6},{5,7},{6,4},{7,5},{8,10},{9,11},{10,... | collective-permute-start | bytes 1486856 | tf_op jit(solution)/shard_map/ppermute | solution.py:33
  73.1 48.4 %copy-start.2 = (s32[16]{0:T(128)S(1)}, s32[16]{0:T(128)}, u32[]{:S(2)}) copy-start(s32[16]{0:T(128)} %lengths_ref.1) | copy-start | bytes 196
  73.2 16.6 %collective-permute-start.3 = (bf16[16,1536]{1,0:T(8,128)(2,1)S(1)}, bf16[16,1536]{1,0:T(8,128)(2,1)S(1)}, u32[]{:S(2)}, u32[]{:S(2)}) collective-permute-start(bf16[16,1536]{1,0:T(8,128)(2,1)S(1)} %reduce_sum.12.r0_ref), channel_id=1, source_target_pairs={{0,3},{1,0},{2,1},{3,2},{4,7},{5,4},{6,5},{7,6},{8,11},{9,8},{10,9... | collective-permute-start | bytes 147464 | tf_op jit(solution)/shard_map/ppermute | solution.py:33
  75.1 16.5 %collective-permute-start.2 = (bf16[16,1536]{1,0:T(8,128)(2,1)S(1)}, bf16[16,1536]{1,0:T(8,128)(2,1)S(1)}, u32[]{:S(2)}, u32[]{:S(2)}) collective-permute-start(bf16[16,1536]{1,0:T(8,128)(2,1)S(1)} %reduce_sum.12.r0_ref), channel_id=1, source_target_pairs={{0,2},{1,3},{2,0},{3,1},{4,6},{5,7},{6,4},{7,5},{8,10},{9,11},{10,... | collective-permute-start | bytes 147464 | tf_op jit(solution)/shard_map/ppermute | solution.py:33
  89.7 5.7 %collective-permute-start.1 = (bf16[16,1536]{1,0:T(8,128)(2,1)S(1)}, bf16[16,1536]{1,0:T(8,128)(2,1)S(1)}, u32[]{:S(2)}, u32[]{:S(2)}) collective-permute-start(bf16[16,1536]{1,0:T(8,128)(2,1)S(1)} %reduce_sum.12.r0_ref), channel_id=1, source_target_pairs={{0,1},{1,2},{2,3},{3,0},{4,5},{5,6},{6,7},{7,4},{8,9},{9,10},{10,1... | collective-permute-start | bytes 147464 | tf_op jit(solution)/shard_map/ppermute | solution.py:33
  97.8 42.3 %copy-start.1 = (bf16[352,1408]{1,0:T(8,128)(2,1)S(1)}, bf16[352,1408]{1,0:T(8,128)(2,1)}, u32[]{:S(2)}) copy-start(bf16[352,1408]{1,0:T(8,128)(2,1)} %w0_ref) | copy-start | bytes 2973700
  107.1 10.6 %collective-permute-start.8 = (bf16[4,2,88,128]{3,2,1,0:T(8,128)(2,1)S(1)}, bf16[4,2,88,128]{3,2,1,0:T(8,128)(2,1)S(1)}, u32[]{:S(2)}, u32[]{:S(2)}) collective-permute-start(bf16[4,2,88,128]{3,2,1,0:T(8,128)(2,1)S(1)} %slice.12), channel_id=1, source_target_pairs={{0,64},{32,96},{64,128},{96,160},{128,192},{160,224},{1,65},{33,97... | collective-permute-start | bytes 540680 | tf_op jit(solution)/shard_map/ppermute | solution.py:28
  112.6 7.4 %collective-permute-start.7 = (bf16[4,2,88,128]{3,2,1,0:T(8,128)(2,1)S(1)}, bf16[4,2,88,128]{3,2,1,0:T(8,128)(2,1)S(1)}, u32[]{:S(2)}, u32[]{:S(2)}) collective-permute-start(bf16[4,2,88,128]{3,2,1,0:T(8,128)(2,1)S(1)} %slice.12), channel_id=1, source_target_pairs={{0,32},{32,64},{64,96},{96,128},{128,160},{160,192},{192,224},{1,3... | collective-permute-start | bytes 540680 | tf_op jit(solution)/shard_map/ppermute | solution.py:28
  115.1 5.5 %collective-permute-start.9 = (bf16[4,2,88,128]{3,2,1,0:T(8,128)(2,1)S(1)}, bf16[4,2,88,128]{3,2,1,0:T(8,128)(2,1)S(1)}, u32[]{:S(2)}, u32[]{:S(2)}) collective-permute-start(bf16[4,2,88,128]{3,2,1,0:T(8,128)(2,1)S(1)} %slice.12), channel_id=1, source_target_pairs={{0,4},{4,0},{1,5},{5,1},{2,6},{6,2},{3,7},{7,3},{8,12},{12,8},{9,1... | collective-permute-start | bytes 540680 | tf_op jit(solution)/shard_map/ppermute | solution.py:33
  117.7 3.3 %collective-permute-start.11 = (bf16[4,2,88,128]{3,2,1,0:T(8,128)(2,1)S(1)}, bf16[4,2,88,128]{3,2,1,0:T(8,128)(2,1)S(1)}, u32[]{:S(2)}, u32[]{:S(2)}) collective-permute-start(bf16[4,2,88,128]{3,2,1,0:T(8,128)(2,1)S(1)} %collective-permute-done.8.far_ref), channel_id=1, source_target_pairs={{0,4},{4,0},{1,5},{5,1},{2,6},{6,2},{3,7},{7,3},{8,12},{12,8},{9,1... | collective-permute-start | bytes 540680 | tf_op jit(solution)/shard_map/ppermute | solution.py:33
  120.0 1.6 %collective-permute-start.10 = (bf16[4,2,88,128]{3,2,1,0:T(8,128)(2,1)S(1)}, bf16[4,2,88,128]{3,2,1,0:T(8,128)(2,1)S(1)}, u32[]{:S(2)}, u32[]{:S(2)}) collective-permute-start(bf16[4,2,88,128]{3,2,1,0:T(8,128)(2,1)S(1)} %collective-permute-done.7.near_ref), channel_id=1, source_target_pairs={{0,4},{4,0},{1,5},{5,1},{2,6},{6,2},{3,7},{7,3},{8,12},{12,8},{9,1... | collective-permute-start | bytes 540680 | tf_op jit(solution)/shard_map/ppermute | solution.py:33
  120.0 12.8 %collective-permute-start.17 = (bf16[176,1408]{1,0:T(8,128)(2,1)}, bf16[176,1408]{1,0:T(8,128)(2,1)S(1)}, u32[]{:S(2)}, u32[]{:S(2)}) collective-permute-start(bf16[176,1408]{1,0:T(8,128)(2,1)} %collective-permute-done.14.m3_ref), channel_id=1, source_target_pairs={{0,4},{4,0},{1,5},{5,1},{2,6},{6,2},{3,7},{7,3},{8,12},{12,8},{9,1... | collective-permute-start | bytes 1486856 | tf_op jit(solution)/shard_map/ppermute | solution.py:33
  120.5 12.3 %collective-permute-start.16 = (bf16[176,1408]{1,0:T(8,128)(2,1)}, bf16[176,1408]{1,0:T(8,128)(2,1)S(1)}, u32[]{:S(2)}, u32[]{:S(2)}) collective-permute-start(bf16[176,1408]{1,0:T(8,128)(2,1)} %collective-permute-done.13.m1_ref), channel_id=1, source_target_pairs={{0,4},{4,0},{1,5},{5,1},{2,6},{6,2},{3,7},{7,3},{8,12},{12,8},{9,1... | collective-permute-start | bytes 1486856 | tf_op jit(solution)/shard_map/ppermute | solution.py:33
  120.6 12.2 %collective-permute-start.15 = (bf16[176,1408]{1,0:T(8,128)(2,1)}, bf16[176,1408]{1,0:T(8,128)(2,1)}, u32[]{:S(2)}, u32[]{:S(2)}) collective-permute-start(bf16[176,1408]{1,0:T(8,128)(2,1)} %collective-permute-done.12.m2_ref), channel_id=1, source_target_pairs={{0,4},{4,0},{1,5},{5,1},{2,6},{6,2},{3,7},{7,3},{8,12},{12,8},{9,1... | collective-permute-start | bytes 1486856 | tf_op jit(solution)/shard_map/ppermute | solution.py:33
  126.3 13.8 %all-to-all-start.4 = ((bf16[16,88,128]{2,1,0:T(8,128)(2,1)}), bf16[16,88,128]{2,1,0:T(8,128)(2,1)S(1)}, u32[]{:S(2)}, u32[]{:S(2)}) async-start(bf16[16,88,128]{2,1,0:T(8,128)(2,1)} %bitcast.20), calls=%async_computation.4 | async-start | bytes 720896 | tf_op jit(solution)/shard_map/all_to_all | solution.py:351
  (4 other events, 60.1 us)

commit v6 on v5

--- a/solution.py
+++ b/solution.py
@@ -12,7 +12,7 @@
 BLOCK = 128
 MERGED = 64
 EPSILON = 1e-06
-SCALE = HEAD ** (-0.5)
+SCALE2 = HEAD ** (-0.5) / float(np.log(2.0))
 BF = jnp.bfloat16
 F32 = jnp.float32
 I32 = jnp.int32
@@ -74,7 +74,8 @@
 
 
 def vision_kernel(
-    grid_ref, picture_hbm, qkv_hbm, out_hbm, share_ref, picture_ref, qkv_ref, out_ref, arrived
+    place_ref, grid_ref, picture_hbm, qkv_hbm, out_hbm, s0_ref, s1_ref, s2_ref, s3_ref,
+    picture_ref, qkv_ref, out_ref, arrived,
 ):
     copies = [pltpu.make_async_copy(picture_hbm, picture_ref, arrived.at[0])]
     for part in range(3):
@@ -97,16 +98,18 @@
     contexts = []
     for first in range(0, local_width, HEAD):
         q, k, v = (x[first : first + HEAD].astype(BF) for x in parts)
-        scores = dot(k, q, (0, 0)) * SCALE
-        scores = jnp.where(usable, scores, -jnp.inf)
-        expons = jnp.exp(scores - jnp.max(scores, axis=0, keepdims=True))
+        scores = jnp.where(usable, dot(k, q, (0, 0)), -jnp.inf)
+        expons = jnp.exp2((scores - jnp.max(scores, axis=0, keepdims=True)) * SCALE2)
         total = jnp.sum(expons, axis=0, keepdims=True)
         contexts.append(dot(v, expons.astype(BF), (1, 0)) / total)
     context = jnp.concatenate(contexts, axis=0).astype(BF)
-    order = slot_of(iota((count, count), 0)) == iota((count, count), 1)
+    row = (iota((count, count), 0) + place_ref[2] * MERGED) % count
+    order = slot_of(row) == iota((count, count), 1)
     context = dot(order.astype(BF), context, (1, 1)).astype(BF)
     copies[4].wait()
-    share_ref[...] = dot(context, out_ref[...], (1, 0)).astype(BF)
+    share = dot(context, out_ref[...], (1, 0)).astype(BF)
+    for by, share_ref in enumerate((s0_ref, s1_ref, s2_ref, s3_ref)):
+        share_ref[...] = share[by * MERGED : (by + 1) * MERGED]
 
 
 def sum_kernel(parts_ref, rows_ref):
@@ -133,25 +136,12 @@
     routed_ref[...] = routed.astype(BF).reshape(8, 16, wide)
 
 
-def merge_kernel(
-    facts_ref, own_ref, shares_ref, weight_hbm, rows_ref, weight_ref, arrived
-):
+def merge_kernel(facts_ref, own_ref, s0_ref, s1_ref, s2_ref, s3_ref, weight_ref, rows_ref):
     width = own_ref.shape[1]
-    deep = width // 4
-    copies = []
-    for piece in range(4):
-        at = pl.ds(piece * deep, deep)
-        copies.append(
-            pltpu.make_async_copy(weight_hbm.at[at], weight_ref.at[at], arrived.at[piece])
-        )
-        copies[-1].start()
     total = own_ref[...].astype(F32)
-    for other in range(4):
-        total = total + shares_ref[other].astype(F32)
-    normed = normalize(total)
-    for copy in copies:
-        copy.wait()
-    merged = dot(normed, weight_ref[...], (1, 0)).astype(BF)
+    for share in (s0_ref, s1_ref, s2_ref, s3_ref):
+        total = total + share[...].astype(F32)
+    merged = dot(normalize(total), weight_ref[...], (1, 0)).astype(BF)
     lane = iota((MERGED, FACTS), 1)
     facts = jnp.zeros((MERGED, FACTS), I32)
     for index in range(5):
@@ -227,10 +217,10 @@
             start = jnp.where(end <= here + base, end, start)
         query = own_ref[j, 0]
         window = pl.ds(j * 256, WINDOW)
-        scores = dot(query, keys_ref[:, window], (0, 0)) * SCALE
+        scores = dot(query, keys_ref[:, window], (0, 0))
         visible = (column <= here) & (column >= start - base)
         scores = jnp.where(visible, scores, -jnp.inf)
-        expons = jnp.exp(scores - jnp.max(scores, axis=1, keepdims=True))
+        expons = jnp.exp2((scores - jnp.max(scores, axis=1, keepdims=True)) * SCALE2)
         total = jnp.sum(expons, axis=1, keepdims=True)
         summed = dot(values_ref[:, window], expons.astype(BF), (1, 1))
         total = jnp.transpose(jnp.broadcast_to(total, (BLOCK, BLOCK)))
@@ -284,8 +274,8 @@
     place = jnp.stack([z, c, t]).astype(I32)
     share = call(
         vision_kernel,
-        shape((count, width)),
-        [SMEM, HBM, HBM, HBM],
+        [shape((MERGED, width))] * 4,
+        [SMEM, SMEM, HBM, HBM, HBM],
         [
             VMEM((count, width), BF),
             VMEM((3, local_width, width), BF),
@@ -293,21 +283,15 @@
             pltpu.SemaphoreType.DMA((5,)),
         ],
         limit=60,
-    )(picture_grid, picture, vision_qkv.transpose(1, 2, 0), vision_out)
-    shares = lax.all_to_all(share.reshape(4, MERGED, width), "t", 0, 0, tiled=True)
+    )(place, picture_grid, picture, vision_qkv.transpose(1, 2, 0), vision_out)
+    shares = [share[0]] + [around(share[by], "t", by) for by in range(1, 4)]
     chosen = slot_of(t * MERGED + jnp.arange(MERGED))[:, None] == jnp.arange(count)[None, :]
     own = jnp.dot(chosen.astype(BF), picture, preferred_element_type=F32).astype(BF)
     facts = jnp.stack([block, picture_offset[0], picture_grid[0, 0], picture_grid[0, 1], 1])
     facts = jnp.where(t == 0, facts, 0)
     facts = jnp.concatenate([facts, (block % 8 // 2)[None]]).astype(I32)
-    routed = call(
-        merge_kernel,
-        shape((4, MERGED, wide)),
-        [SMEM, VMEM, VMEM, HBM],
-        [VMEM((width, width), BF), pltpu.SemaphoreType.DMA((4,))],
-        limit=60,
-    )(
-        facts, own, shares, merge_weight[0]
+    routed = call(merge_kernel, shape((4, MERGED, wide)), [SMEM] + [VMEM] * 6)(
+        facts, own, *shares, merge_weight[0]
     )
 
     got = lax.all_to_all(routed.reshape(16, 16, wide), ("y", "t"), 0, 0, tiled=True)
@@ -318,7 +302,7 @@
     half = local_width // 2
     near_half = lax.dynamic_slice_in_dim(text_out, c * half, half, 0)
     near_half, tokens = lax.optimization_barrier((near_half, tokens))
-    halves = [around(near_half, "t", by) for by in (2, 1, 3)]
+    halves = [None] + [around(near_half, "t", by) for by in (1, 3)]
     pieces = [tokens] + [around(tokens, "t", by) for by in range(1, 4)]
     got = lax.all_to_all(routed, "z", 0, 0, tiled=True)
     got = jnp.sum(got.astype(F32), axis=0).astype(BF)
@@ -332,7 +316,8 @@
         shape((4, 3, HEAD, BLOCK)),
         [SMEM] + [VMEM] * 6,
     )(place, *rows, own_tokens, text_qkv.transpose(1, 2, 0))
-    heads, late_tokens = lax.optimization_barrier((heads, own_tokens))
+    heads, late_tokens, near_half = lax.optimization_barrier((heads, own_tokens, near_half))
+    halves[0] = around(near_half, "t", 2)
     mine = lax.all_to_all(heads, "y", 0, 0, tiled=True)
     prompt_in = call(place_kernel, shape((BLOCK, width)), [SMEM] + [VMEM] * 5)(
         place, *rows, late_tokens

time: 144 us -> 132 us (0.917)
  waiting for transfers between devices: 39.2 us -> 27.1 us
  Pallas kernels: 25.4 us -> 22 us
  local copies, waits for them, and re-layouts: 10.4 us -> 11.9 us
    ppermute x16 -> x19, waiting for transfers between devices: 20.4 us -> 12.5 us  [around(): return lax.ppermute(x, axis, [(i, (i + by) % count) for i in range(count)])]
    all_to_all x1 -> x0, waiting for transfers between devices: 6.67 us -> none  [local(): lax.all_to_all(share.reshape(4, MERGED, width), 't', 0, 0, tiled=True)]
    ppermute x16 -> x19, starting transfers between devices: 11.9 us -> 16.8 us  [around(): return lax.ppermute(x, axis, [(i, (i + by) % count) for i in range(count)])]
    all_to_all x1 -> x0, starting transfers between devices: 4.3 us -> none  [local(): lax.all_to_all(share.reshape(4, MERGED, width), 't', 0, 0, tiled=True)]
    pallas_call x2, Pallas kernels: 12 us -> 8.67 us  [the longest x1 7.1 us: local(): call(vision_kernel, [shape((MERGED, width))] * 4, [SMEM, SMEM, HBM, HBM,...]
    unnamed x14 -> x18, local copies, waits for them, and re-layouts: 0.93 us -> 3.8 us
    ppermute x2, waiting for transfers between devices: 4.78 us -> 6.53 us  [ahead(): return lax.ppermute(x, axis, [(i, i + by) for i in range(count - by)])]
    all_to_all x1, blocking collectives: 18.5 us -> 20.1 us  [local(): lax.all_to_all(routed.reshape(16, 16, wide), ('y', 't'), 0, 0, tiled=True)]
  transfers between devices with their start and end apart: 21 -> 23, of which waited for: 9 -> 11; matrix products, arithmetic and copies ran while one was open for 9% -> 7% of each run, Pallas kernels for 6% -> 6%
where the time goes in v6:
time: 132 us; the launch traced here: 131 us
  starting transfers between devices  36.6 us (28%)
  blocking collectives  29.2 us (22%)
  waiting for transfers between devices  27.1 us (21%)
  Pallas kernels  22 us (17%)
  local copies, waits for them, and re-layouts  11.9 us (9%)
  other arithmetic  1.82 us (1%)
  between operations  1.67 us (1%)
    all_to_all x1, blocking collectives, local(): lax.all_to_all(routed.reshape(16, 16, wide), ('y', 't'), 0, 0, tiled=True)  20.1 us
    ppermute x19, starting transfers between devices, around(): return lax.ppermute(x, axis, [(i, (i + by) % count) for i in range(count)])  16.8 us
    ppermute x19, waiting for transfers between devices, around(): return lax.ppermute(x, axis, [(i, (i + by) % count) for i in range(count)])  12.5 us
    all_to_all x1, blocking collectives, local(): mine = lax.all_to_all(heads, 'y', 0, 0, tiled=True)  9.1 us
    all_to_all x1, starting transfers between devices, local(): got = lax.all_to_all(routed, 'z', 0, 0, tiled=True)  8.11 us
    ppermute x2, starting transfers between devices, ahead(): return lax.ppermute(x, axis, [(i, i + by) for i in range(count - by)])  7.95 us
    all_to_all x1, waiting for transfers between devices, local(): lax.all_to_all(sent.reshape(16, HEAD, BLOCK), ('t', 'y'), 0, 0, tiled=True)  7.47 us
    pallas_call x1, Pallas kernels, local(): call(vision_kernel, [shape((MERGED, width))] * 4, [SMEM, SMEM, HBM, HBM,...  7.1 us
  transfers between devices with their start and end apart: 23, of which 11 were waited for; matrix products, arithmetic and copies ran while one was open for 7% of the time, Pallas kernels for 6%

profile of v6, /device:TPU:64, one launch (start us, length us, event | category | flops | bytes accessed | tf_op | source)
XLA Modules:
  0.0 130.5 jit_solution(14567688333175579256)
XLA Ops:
  0.7 7.1 %shard_map.109 = (bf16[64,1408]{1,0:T(8,128)(2,1)}, bf16[64,1408]{1,0:T(8,128)(2,1)}, bf16[64,1408]{1,0:T(8,128)(2,1)}, bf16[64,1408]{1,0:T(8,128)(2,1)}) custom-call(s32[3]{0:T(128)} %pad_add_fusion.place_ref.facts_ref, s32[1,2]{1,0:T(1,128)} %grid_ref.1, bf16[256,1408]{1,0:T(8,128)(2,1)} %bitcast.39, bf16[3,352,1408]{2,1,0:T(8,128)(2,1)} %bitcast.38, ...), custom_call_target="tpu_custom_call" | custom-call | tf_op jit(solution)/shard_map/pallas_call | solution.py:275
  9.3 2.7 %collective-permute-start.1 = (bf16[64,1408]{1,0:T(8,128)(2,1)}, bf16[64,1408]{1,0:T(8,128)(2,1)S(1)}, u32[]{:S(2)}, u32[]{:S(2)}) collective-permute-start(bf16[64,1408]{1,0:T(8,128)(2,1)} %get-tuple-element.18), channel_id=1, source_target_pairs={{0,2},{1,3},{2,0},{3,1},{4,6},{5,7},{6,4},{7,5},{8,10},{9,11},{10,... | collective-permute-start | bytes 540680 | tf_op jit(solution)/shard_map/ppermute | solution.py:33
  17.3 3.1 %collective-permute-done.1.s2_ref = bf16[64,1408]{1,0:T(8,128)(2,1)S(1)} collective-permute-done((bf16[64,1408]{1,0:T(8,128)(2,1)}, bf16[64,1408]{1,0:T(8,128)(2,1)S(1)}, u32[]{:S(2)}, u32[]{:S(2)}) %collective-permute-start.1) | collective-permute-done | bytes 180256 | tf_op jit(solution)/shard_map/ppermute | solution.py:33
  20.4 2.1 %copy-done = bf16[1,1408,1408]{2,1,0:T(8,128)(2,1)S(1)} copy-done((bf16[1,1408,1408]{2,1,0:T(8,128)(2,1)S(1)}, bf16[1,1408,1408]{2,1,0:T(8,128)(2,1)}, u32[]{:S(2)}) %copy-start) | copy-done | bytes 3964952
  25.0 20.1 %all_to_all.20 = bf16[16,16,1536]{2,1,0:T(8,128)(2,1)S(1)} all-to-all(bf16[16,16,1536]{2,1,0:T(8,128)(2,1)S(1)} %bitcast.33), channel_id=1, replica_groups=mesh['z'=8,'y'=4,'c'=2,'t'=4] {'y','t'}, dimensions={0} | all-to-all | bytes 1572864 | tf_op jit(solution)/shard_map/all_to_all | solution.py:297
  46.8 1.7 %shard_map.112 = bf16[8,16,1536]{2,1,0:T(8,128)(2,1)} custom-call(s32[3]{0:T(128)S(1)} %copy-done.4, bf16[4,16,1536]{2,1,0:T(8,128)(2,1)S(1)} %shard_map.111.mine_ref, bf16[4,16,1536]{2,1,0:T(8,128)(2,1)S(1)} %collective-permute-done.3.other_ref), custom_call_target="tpu_custom_call" | custom-call | tf_op jit(solution)/shard_map/pallas_call | solution.py:300
  48.5 8.1 %all-to-all-start.1 = ((bf16[8,16,1536]{2,1,0:T(8,128)(2,1)}), bf16[8,16,1536]{2,1,0:T(8,128)(2,1)}, u32[]{:S(2)}, u32[]{:S(2)}) async-start(bf16[8,16,1536]{2,1,0:T(8,128)(2,1)} %shard_map.112), calls=%async_computation.1 | async-start | bytes 786432 | tf_op jit(solution)/shard_map/all_to_all | solution.py:307
  56.6 1.9 %constant_dynamic-slice_fusion = bf16[176,1408]{1,0:T(8,128)(2,1)} fusion(bf16[352,1408]{1,0:T(8,128)(2,1)} %w0_ref, s32[]{:T(128)S(6)} %select_n.110), kind=kLoop, calls=%fused_computation.17 | loop fusion | bytes 991236 | tf_op jit(solution)/shard_map/dynamic_slice | solution.py:303
  59.2 1.9 %collective-permute-start.8 = (bf16[128,352]{0,1:T(8,128)(2,1)}, bf16[128,352]{0,1:T(8,128)(2,1)S(1)}, u32[]{:S(2)}, u32[]{:S(2)}) collective-permute-start(bf16[128,352]{0,1:T(8,128)(2,1)} %param.18), channel_id=1, source_target_pairs={{0,2},{1,3},{2,0},{3,1},{4,6},{5,7},{6,4},{7,5},{8,10},{9,11},{10,... | collective-permute-start | bytes 270344 | tf_op jit(solution)/shard_map/ppermute | solution.py:33
  61.1 3.2 %collective-permute-start.17 = (bf16[176,1408]{1,0:T(8,128)(2,1)}, bf16[176,1408]{1,0:T(8,128)(2,1)}, u32[]{:S(2)}, u32[]{:S(2)}) collective-permute-start(bf16[176,1408]{1,0:T(8,128)(2,1)} %constant_dynamic-slice_fusion), channel_id=1, source_target_pairs={{0,3},{1,0},{2,1},{3,2},{4,7},{5,4},{6,5},{7,6},{8,11},{9,8},{10,9... | collective-permute-start | bytes 1486856 | tf_op jit(solution)/shard_map/ppermute | solution.py:33
  65.3 2.4 %collective-permute-done.7 = bf16[128,352]{0,1:T(8,128)(2,1)S(1)} collective-permute-done((bf16[128,352]{0,1:T(8,128)(2,1)}, bf16[128,352]{0,1:T(8,128)(2,1)S(1)}, u32[]{:S(2)}, u32[]{:S(2)}) %collective-permute-start.7) | collective-permute-done | bytes 90144 | tf_op jit(solution)/shard_map/ppermute | solution.py:33
  70.2 1.9 %collective-permute-start.5 = (bf16[16,1536]{1,0:T(8,128)(2,1)S(1)}, bf16[16,1536]{1,0:T(8,128)(2,1)S(1)}, u32[]{:S(2)}, u32[]{:S(2)}) collective-permute-start(bf16[16,1536]{1,0:T(8,128)(2,1)S(1)} %reduce_sum.12.r0_ref), channel_id=1, source_target_pairs={{0,2},{1,3},{2,0},{3,1},{4,6},{5,7},{6,4},{7,5},{8,10},{9,11},{10,... | collective-permute-start | bytes 147464 | tf_op jit(solution)/shard_map/ppermute | solution.py:33
  74.9 2.1 %collective-permute-done.6.r3_ref = bf16[16,1536]{1,0:T(8,128)(2,1)S(1)} collective-permute-done((bf16[16,1536]{1,0:T(8,128)(2,1)S(1)}, bf16[16,1536]{1,0:T(8,128)(2,1)S(1)}, u32[]{:S(2)}, u32[]{:S(2)}) %collective-permute-start.6) | collective-permute-done | bytes 49184 | tf_op jit(solution)/shard_map/ppermute | solution.py:33
  77.0 2.6 %collective-permute-done.5.r2_ref = bf16[16,1536]{1,0:T(8,128)(2,1)S(1)} collective-permute-done((bf16[16,1536]{1,0:T(8,128)(2,1)S(1)}, bf16[16,1536]{1,0:T(8,128)(2,1)S(1)}, u32[]{:S(2)}, u32[]{:S(2)}) %collective-permute-start.5) | collective-permute-done | bytes 49184 | tf_op jit(solution)/shard_map/ppermute | solution.py:33
  79.9 2.4 %shard_map.113 = bf16[4,3,88,128]{3,2,1,0:T(8,128)(2,1)S(1)} custom-call(s32[3]{0:T(128)S(1)} %copy-done.4, bf16[16,1536]{1,0:T(8,128)(2,1)S(1)} %reduce_sum.12.r0_ref, bf16[16,1536]{1,0:T(8,128)(2,1)S(1)} %collective-permute-done.4.r1_ref, bf16[16,1536]{1,0:T(8,128)(2,1)S(1)} %collective-permute-done.5.r2_ref, ...), custom_call_target="tpu_custom_call" | custom-call | tf_op jit(solution)/shard_map/pallas_call | solution.py:314
  83.6 9.1 %all_to_all.21.own_ref = bf16[4,3,88,128]{3,2,1,0:T(8,128)(2,1)S(1)} all-to-all(bf16[4,3,88,128]{3,2,1,0:T(8,128)(2,1)S(1)} %shard_map.113), channel_id=1, replica_groups=mesh['z'=8,'y'=4,'c'=2,'t'=4] {'y'}, dimensions={0} | all-to-all | bytes 540672 | tf_op jit(solution)/shard_map/all_to_all | solution.py:321
  92.8 5.5 %collective-permute-start.11 = (bf16[4,2,88,128]{3,2,1,0:T(8,128)(2,1)S(1)}, bf16[4,2,88,128]{3,2,1,0:T(8,128)(2,1)S(1)}, u32[]{:S(2)}, u32[]{:S(2)}) collective-permute-start(bf16[4,2,88,128]{3,2,1,0:T(8,128)(2,1)S(1)} %slice.12), channel_id=1, source_target_pairs={{0,64},{32,96},{64,128},{96,160},{128,192},{160,224},{1,65},{33,97... | collective-permute-start | bytes 540680 | tf_op jit(solution)/shard_map/ppermute | solution.py:28
  98.2 2.5 %collective-permute-start.10 = (bf16[4,2,88,128]{3,2,1,0:T(8,128)(2,1)S(1)}, bf16[4,2,88,128]{3,2,1,0:T(8,128)(2,1)S(1)}, u32[]{:S(2)}, u32[]{:S(2)}) collective-permute-start(bf16[4,2,88,128]{3,2,1,0:T(8,128)(2,1)S(1)} %slice.12), channel_id=1, source_target_pairs={{0,32},{32,64},{64,96},{96,128},{128,160},{160,192},{192,224},{1,3... | collective-permute-start | bytes 540680 | tf_op jit(solution)/shard_map/ppermute | solution.py:28
  100.8 4.2 %collective-permute-done.11.far_ref = bf16[4,2,88,128]{3,2,1,0:T(8,128)(2,1)S(1)} collective-permute-done((bf16[4,2,88,128]{3,2,1,0:T(8,128)(2,1)S(1)}, bf16[4,2,88,128]{3,2,1,0:T(8,128)(2,1)S(1)}, u32[]{:S(2)}, u32[]{:S(2)}) %collective-permute-start.11) | collective-permute-done | bytes 180256 | tf_op jit(solution)/shard_map/ppermute | solution.py:28
  105.0 2.3 %collective-permute-done.10.near_ref = bf16[4,2,88,128]{3,2,1,0:T(8,128)(2,1)S(1)} collective-permute-done((bf16[4,2,88,128]{3,2,1,0:T(8,128)(2,1)S(1)}, bf16[4,2,88,128]{3,2,1,0:T(8,128)(2,1)S(1)}, u32[]{:S(2)}, u32[]{:S(2)}) %collective-permute-start.10) | collective-permute-done | bytes 180256 | tf_op jit(solution)/shard_map/ppermute | solution.py:28
  109.0 4.7 %shard_map.114 = bf16[4,4,88,128]{3,2,1,0:T(8,128)(2,1)} custom-call(s32[3]{0:T(128)S(1)} %copy-done.4, s32[16]{0:T(128)S(1)} %copy-done.5, bf16[4,3,88,128]{3,2,1,0:T(8,128)(2,1)S(1)} %all_to_all.21.own_ref, bf16[4,2,88,128]{3,2,1,0:T(8,128)(2,1)S(1)} %collective-permute-done.10.near_ref, bf16[4,2,88,128]{3,2,1,0:T(8,128)(2,1)S(1)} %collective-permute-done.11.far_ref, ...), custom_call_target="tpu_custom_call" | custom-call | tf_op jit(solution)/shard_map/pallas_call | solution.py:329
  113.7 3.7 %all-to-all-start.3 = ((bf16[16,88,128]{2,1,0:T(8,128)(2,1)}), bf16[16,88,128]{2,1,0:T(8,128)(2,1)S(1)}, u32[]{:S(2)}, u32[]{:S(2)}) async-start(bf16[16,88,128]{2,1,0:T(8,128)(2,1)} %bitcast.19), calls=%async_computation.3 | async-start | bytes 720896 | tf_op jit(solution)/shard_map/all_to_all | solution.py:336
  119.8 7.5 %all-to-all-done.3 = bf16[16,88,128]{2,1,0:T(8,128)(2,1)S(1)} async-done(((bf16[16,88,128]{2,1,0:T(8,128)(2,1)}), bf16[16,88,128]{2,1,0:T(8,128)(2,1)S(1)}, u32[]{:S(2)}, u32[]{:S(2)}) %all-to-all-start.3) | async-done | bytes 360480 | tf_op jit(solution)/shard_map/all_to_all | solution.py:336
  127.3 3.3 %shard_map.116 = bf16[128,1408]{1,0:T(8,128)(2,1)} custom-call(s32[3]{0:T(128)S(1)} %copy-done.4, bf16[4,2,176,128]{3,2,1,0:T(8,128)(2,1)S(1)} %bitcast.35, bf16[352,1408]{1,0:T(8,128)(2,1)S(1)} %copy-done.2, bf16[176,1408]{1,0:T(8,128)(2,1)S(1)} %collective-permute-done.15.m2_ref, bf16[176,1408]{1,0:T(8,128)(2,1)} %collective-permute-done.16.m1_ref, ...), custom_call_target="tpu_custom_call" | custom-call | tf_op jit(solution)/shard_map/pallas_call | solution.py:337
  (67 shorter events, 22.9 us)
Async XLA Ops:
  7.8 9.5 %collective-permute-start = (bf16[64,1408]{1,0:T(8,128)(2,1)}, bf16[64,1408]{1,0:T(8,128)(2,1)S(1)}, u32[]{:S(2)}, u32[]{:S(2)}) collective-permute-start(bf16[64,1408]{1,0:T(8,128)(2,1)} %get-tuple-element.17), channel_id=1, source_target_pairs={{0,1},{1,2},{2,3},{3,0},{4,5},{5,6},{6,7},{7,4},{8,9},{9,10},{10,1... | collective-permute-start | bytes 540680 | tf_op jit(solution)/shard_map/ppermute | solution.py:33
  9.3 11.1 %collective-permute-start.1 = (bf16[64,1408]{1,0:T(8,128)(2,1)}, bf16[64,1408]{1,0:T(8,128)(2,1)S(1)}, u32[]{:S(2)}, u32[]{:S(2)}) collective-permute-start(bf16[64,1408]{1,0:T(8,128)(2,1)} %get-tuple-element.18), channel_id=1, source_target_pairs={{0,2},{1,3},{2,0},{3,1},{4,6},{5,7},{6,4},{7,5},{8,10},{9,11},{10,... | collective-permute-start | bytes 540680 | tf_op jit(solution)/shard_map/ppermute | solution.py:33
  12.1 8.3 %collective-permute-start.2 = (bf16[64,1408]{1,0:T(8,128)(2,1)}, bf16[64,1408]{1,0:T(8,128)(2,1)S(1)}, u32[]{:S(2)}, u32[]{:S(2)}) collective-permute-start(bf16[64,1408]{1,0:T(8,128)(2,1)} %get-tuple-element.19), channel_id=1, source_target_pairs={{0,3},{1,0},{2,1},{3,2},{4,7},{5,4},{6,5},{7,6},{8,11},{9,8},{10,9... | collective-permute-start | bytes 540680 | tf_op jit(solution)/shard_map/ppermute | solution.py:33
  45.2 1.5 %collective-permute-start.3 = (bf16[4,16,1536]{2,1,0:T(8,128)(2,1)S(1)}, bf16[4,16,1536]{2,1,0:T(8,128)(2,1)S(1)}, u32[]{:S(2)}, u32[]{:S(2)}) collective-permute-start(bf16[4,16,1536]{2,1,0:T(8,128)(2,1)S(1)} %shard_map.111.mine_ref), channel_id=1, source_target_pairs={{0,4},{4,0},{1,5},{5,1},{2,6},{6,2},{3,7},{7,3},{8,12},{12,8},{9,1... | collective-permute-start | bytes 589832 | tf_op jit(solution)/shard_map/ppermute | solution.py:33
  48.5 19.8 %all-to-all-start.1 = ((bf16[8,16,1536]{2,1,0:T(8,128)(2,1)}), bf16[8,16,1536]{2,1,0:T(8,128)(2,1)}, u32[]{:S(2)}, u32[]{:S(2)}) async-start(bf16[8,16,1536]{2,1,0:T(8,128)(2,1)} %shard_map.112), calls=%async_computation.1 | async-start | bytes 786432 | tf_op jit(solution)/shard_map/all_to_all | solution.py:307
  58.5 13.6 %collective-permute-start.9 = (bf16[128,352]{0,1:T(8,128)(2,1)}, bf16[128,352]{0,1:T(8,128)(2,1)}, u32[]{:S(2)}, u32[]{:S(2)}) collective-permute-start(bf16[128,352]{0,1:T(8,128)(2,1)} %param.18), channel_id=1, source_target_pairs={{0,3},{1,0},{2,1},{3,2},{4,7},{5,4},{6,5},{7,6},{8,11},{9,8},{10,9... | collective-permute-start | bytes 270344 | tf_op jit(solution)/shard_map/ppermute | solution.py:33
  59.2 8.5 %collective-permute-start.8 = (bf16[128,352]{0,1:T(8,128)(2,1)}, bf16[128,352]{0,1:T(8,128)(2,1)S(1)}, u32[]{:S(2)}, u32[]{:S(2)}) collective-permute-start(bf16[128,352]{0,1:T(8,128)(2,1)} %param.18), channel_id=1, source_target_pairs={{0,2},{1,3},{2,0},{3,1},{4,6},{5,7},{6,4},{7,5},{8,10},{9,11},{10,... | collective-permute-start | bytes 270344 | tf_op jit(solution)/shard_map/ppermute | solution.py:33
  61.1 6.6 %collective-permute-start.7 = (bf16[128,352]{0,1:T(8,128)(2,1)}, bf16[128,352]{0,1:T(8,128)(2,1)S(1)}, u32[]{:S(2)}, u32[]{:S(2)}) collective-permute-start(bf16[128,352]{0,1:T(8,128)(2,1)} %param.18), channel_id=1, source_target_pairs={{0,1},{1,2},{2,3},{3,0},{4,5},{5,6},{6,7},{7,4},{8,9},{9,10},{10,1... | collective-permute-start | bytes 270344 | tf_op jit(solution)/shard_map/ppermute | solution.py:33
  61.1 39.6 %collective-permute-start.17 = (bf16[176,1408]{1,0:T(8,128)(2,1)}, bf16[176,1408]{1,0:T(8,128)(2,1)}, u32[]{:S(2)}, u32[]{:S(2)}) collective-permute-start(bf16[176,1408]{1,0:T(8,128)(2,1)} %constant_dynamic-slice_fusion), channel_id=1, source_target_pairs={{0,3},{1,0},{2,1},{3,2},{4,7},{5,4},{6,5},{7,6},{8,11},{9,8},{10,9... | collective-permute-start | bytes 1486856 | tf_op jit(solution)/shard_map/ppermute | solution.py:33
  64.3 43.0 %collective-permute-start.16 = (bf16[176,1408]{1,0:T(8,128)(2,1)}, bf16[176,1408]{1,0:T(8,128)(2,1)}, u32[]{:S(2)}, u32[]{:S(2)}) collective-permute-start(bf16[176,1408]{1,0:T(8,128)(2,1)} %constant_dynamic-slice_fusion), channel_id=1, source_target_pairs={{0,1},{1,2},{2,3},{3,0},{4,5},{5,6},{6,7},{7,4},{8,9},{9,10},{10,1... | collective-permute-start | bytes 1486856 | tf_op jit(solution)/shard_map/ppermute | solution.py:33
  69.4 7.6 %collective-permute-start.6 = (bf16[16,1536]{1,0:T(8,128)(2,1)S(1)}, bf16[16,1536]{1,0:T(8,128)(2,1)S(1)}, u32[]{:S(2)}, u32[]{:S(2)}) collective-permute-start(bf16[16,1536]{1,0:T(8,128)(2,1)S(1)} %reduce_sum.12.r0_ref), channel_id=1, source_target_pairs={{0,3},{1,0},{2,1},{3,2},{4,7},{5,4},{6,5},{7,6},{8,11},{9,8},{10,9... | collective-permute-start | bytes 147464 | tf_op jit(solution)/shard_map/ppermute | solution.py:33
  70.2 9.4 %collective-permute-start.5 = (bf16[16,1536]{1,0:T(8,128)(2,1)S(1)}, bf16[16,1536]{1,0:T(8,128)(2,1)S(1)}, u32[]{:S(2)}, u32[]{:S(2)}) collective-permute-start(bf16[16,1536]{1,0:T(8,128)(2,1)S(1)} %reduce_sum.12.r0_ref), channel_id=1, source_target_pairs={{0,2},{1,3},{2,0},{3,1},{4,6},{5,7},{6,4},{7,5},{8,10},{9,11},{10,... | collective-permute-start | bytes 147464 | tf_op jit(solution)/shard_map/ppermute | solution.py:33
  72.1 7.8 %collective-permute-start.4 = (bf16[16,1536]{1,0:T(8,128)(2,1)S(1)}, bf16[16,1536]{1,0:T(8,128)(2,1)S(1)}, u32[]{:S(2)}, u32[]{:S(2)}) collective-permute-start(bf16[16,1536]{1,0:T(8,128)(2,1)S(1)} %reduce_sum.12.r0_ref), channel_id=1, source_target_pairs={{0,1},{1,2},{2,3},{3,0},{4,5},{5,6},{6,7},{7,4},{8,9},{9,10},{10,1... | collective-permute-start | bytes 147464 | tf_op jit(solution)/shard_map/ppermute | solution.py:33
  82.3 44.9 %copy-start.2 = (bf16[352,1408]{1,0:T(8,128)(2,1)S(1)}, bf16[352,1408]{1,0:T(8,128)(2,1)}, u32[]{:S(2)}) copy-start(bf16[352,1408]{1,0:T(8,128)(2,1)} %w0_ref) | copy-start | bytes 2973700
  82.3 25.6 %collective-permute-start.15 = (bf16[176,1408]{1,0:T(8,128)(2,1)}, bf16[176,1408]{1,0:T(8,128)(2,1)S(1)}, u32[]{:S(2)}, u32[]{:S(2)}) collective-permute-start(bf16[176,1408]{1,0:T(8,128)(2,1)} %constant_dynamic-slice_fusion), channel_id=1, source_target_pairs={{0,2},{1,3},{2,0},{3,1},{4,6},{5,7},{6,4},{7,5},{8,10},{9,11},{10,... | collective-permute-start | bytes 1486856 | tf_op jit(solution)/shard_map/ppermute | solution.py:33
  92.8 12.3 %collective-permute-start.11 = (bf16[4,2,88,128]{3,2,1,0:T(8,128)(2,1)S(1)}, bf16[4,2,88,128]{3,2,1,0:T(8,128)(2,1)S(1)}, u32[]{:S(2)}, u32[]{:S(2)}) collective-permute-start(bf16[4,2,88,128]{3,2,1,0:T(8,128)(2,1)S(1)} %slice.12), channel_id=1, source_target_pairs={{0,64},{32,96},{64,128},{96,160},{128,192},{160,224},{1,65},{33,97... | collective-permute-start | bytes 540680 | tf_op jit(solution)/shard_map/ppermute | solution.py:28
  98.2 9.1 %collective-permute-start.10 = (bf16[4,2,88,128]{3,2,1,0:T(8,128)(2,1)S(1)}, bf16[4,2,88,128]{3,2,1,0:T(8,128)(2,1)S(1)}, u32[]{:S(2)}, u32[]{:S(2)}) collective-permute-start(bf16[4,2,88,128]{3,2,1,0:T(8,128)(2,1)S(1)} %slice.12), channel_id=1, source_target_pairs={{0,32},{32,64},{64,96},{96,128},{128,160},{160,192},{192,224},{1,3... | collective-permute-start | bytes 540680 | tf_op jit(solution)/shard_map/ppermute | solution.py:28
  100.7 7.2 %collective-permute-start.12 = (bf16[4,2,88,128]{3,2,1,0:T(8,128)(2,1)S(1)}, bf16[4,2,88,128]{3,2,1,0:T(8,128)(2,1)S(1)}, u32[]{:S(2)}, u32[]{:S(2)}) collective-permute-start(bf16[4,2,88,128]{3,2,1,0:T(8,128)(2,1)S(1)} %slice.12), channel_id=1, source_target_pairs={{0,4},{4,0},{1,5},{5,1},{2,6},{6,2},{3,7},{7,3},{8,12},{12,8},{9,1... | collective-permute-start | bytes 540680 | tf_op jit(solution)/shard_map/ppermute | solution.py:33
  105.0 3.4 %collective-permute-start.14 = (bf16[4,2,88,128]{3,2,1,0:T(8,128)(2,1)S(1)}, bf16[4,2,88,128]{3,2,1,0:T(8,128)(2,1)S(1)}, u32[]{:S(2)}, u32[]{:S(2)}) collective-permute-start(bf16[4,2,88,128]{3,2,1,0:T(8,128)(2,1)S(1)} %collective-permute-done.11.far_ref), channel_id=1, source_target_pairs={{0,4},{4,0},{1,5},{5,1},{2,6},{6,2},{3,7},{7,3},{8,12},{12,8},{9,1... | collective-permute-start | bytes 540680 | tf_op jit(solution)/shard_map/ppermute | solution.py:33
  107.4 1.6 %collective-permute-start.13 = (bf16[4,2,88,128]{3,2,1,0:T(8,128)(2,1)S(1)}, bf16[4,2,88,128]{3,2,1,0:T(8,128)(2,1)S(1)}, u32[]{:S(2)}, u32[]{:S(2)}) collective-permute-start(bf16[4,2,88,128]{3,2,1,0:T(8,128)(2,1)S(1)} %collective-permute-done.10.near_ref), channel_id=1, source_target_pairs={{0,4},{4,0},{1,5},{5,1},{2,6},{6,2},{3,7},{7,3},{8,12},{12,8},{9,1... | collective-permute-start | bytes 540680 | tf_op jit(solution)/shard_map/ppermute | solution.py:33
  107.4 12.4 %collective-permute-start.20 = (bf16[176,1408]{1,0:T(8,128)(2,1)}, bf16[176,1408]{1,0:T(8,128)(2,1)S(1)}, u32[]{:S(2)}, u32[]{:S(2)}) collective-permute-start(bf16[176,1408]{1,0:T(8,128)(2,1)} %collective-permute-done.17.m3_ref), channel_id=1, source_target_pairs={{0,4},{4,0},{1,5},{5,1},{2,6},{6,2},{3,7},{7,3},{8,12},{12,8},{9,1... | collective-permute-start | bytes 1486856 | tf_op jit(solution)/shard_map/ppermute | solution.py:33
  107.9 11.9 %collective-permute-start.19 = (bf16[176,1408]{1,0:T(8,128)(2,1)}, bf16[176,1408]{1,0:T(8,128)(2,1)}, u32[]{:S(2)}, u32[]{:S(2)}) collective-permute-start(bf16[176,1408]{1,0:T(8,128)(2,1)} %collective-permute-done.16.m1_ref), channel_id=1, source_target_pairs={{0,4},{4,0},{1,5},{5,1},{2,6},{6,2},{3,7},{7,3},{8,12},{12,8},{9,1... | collective-permute-start | bytes 1486856 | tf_op jit(solution)/shard_map/ppermute | solution.py:33
  108.0 19.3 %collective-permute-start.18 = (bf16[176,1408]{1,0:T(8,128)(2,1)S(1)}, bf16[176,1408]{1,0:T(8,128)(2,1)}, u32[]{:S(2)}, u32[]{:S(2)}) collective-permute-start(bf16[176,1408]{1,0:T(8,128)(2,1)S(1)} %collective-permute-done.15.m2_ref), channel_id=1, source_target_pairs={{0,4},{4,0},{1,5},{5,1},{2,6},{6,2},{3,7},{7,3},{8,12},{12,8},{9,1... | collective-permute-start | bytes 1486856 | tf_op jit(solution)/shard_map/ppermute | solution.py:33
  113.7 13.6 %all-to-all-start.3 = ((bf16[16,88,128]{2,1,0:T(8,128)(2,1)}), bf16[16,88,128]{2,1,0:T(8,128)(2,1)S(1)}, u32[]{:S(2)}, u32[]{:S(2)}) async-start(bf16[16,88,128]{2,1,0:T(8,128)(2,1)} %bitcast.19), calls=%async_computation.3 | async-start | bytes 720896 | tf_op jit(solution)/shard_map/all_to_all | solution.py:336
  (8 other events, 134.3 us)

commit v7 on v6

--- a/solution.py
+++ b/solution.py
@@ -20,6 +20,7 @@
 SMEM = pltpu.SMEM
 HBM = pltpu.HBM
 FACTS = 128
+STRIP = 256
 WINDOW = 18 * BLOCK
 
 
@@ -33,9 +34,10 @@
     return lax.ppermute(x, axis, [(i, (i + by) % count) for i in range(count)])
 
 
-def call(kernel, out_shape, spaces, scratch=(), limit=8):
+def call(kernel, out_shape, spaces, scratch=(), limit=8, flops=None):
     single = not isinstance(out_shape, (list, tuple))
     outs = pl.BlockSpec(memory_space=VMEM)
+    cost = flops and pl.CostEstimate(flops=flops, transcendentals=0, bytes_accessed=flops // 400)
     return pl.pallas_call(
         kernel,
         out_shape=out_shape,
@@ -43,6 +45,7 @@
         out_specs=outs if single else [outs] * len(out_shape),
         scratch_shapes=scratch,
         compiler_params=pltpu.CompilerParams(vmem_limit_bytes=limit << 20),
+        cost_estimate=cost,
     )
 
 
@@ -136,12 +139,22 @@
     routed_ref[...] = routed.astype(BF).reshape(8, 16, wide)
 
 
-def merge_kernel(facts_ref, own_ref, s0_ref, s1_ref, s2_ref, s3_ref, weight_ref, rows_ref):
+def own_kernel(place_ref, picture_ref, share_ref, own_ref):
+    count = picture_ref.shape[0]
+    row = iota((MERGED, count), 0) + place_ref[2] * MERGED
+    chosen = (slot_of(row) == iota((MERGED, count), 1)).astype(BF)
+    own_ref[...] = dot(chosen, picture_ref[...], (1, 0)) + share_ref[...].astype(F32)
+
+
+def merge_kernel(facts_ref, own_ref, s1_ref, s2_ref, s3_ref, top_ref, low_ref, rows_ref):
     width = own_ref.shape[1]
-    total = own_ref[...].astype(F32)
-    for share in (s0_ref, s1_ref, s2_ref, s3_ref):
+    total = own_ref[...]
+    for share in (s1_ref, s2_ref, s3_ref):
         total = total + share[...].astype(F32)
-    merged = dot(normalize(total), weight_ref[...], (1, 0)).astype(BF)
+    normed = normalize(total)
+    deep = top_ref.shape[0]
+    merged = dot(normed[:, :deep], top_ref[...], (1, 0))
+    merged = (merged + dot(normed[:, deep:], low_ref[...], (1, 0))).astype(BF)
     lane = iota((MERGED, FACTS), 1)
     facts = jnp.zeros((MERGED, FACTS), I32)
     for index in range(5):
@@ -198,15 +211,13 @@
         skip = 1 if plane == 2 else 0
         for y in range(4):
             at = (plane * 8 + 2 * y) * BLOCK
-            for half in range(2):
-                lanes = pl.ds(at + half * BLOCK, BLOCK)
-                for part, store in ((0, keys_ref), (1, values_ref)):
-                    picked = jnp.where(
-                        c == half, mine[y, skip + part], other[y, part]
-                    )
-                    store[:, lanes] = picked
+            mine_at = pl.ds(pl.multiple_of(at + c * BLOCK, BLOCK), BLOCK)
+            other_at = pl.ds(pl.multiple_of(at + (1 - c) * BLOCK, BLOCK), BLOCK)
+            for part, store in ((0, keys_ref), (1, values_ref)):
+                store[:, mine_at] = mine[y, skip + part]
+                store[:, other_at] = other[y, part]
     row = iota((BLOCK, 1), 0)
-    column = iota((BLOCK, WINDOW), 1)
+    column = iota((BLOCK, STRIP), 1)
     for j in range(4):
         base = (z - 2) * 1024 + j * 256
         here = 2048 + c * BLOCK + row
@@ -215,14 +226,26 @@
         for prompt in range(16):
             end = end + lengths_ref[prompt]
             start = jnp.where(end <= here + base, end, start)
-        query = own_ref[j, 0]
-        window = pl.ds(j * 256, WINDOW)
-        scores = dot(query, keys_ref[:, window], (0, 0))
-        visible = (column <= here) & (column >= start - base)
-        scores = jnp.where(visible, scores, -jnp.inf)
-        expons = jnp.exp2((scores - jnp.max(scores, axis=1, keepdims=True)) * SCALE2)
-        total = jnp.sum(expons, axis=1, keepdims=True)
-        summed = dot(values_ref[:, window], expons.astype(BF), (1, 1))
+        low = start - base
+        query = own_ref[j, 0].T
+        strips, top = [], None
+        for first in range(0, WINDOW, STRIP):
+            scores = dot(query, keys_ref[:, pl.ds(j * 256 + first, STRIP)], (1, 0))
+            visible = column >= low - first
+            if first + STRIP > 2048:
+                visible = visible & (column <= here - first)
+            scores = jnp.where(visible, scores, -jnp.inf)
+            top = scores if top is None else jnp.maximum(top, scores)
+            strips.append(scores)
+        top = jnp.max(top, axis=1, keepdims=True)
+        total = jnp.zeros((BLOCK, STRIP), F32)
+        summed = jnp.zeros((HEAD, BLOCK), F32)
+        for strip, scores in enumerate(strips):
+            expons = jnp.exp2((scores - top) * SCALE2)
+            total = total + expons
+            values = values_ref[:, pl.ds(j * 256 + strip * STRIP, STRIP)]
+            summed = summed + dot(values, expons.astype(BF), (1, 1))
+        total = jnp.sum(total, axis=1, keepdims=True)
         total = jnp.transpose(jnp.broadcast_to(total, (BLOCK, BLOCK)))
         context = (summed / total[:HEAD]).astype(BF)
         for t in range(4):
@@ -284,14 +307,17 @@
         ],
         limit=60,
     )(place, picture_grid, picture, vision_qkv.transpose(1, 2, 0), vision_out)
-    shares = [share[0]] + [around(share[by], "t", by) for by in range(1, 4)]
-    chosen = slot_of(t * MERGED + jnp.arange(MERGED))[:, None] == jnp.arange(count)[None, :]
-    own = jnp.dot(chosen.astype(BF), picture, preferred_element_type=F32).astype(BF)
+    shares = [around(share[by], "t", by) for by in range(1, 4)]
+    own = call(own_kernel, shape((MERGED, width), F32), [SMEM, VMEM, VMEM], flops=8 * 10**9)(
+        place, picture, share[0]
+    )
+    own, merge_weight = lax.optimization_barrier((own, merge_weight))
+    merge_parts = (merge_weight[0, : width // 2], merge_weight[0, width // 2 :])
     facts = jnp.stack([block, picture_offset[0], picture_grid[0, 0], picture_grid[0, 1], 1])
     facts = jnp.where(t == 0, facts, 0)
     facts = jnp.concatenate([facts, (block % 8 // 2)[None]]).astype(I32)
     routed = call(merge_kernel, shape((4, MERGED, wide)), [SMEM] + [VMEM] * 6)(
-        facts, own, *shares, merge_weight[0]
+        facts, own, *shares, *merge_parts
     )
 
     got = lax.all_to_all(routed.reshape(16, 16, wide), ("y", "t"), 0, 0, tiled=True)

time: 132 us -> 129 us (0.977)
  waiting for transfers between devices: 27.1 us -> 21.1 us
  local copies, waits for them, and re-layouts: 11.9 us -> 14.3 us
  starting transfers between devices: 36.6 us -> 38.2 us
    ppermute x19, waiting for transfers between devices: 12.5 us -> 5.2 us  [around(): return lax.ppermute(x, axis, [(i, (i + by) % count) for i in range(count)])]
    ppermute x19, starting transfers between devices: 16.8 us -> 18.6 us  [around(): return lax.ppermute(x, axis, [(i, (i + by) % count) for i in range(count)])]
    squeeze x0 -> x1, local copies, waits for them, and re-layouts: none -> 1.6 us  [local(): merge_parts = (merge_weight[0, :width // 2], merge_weight[0, width // 2:])]
    all_to_all x1, waiting for transfers between devices: 0.6 us -> 1.94 us  [local(): got = lax.all_to_all(routed, 'z', 0, 0, tiled=True)]
    unnamed x18 -> x20, local copies, waits for them, and re-layouts: 3.8 us -> 4.53 us
  transfers between devices with their start and end apart: 23 -> 23, of which waited for: 11 -> 9; matrix products, arithmetic and copies ran while one was open for 7% -> 9% of each run, Pallas kernels for 6% -> 7%
where the time goes in v7:
time: 129 us; the launch traced here: 128 us
  starting transfers between devices  38.2 us (30%)
  blocking collectives  28 us (22%)
  Pallas kernels  22.6 us (18%)
  waiting for transfers between devices  21.1 us (16%)
  local copies, waits for them, and re-layouts  14.3 us (11%)
  other arithmetic  1.72 us (1%)
  between operations  1.62 us (1%)
    all_to_all x1, blocking collectives, local(): lax.all_to_all(routed.reshape(16, 16, wide), ('y', 't'), 0, 0, tiled=True)  18.9 us
    ppermute x19, starting transfers between devices, around(): return lax.ppermute(x, axis, [(i, (i + by) % count) for i in range(count)])  18.6 us
    all_to_all x1, blocking collectives, local(): mine = lax.all_to_all(heads, 'y', 0, 0, tiled=True)  9.11 us
    all_to_all x1, starting transfers between devices, local(): got = lax.all_to_all(routed, 'z', 0, 0, tiled=True)  8.13 us
    ppermute x2, starting transfers between devices, ahead(): return lax.ppermute(x, axis, [(i, i + by) for i in range(count - by)])  7.95 us
    all_to_all x1, waiting for transfers between devices, local(): lax.all_to_all(sent.reshape(16, HEAD, BLOCK), ('t', 'y'), 0, 0, tiled=True)  7.59 us
    pallas_call x1, Pallas kernels, local(): call(vision_kernel, [shape((MERGED, width))] * 4, [SMEM, SMEM, HBM, HBM,...  7.18 us
    ppermute x2, waiting for transfers between devices, ahead(): return lax.ppermute(x, axis, [(i, i + by) for i in range(count - by)])  6.35 us
  transfers between devices with their start and end apart: 23, of which 9 were waited for; matrix products, arithmetic and copies ran while one was open for 9% of the time, Pallas kernels for 7%

profile of v7, /device:TPU:64, one launch (start us, length us, event | category | flops | bytes accessed | tf_op | source)
XLA Modules:
  0.0 127.6 jit_solution(17341444791689365559)
XLA Ops:
  0.6 7.2 %shard_map.109 = (bf16[64,1408]{1,0:T(8,128)(2,1)}, bf16[64,1408]{1,0:T(8,128)(2,1)}, bf16[64,1408]{1,0:T(8,128)(2,1)}, bf16[64,1408]{1,0:T(8,128)(2,1)}) custom-call(s32[3]{0:T(128)} %pad_add_fusion.place_ref.facts_ref, s32[1,2]{1,0:T(1,128)} %grid_ref.1, bf16[256,1408]{1,0:T(8,128)(2,1)} %bitcast.36, bf16[3,352,1408]{2,1,0:T(8,128)(2,1)} %bitcast.40, ...), custom_call_target="tpu_custom_call" | custom-call | tf_op jit(solution)/shard_map/pallas_call | solution.py:298
  7.8 1.6 %collective-permute-start = (bf16[64,1408]{1,0:T(8,128)(2,1)}, bf16[64,1408]{1,0:T(8,128)(2,1)S(1)}, u32[]{:S(2)}, u32[]{:S(2)}) collective-permute-start(bf16[64,1408]{1,0:T(8,128)(2,1)} %get-tuple-element.20), channel_id=1, source_target_pairs={{0,1},{1,2},{2,3},{3,0},{4,5},{5,6},{6,7},{7,4},{8,9},{9,10},{10,1... | collective-permute-start | bytes 540680 | tf_op jit(solution)/shard_map/ppermute | solution.py:34
  9.3 2.7 %collective-permute-start.1 = (bf16[64,1408]{1,0:T(8,128)(2,1)}, bf16[64,1408]{1,0:T(8,128)(2,1)S(1)}, u32[]{:S(2)}, u32[]{:S(2)}) collective-permute-start(bf16[64,1408]{1,0:T(8,128)(2,1)} %get-tuple-element.21), channel_id=1, source_target_pairs={{0,2},{1,3},{2,0},{3,1},{4,6},{5,7},{6,4},{7,5},{8,10},{9,11},{10,... | collective-permute-start | bytes 540680 | tf_op jit(solution)/shard_map/ppermute | solution.py:34
  18.5 1.6 %slice_bitcast_fusion = (bf16[704,1408]{1,0:T(8,128)(2,1)S(1)}, bf16[704,1408]{1,0:T(8,128)(2,1)}) fusion(bf16[1,1408,1408]{2,1,0:T(8,128)(2,1)S(1)} %copy-done.7), kind=kLoop, calls=%fused_computation | loop fusion | bytes 7929856 | tf_op jit(solution)/shard_map/squeeze | solution.py:315
  21.6 1.5 %copy-done = bf16[704,1408]{1,0:T(8,128)(2,1)S(1)} copy-done((bf16[704,1408]{1,0:T(8,128)(2,1)S(1)}, bf16[704,1408]{1,0:T(8,128)(2,1)}, u32[]{:S(2)}) %copy-start) | copy-done | bytes 1982488
  23.1 1.6 %shard_map.111 = bf16[4,64,1536]{2,1,0:T(8,128)(2,1)S(1)} custom-call(s32[6]{0:T(128)S(1)} %pad_add_fusion.1.facts_ref, f32[64,1408]{1,0:T(8,128)S(1)} %shard_map.110.own_ref, bf16[64,1408]{1,0:T(8,128)(2,1)S(1)} %collective-permute-done.s1_ref, bf16[64,1408]{1,0:T(8,128)(2,1)S(1)} %collective-permute-done.1.s2_ref, ...), custom_call_target="tpu_custom_call" | custom-call | tf_op jit(solution)/shard_map/pallas_call | solution.py:319
  24.7 18.9 %all_to_all.20 = bf16[16,16,1536]{2,1,0:T(8,128)(2,1)S(1)} all-to-all(bf16[16,16,1536]{2,1,0:T(8,128)(2,1)S(1)} %bitcast.33), channel_id=1, replica_groups=mesh['z'=8,'y'=4,'c'=2,'t'=4] {'y','t'}, dimensions={0} | all-to-all | bytes 1572864 | tf_op jit(solution)/shard_map/all_to_all | solution.py:323
  45.3 1.7 %shard_map.113 = bf16[8,16,1536]{2,1,0:T(8,128)(2,1)} custom-call(s32[3]{0:T(128)S(1)} %copy-done.4, bf16[4,16,1536]{2,1,0:T(8,128)(2,1)S(1)} %shard_map.112.mine_ref, bf16[4,16,1536]{2,1,0:T(8,128)(2,1)S(1)} %collective-permute-done.3.other_ref), custom_call_target="tpu_custom_call" | custom-call | tf_op jit(solution)/shard_map/pallas_call | solution.py:326
  47.0 8.1 %all-to-all-start.1 = ((bf16[8,16,1536]{2,1,0:T(8,128)(2,1)}), bf16[8,16,1536]{2,1,0:T(8,128)(2,1)}, u32[]{:S(2)}, u32[]{:S(2)}) async-start(bf16[8,16,1536]{2,1,0:T(8,128)(2,1)} %shard_map.113), calls=%async_computation.1 | async-start | bytes 786432 | tf_op jit(solution)/shard_map/all_to_all | solution.py:333
  55.2 1.9 %constant_dynamic-slice_fusion = bf16[176,1408]{1,0:T(8,128)(2,1)} fusion(bf16[352,1408]{1,0:T(8,128)(2,1)} %w0_ref, s32[]{:T(128)S(6)} %select_n.55), kind=kLoop, calls=%fused_computation.6 | loop fusion | bytes 991236 | tf_op jit(solution)/shard_map/dynamic_slice | solution.py:329
  57.6 1.7 %collective-permute-start.8 = (bf16[128,352]{0,1:T(8,128)(2,1)}, bf16[128,352]{0,1:T(8,128)(2,1)S(1)}, u32[]{:S(2)}, u32[]{:S(2)}) collective-permute-start(bf16[128,352]{0,1:T(8,128)(2,1)} %param.18), channel_id=1, source_target_pairs={{0,2},{1,3},{2,0},{3,1},{4,6},{5,7},{6,4},{7,5},{8,10},{9,11},{10,... | collective-permute-start | bytes 270344 | tf_op jit(solution)/shard_map/ppermute | solution.py:34
  61.3 2.6 %collective-permute-start.17 = (bf16[176,1408]{1,0:T(8,128)(2,1)}, bf16[176,1408]{1,0:T(8,128)(2,1)}, u32[]{:S(2)}, u32[]{:S(2)}) collective-permute-start(bf16[176,1408]{1,0:T(8,128)(2,1)} %constant_dynamic-slice_fusion), channel_id=1, source_target_pairs={{0,3},{1,0},{2,1},{3,2},{4,7},{5,4},{6,5},{7,6},{8,11},{9,8},{10,9... | collective-permute-start | bytes 1486856 | tf_op jit(solution)/shard_map/ppermute | solution.py:34
  65.0 1.9 %all-to-all-done.1 = bf16[8,16,1536]{2,1,0:T(8,128)(2,1)} async-done(((bf16[8,16,1536]{2,1,0:T(8,128)(2,1)}), bf16[8,16,1536]{2,1,0:T(8,128)(2,1)}, u32[]{:S(2)}, u32[]{:S(2)}) %all-to-all-start.1) | async-done | bytes 393248 | tf_op jit(solution)/shard_map/all_to_all | solution.py:333
  68.8 1.7 %collective-permute-start.5 = (bf16[16,1536]{1,0:T(8,128)(2,1)S(1)}, bf16[16,1536]{1,0:T(8,128)(2,1)S(1)}, u32[]{:S(2)}, u32[]{:S(2)}) collective-permute-start(bf16[16,1536]{1,0:T(8,128)(2,1)S(1)} %reduce_sum.12.r0_ref), channel_id=1, source_target_pairs={{0,2},{1,3},{2,0},{3,1},{4,6},{5,7},{6,4},{7,5},{8,10},{9,11},{10,... | collective-permute-start | bytes 147464 | tf_op jit(solution)/shard_map/ppermute | solution.py:34
  74.6 2.6 %collective-permute-done.4.r1_ref = bf16[16,1536]{1,0:T(8,128)(2,1)S(1)} collective-permute-done((bf16[16,1536]{1,0:T(8,128)(2,1)S(1)}, bf16[16,1536]{1,0:T(8,128)(2,1)S(1)}, u32[]{:S(2)}, u32[]{:S(2)}) %collective-permute-start.4) | collective-permute-done | bytes 49184 | tf_op jit(solution)/shard_map/ppermute | solution.py:34
  77.8 2.4 %shard_map.114 = bf16[4,3,88,128]{3,2,1,0:T(8,128)(2,1)S(1)} custom-call(s32[3]{0:T(128)S(1)} %copy-done.4, bf16[16,1536]{1,0:T(8,128)(2,1)S(1)} %reduce_sum.12.r0_ref, bf16[16,1536]{1,0:T(8,128)(2,1)S(1)} %collective-permute-done.4.r1_ref, bf16[16,1536]{1,0:T(8,128)(2,1)S(1)} %collective-permute-done.5.r2_ref, ...), custom_call_target="tpu_custom_call" | custom-call | tf_op jit(solution)/shard_map/pallas_call | solution.py:340
  81.2 9.1 %all_to_all.21.own_ref = bf16[4,3,88,128]{3,2,1,0:T(8,128)(2,1)S(1)} all-to-all(bf16[4,3,88,128]{3,2,1,0:T(8,128)(2,1)S(1)} %shard_map.114), channel_id=1, replica_groups=mesh['z'=8,'y'=4,'c'=2,'t'=4] {'y'}, dimensions={0} | all-to-all | bytes 540672 | tf_op jit(solution)/shard_map/all_to_all | solution.py:347
  90.4 3.4 %collective-permute-start.10 = (bf16[4,2,88,128]{3,2,1,0:T(8,128)(2,1)S(1)}, bf16[4,2,88,128]{3,2,1,0:T(8,128)(2,1)S(1)}, u32[]{:S(2)}, u32[]{:S(2)}) collective-permute-start(bf16[4,2,88,128]{3,2,1,0:T(8,128)(2,1)S(1)} %slice.20), channel_id=1, source_target_pairs={{0,32},{32,64},{64,96},{96,128},{128,160},{160,192},{192,224},{1,3... | collective-permute-start | bytes 540680 | tf_op jit(solution)/shard_map/ppermute | solution.py:29
  93.7 4.6 %collective-permute-start.11 = (bf16[4,2,88,128]{3,2,1,0:T(8,128)(2,1)S(1)}, bf16[4,2,88,128]{3,2,1,0:T(8,128)(2,1)S(1)}, u32[]{:S(2)}, u32[]{:S(2)}) collective-permute-start(bf16[4,2,88,128]{3,2,1,0:T(8,128)(2,1)S(1)} %slice.20), channel_id=1, source_target_pairs={{0,64},{32,96},{64,128},{96,160},{128,192},{160,224},{1,65},{33,97... | collective-permute-start | bytes 540680 | tf_op jit(solution)/shard_map/ppermute | solution.py:29
  99.5 5.3 %collective-permute-done.11.far_ref = bf16[4,2,88,128]{3,2,1,0:T(8,128)(2,1)S(1)} collective-permute-done((bf16[4,2,88,128]{3,2,1,0:T(8,128)(2,1)S(1)}, bf16[4,2,88,128]{3,2,1,0:T(8,128)(2,1)S(1)}, u32[]{:S(2)}, u32[]{:S(2)}) %collective-permute-start.11) | collective-permute-done | bytes 180256 | tf_op jit(solution)/shard_map/ppermute | solution.py:29
  106.4 4.4 %shard_map.115 = bf16[4,4,88,128]{3,2,1,0:T(8,128)(2,1)} custom-call(s32[3]{0:T(128)S(1)} %copy-done.4, s32[16]{0:T(128)S(1)} %copy-done.5, bf16[4,3,88,128]{3,2,1,0:T(8,128)(2,1)S(1)} %all_to_all.21.own_ref, bf16[4,2,88,128]{3,2,1,0:T(8,128)(2,1)S(1)} %collective-permute-done.10.near_ref, bf16[4,2,88,128]{3,2,1,0:T(8,128)(2,1)S(1)} %collective-permute-done.11.far_ref, ...), custom_call_target="tpu_custom_call" | custom-call | tf_op jit(solution)/shard_map/pallas_call | solution.py:355
  110.8 3.5 %all-to-all-start.3 = ((bf16[16,88,128]{2,1,0:T(8,128)(2,1)}), bf16[16,88,128]{2,1,0:T(8,128)(2,1)S(1)}, u32[]{:S(2)}, u32[]{:S(2)}) async-start(bf16[16,88,128]{2,1,0:T(8,128)(2,1)} %bitcast.20), calls=%async_computation.3 | async-start | bytes 720896 | tf_op jit(solution)/shard_map/all_to_all | solution.py:362
  116.8 7.6 %all-to-all-done.3 = bf16[16,88,128]{2,1,0:T(8,128)(2,1)S(1)} async-done(((bf16[16,88,128]{2,1,0:T(8,128)(2,1)}), bf16[16,88,128]{2,1,0:T(8,128)(2,1)S(1)}, u32[]{:S(2)}, u32[]{:S(2)}) %all-to-all-start.3) | async-done | bytes 360480 | tf_op jit(solution)/shard_map/all_to_all | solution.py:362
  124.4 3.3 %shard_map.117 = bf16[128,1408]{1,0:T(8,128)(2,1)} custom-call(s32[3]{0:T(128)S(1)} %copy-done.4, bf16[4,2,176,128]{3,2,1,0:T(8,128)(2,1)S(1)} %bitcast.35, bf16[352,1408]{1,0:T(8,128)(2,1)S(1)} %copy-done.2, bf16[176,1408]{1,0:T(8,128)(2,1)S(1)} %collective-permute-done.15.m2_ref, bf16[176,1408]{1,0:T(8,128)(2,1)} %collective-permute-done.16.m1_ref, ...), custom_call_target="tpu_custom_call" | custom-call | tf_op jit(solution)/shard_map/pallas_call | solution.py:363
  (69 shorter events, 25.2 us)
Async XLA Ops:
  7.8 13.8 %collective-permute-start = (bf16[64,1408]{1,0:T(8,128)(2,1)}, bf16[64,1408]{1,0:T(8,128)(2,1)S(1)}, u32[]{:S(2)}, u32[]{:S(2)}) collective-permute-start(bf16[64,1408]{1,0:T(8,128)(2,1)} %get-tuple-element.20), channel_id=1, source_target_pairs={{0,1},{1,2},{2,3},{3,0},{4,5},{5,6},{6,7},{7,4},{8,9},{9,10},{10,1... | collective-permute-start | bytes 540680 | tf_op jit(solution)/shard_map/ppermute | solution.py:34
  9.3 12.2 %collective-permute-start.1 = (bf16[64,1408]{1,0:T(8,128)(2,1)}, bf16[64,1408]{1,0:T(8,128)(2,1)S(1)}, u32[]{:S(2)}, u32[]{:S(2)}) collective-permute-start(bf16[64,1408]{1,0:T(8,128)(2,1)} %get-tuple-element.21), channel_id=1, source_target_pairs={{0,2},{1,3},{2,0},{3,1},{4,6},{5,7},{6,4},{7,5},{8,10},{9,11},{10,... | collective-permute-start | bytes 540680 | tf_op jit(solution)/shard_map/ppermute | solution.py:34
  12.1 9.5 %collective-permute-start.2 = (bf16[64,1408]{1,0:T(8,128)(2,1)}, bf16[64,1408]{1,0:T(8,128)(2,1)S(1)}, u32[]{:S(2)}, u32[]{:S(2)}) collective-permute-start(bf16[64,1408]{1,0:T(8,128)(2,1)} %get-tuple-element.22), channel_id=1, source_target_pairs={{0,3},{1,0},{2,1},{3,2},{4,7},{5,4},{6,5},{7,6},{8,11},{9,8},{10,9... | collective-permute-start | bytes 540680 | tf_op jit(solution)/shard_map/ppermute | solution.py:34
  43.8 1.5 %collective-permute-start.3 = (bf16[4,16,1536]{2,1,0:T(8,128)(2,1)S(1)}, bf16[4,16,1536]{2,1,0:T(8,128)(2,1)S(1)}, u32[]{:S(2)}, u32[]{:S(2)}) collective-permute-start(bf16[4,16,1536]{2,1,0:T(8,128)(2,1)S(1)} %shard_map.112.mine_ref), channel_id=1, source_target_pairs={{0,4},{4,0},{1,5},{5,1},{2,6},{6,2},{3,7},{7,3},{8,12},{12,8},{9,1... | collective-permute-start | bytes 589832 | tf_op jit(solution)/shard_map/ppermute | solution.py:34
  47.0 19.9 %all-to-all-start.1 = ((bf16[8,16,1536]{2,1,0:T(8,128)(2,1)}), bf16[8,16,1536]{2,1,0:T(8,128)(2,1)}, u32[]{:S(2)}, u32[]{:S(2)}) async-start(bf16[8,16,1536]{2,1,0:T(8,128)(2,1)} %shard_map.113), calls=%async_computation.1 | async-start | bytes 786432 | tf_op jit(solution)/shard_map/all_to_all | solution.py:333
  57.0 7.9 %collective-permute-start.7 = (bf16[128,352]{0,1:T(8,128)(2,1)}, bf16[128,352]{0,1:T(8,128)(2,1)S(1)}, u32[]{:S(2)}, u32[]{:S(2)}) collective-permute-start(bf16[128,352]{0,1:T(8,128)(2,1)} %param.18), channel_id=1, source_target_pairs={{0,1},{1,2},{2,3},{3,0},{4,5},{5,6},{6,7},{7,4},{8,9},{9,10},{10,1... | collective-permute-start | bytes 270344 | tf_op jit(solution)/shard_map/ppermute | solution.py:34
  57.6 7.3 %collective-permute-start.8 = (bf16[128,352]{0,1:T(8,128)(2,1)}, bf16[128,352]{0,1:T(8,128)(2,1)S(1)}, u32[]{:S(2)}, u32[]{:S(2)}) collective-permute-start(bf16[128,352]{0,1:T(8,128)(2,1)} %param.18), channel_id=1, source_target_pairs={{0,2},{1,3},{2,0},{3,1},{4,6},{5,7},{6,4},{7,5},{8,10},{9,11},{10,... | collective-permute-start | bytes 270344 | tf_op jit(solution)/shard_map/ppermute | solution.py:34
  59.3 11.2 %collective-permute-start.9 = (bf16[128,352]{0,1:T(8,128)(2,1)}, bf16[128,352]{0,1:T(8,128)(2,1)}, u32[]{:S(2)}, u32[]{:S(2)}) collective-permute-start(bf16[128,352]{0,1:T(8,128)(2,1)} %param.18), channel_id=1, source_target_pairs={{0,3},{1,0},{2,1},{3,2},{4,7},{5,4},{6,5},{7,6},{8,11},{9,8},{10,9... | collective-permute-start | bytes 270344 | tf_op jit(solution)/shard_map/ppermute | solution.py:34
  60.6 37.7 %collective-permute-start.16 = (bf16[176,1408]{1,0:T(8,128)(2,1)}, bf16[176,1408]{1,0:T(8,128)(2,1)}, u32[]{:S(2)}, u32[]{:S(2)}) collective-permute-start(bf16[176,1408]{1,0:T(8,128)(2,1)} %constant_dynamic-slice_fusion), channel_id=1, source_target_pairs={{0,1},{1,2},{2,3},{3,0},{4,5},{5,6},{6,7},{7,4},{8,9},{9,10},{10,1... | collective-permute-start | bytes 1486856 | tf_op jit(solution)/shard_map/ppermute | solution.py:34
  61.3 43.5 %collective-permute-start.17 = (bf16[176,1408]{1,0:T(8,128)(2,1)}, bf16[176,1408]{1,0:T(8,128)(2,1)}, u32[]{:S(2)}, u32[]{:S(2)}) collective-permute-start(bf16[176,1408]{1,0:T(8,128)(2,1)} %constant_dynamic-slice_fusion), channel_id=1, source_target_pairs={{0,3},{1,0},{2,1},{3,2},{4,7},{5,4},{6,5},{7,6},{8,11},{9,8},{10,9... | collective-permute-start | bytes 1486856 | tf_op jit(solution)/shard_map/ppermute | solution.py:34
  67.9 9.3 %collective-permute-start.4 = (bf16[16,1536]{1,0:T(8,128)(2,1)S(1)}, bf16[16,1536]{1,0:T(8,128)(2,1)S(1)}, u32[]{:S(2)}, u32[]{:S(2)}) collective-permute-start(bf16[16,1536]{1,0:T(8,128)(2,1)S(1)} %reduce_sum.12.r0_ref), channel_id=1, source_target_pairs={{0,1},{1,2},{2,3},{3,0},{4,5},{5,6},{6,7},{7,4},{8,9},{9,10},{10,1... | collective-permute-start | bytes 147464 | tf_op jit(solution)/shard_map/ppermute | solution.py:34
  68.8 8.5 %collective-permute-start.5 = (bf16[16,1536]{1,0:T(8,128)(2,1)S(1)}, bf16[16,1536]{1,0:T(8,128)(2,1)S(1)}, u32[]{:S(2)}, u32[]{:S(2)}) collective-permute-start(bf16[16,1536]{1,0:T(8,128)(2,1)S(1)} %reduce_sum.12.r0_ref), channel_id=1, source_target_pairs={{0,2},{1,3},{2,0},{3,1},{4,6},{5,7},{6,4},{7,5},{8,10},{9,11},{10,... | collective-permute-start | bytes 147464 | tf_op jit(solution)/shard_map/ppermute | solution.py:34
  70.4 7.4 %collective-permute-start.6 = (bf16[16,1536]{1,0:T(8,128)(2,1)S(1)}, bf16[16,1536]{1,0:T(8,128)(2,1)S(1)}, u32[]{:S(2)}, u32[]{:S(2)}) collective-permute-start(bf16[16,1536]{1,0:T(8,128)(2,1)S(1)} %reduce_sum.12.r0_ref), channel_id=1, source_target_pairs={{0,3},{1,0},{2,1},{3,2},{4,7},{5,4},{6,5},{7,6},{8,11},{9,8},{10,9... | collective-permute-start | bytes 147464 | tf_op jit(solution)/shard_map/ppermute | solution.py:34
  80.2 44.2 %copy-start.2 = (bf16[352,1408]{1,0:T(8,128)(2,1)S(1)}, bf16[352,1408]{1,0:T(8,128)(2,1)}, u32[]{:S(2)}) copy-start(bf16[352,1408]{1,0:T(8,128)(2,1)} %w0_ref) | copy-start | bytes 2973700
  80.2 25.2 %collective-permute-start.15 = (bf16[176,1408]{1,0:T(8,128)(2,1)}, bf16[176,1408]{1,0:T(8,128)(2,1)S(1)}, u32[]{:S(2)}, u32[]{:S(2)}) collective-permute-start(bf16[176,1408]{1,0:T(8,128)(2,1)} %constant_dynamic-slice_fusion), channel_id=1, source_target_pairs={{0,2},{1,3},{2,0},{3,1},{4,6},{5,7},{6,4},{7,5},{8,10},{9,11},{10,... | collective-permute-start | bytes 1486856 | tf_op jit(solution)/shard_map/ppermute | solution.py:34
  90.4 9.1 %collective-permute-start.10 = (bf16[4,2,88,128]{3,2,1,0:T(8,128)(2,1)S(1)}, bf16[4,2,88,128]{3,2,1,0:T(8,128)(2,1)S(1)}, u32[]{:S(2)}, u32[]{:S(2)}) collective-permute-start(bf16[4,2,88,128]{3,2,1,0:T(8,128)(2,1)S(1)} %slice.20), channel_id=1, source_target_pairs={{0,32},{32,64},{64,96},{96,128},{128,160},{160,192},{192,224},{1,3... | collective-permute-start | bytes 540680 | tf_op jit(solution)/shard_map/ppermute | solution.py:29
  93.7 11.1 %collective-permute-start.11 = (bf16[4,2,88,128]{3,2,1,0:T(8,128)(2,1)S(1)}, bf16[4,2,88,128]{3,2,1,0:T(8,128)(2,1)S(1)}, u32[]{:S(2)}, u32[]{:S(2)}) collective-permute-start(bf16[4,2,88,128]{3,2,1,0:T(8,128)(2,1)S(1)} %slice.20), channel_id=1, source_target_pairs={{0,64},{32,96},{64,128},{96,160},{128,192},{160,224},{1,65},{33,97... | collective-permute-start | bytes 540680 | tf_op jit(solution)/shard_map/ppermute | solution.py:29
  98.3 7.0 %collective-permute-start.12 = (bf16[4,2,88,128]{3,2,1,0:T(8,128)(2,1)S(1)}, bf16[4,2,88,128]{3,2,1,0:T(8,128)(2,1)S(1)}, u32[]{:S(2)}, u32[]{:S(2)}) collective-permute-start(bf16[4,2,88,128]{3,2,1,0:T(8,128)(2,1)S(1)} %slice.20), channel_id=1, source_target_pairs={{0,4},{4,0},{1,5},{5,1},{2,6},{6,2},{3,7},{7,3},{8,12},{12,8},{9,1... | collective-permute-start | bytes 540680 | tf_op jit(solution)/shard_map/ppermute | solution.py:34
  99.5 6.3 %collective-permute-start.13 = (bf16[4,2,88,128]{3,2,1,0:T(8,128)(2,1)S(1)}, bf16[4,2,88,128]{3,2,1,0:T(8,128)(2,1)S(1)}, u32[]{:S(2)}, u32[]{:S(2)}) collective-permute-start(bf16[4,2,88,128]{3,2,1,0:T(8,128)(2,1)S(1)} %collective-permute-done.10.near_ref), channel_id=1, source_target_pairs={{0,4},{4,0},{1,5},{5,1},{2,6},{6,2},{3,7},{7,3},{8,12},{12,8},{9,1... | collective-permute-start | bytes 540680 | tf_op jit(solution)/shard_map/ppermute | solution.py:34
  104.8 1.6 %collective-permute-start.14 = (bf16[4,2,88,128]{3,2,1,0:T(8,128)(2,1)S(1)}, bf16[4,2,88,128]{3,2,1,0:T(8,128)(2,1)S(1)}, u32[]{:S(2)}, u32[]{:S(2)}) collective-permute-start(bf16[4,2,88,128]{3,2,1,0:T(8,128)(2,1)S(1)} %collective-permute-done.11.far_ref), channel_id=1, source_target_pairs={{0,4},{4,0},{1,5},{5,1},{2,6},{6,2},{3,7},{7,3},{8,12},{12,8},{9,1... | collective-permute-start | bytes 540680 | tf_op jit(solution)/shard_map/ppermute | solution.py:34
  104.8 11.9 %collective-permute-start.19 = (bf16[176,1408]{1,0:T(8,128)(2,1)}, bf16[176,1408]{1,0:T(8,128)(2,1)S(1)}, u32[]{:S(2)}, u32[]{:S(2)}) collective-permute-start(bf16[176,1408]{1,0:T(8,128)(2,1)} %collective-permute-done.16.m1_ref), channel_id=1, source_target_pairs={{0,4},{4,0},{1,5},{5,1},{2,6},{6,2},{3,7},{7,3},{8,12},{12,8},{9,1... | collective-permute-start | bytes 1486856 | tf_op jit(solution)/shard_map/ppermute | solution.py:34
  105.3 11.4 %collective-permute-start.20 = (bf16[176,1408]{1,0:T(8,128)(2,1)}, bf16[176,1408]{1,0:T(8,128)(2,1)}, u32[]{:S(2)}, u32[]{:S(2)}) collective-permute-start(bf16[176,1408]{1,0:T(8,128)(2,1)} %collective-permute-done.17.m3_ref), channel_id=1, source_target_pairs={{0,4},{4,0},{1,5},{5,1},{2,6},{6,2},{3,7},{7,3},{8,12},{12,8},{9,1... | collective-permute-start | bytes 1486856 | tf_op jit(solution)/shard_map/ppermute | solution.py:34
  105.4 19.0 %collective-permute-start.18 = (bf16[176,1408]{1,0:T(8,128)(2,1)S(1)}, bf16[176,1408]{1,0:T(8,128)(2,1)}, u32[]{:S(2)}, u32[]{:S(2)}) collective-permute-start(bf16[176,1408]{1,0:T(8,128)(2,1)S(1)} %collective-permute-done.15.m2_ref), channel_id=1, source_target_pairs={{0,4},{4,0},{1,5},{5,1},{2,6},{6,2},{3,7},{7,3},{8,12},{12,8},{9,1... | collective-permute-start | bytes 1486856 | tf_op jit(solution)/shard_map/ppermute | solution.py:34
  110.8 13.6 %all-to-all-start.3 = ((bf16[16,88,128]{2,1,0:T(8,128)(2,1)}), bf16[16,88,128]{2,1,0:T(8,128)(2,1)S(1)}, u32[]{:S(2)}, u32[]{:S(2)}) async-start(bf16[16,88,128]{2,1,0:T(8,128)(2,1)} %bitcast.20), calls=%async_computation.3 | async-start | bytes 720896 | tf_op jit(solution)/shard_map/all_to_all | solution.py:362
  (9 other events, 124.6 us)

commit v8 on v7

--- a/solution.py
+++ b/solution.py
@@ -21,7 +21,6 @@
 HBM = pltpu.HBM
 FACTS = 128
 STRIP = 256
-WINDOW = 18 * BLOCK
 
 
 def ahead(x, axis, by):
@@ -202,13 +201,30 @@
             heads_ref[head, part] = projected[head * HEAD : (head + 1) * HEAD].astype(BF)
 
 
-def attend_kernel(facts_ref, lengths_ref, own_ref, near_ref, far_ref,
-                  own2_ref, near2_ref, far2_ref, sent_ref, keys_ref, values_ref):
-    z, c = facts_ref[0], facts_ref[1]
-    for plane, (mine, other) in enumerate(
-        ((far_ref, far2_ref), (near_ref, near2_ref), (own_ref, own2_ref))
-    ):
-        skip = 1 if plane == 2 else 0
+def cut_kernel(place_ref, after_hbm, text_hbm, tokens_hbm, near_hbm, copy_hbm, done):
+    half = near_hbm.shape[0]
+    mine = text_hbm.at[pl.ds(pl.multiple_of(place_ref[1] * half, 16), half)]
+    copies = [
+        pltpu.make_async_copy(mine, near_hbm, done.at[0]),
+        pltpu.make_async_copy(tokens_hbm, copy_hbm, done.at[1]),
+    ]
+    for copy in copies:
+        copy.start()
+    for copy in copies:
+        copy.wait()
+
+
+def prompt_start(lengths_ref, position):
+    start = jnp.zeros(position.shape, I32)
+    end = jnp.int32(0)
+    for prompt in range(16):
+        end = end + lengths_ref[prompt]
+        start = jnp.where(end <= position, end, start)
+    return start
+
+
+def lay_keys(c, planes, keys_ref, values_ref):
+    for plane, (mine, other, skip) in enumerate(planes):
         for y in range(4):
             at = (plane * 8 + 2 * y) * BLOCK
             mine_at = pl.ds(pl.multiple_of(at + c * BLOCK, BLOCK), BLOCK)
@@ -216,38 +232,71 @@
             for part, store in ((0, keys_ref), (1, values_ref)):
                 store[:, mine_at] = mine[y, skip + part]
                 store[:, other_at] = other[y, part]
-    row = iota((BLOCK, 1), 0)
+
+
+def turned(column):
+    return jnp.transpose(jnp.broadcast_to(column, (BLOCK, BLOCK)))
+
+
+def weigh(strips, top, values_of):
+    total = jnp.zeros((BLOCK, STRIP), F32)
+    summed = jnp.zeros((HEAD, BLOCK), F32)
+    for first, scores in strips:
+        expons = jnp.exp2((scores - top) * SCALE2)
+        total = total + expons
+        summed = summed + dot(values_of(first), expons.astype(BF), (1, 1))
+    return jnp.sum(total, axis=1, keepdims=True), summed
+
+
+def near_kernel(place_ref, lengths_ref, own_ref, near_ref, own2_ref, near2_ref,
+                top_ref, total_ref, summed_ref, keys_ref, values_ref):
+    z, c = place_ref[0], place_ref[1]
+    planes = ((near_ref, near2_ref, 0), (own_ref, own2_ref, 1))
+    lay_keys(c, planes, keys_ref, values_ref)
     column = iota((BLOCK, STRIP), 1)
     for j in range(4):
-        base = (z - 2) * 1024 + j * 256
-        here = 2048 + c * BLOCK + row
-        start = jnp.zeros((BLOCK, 1), I32)
-        end = jnp.int32(0)
-        for prompt in range(16):
-            end = end + lengths_ref[prompt]
-            start = jnp.where(end <= here + base, end, start)
-        low = start - base
+        here = 1024 + j * 256 + c * BLOCK + iota((BLOCK, 1), 0)
+        base = (z - 1) * 1024
+        low = prompt_start(lengths_ref, here + base) - base
         query = own_ref[j, 0].T
         strips, top = [], None
-        for first in range(0, WINDOW, STRIP):
-            scores = dot(query, keys_ref[:, pl.ds(j * 256 + first, STRIP)], (1, 0))
+        for first in range(0, 1024 + (j + 1) * 256, STRIP):
+            scores = dot(query, keys_ref[:, first : first + STRIP], (1, 0))
             visible = column >= low - first
-            if first + STRIP > 2048:
+            if first >= 1024:
                 visible = visible & (column <= here - first)
             scores = jnp.where(visible, scores, -jnp.inf)
             top = scores if top is None else jnp.maximum(top, scores)
-            strips.append(scores)
+            strips.append((first, scores))
         top = jnp.max(top, axis=1, keepdims=True)
-        total = jnp.zeros((BLOCK, STRIP), F32)
-        summed = jnp.zeros((HEAD, BLOCK), F32)
-        for strip, scores in enumerate(strips):
-            expons = jnp.exp2((scores - top) * SCALE2)
-            total = total + expons
-            values = values_ref[:, pl.ds(j * 256 + strip * STRIP, STRIP)]
-            summed = summed + dot(values, expons.astype(BF), (1, 1))
-        total = jnp.sum(total, axis=1, keepdims=True)
-        total = jnp.transpose(jnp.broadcast_to(total, (BLOCK, BLOCK)))
-        context = (summed / total[:HEAD]).astype(BF)
+        total, summed = weigh(strips, top, lambda first: values_ref[:, first : first + STRIP])
+        top_ref[j] = jnp.broadcast_to(top, (BLOCK, BLOCK))
+        total_ref[j] = turned(total)[:8]
+        summed_ref[j] = summed
+
+
+def far_kernel(place_ref, lengths_ref, own_ref, far_ref, far2_ref,
+               top_ref, total_ref, summed_ref, sent_ref, keys_ref, values_ref):
+    z, c = place_ref[0], place_ref[1]
+    lay_keys(c, ((far_ref, far2_ref, 0),), keys_ref, values_ref)
+    column = iota((BLOCK, STRIP), 1)
+    for j in range(4):
+        here = 2048 + j * 256 + c * BLOCK + iota((BLOCK, 1), 0)
+        base = (z - 2) * 1024
+        low = prompt_start(lengths_ref, here + base) - base
+        query = own_ref[j, 0].T
+        old_top = top_ref[j][:, :1]
+        strips, top = [], None
+        for first in range(j * 256, 1024, STRIP):
+            scores = dot(query, keys_ref[:, first : first + STRIP], (1, 0))
+            scores = jnp.where(column >= low - first, scores, -jnp.inf)
+            top = scores if top is None else jnp.maximum(top, scores)
+            strips.append((first, scores))
+        top = jnp.maximum(jnp.max(top, axis=1, keepdims=True), old_top)
+        total, summed = weigh(strips, top, lambda first: values_ref[:, first : first + STRIP])
+        factor = turned(jnp.exp2((old_top - top) * SCALE2))
+        total = total_ref[j][:1] * factor[:1] + turned(total)[:1]
+        context = ((summed_ref[j] * factor[:HEAD] + summed) / total).astype(BF)
         for t in range(4):
             sent_ref[t, j] = context
 
@@ -324,41 +373,52 @@
     got = call(sum_kernel, shape((4, 16, wide)), [VMEM])(got.reshape(4, 4, 16, wide))
     other = around(got, "c", 1)
     routed = call(select_kernel, shape((8, 16, wide)), [SMEM, VMEM, VMEM])(place, got, other)
-    routed, text_out = lax.optimization_barrier((routed, text_out))
     half = local_width // 2
-    near_half = lax.dynamic_slice_in_dim(text_out, c * half, half, 0)
-    near_half, tokens = lax.optimization_barrier((near_half, tokens))
-    halves = [None] + [around(near_half, "t", by) for by in (1, 3)]
-    pieces = [tokens] + [around(tokens, "t", by) for by in range(1, 4)]
+    near_half, columns = pl.pallas_call(
+        cut_kernel,
+        out_shape=[shape((half, width)), shape((local_width, BLOCK))],
+        in_specs=[pl.BlockSpec(memory_space=SMEM)] + [pl.BlockSpec(memory_space=HBM)] * 3,
+        out_specs=[pl.BlockSpec(memory_space=HBM)] * 2,
+        scratch_shapes=[pltpu.SemaphoreType.DMA((2,))],
+    )(place, routed, text_out, tokens.T)
+    near_halves = [around(near_half, "t", by) for by in (1, 3)]
+    pieces = [columns] + [around(columns, "t", by) for by in range(1, 4)]
     got = lax.all_to_all(routed, "z", 0, 0, tiled=True)
     got = jnp.sum(got.astype(F32), axis=0).astype(BF)
     rows = [got] + [around(got, "t", by) for by in range(1, 4)]
-    own_tokens = jnp.zeros((4, BLOCK, local_width), BF)
+    own_tokens = jnp.zeros((4, local_width, BLOCK), BF)
     for by, piece in enumerate(pieces):
         own_tokens = lax.dynamic_update_index_in_dim(own_tokens, piece, (t - by) % 4, 0)
-    own_tokens = own_tokens.transpose(1, 0, 2).reshape(BLOCK, width)
+    own_tokens = own_tokens.reshape(width, BLOCK).T
     heads = call(
         project_kernel,
         shape((4, 3, HEAD, BLOCK)),
         [SMEM] + [VMEM] * 6,
     )(place, *rows, own_tokens, text_qkv.transpose(1, 2, 0))
     heads, late_tokens, near_half = lax.optimization_barrier((heads, own_tokens, near_half))
-    halves[0] = around(near_half, "t", 2)
+    halves = [around(near_half, "t", 2)] + near_halves
     mine = lax.all_to_all(heads, "y", 0, 0, tiled=True)
     prompt_in = call(place_kernel, shape((BLOCK, width)), [SMEM] + [VMEM] * 5)(
         place, *rows, late_tokens
     )
     pair = mine[:, 1:]
     near, far = ahead(pair, "z", 1), ahead(pair, "z", 2)
-    others = [around(x, "c", 1) for x in (pair, near, far)]
+    own2, near2, far2 = (around(x, "c", 1) for x in (pair, near, far))
     halves = halves + [around(x, "c", 1) for x in halves]
+    parts = call(
+        near_kernel,
+        [shape((4, BLOCK, BLOCK), F32), shape((4, 8, BLOCK), F32), shape((4, HEAD, BLOCK), F32)],
+        [SMEM, SMEM] + [VMEM] * 4,
+        [VMEM((HEAD, 2048), BF)] * 2,
+        limit=16,
+    )(place, prompt_lengths, mine, near, own2, near2)
     sent = call(
-        attend_kernel,
+        far_kernel,
         shape((4, 4, HEAD, BLOCK)),
         [SMEM, SMEM] + [VMEM] * 6,
-        [pltpu.VMEM((HEAD, 24 * BLOCK), BF)] * 2,
+        [VMEM((HEAD, 1024), BF)] * 2,
         limit=16,
-    )(place, prompt_lengths, mine, near, far, *others)
+    )(place, prompt_lengths, mine, far, far2, *parts)
     context = lax.all_to_all(sent.reshape(16, HEAD, BLOCK), ("t", "y"), 0, 0, tiled=True)
     return call(output_kernel, shape((BLOCK, width)), [SMEM] + [VMEM] * 9)(
         place, context.reshape(4, 2, half, BLOCK), text_out, *halves, prompt_in

time: 129 us -> 150 us (1.16)
  Pallas kernels: 22.6 us -> 44.1 us
  local copies, waits for them, and re-layouts: 14.3 us -> 10.3 us
  waiting for transfers between devices: 21.1 us -> 24.4 us
    pallas_call x1 -> x3, Pallas kernels: 4.39 us -> 25.9 us  [the longest x1 19.5 us: local(): pl.pallas_call(cut_kernel, out_shape=[shape((half, width)), shape((local_...]
    ppermute x19, waiting for transfers between devices: 5.2 us -> 9.31 us  [around(): return lax.ppermute(x, axis, [(i, (i + by) % count) for i in range(count)])]
    all_to_all x1, waiting for transfers between devices: 1.94 us -> 0.01 us  [local(): got = lax.all_to_all(routed, 'z', 0, 0, tiled=True)]
    dynamic_slice x1 -> x0, local copies, waits for them, and re-layouts: 1.87 us -> none  [local(): near_half = lax.dynamic_slice_in_dim(text_out, c * half, half, 0)]
  transfers between devices with their start and end apart: 23 -> 23, of which waited for: 9 -> 7; matrix products, arithmetic and copies ran while one was open for 9% -> 3% of each run, Pallas kernels for 7% -> 20%
where the time goes in v8:
time: 150 us; the launch traced here: 149 us
  Pallas kernels  44.1 us (29%)
  starting transfers between devices  39.2 us (26%)
  blocking collectives  28.2 us (19%)
  waiting for transfers between devices  24.4 us (16%)
  local copies, waits for them, and re-layouts  10.3 us (7%)
  between operations  1.6 us (1%)
    ppermute x19, starting transfers between devices, around(): return lax.ppermute(x, axis, [(i, (i + by) % count) for i in range(count)])  19.6 us
    pallas_call x1, Pallas kernels, local(): pl.pallas_call(cut_kernel, out_shape=[shape((half, width)), shape((local_...  19.5 us
    all_to_all x1, blocking collectives, local(): lax.all_to_all(routed.reshape(16, 16, wide), ('y', 't'), 0, 0, tiled=True)  19.1 us
    ppermute x19, waiting for transfers between devices, around(): return lax.ppermute(x, axis, [(i, (i + by) % count) for i in range(count)])  9.31 us
    all_to_all x1, blocking collectives, local(): mine = lax.all_to_all(heads, 'y', 0, 0, tiled=True)  9.1 us
    all_to_all x1, waiting for transfers between devices, local(): lax.all_to_all(sent.reshape(16, HEAD, BLOCK), ('t', 'y'), 0, 0, tiled=True)  8.74 us
    all_to_all x1, starting transfers between devices, local(): got = lax.all_to_all(routed, 'z', 0, 0, tiled=True)  8.12 us
    ppermute x2, starting transfers between devices, ahead(): return lax.ppermute(x, axis, [(i, i + by) for i in range(count - by)])  7.95 us
  transfers between devices with their start and end apart: 23, of which 7 were waited for; matrix products, arithmetic and copies ran while one was open for 3% of the time, Pallas kernels for 20%

profile of v8, /device:TPU:64, one launch (start us, length us, event | category | flops | bytes accessed | tf_op | source)
XLA Modules:
  0.0 148.6 jit_solution(68777273020429975)
XLA Ops:
  0.6 7.2 %shard_map.109 = (bf16[64,1408]{1,0:T(8,128)(2,1)}, bf16[64,1408]{1,0:T(8,128)(2,1)}, bf16[64,1408]{1,0:T(8,128)(2,1)}, bf16[64,1408]{1,0:T(8,128)(2,1)}) custom-call(s32[3]{0:T(128)} %pad_add_fusion.place_ref, s32[1,2]{1,0:T(1,128)} %grid_ref.1, bf16[256,1408]{1,0:T(8,128)(2,1)} %bitcast.38, bf16[3,352,1408]{2,1,0:T(8,128)(2,1)} %bitcast.40, ...), custom_call_target="tpu_custom_call" | custom-call | tf_op jit(solution)/shard_map/pallas_call | solution.py:347
  7.7 1.6 %collective-permute-start = (bf16[64,1408]{1,0:T(8,128)(2,1)}, bf16[64,1408]{1,0:T(8,128)(2,1)S(1)}, u32[]{:S(2)}, u32[]{:S(2)}) collective-permute-start(bf16[64,1408]{1,0:T(8,128)(2,1)} %get-tuple-element.21), channel_id=1, source_target_pairs={{0,1},{1,2},{2,3},{3,0},{4,5},{5,6},{6,7},{7,4},{8,9},{9,10},{10,1... | collective-permute-start | bytes 540680 | tf_op jit(solution)/shard_map/ppermute | solution.py:33
  9.3 2.7 %collective-permute-start.1 = (bf16[64,1408]{1,0:T(8,128)(2,1)}, bf16[64,1408]{1,0:T(8,128)(2,1)S(1)}, u32[]{:S(2)}, u32[]{:S(2)}) collective-permute-start(bf16[64,1408]{1,0:T(8,128)(2,1)} %get-tuple-element.22), channel_id=1, source_target_pairs={{0,2},{1,3},{2,0},{3,1},{4,6},{5,7},{6,4},{7,5},{8,10},{9,11},{10,... | collective-permute-start | bytes 540680 | tf_op jit(solution)/shard_map/ppermute | solution.py:33
  18.4 1.6 %slice_bitcast_fusion = (bf16[704,1408]{1,0:T(8,128)(2,1)S(1)}, bf16[704,1408]{1,0:T(8,128)(2,1)}) fusion(bf16[1,1408,1408]{2,1,0:T(8,128)(2,1)S(1)} %copy-done.8), kind=kLoop, calls=%fused_computation | loop fusion | bytes 7929856 | tf_op jit(solution)/shard_map/squeeze | solution.py:364
  22.9 1.6 %shard_map.111 = bf16[4,64,1536]{2,1,0:T(8,128)(2,1)S(1)} custom-call(s32[6]{0:T(128)S(1)} %pad_add_fusion.1.facts_ref, f32[64,1408]{1,0:T(8,128)S(1)} %shard_map.110.own_ref, bf16[64,1408]{1,0:T(8,128)(2,1)S(1)} %collective-permute-done.s1_ref, bf16[64,1408]{1,0:T(8,128)(2,1)S(1)} %collective-permute-done.1.s2_ref, ...), custom_call_target="tpu_custom_call" | custom-call | tf_op jit(solution)/shard_map/pallas_call | solution.py:368
  24.5 19.1 %all_to_all.20 = bf16[16,16,1536]{2,1,0:T(8,128)(2,1)S(1)} all-to-all(bf16[16,16,1536]{2,1,0:T(8,128)(2,1)S(1)} %bitcast.35), channel_id=1, replica_groups=mesh['z'=8,'y'=4,'c'=2,'t'=4] {'y','t'}, dimensions={0} | all-to-all | bytes 1572864 | tf_op jit(solution)/shard_map/all_to_all | solution.py:372
  45.3 1.7 %shard_map.113.after_hbm = bf16[8,16,1536]{2,1,0:T(8,128)(2,1)} custom-call(s32[3]{0:T(128)S(1)} %copy-done.4, bf16[4,16,1536]{2,1,0:T(8,128)(2,1)S(1)} %shard_map.112.mine_ref, bf16[4,16,1536]{2,1,0:T(8,128)(2,1)S(1)} %collective-permute-done.3.other_ref), custom_call_target="tpu_custom_call" | custom-call | tf_op jit(solution)/shard_map/pallas_call | solution.py:375
  47.0 8.1 %all-to-all-start.1 = ((bf16[8,16,1536]{2,1,0:T(8,128)(2,1)}), bf16[8,16,1536]{2,1,0:T(8,128)(2,1)S(1)}, u32[]{:S(2)}, u32[]{:S(2)}) async-start(bf16[8,16,1536]{2,1,0:T(8,128)(2,1)} %shard_map.113.after_hbm), calls=%async_computation.1 | async-start | bytes 786432 | tf_op jit(solution)/shard_map/all_to_all | solution.py:386
  55.1 19.5 %shard_map.114 = (bf16[176,1408]{1,0:T(8,128)(2,1)}, bf16[352,128]{1,0:T(8,128)(2,1)}) custom-call(s32[3]{0:T(128)} %pad_add_fusion.place_ref, bf16[8,16,1536]{2,1,0:T(8,128)(2,1)} %shard_map.113.after_hbm, bf16[352,1408]{1,0:T(8,128)(2,1)} %w0_ref.1, bf16[352,128]{1,0:T(8,128)(2,1)} %bitcast.42), custom_call_target="tpu_custom_call" | custom-call | tf_op jit(solution)/shard_map/pallas_call | solution.py:377
  75.3 1.7 %collective-permute-start.8 = (bf16[352,128]{1,0:T(8,128)(2,1)}, bf16[352,128]{1,0:T(8,128)(2,1)S(1)}, u32[]{:S(2)}, u32[]{:S(2)}) collective-permute-start(bf16[352,128]{1,0:T(8,128)(2,1)} %get-tuple-element.25), channel_id=1, source_target_pairs={{0,2},{1,3},{2,0},{3,1},{4,6},{5,7},{6,4},{7,5},{8,10},{9,11},{10,... | collective-permute-start | bytes 270344 | tf_op jit(solution)/shard_map/ppermute | solution.py:33
  79.0 2.6 %collective-permute-start.17 = (bf16[176,1408]{1,0:T(8,128)(2,1)}, bf16[176,1408]{1,0:T(8,128)(2,1)S(1)}, u32[]{:S(2)}, u32[]{:S(2)}) collective-permute-start(bf16[176,1408]{1,0:T(8,128)(2,1)} %get-tuple-element.31), channel_id=1, source_target_pairs={{0,3},{1,0},{2,1},{3,2},{4,7},{5,4},{6,5},{7,6},{8,11},{9,8},{10,9... | collective-permute-start | bytes 1486856 | tf_op jit(solution)/shard_map/ppermute | solution.py:33
  83.0 4.1 %collective-permute-start.5 = (bf16[16,1536]{1,0:T(8,128)(2,1)S(1)}, bf16[16,1536]{1,0:T(8,128)(2,1)S(1)}, u32[]{:S(2)}, u32[]{:S(2)}) collective-permute-start(bf16[16,1536]{1,0:T(8,128)(2,1)S(1)} %reduce_sum.12.r0_ref), channel_id=1, source_target_pairs={{0,2},{1,3},{2,0},{3,1},{4,6},{5,7},{6,4},{7,5},{8,10},{9,11},{10,... | collective-permute-start | bytes 147464 | tf_op jit(solution)/shard_map/ppermute | solution.py:33
  87.7 7.3 %collective-permute-done.4.r1_ref = bf16[16,1536]{1,0:T(8,128)(2,1)S(1)} collective-permute-done((bf16[16,1536]{1,0:T(8,128)(2,1)S(1)}, bf16[16,1536]{1,0:T(8,128)(2,1)S(1)}, u32[]{:S(2)}, u32[]{:S(2)}) %collective-permute-start.4) | collective-permute-done | bytes 49184 | tf_op jit(solution)/shard_map/ppermute | solution.py:33
  95.5 1.8 %copy-done.2 = bf16[1408,3,352]{0,2,1:T(8,128)(2,1)S(1)} copy-done((bf16[1408,3,352]{0,2,1:T(8,128)(2,1)S(1)}, bf16[1408,3,352]{0,2,1:T(8,128)(2,1)}, u32[]{:S(2)}) %copy-start.2) | copy-done | bytes 2973720
  97.4 2.4 %shard_map.115 = bf16[4,3,88,128]{3,2,1,0:T(8,128)(2,1)S(1)} custom-call(s32[3]{0:T(128)S(1)} %copy-done.5, bf16[16,1536]{1,0:T(8,128)(2,1)S(1)} %reduce_sum.12.r0_ref, bf16[16,1536]{1,0:T(8,128)(2,1)S(1)} %collective-permute-done.4.r1_ref, bf16[16,1536]{1,0:T(8,128)(2,1)S(1)} %collective-permute-done.5.r2_ref, ...), custom_call_target="tpu_custom_call" | custom-call | tf_op jit(solution)/shard_map/pallas_call | solution.py:393
  100.8 9.1 %all_to_all.21.own_ref = bf16[4,3,88,128]{3,2,1,0:T(8,128)(2,1)S(1)} all-to-all(bf16[4,3,88,128]{3,2,1,0:T(8,128)(2,1)S(1)} %shard_map.115), channel_id=1, replica_groups=mesh['z'=8,'y'=4,'c'=2,'t'=4] {'y'}, dimensions={0} | all-to-all | bytes 540672 | tf_op jit(solution)/shard_map/all_to_all | solution.py:400
  109.9 3.4 %collective-permute-start.12 = (bf16[4,2,88,128]{3,2,1,0:T(8,128)(2,1)S(1)}, bf16[4,2,88,128]{3,2,1,0:T(8,128)(2,1)S(1)}, u32[]{:S(2)}, u32[]{:S(2)}) collective-permute-start(bf16[4,2,88,128]{3,2,1,0:T(8,128)(2,1)S(1)} %slice.20), channel_id=1, source_target_pairs={{0,32},{32,64},{64,96},{96,128},{128,160},{160,192},{192,224},{1,3... | collective-permute-start | bytes 540680 | tf_op jit(solution)/shard_map/ppermute | solution.py:28
  113.3 4.6 %collective-permute-start.10 = (bf16[4,2,88,128]{3,2,1,0:T(8,128)(2,1)S(1)}, bf16[4,2,88,128]{3,2,1,0:T(8,128)(2,1)S(1)}, u32[]{:S(2)}, u32[]{:S(2)}) collective-permute-start(bf16[4,2,88,128]{3,2,1,0:T(8,128)(2,1)S(1)} %slice.20), channel_id=1, source_target_pairs={{0,64},{32,96},{64,128},{96,160},{128,192},{160,224},{1,65},{33,97... | collective-permute-start | bytes 540680 | tf_op jit(solution)/shard_map/ppermute | solution.py:28
  119.6 4.8 %collective-permute-done.10.far_ref = bf16[4,2,88,128]{3,2,1,0:T(8,128)(2,1)S(1)} collective-permute-done((bf16[4,2,88,128]{3,2,1,0:T(8,128)(2,1)S(1)}, bf16[4,2,88,128]{3,2,1,0:T(8,128)(2,1)S(1)}, u32[]{:S(2)}, u32[]{:S(2)}) %collective-permute-start.10) | collective-permute-done | bytes 180256 | tf_op jit(solution)/shard_map/ppermute | solution.py:28
  125.4 3.2 %shard_map.116 = (f32[4,128,128]{2,1,0:T(8,128)S(1)}, f32[4,8,128]{2,1,0:T(8,128)S(1)}, f32[4,88,128]{2,1,0:T(8,128)S(1)}) custom-call(s32[3]{0:T(128)S(1)} %copy-done.5, s32[16]{0:T(128)S(1)} %copy-done.6, bf16[4,3,88,128]{3,2,1,0:T(8,128)(2,1)S(1)} %all_to_all.21.own_ref, bf16[4,2,88,128]{3,2,1,0:T(8,128)(2,1)S(1)} %collective-permute-done.12.near_ref, ...), custom_call_target="tpu_custom_call" | custom-call | tf_op jit(solution)/shard_map/pallas_call | solution.py:408
  128.7 3.1 %shard_map.117 = bf16[4,4,88,128]{3,2,1,0:T(8,128)(2,1)} custom-call(s32[3]{0:T(128)S(1)} %copy-done.5, s32[16]{0:T(128)S(1)} %copy-done.6, bf16[4,3,88,128]{3,2,1,0:T(8,128)(2,1)S(1)} %all_to_all.21.own_ref, bf16[4,2,88,128]{3,2,1,0:T(8,128)(2,1)S(1)} %collective-permute-done.10.far_ref, bf16[4,2,88,128]{3,2,1,0:T(8,128)(2,1)S(1)} %collective-permute-done.11.far2_ref, ...), custom_call_target="tpu_custom_call" | custom-call | tf_op jit(solution)/shard_map/pallas_call | solution.py:415
  131.8 3.5 %all-to-all-start.3 = ((bf16[16,88,128]{2,1,0:T(8,128)(2,1)}), bf16[16,88,128]{2,1,0:T(8,128)(2,1)S(1)}, u32[]{:S(2)}, u32[]{:S(2)}) async-start(bf16[16,88,128]{2,1,0:T(8,128)(2,1)} %bitcast.21), calls=%async_computation.3 | async-start | bytes 720896 | tf_op jit(solution)/shard_map/all_to_all | solution.py:422
  136.6 8.7 %all-to-all-done.3 = bf16[16,88,128]{2,1,0:T(8,128)(2,1)S(1)} async-done(((bf16[16,88,128]{2,1,0:T(8,128)(2,1)}), bf16[16,88,128]{2,1,0:T(8,128)(2,1)S(1)}, u32[]{:S(2)}, u32[]{:S(2)}) %all-to-all-start.3) | async-done | bytes 360480 | tf_op jit(solution)/shard_map/all_to_all | solution.py:422
  145.3 3.2 %shard_map.119 = bf16[128,1408]{1,0:T(8,128)(2,1)} custom-call(s32[3]{0:T(128)S(1)} %copy-done.5, bf16[4,2,176,128]{3,2,1,0:T(8,128)(2,1)S(1)} %bitcast.37, bf16[352,1408]{1,0:T(8,128)(2,1)S(1)} %copy-done.1, bf16[176,1408]{1,0:T(8,128)(2,1)} %collective-permute-done.15.m2_ref, bf16[176,1408]{1,0:T(8,128)(2,1)S(1)} %collective-permute-done.16.m1_ref, ...), custom_call_target="tpu_custom_call" | custom-call | tf_op jit(solution)/shard_map/pallas_call | solution.py:423
  (69 shorter events, 20.2 us)
Async XLA Ops:
  7.7 13.6 %collective-permute-start = (bf16[64,1408]{1,0:T(8,128)(2,1)}, bf16[64,1408]{1,0:T(8,128)(2,1)S(1)}, u32[]{:S(2)}, u32[]{:S(2)}) collective-permute-start(bf16[64,1408]{1,0:T(8,128)(2,1)} %get-tuple-element.21), channel_id=1, source_target_pairs={{0,1},{1,2},{2,3},{3,0},{4,5},{5,6},{6,7},{7,4},{8,9},{9,10},{10,1... | collective-permute-start | bytes 540680 | tf_op jit(solution)/shard_map/ppermute | solution.py:33
  9.3 12.0 %collective-permute-start.1 = (bf16[64,1408]{1,0:T(8,128)(2,1)}, bf16[64,1408]{1,0:T(8,128)(2,1)S(1)}, u32[]{:S(2)}, u32[]{:S(2)}) collective-permute-start(bf16[64,1408]{1,0:T(8,128)(2,1)} %get-tuple-element.22), channel_id=1, source_target_pairs={{0,2},{1,3},{2,0},{3,1},{4,6},{5,7},{6,4},{7,5},{8,10},{9,11},{10,... | collective-permute-start | bytes 540680 | tf_op jit(solution)/shard_map/ppermute | solution.py:33
  12.0 9.3 %collective-permute-start.2 = (bf16[64,1408]{1,0:T(8,128)(2,1)}, bf16[64,1408]{1,0:T(8,128)(2,1)S(1)}, u32[]{:S(2)}, u32[]{:S(2)}) collective-permute-start(bf16[64,1408]{1,0:T(8,128)(2,1)} %get-tuple-element.23), channel_id=1, source_target_pairs={{0,3},{1,0},{2,1},{3,2},{4,7},{5,4},{6,5},{7,6},{8,11},{9,8},{10,9... | collective-permute-start | bytes 540680 | tf_op jit(solution)/shard_map/ppermute | solution.py:33
  43.7 51.9 %copy-start.5 = (s32[3]{0:T(128)S(1)}, s32[3]{0:T(128)}, u32[]{:S(2)}) copy-start(s32[3]{0:T(128)} %pad_add_fusion.place_ref) | copy-start | bytes 40
  43.8 1.5 %collective-permute-start.3 = (bf16[4,16,1536]{2,1,0:T(8,128)(2,1)S(1)}, bf16[4,16,1536]{2,1,0:T(8,128)(2,1)S(1)}, u32[]{:S(2)}, u32[]{:S(2)}) collective-permute-start(bf16[4,16,1536]{2,1,0:T(8,128)(2,1)S(1)} %shard_map.112.mine_ref), channel_id=1, source_target_pairs={{0,4},{4,0},{1,5},{5,1},{2,6},{6,2},{3,7},{7,3},{8,12},{12,8},{9,1... | collective-permute-start | bytes 589832 | tf_op jit(solution)/shard_map/ppermute | solution.py:33
  47.0 35.6 %all-to-all-start.1 = ((bf16[8,16,1536]{2,1,0:T(8,128)(2,1)}), bf16[8,16,1536]{2,1,0:T(8,128)(2,1)S(1)}, u32[]{:S(2)}, u32[]{:S(2)}) async-start(bf16[8,16,1536]{2,1,0:T(8,128)(2,1)} %shard_map.113.after_hbm), calls=%async_computation.1 | async-start | bytes 786432 | tf_op jit(solution)/shard_map/all_to_all | solution.py:386
  74.7 7.9 %collective-permute-start.7 = (bf16[352,128]{1,0:T(8,128)(2,1)}, bf16[352,128]{1,0:T(8,128)(2,1)S(1)}, u32[]{:S(2)}, u32[]{:S(2)}) collective-permute-start(bf16[352,128]{1,0:T(8,128)(2,1)} %get-tuple-element.25), channel_id=1, source_target_pairs={{0,1},{1,2},{2,3},{3,0},{4,5},{5,6},{6,7},{7,4},{8,9},{9,10},{10,1... | collective-permute-start | bytes 270344 | tf_op jit(solution)/shard_map/ppermute | solution.py:33
  75.3 7.3 %collective-permute-start.8 = (bf16[352,128]{1,0:T(8,128)(2,1)}, bf16[352,128]{1,0:T(8,128)(2,1)S(1)}, u32[]{:S(2)}, u32[]{:S(2)}) collective-permute-start(bf16[352,128]{1,0:T(8,128)(2,1)} %get-tuple-element.25), channel_id=1, source_target_pairs={{0,2},{1,3},{2,0},{3,1},{4,6},{5,7},{6,4},{7,5},{8,10},{9,11},{10,... | collective-permute-start | bytes 270344 | tf_op jit(solution)/shard_map/ppermute | solution.py:33
  77.0 10.1 %collective-permute-start.9 = (bf16[352,128]{1,0:T(8,128)(2,1)}, bf16[352,128]{1,0:T(8,128)(2,1)S(1)}, u32[]{:S(2)}, u32[]{:S(2)}) collective-permute-start(bf16[352,128]{1,0:T(8,128)(2,1)} %get-tuple-element.25), channel_id=1, source_target_pairs={{0,3},{1,0},{2,1},{3,2},{4,7},{5,4},{6,5},{7,6},{8,11},{9,8},{10,9... | collective-permute-start | bytes 270344 | tf_op jit(solution)/shard_map/ppermute | solution.py:33
  78.3 39.6 %collective-permute-start.16 = (bf16[176,1408]{1,0:T(8,128)(2,1)}, bf16[176,1408]{1,0:T(8,128)(2,1)S(1)}, u32[]{:S(2)}, u32[]{:S(2)}) collective-permute-start(bf16[176,1408]{1,0:T(8,128)(2,1)} %get-tuple-element.31), channel_id=1, source_target_pairs={{0,1},{1,2},{2,3},{3,0},{4,5},{5,6},{6,7},{7,4},{8,9},{9,10},{10,1... | collective-permute-start | bytes 1486856 | tf_op jit(solution)/shard_map/ppermute | solution.py:33
  79.0 45.4 %collective-permute-start.17 = (bf16[176,1408]{1,0:T(8,128)(2,1)}, bf16[176,1408]{1,0:T(8,128)(2,1)S(1)}, u32[]{:S(2)}, u32[]{:S(2)}) collective-permute-start(bf16[176,1408]{1,0:T(8,128)(2,1)} %get-tuple-element.31), channel_id=1, source_target_pairs={{0,3},{1,0},{2,1},{3,2},{4,7},{5,4},{6,5},{7,6},{8,11},{9,8},{10,9... | collective-permute-start | bytes 1486856 | tf_op jit(solution)/shard_map/ppermute | solution.py:33
  82.7 12.2 %collective-permute-start.4 = (bf16[16,1536]{1,0:T(8,128)(2,1)S(1)}, bf16[16,1536]{1,0:T(8,128)(2,1)S(1)}, u32[]{:S(2)}, u32[]{:S(2)}) collective-permute-start(bf16[16,1536]{1,0:T(8,128)(2,1)S(1)} %reduce_sum.12.r0_ref), channel_id=1, source_target_pairs={{0,1},{1,2},{2,3},{3,0},{4,5},{5,6},{6,7},{7,4},{8,9},{9,10},{10,1... | collective-permute-start | bytes 147464 | tf_op jit(solution)/shard_map/ppermute | solution.py:33
  83.0 12.0 %collective-permute-start.5 = (bf16[16,1536]{1,0:T(8,128)(2,1)S(1)}, bf16[16,1536]{1,0:T(8,128)(2,1)S(1)}, u32[]{:S(2)}, u32[]{:S(2)}) collective-permute-start(bf16[16,1536]{1,0:T(8,128)(2,1)S(1)} %reduce_sum.12.r0_ref), channel_id=1, source_target_pairs={{0,2},{1,3},{2,0},{3,1},{4,6},{5,7},{6,4},{7,5},{8,10},{9,11},{10,... | collective-permute-start | bytes 147464 | tf_op jit(solution)/shard_map/ppermute | solution.py:33
  87.1 8.4 %collective-permute-start.6 = (bf16[16,1536]{1,0:T(8,128)(2,1)S(1)}, bf16[16,1536]{1,0:T(8,128)(2,1)S(1)}, u32[]{:S(2)}, u32[]{:S(2)}) collective-permute-start(bf16[16,1536]{1,0:T(8,128)(2,1)S(1)} %reduce_sum.12.r0_ref), channel_id=1, source_target_pairs={{0,3},{1,0},{2,1},{3,2},{4,7},{5,4},{6,5},{7,6},{8,11},{9,8},{10,9... | collective-permute-start | bytes 147464 | tf_op jit(solution)/shard_map/ppermute | solution.py:33
  99.8 25.2 %collective-permute-start.15 = (bf16[176,1408]{1,0:T(8,128)(2,1)}, bf16[176,1408]{1,0:T(8,128)(2,1)}, u32[]{:S(2)}, u32[]{:S(2)}) collective-permute-start(bf16[176,1408]{1,0:T(8,128)(2,1)} %get-tuple-element.31), channel_id=1, source_target_pairs={{0,2},{1,3},{2,0},{3,1},{4,6},{5,7},{6,4},{7,5},{8,10},{9,11},{10,... | collective-permute-start | bytes 1486856 | tf_op jit(solution)/shard_map/ppermute | solution.py:33
  109.9 9.6 %collective-permute-start.12 = (bf16[4,2,88,128]{3,2,1,0:T(8,128)(2,1)S(1)}, bf16[4,2,88,128]{3,2,1,0:T(8,128)(2,1)S(1)}, u32[]{:S(2)}, u32[]{:S(2)}) collective-permute-start(bf16[4,2,88,128]{3,2,1,0:T(8,128)(2,1)S(1)} %slice.20), channel_id=1, source_target_pairs={{0,32},{32,64},{64,96},{96,128},{128,160},{160,192},{192,224},{1,3... | collective-permute-start | bytes 540680 | tf_op jit(solution)/shard_map/ppermute | solution.py:28
  113.3 11.1 %collective-permute-start.10 = (bf16[4,2,88,128]{3,2,1,0:T(8,128)(2,1)S(1)}, bf16[4,2,88,128]{3,2,1,0:T(8,128)(2,1)S(1)}, u32[]{:S(2)}, u32[]{:S(2)}) collective-permute-start(bf16[4,2,88,128]{3,2,1,0:T(8,128)(2,1)S(1)} %slice.20), channel_id=1, source_target_pairs={{0,64},{32,96},{64,128},{96,160},{128,192},{160,224},{1,65},{33,97... | collective-permute-start | bytes 540680 | tf_op jit(solution)/shard_map/ppermute | solution.py:28
  117.9 7.0 %collective-permute-start.13 = (bf16[4,2,88,128]{3,2,1,0:T(8,128)(2,1)S(1)}, bf16[4,2,88,128]{3,2,1,0:T(8,128)(2,1)S(1)}, u32[]{:S(2)}, u32[]{:S(2)}) collective-permute-start(bf16[4,2,88,128]{3,2,1,0:T(8,128)(2,1)S(1)} %slice.20), channel_id=1, source_target_pairs={{0,4},{4,0},{1,5},{5,1},{2,6},{6,2},{3,7},{7,3},{8,12},{12,8},{9,1... | collective-permute-start | bytes 540680 | tf_op jit(solution)/shard_map/ppermute | solution.py:33
  119.6 5.9 %collective-permute-start.14 = (bf16[4,2,88,128]{3,2,1,0:T(8,128)(2,1)S(1)}, bf16[4,2,88,128]{3,2,1,0:T(8,128)(2,1)S(1)}, u32[]{:S(2)}, u32[]{:S(2)}) collective-permute-start(bf16[4,2,88,128]{3,2,1,0:T(8,128)(2,1)S(1)} %collective-permute-done.12.near_ref), channel_id=1, source_target_pairs={{0,4},{4,0},{1,5},{5,1},{2,6},{6,2},{3,7},{7,3},{8,12},{12,8},{9,1... | collective-permute-start | bytes 540680 | tf_op jit(solution)/shard_map/ppermute | solution.py:33
  124.4 4.3 %collective-permute-start.11 = (bf16[4,2,88,128]{3,2,1,0:T(8,128)(2,1)S(1)}, bf16[4,2,88,128]{3,2,1,0:T(8,128)(2,1)S(1)}, u32[]{:S(2)}, u32[]{:S(2)}) collective-permute-start(bf16[4,2,88,128]{3,2,1,0:T(8,128)(2,1)S(1)} %collective-permute-done.10.far_ref), channel_id=1, source_target_pairs={{0,4},{4,0},{1,5},{5,1},{2,6},{6,2},{3,7},{7,3},{8,12},{12,8},{9,1... | collective-permute-start | bytes 540680 | tf_op jit(solution)/shard_map/ppermute | solution.py:33
  124.4 12.2 %collective-permute-start.19 = (bf16[176,1408]{1,0:T(8,128)(2,1)S(1)}, bf16[176,1408]{1,0:T(8,128)(2,1)}, u32[]{:S(2)}, u32[]{:S(2)}) collective-permute-start(bf16[176,1408]{1,0:T(8,128)(2,1)S(1)} %collective-permute-done.16.m1_ref), channel_id=1, source_target_pairs={{0,4},{4,0},{1,5},{5,1},{2,6},{6,2},{3,7},{7,3},{8,12},{12,8},{9,1... | collective-permute-start | bytes 1486856 | tf_op jit(solution)/shard_map/ppermute | solution.py:33
  124.9 11.7 %collective-permute-start.20 = (bf16[176,1408]{1,0:T(8,128)(2,1)S(1)}, bf16[176,1408]{1,0:T(8,128)(2,1)}, u32[]{:S(2)}, u32[]{:S(2)}) collective-permute-start(bf16[176,1408]{1,0:T(8,128)(2,1)S(1)} %collective-permute-done.17.m3_ref), channel_id=1, source_target_pairs={{0,4},{4,0},{1,5},{5,1},{2,6},{6,2},{3,7},{7,3},{8,12},{12,8},{9,1... | collective-permute-start | bytes 1486856 | tf_op jit(solution)/shard_map/ppermute | solution.py:33
  125.0 20.3 %collective-permute-start.18 = (bf16[176,1408]{1,0:T(8,128)(2,1)}, bf16[176,1408]{1,0:T(8,128)(2,1)}, u32[]{:S(2)}, u32[]{:S(2)}) collective-permute-start(bf16[176,1408]{1,0:T(8,128)(2,1)} %collective-permute-done.15.m2_ref), channel_id=1, source_target_pairs={{0,4},{4,0},{1,5},{5,1},{2,6},{6,2},{3,7},{7,3},{8,12},{12,8},{9,1... | collective-permute-start | bytes 1486856 | tf_op jit(solution)/shard_map/ppermute | solution.py:33
  131.8 13.5 %all-to-all-start.3 = ((bf16[16,88,128]{2,1,0:T(8,128)(2,1)}), bf16[16,88,128]{2,1,0:T(8,128)(2,1)S(1)}, u32[]{:S(2)}, u32[]{:S(2)}) async-start(bf16[16,88,128]{2,1,0:T(8,128)(2,1)} %bitcast.21), calls=%async_computation.3 | async-start | bytes 720896 | tf_op jit(solution)/shard_map/all_to_all | solution.py:422
  (9 other events, 138.5 us)

commit v9 on v7

--- a/solution.py
+++ b/solution.py
@@ -21,7 +21,6 @@
 HBM = pltpu.HBM
 FACTS = 128
 STRIP = 256
-WINDOW = 18 * BLOCK
 
 
 def ahead(x, axis, by):
@@ -77,7 +76,7 @@
 
 
 def vision_kernel(
-    place_ref, grid_ref, picture_hbm, qkv_hbm, out_hbm, s0_ref, s1_ref, s2_ref, s3_ref,
+    grid_ref, picture_hbm, qkv_hbm, out_hbm, s0_ref, s1_ref, s2_ref, s3_ref,
     picture_ref, qkv_ref, out_ref, arrived,
 ):
     copies = [pltpu.make_async_copy(picture_hbm, picture_ref, arrived.at[0])]
@@ -106,7 +105,7 @@
         total = jnp.sum(expons, axis=0, keepdims=True)
         contexts.append(dot(v, expons.astype(BF), (1, 0)) / total)
     context = jnp.concatenate(contexts, axis=0).astype(BF)
-    row = (iota((count, count), 0) + place_ref[2] * MERGED) % count
+    row = (iota((count, count), 0) + lax.axis_index("t") * MERGED) % count
     order = slot_of(row) == iota((count, count), 1)
     context = dot(order.astype(BF), context, (1, 1)).astype(BF)
     copies[4].wait()
@@ -146,15 +145,18 @@
     own_ref[...] = dot(chosen, picture_ref[...], (1, 0)) + share_ref[...].astype(F32)
 
 
-def merge_kernel(facts_ref, own_ref, s1_ref, s2_ref, s3_ref, top_ref, low_ref, rows_ref):
+def merge_kernel(facts_ref, own_ref, s1_ref, s2_ref, s3_ref, w0_ref, w1_ref, w2_ref, rows_ref):
     width = own_ref.shape[1]
     total = own_ref[...]
     for share in (s1_ref, s2_ref, s3_ref):
         total = total + share[...].astype(F32)
     normed = normalize(total)
-    deep = top_ref.shape[0]
-    merged = dot(normed[:, :deep], top_ref[...], (1, 0))
-    merged = (merged + dot(normed[:, deep:], low_ref[...], (1, 0))).astype(BF)
+    first, merged = 0, jnp.zeros((MERGED, width), F32)
+    for weight in (w0_ref, w1_ref, w2_ref):
+        deep = weight.shape[0]
+        merged = merged + dot(normed[:, first : first + deep], weight[...], (1, 0))
+        first = first + deep
+    merged = merged.astype(BF)
     lane = iota((MERGED, FACTS), 1)
     facts = jnp.zeros((MERGED, FACTS), I32)
     for index in range(5):
@@ -203,24 +205,24 @@
 
 
 def attend_kernel(facts_ref, lengths_ref, own_ref, near_ref, far_ref,
-                  own2_ref, near2_ref, far2_ref, sent_ref, keys_ref, values_ref):
+                  own2_ref, near2_ref, far2_ref, sent_ref):
     z, c = facts_ref[0], facts_ref[1]
-    for plane, (mine, other) in enumerate(
-        ((far_ref, far2_ref), (near_ref, near2_ref), (own_ref, own2_ref))
+    blocks = []
+    for mine, other, skip in (
+        (far_ref, far2_ref, 0), (near_ref, near2_ref, 0), (own_ref, own2_ref, 1)
     ):
-        skip = 1 if plane == 2 else 0
-        for y in range(4):
-            at = (plane * 8 + 2 * y) * BLOCK
-            mine_at = pl.ds(pl.multiple_of(at + c * BLOCK, BLOCK), BLOCK)
-            other_at = pl.ds(pl.multiple_of(at + (1 - c) * BLOCK, BLOCK), BLOCK)
-            for part, store in ((0, keys_ref), (1, values_ref)):
-                store[:, mine_at] = mine[y, skip + part]
-                store[:, other_at] = other[y, part]
+        blocks += [(mine, other, skip, y) for y in range(4)]
+
+    def strip_of(strip, part):
+        mine, other, skip, y = blocks[strip]
+        return jnp.concatenate([mine[y, skip + part], other[y, part]], axis=1)
+
     row = iota((BLOCK, 1), 0)
-    column = iota((BLOCK, STRIP), 1)
+    lane = iota((BLOCK, STRIP), 1)
+    column = lane + jnp.where(lane < BLOCK, c * BLOCK, -c * BLOCK)
+    base = (z - 2) * 1024
     for j in range(4):
-        base = (z - 2) * 1024 + j * 256
-        here = 2048 + c * BLOCK + row
+        here = 2048 + j * 256 + c * BLOCK + row
         start = jnp.zeros((BLOCK, 1), I32)
         end = jnp.int32(0)
         for prompt in range(16):
@@ -229,22 +231,21 @@
         low = start - base
         query = own_ref[j, 0].T
         strips, top = [], None
-        for first in range(0, WINDOW, STRIP):
-            scores = dot(query, keys_ref[:, pl.ds(j * 256 + first, STRIP)], (1, 0))
-            visible = column >= low - first
-            if first + STRIP > 2048:
-                visible = visible & (column <= here - first)
+        for strip in range(j, j + 9):
+            scores = dot(query, strip_of(strip, 0), (1, 0))
+            visible = column >= low - strip * STRIP
+            if strip >= 8:
+                visible = visible & (column <= here - strip * STRIP)
             scores = jnp.where(visible, scores, -jnp.inf)
             top = scores if top is None else jnp.maximum(top, scores)
-            strips.append(scores)
+            strips.append((strip, scores))
         top = jnp.max(top, axis=1, keepdims=True)
         total = jnp.zeros((BLOCK, STRIP), F32)
         summed = jnp.zeros((HEAD, BLOCK), F32)
-        for strip, scores in enumerate(strips):
+        for strip, scores in strips:
             expons = jnp.exp2((scores - top) * SCALE2)
             total = total + expons
-            values = values_ref[:, pl.ds(j * 256 + strip * STRIP, STRIP)]
-            summed = summed + dot(values, expons.astype(BF), (1, 1))
+            summed = summed + dot(strip_of(strip, 1), expons.astype(BF), (1, 1))
         total = jnp.sum(total, axis=1, keepdims=True)
         total = jnp.transpose(jnp.broadcast_to(total, (BLOCK, BLOCK)))
         context = (summed / total[:HEAD]).astype(BF)
@@ -298,7 +299,7 @@
     share = call(
         vision_kernel,
         [shape((MERGED, width))] * 4,
-        [SMEM, SMEM, HBM, HBM, HBM],
+        [SMEM, HBM, HBM, HBM],
         [
             VMEM((count, width), BF),
             VMEM((3, local_width, width), BF),
@@ -306,17 +307,17 @@
             pltpu.SemaphoreType.DMA((5,)),
         ],
         limit=60,
-    )(place, picture_grid, picture, vision_qkv.transpose(1, 2, 0), vision_out)
+    )(picture_grid, picture, vision_qkv.transpose(1, 2, 0), vision_out)
     shares = [around(share[by], "t", by) for by in range(1, 4)]
     own = call(own_kernel, shape((MERGED, width), F32), [SMEM, VMEM, VMEM], flops=8 * 10**9)(
         place, picture, share[0]
     )
     own, merge_weight = lax.optimization_barrier((own, merge_weight))
-    merge_parts = (merge_weight[0, : width // 2], merge_weight[0, width // 2 :])
+    merge_parts = jnp.split(merge_weight[0], [640, 1024], axis=0)
     facts = jnp.stack([block, picture_offset[0], picture_grid[0, 0], picture_grid[0, 1], 1])
     facts = jnp.where(t == 0, facts, 0)
     facts = jnp.concatenate([facts, (block % 8 // 2)[None]]).astype(I32)
-    routed = call(merge_kernel, shape((4, MERGED, wide)), [SMEM] + [VMEM] * 6)(
+    routed = call(merge_kernel, shape((4, MERGED, wide)), [SMEM] + [VMEM] * 7)(
         facts, own, *shares, *merge_parts
     )
 
@@ -356,7 +357,6 @@
         attend_kernel,
         shape((4, 4, HEAD, BLOCK)),
         [SMEM, SMEM] + [VMEM] * 6,
-        [pltpu.VMEM((HEAD, 24 * BLOCK), BF)] * 2,
         limit=16,
     )(place, prompt_lengths, mine, near, far, *others)
     context = lax.all_to_all(sent.reshape(16, HEAD, BLOCK), ("t", "y"), 0, 0, tiled=True)

time: 129 us -> 129 us (level)
  local copies, waits for them, and re-layouts: 14.3 us -> 12.9 us
    squeeze x1 -> x0, local copies, waits for them, and re-layouts: 1.6 us -> none  [local(): merge_parts = (merge_weight[0, :width // 2], merge_weight[0, width // 2:])]
  transfers between devices with their start and end apart: 23 -> 23, of which waited for: 9 -> 9; matrix products, arithmetic and copies ran while one was open for 9% -> 8% of each run, Pallas kernels for 7% -> 7%
where the time goes in v9:
time: 129 us; the launch traced here: 127 us
  starting transfers between devices  38.4 us (30%)
  blocking collectives  28.4 us (22%)
  Pallas kernels  23 us (18%)
  waiting for transfers between devices  22.1 us (17%)
  local copies, waits for them, and re-layouts  12.9 us (10%)
  between operations  1.6 us (1%)
    all_to_all x1, blocking collectives, local(): lax.all_to_all(routed.reshape(16, 16, wide), ('y', 't'), 0, 0, tiled=True)  19.3 us
    ppermute x19, starting transfers between devices, around(): return lax.ppermute(x, axis, [(i, (i + by) % count) for i in range(count)])  18.6 us
    all_to_all x1, blocking collectives, local(): mine = lax.all_to_all(heads, 'y', 0, 0, tiled=True)  9.11 us
    all_to_all x1, waiting for transfers between devices, local(): lax.all_to_all(sent.reshape(16, HEAD, BLOCK), ('t', 'y'), 0, 0, tiled=True)  8.56 us
    all_to_all x1, starting transfers between devices, local(): got = lax.all_to_all(routed, 'z', 0, 0, tiled=True)  8.13 us
    ppermute x2, starting transfers between devices, ahead(): return lax.ppermute(x, axis, [(i, i + by) for i in range(count - by)])  8.08 us
    pallas_call x1, Pallas kernels, local(): call(vision_kernel, [shape((MERGED, width))] * 4, [SMEM, HBM, HBM, HBM],...  7.21 us
    ppermute x2, waiting for transfers between devices, ahead(): return lax.ppermute(x, axis, [(i, i + by) for i in range(count - by)])  6.35 us
  transfers between devices with their start and end apart: 23, of which 9 were waited for; matrix products, arithmetic and copies ran while one was open for 8% of the time, Pallas kernels for 7%

profile of v9, /device:TPU:64, one launch (start us, length us, event | category | flops | bytes accessed | tf_op | source)
XLA Modules:
  0.0 127.5 jit_solution(15807560718275459971)
XLA Ops:
  0.0 7.2 %shard_map.109 = (bf16[64,1408]{1,0:T(8,128)(2,1)}, bf16[64,1408]{1,0:T(8,128)(2,1)}, bf16[64,1408]{1,0:T(8,128)(2,1)}, bf16[64,1408]{1,0:T(8,128)(2,1)}) custom-call(s32[1,2]{1,0:T(1,128)} %grid_ref.1, bf16[256,1408]{1,0:T(8,128)(2,1)} %bitcast.38, bf16[3,352,1408]{2,1,0:T(8,128)(2,1)} %bitcast.42, bf16[352,1408]{1,0:T(8,128)(2,1)} %out_hbm.1), custom_call_target="tpu_custom_call" | custom-call | tf_op jit(solution)/shard_map/pallas_call | solution.py:299
  7.2 1.6 %collective-permute-start = (bf16[64,1408]{1,0:T(8,128)(2,1)}, bf16[64,1408]{1,0:T(8,128)(2,1)S(1)}, u32[]{:S(2)}, u32[]{:S(2)}) collective-permute-start(bf16[64,1408]{1,0:T(8,128)(2,1)} %get-tuple-element.20), channel_id=1, source_target_pairs={{0,1},{1,2},{2,3},{3,0},{4,5},{5,6},{6,7},{7,4},{8,9},{9,10},{10,1... | collective-permute-start | bytes 540680 | tf_op jit(solution)/shard_map/ppermute | solution.py:33
  8.8 2.7 %collective-permute-start.1 = (bf16[64,1408]{1,0:T(8,128)(2,1)}, bf16[64,1408]{1,0:T(8,128)(2,1)}, u32[]{:S(2)}, u32[]{:S(2)}) collective-permute-start(bf16[64,1408]{1,0:T(8,128)(2,1)} %get-tuple-element.21), channel_id=1, source_target_pairs={{0,2},{1,3},{2,0},{3,1},{4,6},{5,7},{6,4},{7,5},{8,10},{9,11},{10,... | collective-permute-start | bytes 540680 | tf_op jit(solution)/shard_map/ppermute | solution.py:33
  11.5 1.4 %collective-permute-start.2 = (bf16[64,1408]{1,0:T(8,128)(2,1)}, bf16[64,1408]{1,0:T(8,128)(2,1)}, u32[]{:S(2)}, u32[]{:S(2)}) collective-permute-start(bf16[64,1408]{1,0:T(8,128)(2,1)} %get-tuple-element.22), channel_id=1, source_target_pairs={{0,3},{1,0},{2,1},{3,2},{4,7},{5,4},{6,5},{7,6},{8,11},{9,8},{10,9... | collective-permute-start | bytes 540680 | tf_op jit(solution)/shard_map/ppermute | solution.py:33
  22.0 2.0 %shard_map.111 = bf16[4,64,1536]{2,1,0:T(8,128)(2,1)S(1)} custom-call(s32[6]{0:T(128)S(1)} %pad_add_fusion.1.facts_ref, f32[64,1408]{1,0:T(8,128)S(1)} %shard_map.110.own_ref, bf16[64,1408]{1,0:T(8,128)(2,1)S(1)} %collective-permute-done.s1_ref, bf16[64,1408]{1,0:T(8,128)(2,1)} %collective-permute-done.1.s2_ref, ...), custom_call_target="tpu_custom_call" | custom-call | tf_op jit(solution)/shard_map/pallas_call | solution.py:320
  24.1 19.3 %all_to_all.20 = bf16[16,16,1536]{2,1,0:T(8,128)(2,1)S(1)} all-to-all(bf16[16,16,1536]{2,1,0:T(8,128)(2,1)S(1)} %bitcast.35), channel_id=1, replica_groups=mesh['z'=8,'y'=4,'c'=2,'t'=4] {'y','t'}, dimensions={0} | all-to-all | bytes 1572864 | tf_op jit(solution)/shard_map/all_to_all | solution.py:324
  45.0 1.7 %shard_map.113 = bf16[8,16,1536]{2,1,0:T(8,128)(2,1)} custom-call(s32[3]{0:T(128)S(1)} %pad_add_fusion.place_ref.facts_ref, bf16[4,16,1536]{2,1,0:T(8,128)(2,1)S(1)} %shard_map.112.mine_ref, bf16[4,16,1536]{2,1,0:T(8,128)(2,1)S(1)} %collective-permute-done.3.other_ref), custom_call_target="tpu_custom_call" | custom-call | tf_op jit(solution)/shard_map/pallas_call | solution.py:327
  46.7 8.1 %all-to-all-start.1 = ((bf16[8,16,1536]{2,1,0:T(8,128)(2,1)}), bf16[8,16,1536]{2,1,0:T(8,128)(2,1)}, u32[]{:S(2)}, u32[]{:S(2)}) async-start(bf16[8,16,1536]{2,1,0:T(8,128)(2,1)} %shard_map.113), calls=%async_computation.1 | async-start | bytes 786432 | tf_op jit(solution)/shard_map/all_to_all | solution.py:334
  54.8 2.0 %constant_dynamic-slice_fusion = bf16[176,1408]{1,0:T(8,128)(2,1)} fusion(bf16[352,1408]{1,0:T(8,128)(2,1)} %w0_ref, s32[]{:T(128)S(6)} %select_n.55), kind=kLoop, calls=%fused_computation.7 | loop fusion | bytes 991236 | tf_op jit(solution)/shard_map/dynamic_slice | solution.py:330
  57.4 1.7 %collective-permute-start.8 = (bf16[128,352]{0,1:T(8,128)(2,1)}, bf16[128,352]{0,1:T(8,128)(2,1)S(1)}, u32[]{:S(2)}, u32[]{:S(2)}) collective-permute-start(bf16[128,352]{0,1:T(8,128)(2,1)} %param.18), channel_id=1, source_target_pairs={{0,2},{1,3},{2,0},{3,1},{4,6},{5,7},{6,4},{7,5},{8,10},{9,11},{10,... | collective-permute-start | bytes 270344 | tf_op jit(solution)/shard_map/ppermute | solution.py:33
  61.1 2.6 %collective-permute-start.17 = (bf16[176,1408]{1,0:T(8,128)(2,1)}, bf16[176,1408]{1,0:T(8,128)(2,1)}, u32[]{:S(2)}, u32[]{:S(2)}) collective-permute-start(bf16[176,1408]{1,0:T(8,128)(2,1)} %constant_dynamic-slice_fusion), channel_id=1, source_target_pairs={{0,3},{1,0},{2,1},{3,2},{4,7},{5,4},{6,5},{7,6},{8,11},{9,8},{10,9... | collective-permute-start | bytes 1486856 | tf_op jit(solution)/shard_map/ppermute | solution.py:33
  64.8 1.8 %all-to-all-done.1 = bf16[8,16,1536]{2,1,0:T(8,128)(2,1)} async-done(((bf16[8,16,1536]{2,1,0:T(8,128)(2,1)}), bf16[8,16,1536]{2,1,0:T(8,128)(2,1)}, u32[]{:S(2)}, u32[]{:S(2)}) %all-to-all-start.1) | async-done | bytes 393248 | tf_op jit(solution)/shard_map/all_to_all | solution.py:334
  68.4 1.7 %collective-permute-start.5 = (bf16[16,1536]{1,0:T(8,128)(2,1)S(1)}, bf16[16,1536]{1,0:T(8,128)(2,1)S(1)}, u32[]{:S(2)}, u32[]{:S(2)}) collective-permute-start(bf16[16,1536]{1,0:T(8,128)(2,1)S(1)} %reduce_sum.12.r0_ref), channel_id=1, source_target_pairs={{0,2},{1,3},{2,0},{3,1},{4,6},{5,7},{6,4},{7,5},{8,10},{9,11},{10,... | collective-permute-start | bytes 147464 | tf_op jit(solution)/shard_map/ppermute | solution.py:33
  74.3 2.8 %collective-permute-done.4.r1_ref = bf16[16,1536]{1,0:T(8,128)(2,1)S(1)} collective-permute-done((bf16[16,1536]{1,0:T(8,128)(2,1)S(1)}, bf16[16,1536]{1,0:T(8,128)(2,1)S(1)}, u32[]{:S(2)}, u32[]{:S(2)}) %collective-permute-start.4) | collective-permute-done | bytes 49184 | tf_op jit(solution)/shard_map/ppermute | solution.py:33
  77.6 2.4 %shard_map.114 = bf16[4,3,88,128]{3,2,1,0:T(8,128)(2,1)S(1)} custom-call(s32[3]{0:T(128)S(1)} %pad_add_fusion.place_ref.facts_ref, bf16[16,1536]{1,0:T(8,128)(2,1)S(1)} %reduce_sum.12.r0_ref, bf16[16,1536]{1,0:T(8,128)(2,1)S(1)} %collective-permute-done.4.r1_ref, bf16[16,1536]{1,0:T(8,128)(2,1)S(1)} %collective-permute-done.5.r2_ref, ...), custom_call_target="tpu_custom_call" | custom-call | tf_op jit(solution)/shard_map/pallas_call | solution.py:341
  81.0 9.1 %all_to_all.21.own_ref = bf16[4,3,88,128]{3,2,1,0:T(8,128)(2,1)S(1)} all-to-all(bf16[4,3,88,128]{3,2,1,0:T(8,128)(2,1)S(1)} %shard_map.114), channel_id=1, replica_groups=mesh['z'=8,'y'=4,'c'=2,'t'=4] {'y'}, dimensions={0} | all-to-all | bytes 540672 | tf_op jit(solution)/shard_map/all_to_all | solution.py:348
  90.2 3.5 %collective-permute-start.10 = (bf16[4,2,88,128]{3,2,1,0:T(8,128)(2,1)S(1)}, bf16[4,2,88,128]{3,2,1,0:T(8,128)(2,1)S(1)}, u32[]{:S(2)}, u32[]{:S(2)}) collective-permute-start(bf16[4,2,88,128]{3,2,1,0:T(8,128)(2,1)S(1)} %slice.15), channel_id=1, source_target_pairs={{0,32},{32,64},{64,96},{96,128},{128,160},{160,192},{192,224},{1,3... | collective-permute-start | bytes 540680 | tf_op jit(solution)/shard_map/ppermute | solution.py:28
  93.7 4.6 %collective-permute-start.11 = (bf16[4,2,88,128]{3,2,1,0:T(8,128)(2,1)S(1)}, bf16[4,2,88,128]{3,2,1,0:T(8,128)(2,1)S(1)}, u32[]{:S(2)}, u32[]{:S(2)}) collective-permute-start(bf16[4,2,88,128]{3,2,1,0:T(8,128)(2,1)S(1)} %slice.15), channel_id=1, source_target_pairs={{0,64},{32,96},{64,128},{96,160},{128,192},{160,224},{1,65},{33,97... | collective-permute-start | bytes 540680 | tf_op jit(solution)/shard_map/ppermute | solution.py:28
  98.4 1.6 %collective-permute-done.10.near_ref = bf16[4,2,88,128]{3,2,1,0:T(8,128)(2,1)S(1)} collective-permute-done((bf16[4,2,88,128]{3,2,1,0:T(8,128)(2,1)S(1)}, bf16[4,2,88,128]{3,2,1,0:T(8,128)(2,1)S(1)}, u32[]{:S(2)}, u32[]{:S(2)}) %collective-permute-start.10) | collective-permute-done | bytes 180256 | tf_op jit(solution)/shard_map/ppermute | solution.py:28
  100.0 4.8 %collective-permute-done.11.far_ref = bf16[4,2,88,128]{3,2,1,0:T(8,128)(2,1)S(1)} collective-permute-done((bf16[4,2,88,128]{3,2,1,0:T(8,128)(2,1)S(1)}, bf16[4,2,88,128]{3,2,1,0:T(8,128)(2,1)S(1)}, u32[]{:S(2)}, u32[]{:S(2)}) %collective-permute-start.11) | collective-permute-done | bytes 180256 | tf_op jit(solution)/shard_map/ppermute | solution.py:28
  106.3 4.3 %shard_map.115 = bf16[4,4,88,128]{3,2,1,0:T(8,128)(2,1)} custom-call(s32[3]{0:T(128)S(1)} %pad_add_fusion.place_ref.facts_ref, s32[16]{0:T(128)S(1)} %copy-done.4, bf16[4,3,88,128]{3,2,1,0:T(8,128)(2,1)S(1)} %all_to_all.21.own_ref, bf16[4,2,88,128]{3,2,1,0:T(8,128)(2,1)S(1)} %collective-permute-done.10.near_ref, ...), custom_call_target="tpu_custom_call" | custom-call | tf_op jit(solution)/shard_map/pallas_call | solution.py:356
  110.6 3.5 %all-to-all-start.3 = ((bf16[16,88,128]{2,1,0:T(8,128)(2,1)}), bf16[16,88,128]{2,1,0:T(8,128)(2,1)S(1)}, u32[]{:S(2)}, u32[]{:S(2)}) async-start(bf16[16,88,128]{2,1,0:T(8,128)(2,1)} %bitcast.21), calls=%async_computation.3 | async-start | bytes 720896 | tf_op jit(solution)/shard_map/all_to_all | solution.py:362
  115.7 8.6 %all-to-all-done.3 = bf16[16,88,128]{2,1,0:T(8,128)(2,1)S(1)} async-done(((bf16[16,88,128]{2,1,0:T(8,128)(2,1)}), bf16[16,88,128]{2,1,0:T(8,128)(2,1)S(1)}, u32[]{:S(2)}, u32[]{:S(2)}) %all-to-all-start.3) | async-done | bytes 360480 | tf_op jit(solution)/shard_map/all_to_all | solution.py:362
  124.2 3.3 %shard_map.117 = bf16[128,1408]{1,0:T(8,128)(2,1)} custom-call(s32[3]{0:T(128)S(1)} %pad_add_fusion.place_ref.facts_ref, bf16[4,2,176,128]{3,2,1,0:T(8,128)(2,1)S(1)} %bitcast.37, bf16[352,1408]{1,0:T(8,128)(2,1)S(1)} %copy-done.2, bf16[176,1408]{1,0:T(8,128)(2,1)S(1)} %collective-permute-done.15.m2_ref, bf16[176,1408]{1,0:T(8,128)(2,1)} %collective-permute-done.16.m1_ref, ...), custom_call_target="tpu_custom_call" | custom-call | tf_op jit(solution)/shard_map/pallas_call | solution.py:363
  (70 shorter events, 23.7 us)
Async XLA Ops:
  7.2 13.6 %collective-permute-start = (bf16[64,1408]{1,0:T(8,128)(2,1)}, bf16[64,1408]{1,0:T(8,128)(2,1)S(1)}, u32[]{:S(2)}, u32[]{:S(2)}) collective-permute-start(bf16[64,1408]{1,0:T(8,128)(2,1)} %get-tuple-element.20), channel_id=1, source_target_pairs={{0,1},{1,2},{2,3},{3,0},{4,5},{5,6},{6,7},{7,4},{8,9},{9,10},{10,1... | collective-permute-start | bytes 540680 | tf_op jit(solution)/shard_map/ppermute | solution.py:33
  8.8 12.0 %collective-permute-start.1 = (bf16[64,1408]{1,0:T(8,128)(2,1)}, bf16[64,1408]{1,0:T(8,128)(2,1)}, u32[]{:S(2)}, u32[]{:S(2)}) collective-permute-start(bf16[64,1408]{1,0:T(8,128)(2,1)} %get-tuple-element.21), channel_id=1, source_target_pairs={{0,2},{1,3},{2,0},{3,1},{4,6},{5,7},{6,4},{7,5},{8,10},{9,11},{10,... | collective-permute-start | bytes 540680 | tf_op jit(solution)/shard_map/ppermute | solution.py:33
  11.5 9.3 %collective-permute-start.2 = (bf16[64,1408]{1,0:T(8,128)(2,1)}, bf16[64,1408]{1,0:T(8,128)(2,1)}, u32[]{:S(2)}, u32[]{:S(2)}) collective-permute-start(bf16[64,1408]{1,0:T(8,128)(2,1)} %get-tuple-element.22), channel_id=1, source_target_pairs={{0,3},{1,0},{2,1},{3,2},{4,7},{5,4},{6,5},{7,6},{8,11},{9,8},{10,9... | collective-permute-start | bytes 540680 | tf_op jit(solution)/shard_map/ppermute | solution.py:33
  43.4 1.5 %collective-permute-start.3 = (bf16[4,16,1536]{2,1,0:T(8,128)(2,1)S(1)}, bf16[4,16,1536]{2,1,0:T(8,128)(2,1)S(1)}, u32[]{:S(2)}, u32[]{:S(2)}) collective-permute-start(bf16[4,16,1536]{2,1,0:T(8,128)(2,1)S(1)} %shard_map.112.mine_ref), channel_id=1, source_target_pairs={{0,4},{4,0},{1,5},{5,1},{2,6},{6,2},{3,7},{7,3},{8,12},{12,8},{9,1... | collective-permute-start | bytes 589832 | tf_op jit(solution)/shard_map/ppermute | solution.py:33
  46.7 19.9 %all-to-all-start.1 = ((bf16[8,16,1536]{2,1,0:T(8,128)(2,1)}), bf16[8,16,1536]{2,1,0:T(8,128)(2,1)}, u32[]{:S(2)}, u32[]{:S(2)}) async-start(bf16[8,16,1536]{2,1,0:T(8,128)(2,1)} %shard_map.113), calls=%async_computation.1 | async-start | bytes 786432 | tf_op jit(solution)/shard_map/all_to_all | solution.py:334
  56.8 7.9 %collective-permute-start.7 = (bf16[128,352]{0,1:T(8,128)(2,1)}, bf16[128,352]{0,1:T(8,128)(2,1)S(1)}, u32[]{:S(2)}, u32[]{:S(2)}) collective-permute-start(bf16[128,352]{0,1:T(8,128)(2,1)} %param.18), channel_id=1, source_target_pairs={{0,1},{1,2},{2,3},{3,0},{4,5},{5,6},{6,7},{7,4},{8,9},{9,10},{10,1... | collective-permute-start | bytes 270344 | tf_op jit(solution)/shard_map/ppermute | solution.py:33
  57.4 7.3 %collective-permute-start.8 = (bf16[128,352]{0,1:T(8,128)(2,1)}, bf16[128,352]{0,1:T(8,128)(2,1)S(1)}, u32[]{:S(2)}, u32[]{:S(2)}) collective-permute-start(bf16[128,352]{0,1:T(8,128)(2,1)} %param.18), channel_id=1, source_target_pairs={{0,2},{1,3},{2,0},{3,1},{4,6},{5,7},{6,4},{7,5},{8,10},{9,11},{10,... | collective-permute-start | bytes 270344 | tf_op jit(solution)/shard_map/ppermute | solution.py:33
  59.1 11.1 %collective-permute-start.9 = (bf16[128,352]{0,1:T(8,128)(2,1)}, bf16[128,352]{0,1:T(8,128)(2,1)}, u32[]{:S(2)}, u32[]{:S(2)}) collective-permute-start(bf16[128,352]{0,1:T(8,128)(2,1)} %param.18), channel_id=1, source_target_pairs={{0,3},{1,0},{2,1},{3,2},{4,7},{5,4},{6,5},{7,6},{8,11},{9,8},{10,9... | collective-permute-start | bytes 270344 | tf_op jit(solution)/shard_map/ppermute | solution.py:33
  60.4 37.9 %collective-permute-start.16 = (bf16[176,1408]{1,0:T(8,128)(2,1)}, bf16[176,1408]{1,0:T(8,128)(2,1)}, u32[]{:S(2)}, u32[]{:S(2)}) collective-permute-start(bf16[176,1408]{1,0:T(8,128)(2,1)} %constant_dynamic-slice_fusion), channel_id=1, source_target_pairs={{0,1},{1,2},{2,3},{3,0},{4,5},{5,6},{6,7},{7,4},{8,9},{9,10},{10,1... | collective-permute-start | bytes 1486856 | tf_op jit(solution)/shard_map/ppermute | solution.py:33
  61.1 43.7 %collective-permute-start.17 = (bf16[176,1408]{1,0:T(8,128)(2,1)}, bf16[176,1408]{1,0:T(8,128)(2,1)}, u32[]{:S(2)}, u32[]{:S(2)}) collective-permute-start(bf16[176,1408]{1,0:T(8,128)(2,1)} %constant_dynamic-slice_fusion), channel_id=1, source_target_pairs={{0,3},{1,0},{2,1},{3,2},{4,7},{5,4},{6,5},{7,6},{8,11},{9,8},{10,9... | collective-permute-start | bytes 1486856 | tf_op jit(solution)/shard_map/ppermute | solution.py:33
  67.6 9.4 %collective-permute-start.4 = (bf16[16,1536]{1,0:T(8,128)(2,1)S(1)}, bf16[16,1536]{1,0:T(8,128)(2,1)S(1)}, u32[]{:S(2)}, u32[]{:S(2)}) collective-permute-start(bf16[16,1536]{1,0:T(8,128)(2,1)S(1)} %reduce_sum.12.r0_ref), channel_id=1, source_target_pairs={{0,1},{1,2},{2,3},{3,0},{4,5},{5,6},{6,7},{7,4},{8,9},{9,10},{10,1... | collective-permute-start | bytes 147464 | tf_op jit(solution)/shard_map/ppermute | solution.py:33
  68.4 8.6 %collective-permute-start.5 = (bf16[16,1536]{1,0:T(8,128)(2,1)S(1)}, bf16[16,1536]{1,0:T(8,128)(2,1)S(1)}, u32[]{:S(2)}, u32[]{:S(2)}) collective-permute-start(bf16[16,1536]{1,0:T(8,128)(2,1)S(1)} %reduce_sum.12.r0_ref), channel_id=1, source_target_pairs={{0,2},{1,3},{2,0},{3,1},{4,6},{5,7},{6,4},{7,5},{8,10},{9,11},{10,... | collective-permute-start | bytes 147464 | tf_op jit(solution)/shard_map/ppermute | solution.py:33
  70.2 7.4 %collective-permute-start.6 = (bf16[16,1536]{1,0:T(8,128)(2,1)S(1)}, bf16[16,1536]{1,0:T(8,128)(2,1)S(1)}, u32[]{:S(2)}, u32[]{:S(2)}) collective-permute-start(bf16[16,1536]{1,0:T(8,128)(2,1)S(1)} %reduce_sum.12.r0_ref), channel_id=1, source_target_pairs={{0,3},{1,0},{2,1},{3,2},{4,7},{5,4},{6,5},{7,6},{8,11},{9,8},{10,9... | collective-permute-start | bytes 147464 | tf_op jit(solution)/shard_map/ppermute | solution.py:33
  80.0 34.2 %copy-start.8 = (bf16[4,128,352]{1,2,0:T(8,128)(2,1)S(1)}, bf16[4,128,352]{1,2,0:T(8,128)(2,1)}, u32[]{:S(2)}) copy-start(bf16[4,128,352]{1,2,0:T(8,128)(2,1)} %copy-done.7) | copy-start | bytes 1081348
  80.0 25.4 %collective-permute-start.15 = (bf16[176,1408]{1,0:T(8,128)(2,1)}, bf16[176,1408]{1,0:T(8,128)(2,1)S(1)}, u32[]{:S(2)}, u32[]{:S(2)}) collective-permute-start(bf16[176,1408]{1,0:T(8,128)(2,1)} %constant_dynamic-slice_fusion), channel_id=1, source_target_pairs={{0,2},{1,3},{2,0},{3,1},{4,6},{5,7},{6,4},{7,5},{8,10},{9,11},{10,... | collective-permute-start | bytes 1486856 | tf_op jit(solution)/shard_map/ppermute | solution.py:33
  90.2 9.8 %collective-permute-start.10 = (bf16[4,2,88,128]{3,2,1,0:T(8,128)(2,1)S(1)}, bf16[4,2,88,128]{3,2,1,0:T(8,128)(2,1)S(1)}, u32[]{:S(2)}, u32[]{:S(2)}) collective-permute-start(bf16[4,2,88,128]{3,2,1,0:T(8,128)(2,1)S(1)} %slice.15), channel_id=1, source_target_pairs={{0,32},{32,64},{64,96},{96,128},{128,160},{160,192},{192,224},{1,3... | collective-permute-start | bytes 540680 | tf_op jit(solution)/shard_map/ppermute | solution.py:28
  93.7 11.1 %collective-permute-start.11 = (bf16[4,2,88,128]{3,2,1,0:T(8,128)(2,1)S(1)}, bf16[4,2,88,128]{3,2,1,0:T(8,128)(2,1)S(1)}, u32[]{:S(2)}, u32[]{:S(2)}) collective-permute-start(bf16[4,2,88,128]{3,2,1,0:T(8,128)(2,1)S(1)} %slice.15), channel_id=1, source_target_pairs={{0,64},{32,96},{64,128},{96,160},{128,192},{160,224},{1,65},{33,97... | collective-permute-start | bytes 540680 | tf_op jit(solution)/shard_map/ppermute | solution.py:28
  98.3 7.0 %collective-permute-start.12 = (bf16[4,2,88,128]{3,2,1,0:T(8,128)(2,1)S(1)}, bf16[4,2,88,128]{3,2,1,0:T(8,128)(2,1)S(1)}, u32[]{:S(2)}, u32[]{:S(2)}) collective-permute-start(bf16[4,2,88,128]{3,2,1,0:T(8,128)(2,1)S(1)} %slice.15), channel_id=1, source_target_pairs={{0,4},{4,0},{1,5},{5,1},{2,6},{6,2},{3,7},{7,3},{8,12},{12,8},{9,1... | collective-permute-start | bytes 540680 | tf_op jit(solution)/shard_map/ppermute | solution.py:33
  100.0 5.8 %collective-permute-start.13 = (bf16[4,2,88,128]{3,2,1,0:T(8,128)(2,1)S(1)}, bf16[4,2,88,128]{3,2,1,0:T(8,128)(2,1)S(1)}, u32[]{:S(2)}, u32[]{:S(2)}) collective-permute-start(bf16[4,2,88,128]{3,2,1,0:T(8,128)(2,1)S(1)} %collective-permute-done.10.near_ref), channel_id=1, source_target_pairs={{0,4},{4,0},{1,5},{5,1},{2,6},{6,2},{3,7},{7,3},{8,12},{12,8},{9,1... | collective-permute-start | bytes 540680 | tf_op jit(solution)/shard_map/ppermute | solution.py:33
  104.7 1.6 %collective-permute-start.14 = (bf16[4,2,88,128]{3,2,1,0:T(8,128)(2,1)S(1)}, bf16[4,2,88,128]{3,2,1,0:T(8,128)(2,1)S(1)}, u32[]{:S(2)}, u32[]{:S(2)}) collective-permute-start(bf16[4,2,88,128]{3,2,1,0:T(8,128)(2,1)S(1)} %collective-permute-done.11.far_ref), channel_id=1, source_target_pairs={{0,4},{4,0},{1,5},{5,1},{2,6},{6,2},{3,7},{7,3},{8,12},{12,8},{9,1... | collective-permute-start | bytes 540680 | tf_op jit(solution)/shard_map/ppermute | solution.py:33
  104.7 10.9 %collective-permute-start.19 = (bf16[176,1408]{1,0:T(8,128)(2,1)}, bf16[176,1408]{1,0:T(8,128)(2,1)S(1)}, u32[]{:S(2)}, u32[]{:S(2)}) collective-permute-start(bf16[176,1408]{1,0:T(8,128)(2,1)} %collective-permute-done.16.m1_ref), channel_id=1, source_target_pairs={{0,4},{4,0},{1,5},{5,1},{2,6},{6,2},{3,7},{7,3},{8,12},{12,8},{9,1... | collective-permute-start | bytes 1486856 | tf_op jit(solution)/shard_map/ppermute | solution.py:33
  105.3 10.4 %collective-permute-start.20 = (bf16[176,1408]{1,0:T(8,128)(2,1)}, bf16[176,1408]{1,0:T(8,128)(2,1)}, u32[]{:S(2)}, u32[]{:S(2)}) collective-permute-start(bf16[176,1408]{1,0:T(8,128)(2,1)} %collective-permute-done.17.m3_ref), channel_id=1, source_target_pairs={{0,4},{4,0},{1,5},{5,1},{2,6},{6,2},{3,7},{7,3},{8,12},{12,8},{9,1... | collective-permute-start | bytes 1486856 | tf_op jit(solution)/shard_map/ppermute | solution.py:33
  105.4 18.9 %collective-permute-start.18 = (bf16[176,1408]{1,0:T(8,128)(2,1)S(1)}, bf16[176,1408]{1,0:T(8,128)(2,1)}, u32[]{:S(2)}, u32[]{:S(2)}) collective-permute-start(bf16[176,1408]{1,0:T(8,128)(2,1)S(1)} %collective-permute-done.15.m2_ref), channel_id=1, source_target_pairs={{0,4},{4,0},{1,5},{5,1},{2,6},{6,2},{3,7},{7,3},{8,12},{12,8},{9,1... | collective-permute-start | bytes 1486856 | tf_op jit(solution)/shard_map/ppermute | solution.py:33
  110.6 13.6 %all-to-all-start.3 = ((bf16[16,88,128]{2,1,0:T(8,128)(2,1)}), bf16[16,88,128]{2,1,0:T(8,128)(2,1)S(1)}, u32[]{:S(2)}, u32[]{:S(2)}) async-start(bf16[16,88,128]{2,1,0:T(8,128)(2,1)} %bitcast.21), calls=%async_computation.3 | async-start | bytes 720896 | tf_op jit(solution)/shard_map/all_to_all | solution.py:362
  (9 other events, 117.2 us)

commit v10 on v9

--- a/solution.py
+++ b/solution.py
@@ -122,7 +122,7 @@
         rows_ref[y] = total.astype(BF)
 
 
-def select_kernel(place_ref, mine_ref, other_ref, routed_ref):
+def select_kernel(place_ref, mine_ref, other_ref, *routed_refs):
     wide = mine_ref.shape[2]
     width = wide - FACTS
     rows = jnp.concatenate(
@@ -133,9 +133,18 @@
     same_core = block - 2.0 * jnp.floor(block * 0.5) == place_ref[1].astype(F32)
     to = jnp.where(same_core & (there > 0.0), jnp.floor(block * 0.125), -1.0).astype(I32)
     source, target = iota((128, 128), 0), iota((128, 128), 1)
-    chosen = (to == target // 16) & (source % 16 == target % 16)
-    routed = dot(chosen.astype(BF), rows, (0, 0))
-    routed_ref[...] = routed.astype(BF).reshape(8, 16, wide)
+    plane = (place_ref[0] + target // 16) % 8
+    chosen = (to == plane) & (source % 16 == target % 16)
+    routed = dot(chosen.astype(BF), rows, (0, 0)).astype(BF)
+    for by, routed_ref in enumerate(routed_refs):
+        routed_ref[...] = routed[by * 16 : (by + 1) * 16]
+
+
+def join_kernel(*refs):
+    total = refs[0][...].astype(F32)
+    for ref in refs[1:-1]:
+        total = total + ref[...].astype(F32)
+    refs[-1][...] = total.astype(BF)
 
 
 def own_kernel(place_ref, picture_ref, share_ref, own_ref):
@@ -324,15 +333,15 @@
     got = lax.all_to_all(routed.reshape(16, 16, wide), ("y", "t"), 0, 0, tiled=True)
     got = call(sum_kernel, shape((4, 16, wide)), [VMEM])(got.reshape(4, 4, 16, wide))
     other = around(got, "c", 1)
-    routed = call(select_kernel, shape((8, 16, wide)), [SMEM, VMEM, VMEM])(place, got, other)
-    routed, text_out = lax.optimization_barrier((routed, text_out))
+    routed = call(select_kernel, [shape((16, wide))] * 8, [SMEM, VMEM, VMEM])(place, got, other)
+    *routed, text_out = lax.optimization_barrier((*routed, text_out))
     half = local_width // 2
     near_half = lax.dynamic_slice_in_dim(text_out, c * half, half, 0)
     near_half, tokens = lax.optimization_barrier((near_half, tokens))
     halves = [None] + [around(near_half, "t", by) for by in (1, 3)]
     pieces = [tokens] + [around(tokens, "t", by) for by in range(1, 4)]
-    got = lax.all_to_all(routed, "z", 0, 0, tiled=True)
-    got = jnp.sum(got.astype(F32), axis=0).astype(BF)
+    routed = [routed[0]] + [around(routed[by], "z", by) for by in range(1, 8)]
+    got = call(join_kernel, shape((16, wide)), [VMEM] * 8)(*routed)
     rows = [got] + [around(got, "t", by) for by in range(1, 4)]
     own_tokens = jnp.zeros((4, BLOCK, local_width), BF)
     for by, piece in enumerate(pieces):

time: 129 us -> 135 us (1.047)
  starting transfers between devices: 38.4 us -> 50.6 us
  blocking collectives: 28.4 us -> 19.3 us
  local copies, waits for them, and re-layouts: 12.9 us -> 16 us
  waiting for transfers between devices: 22.1 us -> 24 us
    ppermute x19 -> x26, starting transfers between devices: 18.6 us -> 34.3 us  [around(): return lax.ppermute(x, axis, [(i, (i + by) % count) for i in range(count)])]
    all_to_all x1 -> x0, blocking collectives: 9.11 us -> none  [local(): mine = lax.all_to_all(heads, 'y', 0, 0, tiled=True)]
    all_to_all x1, starting transfers between devices: 8.13 us -> 3.45 us  [local(): mine = lax.all_to_all(heads, 'y', 0, 0, tiled=True)]
    all_to_all x1, starting transfers between devices: 3.55 us -> 6.59 us  [local(): lax.all_to_all(sent.reshape(16, HEAD, BLOCK), ('t', 'y'), 0, 0, tiled=True)]
    ppermute x19 -> x26, waiting for transfers between devices: 5.37 us -> 7.6 us  [around(): return lax.ppermute(x, axis, [(i, (i + by) % count) for i in range(count)])]
    ppermute x2, starting transfers between devices: 8.08 us -> 6.25 us  [ahead(): return lax.ppermute(x, axis, [(i, i + by) for i in range(count - by)])]
    dynamic_update_slice x4, local copies, waits for them, and re-layouts: 1.84 us -> 3.46 us  [local(): lax.dynamic_update_index_in_dim(own_tokens, piece, (t - by) % 4, 0)]
    unnamed x20 -> x18, local copies, waits for them, and re-layouts: 4.22 us -> 4.21 us
  transfers between devices with their start and end apart: 23 -> 30, of which waited for: 9 -> 8; matrix products, arithmetic and copies ran while one was open for 8% -> 9% of each run, Pallas kernels for 7% -> 5%
where the time goes in v10:
time: 135 us; the launch traced here: 134 us
  starting transfers between devices  50.6 us (37%)
  waiting for transfers between devices  24 us (18%)
  Pallas kernels  22.3 us (17%)
  blocking collectives  19.3 us (14%)
  local copies, waits for them, and re-layouts  16 us (12%)
  between operations  1.59 us (1%)
    ppermute x26, starting transfers between devices, around(): return lax.ppermute(x, axis, [(i, (i + by) % count) for i in range(count)])  34.3 us
    all_to_all x1, blocking collectives, local(): lax.all_to_all(routed.reshape(16, 16, wide), ('y', 't'), 0, 0, tiled=True)  19.3 us
    ppermute x26, waiting for transfers between devices, around(): return lax.ppermute(x, axis, [(i, (i + by) % count) for i in range(count)])  7.6 us
    all_to_all x1, waiting for transfers between devices, local(): lax.all_to_all(sent.reshape(16, HEAD, BLOCK), ('t', 'y'), 0, 0, tiled=True)  7.25 us
    pallas_call x1, Pallas kernels, local(): call(vision_kernel, [shape((MERGED, width))] * 4, [SMEM, HBM, HBM, HBM],...  7.22 us
    all_to_all x1, starting transfers between devices, local(): lax.all_to_all(sent.reshape(16, HEAD, BLOCK), ('t', 'y'), 0, 0, tiled=True)  6.59 us
    ppermute x2, starting transfers between devices, ahead(): return lax.ppermute(x, axis, [(i, i + by) for i in range(count - by)])  6.25 us
    ppermute x2, waiting for transfers between devices, ahead(): return lax.ppermute(x, axis, [(i, i + by) for i in range(count - by)])  6.07 us
  transfers between devices with their start and end apart: 30, of which 8 were waited for; matrix products, arithmetic and copies ran while one was open for 9% of the time, Pallas kernels for 5%

profile of v10, /device:TPU:64, one launch (start us, length us, event | category | flops | bytes accessed | tf_op | source)
XLA Modules:
  0.0 133.9 jit_solution(2353578706047185013)
XLA Ops:
  0.0 7.2 %shard_map.109 = (bf16[64,1408]{1,0:T(8,128)(2,1)}, bf16[64,1408]{1,0:T(8,128)(2,1)}, bf16[64,1408]{1,0:T(8,128)(2,1)}, bf16[64,1408]{1,0:T(8,128)(2,1)}) custom-call(s32[1,2]{1,0:T(1,128)} %grid_ref.1, bf16[256,1408]{1,0:T(8,128)(2,1)} %bitcast.38, bf16[3,352,1408]{2,1,0:T(8,128)(2,1)} %bitcast.40, bf16[352,1408]{1,0:T(8,128)(2,1)} %out_hbm.1), custom_call_target="tpu_custom_call" | custom-call | tf_op jit(solution)/shard_map/pallas_call | solution.py:308
  7.2 1.6 %collective-permute-start = (bf16[64,1408]{1,0:T(8,128)(2,1)}, bf16[64,1408]{1,0:T(8,128)(2,1)S(1)}, u32[]{:S(2)}, u32[]{:S(2)}) collective-permute-start(bf16[64,1408]{1,0:T(8,128)(2,1)} %get-tuple-element.35), channel_id=1, source_target_pairs={{0,1},{1,2},{2,3},{3,0},{4,5},{5,6},{6,7},{7,4},{8,9},{9,10},{10,1... | collective-permute-start | bytes 540680 | tf_op jit(solution)/shard_map/ppermute | solution.py:33
  8.8 2.7 %collective-permute-start.1 = (bf16[64,1408]{1,0:T(8,128)(2,1)}, bf16[64,1408]{1,0:T(8,128)(2,1)}, u32[]{:S(2)}, u32[]{:S(2)}) collective-permute-start(bf16[64,1408]{1,0:T(8,128)(2,1)} %get-tuple-element.36), channel_id=1, source_target_pairs={{0,2},{1,3},{2,0},{3,1},{4,6},{5,7},{6,4},{7,5},{8,10},{9,11},{10,... | collective-permute-start | bytes 540680 | tf_op jit(solution)/shard_map/ppermute | solution.py:33
  22.0 2.0 %shard_map.111 = bf16[4,64,1536]{2,1,0:T(8,128)(2,1)S(1)} custom-call(s32[6]{0:T(128)S(1)} %pad_add_fusion.1.facts_ref, f32[64,1408]{1,0:T(8,128)S(1)} %shard_map.110.own_ref, bf16[64,1408]{1,0:T(8,128)(2,1)S(1)} %collective-permute-done.s1_ref, bf16[64,1408]{1,0:T(8,128)(2,1)} %collective-permute-done.1.s2_ref, ...), custom_call_target="tpu_custom_call" | custom-call | tf_op jit(solution)/shard_map/pallas_call | solution.py:329
  24.1 19.3 %all_to_all.15 = bf16[16,16,1536]{2,1,0:T(8,128)(2,1)S(1)} all-to-all(bf16[16,16,1536]{2,1,0:T(8,128)(2,1)S(1)} %bitcast.35), channel_id=1, replica_groups=mesh['z'=8,'y'=4,'c'=2,'t'=4] {'y','t'}, dimensions={0} | all-to-all | bytes 1572864 | tf_op jit(solution)/shard_map/all_to_all | solution.py:333
  46.1 1.9 %collective-permute-start.4 = (bf16[16,1536]{1,0:T(8,128)(2,1)S(1)}, bf16[16,1536]{1,0:T(8,128)(2,1)S(1)}, u32[]{:S(2)}, u32[]{:S(2)}) collective-permute-start(bf16[16,1536]{1,0:T(8,128)(2,1)S(1)} %get-tuple-element.48), channel_id=1, source_target_pairs={{0,32},{32,64},{64,96},{96,128},{128,160},{160,192},{192,224},{224... | collective-permute-start | bytes 147464 | tf_op jit(solution)/shard_map/ppermute | solution.py:33
  48.0 4.5 %collective-permute-start.5 = (bf16[16,1536]{1,0:T(8,128)(2,1)S(1)}, bf16[16,1536]{1,0:T(8,128)(2,1)S(1)}, u32[]{:S(2)}, u32[]{:S(2)}) collective-permute-start(bf16[16,1536]{1,0:T(8,128)(2,1)S(1)} %get-tuple-element.49), channel_id=1, source_target_pairs={{0,64},{32,96},{64,128},{96,160},{128,192},{160,224},{192,0},{224,... | collective-permute-start | bytes 147464 | tf_op jit(solution)/shard_map/ppermute | solution.py:33
  52.5 1.9 %constant_dynamic-slice_fusion = bf16[176,1408]{1,0:T(8,128)(2,1)} fusion(bf16[352,1408]{1,0:T(8,128)(2,1)} %w0_ref, s32[]{:T(128)S(6)} %select_n.55), kind=kLoop, calls=%fused_computation.7 | loop fusion | bytes 991236 | tf_op jit(solution)/shard_map/dynamic_slice | solution.py:339
  54.9 3.1 %collective-permute-start.6 = (bf16[16,1536]{1,0:T(8,128)(2,1)S(1)}, bf16[16,1536]{1,0:T(8,128)(2,1)S(1)}, u32[]{:S(2)}, u32[]{:S(2)}) collective-permute-start(bf16[16,1536]{1,0:T(8,128)(2,1)S(1)} %get-tuple-element.50), channel_id=1, source_target_pairs={{0,96},{32,128},{64,160},{96,192},{128,224},{160,0},{192,32},{224,... | collective-permute-start | bytes 147464 | tf_op jit(solution)/shard_map/ppermute | solution.py:33
  59.5 3.0 %collective-permute-start.8 = (bf16[16,1536]{1,0:T(8,128)(2,1)S(1)}, bf16[16,1536]{1,0:T(8,128)(2,1)S(1)}, u32[]{:S(2)}, u32[]{:S(2)}) collective-permute-start(bf16[16,1536]{1,0:T(8,128)(2,1)S(1)} %get-tuple-element.52), channel_id=1, source_target_pairs={{0,160},{32,192},{64,224},{96,0},{128,32},{160,64},{192,96},{224,1... | collective-permute-start | bytes 147464 | tf_op jit(solution)/shard_map/ppermute | solution.py:33
  66.1 1.7 %collective-permute-start.15 = (bf16[128,352]{0,1:T(8,128)(2,1)}, bf16[128,352]{0,1:T(8,128)(2,1)S(1)}, u32[]{:S(2)}, u32[]{:S(2)}) collective-permute-start(bf16[128,352]{0,1:T(8,128)(2,1)} %param.18), channel_id=1, source_target_pairs={{0,2},{1,3},{2,0},{3,1},{4,6},{5,7},{6,4},{7,5},{8,10},{9,11},{10,... | collective-permute-start | bytes 270344 | tf_op jit(solution)/shard_map/ppermute | solution.py:33
  70.8 3.8 %collective-permute-start.12 = (bf16[16,1536]{1,0:T(8,128)(2,1)S(1)}, bf16[16,1536]{1,0:T(8,128)(2,1)S(1)}, u32[]{:S(2)}, u32[]{:S(2)}) collective-permute-start(bf16[16,1536]{1,0:T(8,128)(2,1)S(1)} %shard_map.114.r0_ref), channel_id=1, source_target_pairs={{0,2},{1,3},{2,0},{3,1},{4,6},{5,7},{6,4},{7,5},{8,10},{9,11},{10,... | collective-permute-start | bytes 147464 | tf_op jit(solution)/shard_map/ppermute | solution.py:33
  78.7 2.4 %shard_map.115 = bf16[4,3,88,128]{3,2,1,0:T(8,128)(2,1)S(1)} custom-call(s32[3]{0:T(128)S(1)} %pad_add_fusion.place_ref.facts_ref, bf16[16,1536]{1,0:T(8,128)(2,1)S(1)} %shard_map.114.r0_ref, bf16[16,1536]{1,0:T(8,128)(2,1)S(1)} %collective-permute-done.11.r1_ref, bf16[16,1536]{1,0:T(8,128)(2,1)S(1)} %collective-permute-done.12.r2_ref, ...), custom_call_target="tpu_custom_call" | custom-call | tf_op jit(solution)/shard_map/pallas_call | solution.py:350
  81.8 3.4 %all-to-all-start.1 = ((bf16[4,3,88,128]{3,2,1,0:T(8,128)(2,1)}), bf16[4,3,88,128]{3,2,1,0:T(8,128)(2,1)S(1)}, u32[]{:S(2)}, u32[]{:S(2)}) async-start(bf16[4,3,88,128]{3,2,1,0:T(8,128)(2,1)} %copy-done.3), calls=%async_computation.1 | async-start | bytes 540672 | tf_op jit(solution)/shard_map/all_to_all | solution.py:357
  86.5 2.1 %collective-permute-start.24 = (bf16[176,1408]{1,0:T(8,128)(2,1)}, bf16[176,1408]{1,0:T(8,128)(2,1)S(1)}, u32[]{:S(2)}, u32[]{:S(2)}) collective-permute-start(bf16[176,1408]{1,0:T(8,128)(2,1)} %constant_dynamic-slice_fusion), channel_id=1, source_target_pairs={{0,3},{1,0},{2,1},{3,2},{4,7},{5,4},{6,5},{7,6},{8,11},{9,8},{10,9... | collective-permute-start | bytes 1486856 | tf_op jit(solution)/shard_map/ppermute | solution.py:33
  88.9 3.1 %all-to-all-done.1.own_ref = bf16[4,3,88,128]{3,2,1,0:T(8,128)(2,1)S(1)} async-done(((bf16[4,3,88,128]{3,2,1,0:T(8,128)(2,1)}), bf16[4,3,88,128]{3,2,1,0:T(8,128)(2,1)S(1)}, u32[]{:S(2)}, u32[]{:S(2)}) %all-to-all-start.1) | async-done | bytes 270368 | tf_op jit(solution)/shard_map/all_to_all | solution.py:357
  92.0 3.2 %collective-permute-start.17 = (bf16[4,2,88,128]{3,2,1,0:T(8,128)(2,1)S(1)}, bf16[4,2,88,128]{3,2,1,0:T(8,128)(2,1)S(1)}, u32[]{:S(2)}, u32[]{:S(2)}) collective-permute-start(bf16[4,2,88,128]{3,2,1,0:T(8,128)(2,1)S(1)} %slice.15), channel_id=1, source_target_pairs={{0,32},{32,64},{64,96},{96,128},{128,160},{160,192},{192,224},{1,3... | collective-permute-start | bytes 540680 | tf_op jit(solution)/shard_map/ppermute | solution.py:28
  95.3 3.0 %collective-permute-start.18 = (bf16[4,2,88,128]{3,2,1,0:T(8,128)(2,1)S(1)}, bf16[4,2,88,128]{3,2,1,0:T(8,128)(2,1)S(1)}, u32[]{:S(2)}, u32[]{:S(2)}) collective-permute-start(bf16[4,2,88,128]{3,2,1,0:T(8,128)(2,1)S(1)} %slice.15), channel_id=1, source_target_pairs={{0,64},{32,96},{64,128},{96,160},{128,192},{160,224},{1,65},{33,97... | collective-permute-start | bytes 540680 | tf_op jit(solution)/shard_map/ppermute | solution.py:28
  98.3 6.1 %collective-permute-done.17.near_ref = bf16[4,2,88,128]{3,2,1,0:T(8,128)(2,1)S(1)} collective-permute-done((bf16[4,2,88,128]{3,2,1,0:T(8,128)(2,1)S(1)}, bf16[4,2,88,128]{3,2,1,0:T(8,128)(2,1)S(1)}, u32[]{:S(2)}, u32[]{:S(2)}) %collective-permute-start.17) | collective-permute-done | bytes 180256 | tf_op jit(solution)/shard_map/ppermute | solution.py:28
  105.9 3.3 %collective-permute-done.23.m1_ref = bf16[176,1408]{1,0:T(8,128)(2,1)S(1)} collective-permute-done((bf16[176,1408]{1,0:T(8,128)(2,1)}, bf16[176,1408]{1,0:T(8,128)(2,1)S(1)}, u32[]{:S(2)}, u32[]{:S(2)}) %collective-permute-start.23) | collective-permute-done | bytes 495648 | tf_op jit(solution)/shard_map/ppermute | solution.py:33
  110.0 4.3 %shard_map.116 = bf16[4,4,88,128]{3,2,1,0:T(8,128)(2,1)} custom-call(s32[3]{0:T(128)S(1)} %pad_add_fusion.place_ref.facts_ref, s32[16]{0:T(128)S(1)} %copy-done.5, bf16[4,3,88,128]{3,2,1,0:T(8,128)(2,1)S(1)} %all-to-all-done.1.own_ref, bf16[4,2,88,128]{3,2,1,0:T(8,128)(2,1)S(1)} %collective-permute-done.17.near_ref, ...), custom_call_target="tpu_custom_call" | custom-call | tf_op jit(solution)/shard_map/pallas_call | solution.py:365
  114.3 6.6 %all-to-all-start.2 = ((bf16[16,88,128]{2,1,0:T(8,128)(2,1)}), bf16[16,88,128]{2,1,0:T(8,128)(2,1)S(1)}, u32[]{:S(2)}, u32[]{:S(2)}) async-start(bf16[16,88,128]{2,1,0:T(8,128)(2,1)} %bitcast.21), calls=%async_computation.2 | async-start | bytes 720896 | tf_op jit(solution)/shard_map/all_to_all | solution.py:371
  123.4 7.3 %all-to-all-done.2 = bf16[16,88,128]{2,1,0:T(8,128)(2,1)S(1)} async-done(((bf16[16,88,128]{2,1,0:T(8,128)(2,1)}), bf16[16,88,128]{2,1,0:T(8,128)(2,1)S(1)}, u32[]{:S(2)}, u32[]{:S(2)}) %all-to-all-start.2) | async-done | bytes 360480 | tf_op jit(solution)/shard_map/all_to_all | solution.py:371
  130.6 3.3 %shard_map.118 = bf16[128,1408]{1,0:T(8,128)(2,1)} custom-call(s32[3]{0:T(128)S(1)} %pad_add_fusion.place_ref.facts_ref, bf16[4,2,176,128]{3,2,1,0:T(8,128)(2,1)S(1)} %bitcast.37, bf16[352,1408]{1,0:T(8,128)(2,1)S(1)} %copy-done.2, bf16[176,1408]{1,0:T(8,128)(2,1)} %collective-permute-done.22.m2_ref, bf16[176,1408]{1,0:T(8,128)(2,1)S(1)} %collective-permute-done.23.m1_ref, ...), custom_call_target="tpu_custom_call" | custom-call | tf_op jit(solution)/shard_map/pallas_call | solution.py:372
  (81 shorter events, 31.6 us)
Async XLA Ops:
  7.2 13.5 %collective-permute-start = (bf16[64,1408]{1,0:T(8,128)(2,1)}, bf16[64,1408]{1,0:T(8,128)(2,1)S(1)}, u32[]{:S(2)}, u32[]{:S(2)}) collective-permute-start(bf16[64,1408]{1,0:T(8,128)(2,1)} %get-tuple-element.35), channel_id=1, source_target_pairs={{0,1},{1,2},{2,3},{3,0},{4,5},{5,6},{6,7},{7,4},{8,9},{9,10},{10,1... | collective-permute-start | bytes 540680 | tf_op jit(solution)/shard_map/ppermute | solution.py:33
  8.8 12.0 %collective-permute-start.1 = (bf16[64,1408]{1,0:T(8,128)(2,1)}, bf16[64,1408]{1,0:T(8,128)(2,1)}, u32[]{:S(2)}, u32[]{:S(2)}) collective-permute-start(bf16[64,1408]{1,0:T(8,128)(2,1)} %get-tuple-element.36), channel_id=1, source_target_pairs={{0,2},{1,3},{2,0},{3,1},{4,6},{5,7},{6,4},{7,5},{8,10},{9,11},{10,... | collective-permute-start | bytes 540680 | tf_op jit(solution)/shard_map/ppermute | solution.py:33
  11.5 9.3 %collective-permute-start.2 = (bf16[64,1408]{1,0:T(8,128)(2,1)}, bf16[64,1408]{1,0:T(8,128)(2,1)}, u32[]{:S(2)}, u32[]{:S(2)}) collective-permute-start(bf16[64,1408]{1,0:T(8,128)(2,1)} %get-tuple-element.37), channel_id=1, source_target_pairs={{0,3},{1,0},{2,1},{3,2},{4,7},{5,4},{6,5},{7,6},{8,11},{9,8},{10,9... | collective-permute-start | bytes 540680 | tf_op jit(solution)/shard_map/ppermute | solution.py:33
  45.9 12.2 %collective-permute-start.10 = (bf16[16,1536]{1,0:T(8,128)(2,1)S(1)}, bf16[16,1536]{1,0:T(8,128)(2,1)S(1)}, u32[]{:S(2)}, u32[]{:S(2)}) collective-permute-start(bf16[16,1536]{1,0:T(8,128)(2,1)S(1)} %get-tuple-element.54), channel_id=1, source_target_pairs={{0,224},{32,0},{64,32},{96,64},{128,96},{160,128},{192,160},{224,1... | collective-permute-start | bytes 147464 | tf_op jit(solution)/shard_map/ppermute | solution.py:33
  46.1 13.4 %collective-permute-start.4 = (bf16[16,1536]{1,0:T(8,128)(2,1)S(1)}, bf16[16,1536]{1,0:T(8,128)(2,1)S(1)}, u32[]{:S(2)}, u32[]{:S(2)}) collective-permute-start(bf16[16,1536]{1,0:T(8,128)(2,1)S(1)} %get-tuple-element.48), channel_id=1, source_target_pairs={{0,32},{32,64},{64,96},{96,128},{128,160},{160,192},{192,224},{224... | collective-permute-start | bytes 147464 | tf_op jit(solution)/shard_map/ppermute | solution.py:33
  48.0 14.5 %collective-permute-start.5 = (bf16[16,1536]{1,0:T(8,128)(2,1)S(1)}, bf16[16,1536]{1,0:T(8,128)(2,1)S(1)}, u32[]{:S(2)}, u32[]{:S(2)}) collective-permute-start(bf16[16,1536]{1,0:T(8,128)(2,1)S(1)} %get-tuple-element.49), channel_id=1, source_target_pairs={{0,64},{32,96},{64,128},{96,160},{128,192},{160,224},{192,0},{224,... | collective-permute-start | bytes 147464 | tf_op jit(solution)/shard_map/ppermute | solution.py:33
  54.4 20.3 %collective-permute-start.14 = (bf16[128,352]{0,1:T(8,128)(2,1)}, bf16[128,352]{0,1:T(8,128)(2,1)S(1)}, u32[]{:S(2)}, u32[]{:S(2)}) collective-permute-start(bf16[128,352]{0,1:T(8,128)(2,1)} %param.18), channel_id=1, source_target_pairs={{0,1},{1,2},{2,3},{3,0},{4,5},{5,6},{6,7},{7,4},{8,9},{9,10},{10,1... | collective-permute-start | bytes 270344 | tf_op jit(solution)/shard_map/ppermute | solution.py:33
  54.9 11.2 %collective-permute-start.6 = (bf16[16,1536]{1,0:T(8,128)(2,1)S(1)}, bf16[16,1536]{1,0:T(8,128)(2,1)S(1)}, u32[]{:S(2)}, u32[]{:S(2)}) collective-permute-start(bf16[16,1536]{1,0:T(8,128)(2,1)S(1)} %get-tuple-element.50), channel_id=1, source_target_pairs={{0,96},{32,128},{64,160},{96,192},{128,224},{160,0},{192,32},{224,... | collective-permute-start | bytes 147464 | tf_op jit(solution)/shard_map/ppermute | solution.py:33
  58.1 9.7 %collective-permute-start.7 = (bf16[16,1536]{1,0:T(8,128)(2,1)S(1)}, bf16[16,1536]{1,0:T(8,128)(2,1)S(1)}, u32[]{:S(2)}, u32[]{:S(2)}) collective-permute-start(bf16[16,1536]{1,0:T(8,128)(2,1)S(1)} %get-tuple-element.51), channel_id=1, source_target_pairs={{0,128},{32,160},{64,192},{96,224},{128,0},{160,32},{192,64},{224,... | collective-permute-start | bytes 147464 | tf_op jit(solution)/shard_map/ppermute | solution.py:33
  59.5 9.6 %collective-permute-start.8 = (bf16[16,1536]{1,0:T(8,128)(2,1)S(1)}, bf16[16,1536]{1,0:T(8,128)(2,1)S(1)}, u32[]{:S(2)}, u32[]{:S(2)}) collective-permute-start(bf16[16,1536]{1,0:T(8,128)(2,1)S(1)} %get-tuple-element.52), channel_id=1, source_target_pairs={{0,160},{32,192},{64,224},{96,0},{128,32},{160,64},{192,96},{224,1... | collective-permute-start | bytes 147464 | tf_op jit(solution)/shard_map/ppermute | solution.py:33
  62.6 7.8 %collective-permute-start.9 = (bf16[16,1536]{1,0:T(8,128)(2,1)S(1)}, bf16[16,1536]{1,0:T(8,128)(2,1)S(1)}, u32[]{:S(2)}, u32[]{:S(2)}) collective-permute-start(bf16[16,1536]{1,0:T(8,128)(2,1)S(1)} %get-tuple-element.53), channel_id=1, source_target_pairs={{0,192},{32,224},{64,0},{96,32},{128,64},{160,96},{192,128},{224,1... | collective-permute-start | bytes 147464 | tf_op jit(solution)/shard_map/ppermute | solution.py:33
  66.1 9.3 %collective-permute-start.15 = (bf16[128,352]{0,1:T(8,128)(2,1)}, bf16[128,352]{0,1:T(8,128)(2,1)S(1)}, u32[]{:S(2)}, u32[]{:S(2)}) collective-permute-start(bf16[128,352]{0,1:T(8,128)(2,1)} %param.18), channel_id=1, source_target_pairs={{0,2},{1,3},{2,0},{3,1},{4,6},{5,7},{6,4},{7,5},{8,10},{9,11},{10,... | collective-permute-start | bytes 270344 | tf_op jit(solution)/shard_map/ppermute | solution.py:33
  67.8 8.3 %collective-permute-start.16 = (bf16[128,352]{0,1:T(8,128)(2,1)}, bf16[128,352]{0,1:T(8,128)(2,1)S(1)}, u32[]{:S(2)}, u32[]{:S(2)}) collective-permute-start(bf16[128,352]{0,1:T(8,128)(2,1)} %param.18), channel_id=1, source_target_pairs={{0,3},{1,0},{2,1},{3,2},{4,7},{5,4},{6,5},{7,6},{8,11},{9,8},{10,9... | collective-permute-start | bytes 270344 | tf_op jit(solution)/shard_map/ppermute | solution.py:33
  70.4 7.5 %collective-permute-start.11 = (bf16[16,1536]{1,0:T(8,128)(2,1)S(1)}, bf16[16,1536]{1,0:T(8,128)(2,1)S(1)}, u32[]{:S(2)}, u32[]{:S(2)}) collective-permute-start(bf16[16,1536]{1,0:T(8,128)(2,1)S(1)} %shard_map.114.r0_ref), channel_id=1, source_target_pairs={{0,1},{1,2},{2,3},{3,0},{4,5},{5,6},{6,7},{7,4},{8,9},{9,10},{10,1... | collective-permute-start | bytes 147464 | tf_op jit(solution)/shard_map/ppermute | solution.py:33
  81.8 10.1 %all-to-all-start.1 = ((bf16[4,3,88,128]{3,2,1,0:T(8,128)(2,1)}), bf16[4,3,88,128]{3,2,1,0:T(8,128)(2,1)S(1)}, u32[]{:S(2)}, u32[]{:S(2)}) async-start(bf16[4,3,88,128]{3,2,1,0:T(8,128)(2,1)} %copy-done.3), calls=%async_computation.1 | async-start | bytes 540672 | tf_op jit(solution)/shard_map/all_to_all | solution.py:357
  85.3 23.9 %collective-permute-start.23 = (bf16[176,1408]{1,0:T(8,128)(2,1)}, bf16[176,1408]{1,0:T(8,128)(2,1)S(1)}, u32[]{:S(2)}, u32[]{:S(2)}) collective-permute-start(bf16[176,1408]{1,0:T(8,128)(2,1)} %constant_dynamic-slice_fusion), channel_id=1, source_target_pairs={{0,1},{1,2},{2,3},{3,0},{4,5},{5,6},{6,7},{7,4},{8,9},{9,10},{10,1... | collective-permute-start | bytes 1486856 | tf_op jit(solution)/shard_map/ppermute | solution.py:33
  86.5 22.7 %collective-permute-start.24 = (bf16[176,1408]{1,0:T(8,128)(2,1)}, bf16[176,1408]{1,0:T(8,128)(2,1)S(1)}, u32[]{:S(2)}, u32[]{:S(2)}) collective-permute-start(bf16[176,1408]{1,0:T(8,128)(2,1)} %constant_dynamic-slice_fusion), channel_id=1, source_target_pairs={{0,3},{1,0},{2,1},{3,2},{4,7},{5,4},{6,5},{7,6},{8,11},{9,8},{10,9... | collective-permute-start | bytes 1486856 | tf_op jit(solution)/shard_map/ppermute | solution.py:33
  88.6 21.1 %collective-permute-start.22 = (bf16[176,1408]{1,0:T(8,128)(2,1)}, bf16[176,1408]{1,0:T(8,128)(2,1)}, u32[]{:S(2)}, u32[]{:S(2)}) collective-permute-start(bf16[176,1408]{1,0:T(8,128)(2,1)} %constant_dynamic-slice_fusion), channel_id=1, source_target_pairs={{0,2},{1,3},{2,0},{3,1},{4,6},{5,7},{6,4},{7,5},{8,10},{9,11},{10,... | collective-permute-start | bytes 1486856 | tf_op jit(solution)/shard_map/ppermute | solution.py:33
  92.0 12.3 %collective-permute-start.17 = (bf16[4,2,88,128]{3,2,1,0:T(8,128)(2,1)S(1)}, bf16[4,2,88,128]{3,2,1,0:T(8,128)(2,1)S(1)}, u32[]{:S(2)}, u32[]{:S(2)}) collective-permute-start(bf16[4,2,88,128]{3,2,1,0:T(8,128)(2,1)S(1)} %slice.15), channel_id=1, source_target_pairs={{0,32},{32,64},{64,96},{96,128},{128,160},{160,192},{192,224},{1,3... | collective-permute-start | bytes 540680 | tf_op jit(solution)/shard_map/ppermute | solution.py:28
  95.3 9.1 %collective-permute-start.18 = (bf16[4,2,88,128]{3,2,1,0:T(8,128)(2,1)S(1)}, bf16[4,2,88,128]{3,2,1,0:T(8,128)(2,1)S(1)}, u32[]{:S(2)}, u32[]{:S(2)}) collective-permute-start(bf16[4,2,88,128]{3,2,1,0:T(8,128)(2,1)S(1)} %slice.15), channel_id=1, source_target_pairs={{0,64},{32,96},{64,128},{96,160},{128,192},{160,224},{1,65},{33,97... | collective-permute-start | bytes 540680 | tf_op jit(solution)/shard_map/ppermute | solution.py:28
  109.2 14.1 %collective-permute-start.26 = (bf16[176,1408]{1,0:T(8,128)(2,1)S(1)}, bf16[176,1408]{1,0:T(8,128)(2,1)}, u32[]{:S(2)}, u32[]{:S(2)}) collective-permute-start(bf16[176,1408]{1,0:T(8,128)(2,1)S(1)} %collective-permute-done.23.m1_ref), channel_id=1, source_target_pairs={{0,4},{4,0},{1,5},{5,1},{2,6},{6,2},{3,7},{7,3},{8,12},{12,8},{9,1... | collective-permute-start | bytes 1486856 | tf_op jit(solution)/shard_map/ppermute | solution.py:33
  109.2 14.1 %collective-permute-start.27 = (bf16[176,1408]{1,0:T(8,128)(2,1)S(1)}, bf16[176,1408]{1,0:T(8,128)(2,1)}, u32[]{:S(2)}, u32[]{:S(2)}) collective-permute-start(bf16[176,1408]{1,0:T(8,128)(2,1)S(1)} %collective-permute-done.24.m3_ref), channel_id=1, source_target_pairs={{0,4},{4,0},{1,5},{5,1},{2,6},{6,2},{3,7},{7,3},{8,12},{12,8},{9,1... | collective-permute-start | bytes 1486856 | tf_op jit(solution)/shard_map/ppermute | solution.py:33
  109.7 20.9 %collective-permute-start.25 = (bf16[176,1408]{1,0:T(8,128)(2,1)}, bf16[176,1408]{1,0:T(8,128)(2,1)}, u32[]{:S(2)}, u32[]{:S(2)}) collective-permute-start(bf16[176,1408]{1,0:T(8,128)(2,1)} %collective-permute-done.22.m2_ref), channel_id=1, source_target_pairs={{0,4},{4,0},{1,5},{5,1},{2,6},{6,2},{3,7},{7,3},{8,12},{12,8},{9,1... | collective-permute-start | bytes 1486856 | tf_op jit(solution)/shard_map/ppermute | solution.py:33
  114.3 16.3 %all-to-all-start.2 = ((bf16[16,88,128]{2,1,0:T(8,128)(2,1)}), bf16[16,88,128]{2,1,0:T(8,128)(2,1)S(1)}, u32[]{:S(2)}, u32[]{:S(2)}) async-start(bf16[16,88,128]{2,1,0:T(8,128)(2,1)} %bitcast.21), calls=%async_computation.2 | async-start | bytes 720896 | tf_op jit(solution)/shard_map/all_to_all | solution.py:371
  (15 other events, 160.8 us)

commit v11 on v9

--- a/solution.py
+++ b/solution.py
@@ -122,6 +122,13 @@
         rows_ref[y] = total.astype(BF)
 
 
+def join_kernel(parts_ref, rows_ref):
+    total = parts_ref[0].astype(F32)
+    for part in range(1, 8):
+        total = total + parts_ref[part].astype(F32)
+    rows_ref[...] = total.astype(BF)
+
+
 def select_kernel(place_ref, mine_ref, other_ref, routed_ref):
     wide = mine_ref.shape[2]
     width = wide - FACTS
@@ -138,11 +145,19 @@
     routed_ref[...] = routed.astype(BF).reshape(8, 16, wide)
 
 
-def own_kernel(place_ref, picture_ref, share_ref, own_ref):
+def own_kernel(
+    place_ref, grid_ref, block_ref, offset_ref, picture_ref, share_ref, own_ref, facts_ref
+):
+    t, block = place_ref[2], block_ref[0]
     count = picture_ref.shape[0]
-    row = iota((MERGED, count), 0) + place_ref[2] * MERGED
+    row = iota((MERGED, count), 0) + t * MERGED
     chosen = (slot_of(row) == iota((MERGED, count), 1)).astype(BF)
     own_ref[...] = dot(chosen, picture_ref[...], (1, 0)) + share_ref[...].astype(F32)
+    lane, line = iota((8, FACTS), 1), iota((8, FACTS), 0)
+    facts = jnp.zeros((8, FACTS), I32)
+    for index, fact in enumerate((block, offset_ref[0], grid_ref[0, 0], grid_ref[0, 1], 1)):
+        facts = jnp.where((lane == index) & (t == 0), fact, facts)
+    facts_ref[...] = jnp.where(line == 0, facts, block % 8 // 2).astype(F32)
 
 
 def merge_kernel(facts_ref, own_ref, s1_ref, s2_ref, s3_ref, w0_ref, w1_ref, w2_ref, rows_ref):
@@ -157,13 +172,10 @@
         merged = merged + dot(normed[:, first : first + deep], weight[...], (1, 0))
         first = first + deep
     merged = merged.astype(BF)
-    lane = iota((MERGED, FACTS), 1)
-    facts = jnp.zeros((MERGED, FACTS), I32)
-    for index in range(5):
-        facts = jnp.where(lane == index, facts_ref[index], facts)
-    facts = facts.astype(F32).astype(BF)
+    facts = jnp.broadcast_to(facts_ref[0:1, :], (MERGED, FACTS)).astype(BF)
+    to_y = facts_ref[1:2, 0:1]
     for y in range(4):
-        here = facts_ref[5] == y
+        here = to_y == float(y)
         rows_ref[y, :, :width] = jnp.where(here, merged, jnp.zeros_like(merged))
         rows_ref[y, :, width:] = jnp.where(here, facts, jnp.zeros_like(facts))
 
@@ -293,7 +305,6 @@
     c = lax.axis_index("c")
     t = lax.axis_index("t")
     picture = patches[0]
-    block = picture_block[0]
 
     place = jnp.stack([z, c, t]).astype(I32)
     share = call(
@@ -309,15 +320,15 @@
         limit=60,
     )(picture_grid, picture, vision_qkv.transpose(1, 2, 0), vision_out)
     shares = [around(share[by], "t", by) for by in range(1, 4)]
-    own = call(own_kernel, shape((MERGED, width), F32), [SMEM, VMEM, VMEM], flops=8 * 10**9)(
-        place, picture, share[0]
-    )
+    own, facts = call(
+        own_kernel,
+        [shape((MERGED, width), F32), shape((8, FACTS), F32)],
+        [SMEM] * 4 + [VMEM] * 2,
+        flops=8 * 10**9,
+    )(place, picture_grid, picture_block, picture_offset, picture, share[0])
     own, merge_weight = lax.optimization_barrier((own, merge_weight))
     merge_parts = jnp.split(merge_weight[0], [640, 1024], axis=0)
-    facts = jnp.stack([block, picture_offset[0], picture_grid[0, 0], picture_grid[0, 1], 1])
-    facts = jnp.where(t == 0, facts, 0)
-    facts = jnp.concatenate([facts, (block % 8 // 2)[None]]).astype(I32)
-    routed = call(merge_kernel, shape((4, MERGED, wide)), [SMEM] + [VMEM] * 7)(
+    routed = call(merge_kernel, shape((4, MERGED, wide)), [VMEM] * 8)(
         facts, own, *shares, *merge_parts
     )
 
@@ -332,7 +343,7 @@
     halves = [None] + [around(near_half, "t", by) for by in (1, 3)]
     pieces = [tokens] + [around(tokens, "t", by) for by in range(1, 4)]
     got = lax.all_to_all(routed, "z", 0, 0, tiled=True)
-    got = jnp.sum(got.astype(F32), axis=0).astype(BF)
+    got = call(join_kernel, shape((16, wide)), [VMEM])(got)
     rows = [got] + [around(got, "t", by) for by in range(1, 4)]
     own_tokens = jnp.zeros((4, BLOCK, local_width), BF)
     for by, piece in enumerate(pieces):

time: 129 us -> 127 us (0.984)
    dynamic_update_slice x4, local copies, waits for them, and re-layouts: 1.84 us -> 4.35 us  [local(): lax.dynamic_update_index_in_dim(own_tokens, piece, (t - by) % 4, 0)]
    ppermute x19, waiting for transfers between devices: 5.37 us -> 7.5 us  [around(): return lax.ppermute(x, axis, [(i, (i + by) % count) for i in range(count)])]
    unnamed x20 -> x14, local copies, waits for them, and re-layouts: 4.22 us -> 2.25 us
    all_to_all x1, waiting for transfers between devices: 1.79 us -> 0.01 us  [local(): got = lax.all_to_all(routed, 'z', 0, 0, tiled=True)]
    another operation x1 -> x0, local copies, waits for them, and re-layouts: 1.39 us -> none  [local(): jnp.stack([block, picture_offset[0], picture_grid[0, 0], picture_grid[0,...]
    pallas_call x2 -> x3, Pallas kernels: 2.83 us -> 1.88 us  [the longest x1 1.02 us: local(): call(merge_kernel, shape((4, MERGED, wide)), [VMEM] * 8)]
  transfers between devices with their start and end apart: 23 -> 23, of which waited for: 9 -> 8; matrix products, arithmetic and copies ran while one was open for 8% -> 8% of each run, Pallas kernels for 7% -> 7%
where the time goes in v11:
time: 127 us; the launch traced here: 125 us
  starting transfers between devices  38.8 us (31%)
  blocking collectives  29.2 us (23%)
  Pallas kernels  22.6 us (18%)
  waiting for transfers between devices  21.2 us (17%)
  local copies, waits for them, and re-layouts  12.1 us (10%)
  between operations  1.57 us (1%)
    all_to_all x1, blocking collectives, local(): lax.all_to_all(routed.reshape(16, 16, wide), ('y', 't'), 0, 0, tiled=True)  20.1 us
    ppermute x19, starting transfers between devices, around(): return lax.ppermute(x, axis, [(i, (i + by) % count) for i in range(count)])  19 us
    all_to_all x1, blocking collectives, local(): mine = lax.all_to_all(heads, 'y', 0, 0, tiled=True)  9.11 us
    all_to_all x1, starting transfers between devices, local(): got = lax.all_to_all(routed, 'z', 0, 0, tiled=True)  8.12 us
    ppermute x2, starting transfers between devices, ahead(): return lax.ppermute(x, axis, [(i, i + by) for i in range(count - by)])  8.08 us
    ppermute x19, waiting for transfers between devices, around(): return lax.ppermute(x, axis, [(i, (i + by) % count) for i in range(count)])  7.5 us
    all_to_all x1, waiting for transfers between devices, local(): lax.all_to_all(sent.reshape(16, HEAD, BLOCK), ('t', 'y'), 0, 0, tiled=True)  7.32 us
    pallas_call x1, Pallas kernels, local(): call(vision_kernel, [shape((MERGED, width))] * 4, [SMEM, HBM, HBM, HBM],...  7.22 us
  transfers between devices with their start and end apart: 23, of which 8 were waited for; matrix products, arithmetic and copies ran while one was open for 8% of the time, Pallas kernels for 7%

profile of v11, /device:TPU:64, one launch (start us, length us, event | category | flops | bytes accessed | tf_op | source)
XLA Modules:
  0.0 125.5 jit_solution(17506828027405503424)
XLA Ops:
  0.0 7.2 %shard_map.109 = (bf16[64,1408]{1,0:T(8,128)(2,1)}, bf16[64,1408]{1,0:T(8,128)(2,1)}, bf16[64,1408]{1,0:T(8,128)(2,1)}, bf16[64,1408]{1,0:T(8,128)(2,1)}) custom-call(s32[1,2]{1,0:T(1,128)} %grid_ref.3, bf16[256,1408]{1,0:T(8,128)(2,1)} %bitcast.31, bf16[3,352,1408]{2,1,0:T(8,128)(2,1)} %bitcast.33, bf16[352,1408]{1,0:T(8,128)(2,1)} %out_hbm.1), custom_call_target="tpu_custom_call" | custom-call | tf_op jit(solution)/shard_map/pallas_call | solution.py:310
  7.2 1.6 %collective-permute-start = (bf16[64,1408]{1,0:T(8,128)(2,1)}, bf16[64,1408]{1,0:T(8,128)(2,1)S(1)}, u32[]{:S(2)}, u32[]{:S(2)}) collective-permute-start(bf16[64,1408]{1,0:T(8,128)(2,1)} %get-tuple-element.24), channel_id=1, source_target_pairs={{0,1},{1,2},{2,3},{3,0},{4,5},{5,6},{6,7},{7,4},{8,9},{9,10},{10,1... | collective-permute-start | bytes 540680 | tf_op jit(solution)/shard_map/ppermute | solution.py:33
  8.8 2.7 %collective-permute-start.1 = (bf16[64,1408]{1,0:T(8,128)(2,1)}, bf16[64,1408]{1,0:T(8,128)(2,1)S(1)}, u32[]{:S(2)}, u32[]{:S(2)}) collective-permute-start(bf16[64,1408]{1,0:T(8,128)(2,1)} %get-tuple-element.25), channel_id=1, source_target_pairs={{0,2},{1,3},{2,0},{3,1},{4,6},{5,7},{6,4},{7,5},{8,10},{9,11},{10,... | collective-permute-start | bytes 540680 | tf_op jit(solution)/shard_map/ppermute | solution.py:33
  17.7 2.2 %collective-permute-done.1.s2_ref = bf16[64,1408]{1,0:T(8,128)(2,1)S(1)} collective-permute-done((bf16[64,1408]{1,0:T(8,128)(2,1)}, bf16[64,1408]{1,0:T(8,128)(2,1)S(1)}, u32[]{:S(2)}, u32[]{:S(2)}) %collective-permute-start.1) | collective-permute-done | bytes 180256 | tf_op jit(solution)/shard_map/ppermute | solution.py:33
  20.9 20.1 %all_to_all.20 = bf16[16,16,1536]{2,1,0:T(8,128)(2,1)S(1)} all-to-all(bf16[16,16,1536]{2,1,0:T(8,128)(2,1)S(1)} %bitcast.27), channel_id=1, replica_groups=mesh['z'=8,'y'=4,'c'=2,'t'=4] {'y','t'}, dimensions={0} | all-to-all | bytes 1572864 | tf_op jit(solution)/shard_map/all_to_all | solution.py:335
  42.6 1.7 %shard_map.113 = bf16[8,16,1536]{2,1,0:T(8,128)(2,1)} custom-call(s32[3]{0:T(128)S(1)} %pad_add_fusion.place_ref.facts_ref, bf16[4,16,1536]{2,1,0:T(8,128)(2,1)S(1)} %shard_map.112.mine_ref, bf16[4,16,1536]{2,1,0:T(8,128)(2,1)S(1)} %collective-permute-done.3.other_ref), custom_call_target="tpu_custom_call" | custom-call | tf_op jit(solution)/shard_map/pallas_call | solution.py:338
  44.4 8.1 %all-to-all-start.1 = ((bf16[8,16,1536]{2,1,0:T(8,128)(2,1)}), bf16[8,16,1536]{2,1,0:T(8,128)(2,1)S(1)}, u32[]{:S(2)}, u32[]{:S(2)}) async-start(bf16[8,16,1536]{2,1,0:T(8,128)(2,1)} %shard_map.113), calls=%async_computation.1 | async-start | bytes 786432 | tf_op jit(solution)/shard_map/all_to_all | solution.py:345
  52.5 2.0 %constant_dynamic-slice_fusion = bf16[176,1408]{1,0:T(8,128)(2,1)} fusion(bf16[352,1408]{1,0:T(8,128)(2,1)} %w0_ref, s32[]{:T(128)S(6)} %select_n.35), kind=kLoop, calls=%fused_computation.7 | loop fusion | bytes 991236 | tf_op jit(solution)/shard_map/dynamic_slice | solution.py:341
  55.1 1.7 %collective-permute-start.8 = (bf16[128,352]{0,1:T(8,128)(2,1)}, bf16[128,352]{0,1:T(8,128)(2,1)S(1)}, u32[]{:S(2)}, u32[]{:S(2)}) collective-permute-start(bf16[128,352]{0,1:T(8,128)(2,1)} %param.18), channel_id=1, source_target_pairs={{0,2},{1,3},{2,0},{3,1},{4,6},{5,7},{6,4},{7,5},{8,10},{9,11},{10,... | collective-permute-start | bytes 270344 | tf_op jit(solution)/shard_map/ppermute | solution.py:33
  58.8 2.5 %collective-permute-start.17 = (bf16[176,1408]{1,0:T(8,128)(2,1)}, bf16[176,1408]{1,0:T(8,128)(2,1)}, u32[]{:S(2)}, u32[]{:S(2)}) collective-permute-start(bf16[176,1408]{1,0:T(8,128)(2,1)} %constant_dynamic-slice_fusion), channel_id=1, source_target_pairs={{0,3},{1,0},{2,1},{3,2},{4,7},{5,4},{6,5},{7,6},{8,11},{9,8},{10,9... | collective-permute-start | bytes 1486856 | tf_op jit(solution)/shard_map/ppermute | solution.py:33
  65.3 2.2 %collective-permute-start.5 = (bf16[16,1536]{1,0:T(8,128)(2,1)S(1)}, bf16[16,1536]{1,0:T(8,128)(2,1)S(1)}, u32[]{:S(2)}, u32[]{:S(2)}) collective-permute-start(bf16[16,1536]{1,0:T(8,128)(2,1)S(1)} %shard_map.114.r0_ref), channel_id=1, source_target_pairs={{0,2},{1,3},{2,0},{3,1},{4,6},{5,7},{6,4},{7,5},{8,10},{9,11},{10,... | collective-permute-start | bytes 147464 | tf_op jit(solution)/shard_map/ppermute | solution.py:33
  67.4 1.8 %collective-permute-start.6 = (bf16[16,1536]{1,0:T(8,128)(2,1)S(1)}, bf16[16,1536]{1,0:T(8,128)(2,1)}, u32[]{:S(2)}, u32[]{:S(2)}) collective-permute-start(bf16[16,1536]{1,0:T(8,128)(2,1)S(1)} %shard_map.114.r0_ref), channel_id=1, source_target_pairs={{0,3},{1,0},{2,1},{3,2},{4,7},{5,4},{6,5},{7,6},{8,11},{9,8},{10,9... | collective-permute-start | bytes 147464 | tf_op jit(solution)/shard_map/ppermute | solution.py:33
  69.3 1.5 %bitcast_dynamic-update-slice_fusion = bf16[4,128,352]{1,2,0:T(8,128)(2,1)} fusion(bf16[4,128,352]{1,2,0:T(8,128)(2,1)} %bitcast_dynamic-update-slice_fusion.1, s32[]{:T(128)S(6)} %select_n.43, bf16[128,352]{0,1:T(8,128)(2,1)} %collective-permute-done.9), kind=kLoop, calls=%fused_computation.3 | loop fusion | bytes 180228 | tf_op jit(solution)/shard_map/jit(dynamic_update_index_in_dim)/dynamic_update_slice | solution.py:350
  72.0 2.7 %collective-permute-done.4.r1_ref = bf16[16,1536]{1,0:T(8,128)(2,1)S(1)} collective-permute-done((bf16[16,1536]{1,0:T(8,128)(2,1)S(1)}, bf16[16,1536]{1,0:T(8,128)(2,1)S(1)}, u32[]{:S(2)}, u32[]{:S(2)}) %collective-permute-start.4) | collective-permute-done | bytes 49184 | tf_op jit(solution)/shard_map/ppermute | solution.py:33
  75.4 2.6 %shard_map.115 = bf16[4,3,88,128]{3,2,1,0:T(8,128)(2,1)S(1)} custom-call(s32[3]{0:T(128)S(1)} %pad_add_fusion.place_ref.facts_ref, bf16[16,1536]{1,0:T(8,128)(2,1)S(1)} %shard_map.114.r0_ref, bf16[16,1536]{1,0:T(8,128)(2,1)S(1)} %collective-permute-done.4.r1_ref, bf16[16,1536]{1,0:T(8,128)(2,1)S(1)} %collective-permute-done.5.r2_ref, ...), custom_call_target="tpu_custom_call" | custom-call | tf_op jit(solution)/shard_map/pallas_call | solution.py:352
  79.1 9.1 %all_to_all.21.own_ref = bf16[4,3,88,128]{3,2,1,0:T(8,128)(2,1)S(1)} all-to-all(bf16[4,3,88,128]{3,2,1,0:T(8,128)(2,1)S(1)} %shard_map.115), channel_id=1, replica_groups=mesh['z'=8,'y'=4,'c'=2,'t'=4] {'y'}, dimensions={0} | all-to-all | bytes 540672 | tf_op jit(solution)/shard_map/all_to_all | solution.py:359
  88.2 3.5 %collective-permute-start.10 = (bf16[4,2,88,128]{3,2,1,0:T(8,128)(2,1)S(1)}, bf16[4,2,88,128]{3,2,1,0:T(8,128)(2,1)S(1)}, u32[]{:S(2)}, u32[]{:S(2)}) collective-permute-start(bf16[4,2,88,128]{3,2,1,0:T(8,128)(2,1)S(1)} %slice.7), channel_id=1, source_target_pairs={{0,32},{32,64},{64,96},{96,128},{128,160},{160,192},{192,224},{1,3... | collective-permute-start | bytes 540680 | tf_op jit(solution)/shard_map/ppermute | solution.py:28
  91.7 4.6 %collective-permute-start.11 = (bf16[4,2,88,128]{3,2,1,0:T(8,128)(2,1)S(1)}, bf16[4,2,88,128]{3,2,1,0:T(8,128)(2,1)S(1)}, u32[]{:S(2)}, u32[]{:S(2)}) collective-permute-start(bf16[4,2,88,128]{3,2,1,0:T(8,128)(2,1)S(1)} %slice.7), channel_id=1, source_target_pairs={{0,64},{32,96},{64,128},{96,160},{128,192},{160,224},{1,65},{33,97... | collective-permute-start | bytes 540680 | tf_op jit(solution)/shard_map/ppermute | solution.py:28
  96.4 3.6 %collective-permute-done.10.near_ref = bf16[4,2,88,128]{3,2,1,0:T(8,128)(2,1)S(1)} collective-permute-done((bf16[4,2,88,128]{3,2,1,0:T(8,128)(2,1)S(1)}, bf16[4,2,88,128]{3,2,1,0:T(8,128)(2,1)S(1)}, u32[]{:S(2)}, u32[]{:S(2)}) %collective-permute-start.10) | collective-permute-done | bytes 180256 | tf_op jit(solution)/shard_map/ppermute | solution.py:28
  100.0 2.7 %collective-permute-done.11.far_ref = bf16[4,2,88,128]{3,2,1,0:T(8,128)(2,1)S(1)} collective-permute-done((bf16[4,2,88,128]{3,2,1,0:T(8,128)(2,1)S(1)}, bf16[4,2,88,128]{3,2,1,0:T(8,128)(2,1)S(1)}, u32[]{:S(2)}, u32[]{:S(2)}) %collective-permute-start.11) | collective-permute-done | bytes 180256 | tf_op jit(solution)/shard_map/ppermute | solution.py:28
  104.4 4.3 %shard_map.116 = bf16[4,4,88,128]{3,2,1,0:T(8,128)(2,1)} custom-call(s32[3]{0:T(128)S(1)} %pad_add_fusion.place_ref.facts_ref, s32[16]{0:T(128)S(1)} %copy-done.4, bf16[4,3,88,128]{3,2,1,0:T(8,128)(2,1)S(1)} %all_to_all.21.own_ref, bf16[4,2,88,128]{3,2,1,0:T(8,128)(2,1)S(1)} %collective-permute-done.10.near_ref, ...), custom_call_target="tpu_custom_call" | custom-call | tf_op jit(solution)/shard_map/pallas_call | solution.py:367
  108.6 3.5 %all-to-all-start.3 = ((bf16[16,88,128]{2,1,0:T(8,128)(2,1)}), bf16[16,88,128]{2,1,0:T(8,128)(2,1)S(1)}, u32[]{:S(2)}, u32[]{:S(2)}) async-start(bf16[16,88,128]{2,1,0:T(8,128)(2,1)} %bitcast.17), calls=%async_computation.3 | async-start | bytes 720896 | tf_op jit(solution)/shard_map/all_to_all | solution.py:373
  114.9 7.3 %all-to-all-done.3 = bf16[16,88,128]{2,1,0:T(8,128)(2,1)S(1)} async-done(((bf16[16,88,128]{2,1,0:T(8,128)(2,1)}), bf16[16,88,128]{2,1,0:T(8,128)(2,1)S(1)}, u32[]{:S(2)}, u32[]{:S(2)}) %all-to-all-start.3) | async-done | bytes 360480 | tf_op jit(solution)/shard_map/all_to_all | solution.py:373
  122.2 3.3 %shard_map.118 = bf16[128,1408]{1,0:T(8,128)(2,1)} custom-call(s32[3]{0:T(128)S(1)} %pad_add_fusion.place_ref.facts_ref, bf16[4,2,176,128]{3,2,1,0:T(8,128)(2,1)S(1)} %bitcast.30, bf16[352,1408]{1,0:T(8,128)(2,1)S(1)} %copy-done.1, bf16[176,1408]{1,0:T(8,128)(2,1)S(1)} %collective-permute-done.15.m2_ref, bf16[176,1408]{1,0:T(8,128)(2,1)} %collective-permute-done.16.m1_ref, ...), custom_call_target="tpu_custom_call" | custom-call | tf_op jit(solution)/shard_map/pallas_call | solution.py:374
  (60 shorter events, 21.2 us)
Async XLA Ops:
  7.2 10.5 %collective-permute-start = (bf16[64,1408]{1,0:T(8,128)(2,1)}, bf16[64,1408]{1,0:T(8,128)(2,1)S(1)}, u32[]{:S(2)}, u32[]{:S(2)}) collective-permute-start(bf16[64,1408]{1,0:T(8,128)(2,1)} %get-tuple-element.24), channel_id=1, source_target_pairs={{0,1},{1,2},{2,3},{3,0},{4,5},{5,6},{6,7},{7,4},{8,9},{9,10},{10,1... | collective-permute-start | bytes 540680 | tf_op jit(solution)/shard_map/ppermute | solution.py:33
  8.8 11.1 %collective-permute-start.1 = (bf16[64,1408]{1,0:T(8,128)(2,1)}, bf16[64,1408]{1,0:T(8,128)(2,1)S(1)}, u32[]{:S(2)}, u32[]{:S(2)}) collective-permute-start(bf16[64,1408]{1,0:T(8,128)(2,1)} %get-tuple-element.25), channel_id=1, source_target_pairs={{0,2},{1,3},{2,0},{3,1},{4,6},{5,7},{6,4},{7,5},{8,10},{9,11},{10,... | collective-permute-start | bytes 540680 | tf_op jit(solution)/shard_map/ppermute | solution.py:33
  11.5 8.3 %collective-permute-start.2 = (bf16[64,1408]{1,0:T(8,128)(2,1)}, bf16[64,1408]{1,0:T(8,128)(2,1)S(1)}, u32[]{:S(2)}, u32[]{:S(2)}) collective-permute-start(bf16[64,1408]{1,0:T(8,128)(2,1)} %get-tuple-element.26), channel_id=1, source_target_pairs={{0,3},{1,0},{2,1},{3,2},{4,7},{5,4},{6,5},{7,6},{8,11},{9,8},{10,9... | collective-permute-start | bytes 540680 | tf_op jit(solution)/shard_map/ppermute | solution.py:33
  41.1 1.5 %collective-permute-start.3 = (bf16[4,16,1536]{2,1,0:T(8,128)(2,1)S(1)}, bf16[4,16,1536]{2,1,0:T(8,128)(2,1)S(1)}, u32[]{:S(2)}, u32[]{:S(2)}) collective-permute-start(bf16[4,16,1536]{2,1,0:T(8,128)(2,1)S(1)} %shard_map.112.mine_ref), channel_id=1, source_target_pairs={{0,4},{4,0},{1,5},{5,1},{2,6},{6,2},{3,7},{7,3},{8,12},{12,8},{9,1... | collective-permute-start | bytes 589832 | tf_op jit(solution)/shard_map/ppermute | solution.py:33
  44.4 20.6 %all-to-all-start.1 = ((bf16[8,16,1536]{2,1,0:T(8,128)(2,1)}), bf16[8,16,1536]{2,1,0:T(8,128)(2,1)S(1)}, u32[]{:S(2)}, u32[]{:S(2)}) async-start(bf16[8,16,1536]{2,1,0:T(8,128)(2,1)} %shard_map.113), calls=%async_computation.1 | async-start | bytes 786432 | tf_op jit(solution)/shard_map/all_to_all | solution.py:345
  54.5 9.1 %collective-permute-start.7 = (bf16[128,352]{0,1:T(8,128)(2,1)}, bf16[128,352]{0,1:T(8,128)(2,1)S(1)}, u32[]{:S(2)}, u32[]{:S(2)}) collective-permute-start(bf16[128,352]{0,1:T(8,128)(2,1)} %param.18), channel_id=1, source_target_pairs={{0,1},{1,2},{2,3},{3,0},{4,5},{5,6},{6,7},{7,4},{8,9},{9,10},{10,1... | collective-permute-start | bytes 270344 | tf_op jit(solution)/shard_map/ppermute | solution.py:33
  55.1 9.2 %collective-permute-start.8 = (bf16[128,352]{0,1:T(8,128)(2,1)}, bf16[128,352]{0,1:T(8,128)(2,1)S(1)}, u32[]{:S(2)}, u32[]{:S(2)}) collective-permute-start(bf16[128,352]{0,1:T(8,128)(2,1)} %param.18), channel_id=1, source_target_pairs={{0,2},{1,3},{2,0},{3,1},{4,6},{5,7},{6,4},{7,5},{8,10},{9,11},{10,... | collective-permute-start | bytes 270344 | tf_op jit(solution)/shard_map/ppermute | solution.py:33
  56.7 10.7 %collective-permute-start.9 = (bf16[128,352]{0,1:T(8,128)(2,1)}, bf16[128,352]{0,1:T(8,128)(2,1)}, u32[]{:S(2)}, u32[]{:S(2)}) collective-permute-start(bf16[128,352]{0,1:T(8,128)(2,1)} %param.18), channel_id=1, source_target_pairs={{0,3},{1,0},{2,1},{3,2},{4,7},{5,4},{6,5},{7,6},{8,11},{9,8},{10,9... | collective-permute-start | bytes 270344 | tf_op jit(solution)/shard_map/ppermute | solution.py:33
  58.1 38.2 %collective-permute-start.16 = (bf16[176,1408]{1,0:T(8,128)(2,1)}, bf16[176,1408]{1,0:T(8,128)(2,1)}, u32[]{:S(2)}, u32[]{:S(2)}) collective-permute-start(bf16[176,1408]{1,0:T(8,128)(2,1)} %constant_dynamic-slice_fusion), channel_id=1, source_target_pairs={{0,1},{1,2},{2,3},{3,0},{4,5},{5,6},{6,7},{7,4},{8,9},{9,10},{10,1... | collective-permute-start | bytes 1486856 | tf_op jit(solution)/shard_map/ppermute | solution.py:33
  58.8 44.0 %collective-permute-start.17 = (bf16[176,1408]{1,0:T(8,128)(2,1)}, bf16[176,1408]{1,0:T(8,128)(2,1)}, u32[]{:S(2)}, u32[]{:S(2)}) collective-permute-start(bf16[176,1408]{1,0:T(8,128)(2,1)} %constant_dynamic-slice_fusion), channel_id=1, source_target_pairs={{0,3},{1,0},{2,1},{3,2},{4,7},{5,4},{6,5},{7,6},{8,11},{9,8},{10,9... | collective-permute-start | bytes 1486856 | tf_op jit(solution)/shard_map/ppermute | solution.py:33
  65.0 9.7 %collective-permute-start.4 = (bf16[16,1536]{1,0:T(8,128)(2,1)S(1)}, bf16[16,1536]{1,0:T(8,128)(2,1)S(1)}, u32[]{:S(2)}, u32[]{:S(2)}) collective-permute-start(bf16[16,1536]{1,0:T(8,128)(2,1)S(1)} %shard_map.114.r0_ref), channel_id=1, source_target_pairs={{0,1},{1,2},{2,3},{3,0},{4,5},{5,6},{6,7},{7,4},{8,9},{9,10},{10,1... | collective-permute-start | bytes 147464 | tf_op jit(solution)/shard_map/ppermute | solution.py:33
  65.3 9.5 %collective-permute-start.5 = (bf16[16,1536]{1,0:T(8,128)(2,1)S(1)}, bf16[16,1536]{1,0:T(8,128)(2,1)S(1)}, u32[]{:S(2)}, u32[]{:S(2)}) collective-permute-start(bf16[16,1536]{1,0:T(8,128)(2,1)S(1)} %shard_map.114.r0_ref), channel_id=1, source_target_pairs={{0,2},{1,3},{2,0},{3,1},{4,6},{5,7},{6,4},{7,5},{8,10},{9,11},{10,... | collective-permute-start | bytes 147464 | tf_op jit(solution)/shard_map/ppermute | solution.py:33
  67.4 7.9 %collective-permute-start.6 = (bf16[16,1536]{1,0:T(8,128)(2,1)S(1)}, bf16[16,1536]{1,0:T(8,128)(2,1)}, u32[]{:S(2)}, u32[]{:S(2)}) collective-permute-start(bf16[16,1536]{1,0:T(8,128)(2,1)S(1)} %shard_map.114.r0_ref), channel_id=1, source_target_pairs={{0,3},{1,0},{2,1},{3,2},{4,7},{5,4},{6,5},{7,6},{8,11},{9,8},{10,9... | collective-permute-start | bytes 147464 | tf_op jit(solution)/shard_map/ppermute | solution.py:33
  78.0 25.3 %collective-permute-start.15 = (bf16[176,1408]{1,0:T(8,128)(2,1)}, bf16[176,1408]{1,0:T(8,128)(2,1)S(1)}, u32[]{:S(2)}, u32[]{:S(2)}) collective-permute-start(bf16[176,1408]{1,0:T(8,128)(2,1)} %constant_dynamic-slice_fusion), channel_id=1, source_target_pairs={{0,2},{1,3},{2,0},{3,1},{4,6},{5,7},{6,4},{7,5},{8,10},{9,11},{10,... | collective-permute-start | bytes 1486856 | tf_op jit(solution)/shard_map/ppermute | solution.py:33
  88.2 34.0 %copy-start.1 = (bf16[352,1408]{1,0:T(8,128)(2,1)S(1)}, bf16[352,1408]{1,0:T(8,128)(2,1)}, u32[]{:S(2)}) copy-start(bf16[352,1408]{1,0:T(8,128)(2,1)} %w0_ref) | copy-start | bytes 2973700
  88.2 11.8 %collective-permute-start.10 = (bf16[4,2,88,128]{3,2,1,0:T(8,128)(2,1)S(1)}, bf16[4,2,88,128]{3,2,1,0:T(8,128)(2,1)S(1)}, u32[]{:S(2)}, u32[]{:S(2)}) collective-permute-start(bf16[4,2,88,128]{3,2,1,0:T(8,128)(2,1)S(1)} %slice.7), channel_id=1, source_target_pairs={{0,32},{32,64},{64,96},{96,128},{128,160},{160,192},{192,224},{1,3... | collective-permute-start | bytes 540680 | tf_op jit(solution)/shard_map/ppermute | solution.py:28
  91.7 11.0 %collective-permute-start.11 = (bf16[4,2,88,128]{3,2,1,0:T(8,128)(2,1)S(1)}, bf16[4,2,88,128]{3,2,1,0:T(8,128)(2,1)S(1)}, u32[]{:S(2)}, u32[]{:S(2)}) collective-permute-start(bf16[4,2,88,128]{3,2,1,0:T(8,128)(2,1)S(1)} %slice.7), channel_id=1, source_target_pairs={{0,64},{32,96},{64,128},{96,160},{128,192},{160,224},{1,65},{33,97... | collective-permute-start | bytes 540680 | tf_op jit(solution)/shard_map/ppermute | solution.py:28
  96.3 7.0 %collective-permute-start.12 = (bf16[4,2,88,128]{3,2,1,0:T(8,128)(2,1)S(1)}, bf16[4,2,88,128]{3,2,1,0:T(8,128)(2,1)S(1)}, u32[]{:S(2)}, u32[]{:S(2)}) collective-permute-start(bf16[4,2,88,128]{3,2,1,0:T(8,128)(2,1)S(1)} %slice.7), channel_id=1, source_target_pairs={{0,4},{4,0},{1,5},{5,1},{2,6},{6,2},{3,7},{7,3},{8,12},{12,8},{9,1... | collective-permute-start | bytes 540680 | tf_op jit(solution)/shard_map/ppermute | solution.py:33
  100.0 3.8 %collective-permute-start.13 = (bf16[4,2,88,128]{3,2,1,0:T(8,128)(2,1)S(1)}, bf16[4,2,88,128]{3,2,1,0:T(8,128)(2,1)S(1)}, u32[]{:S(2)}, u32[]{:S(2)}) collective-permute-start(bf16[4,2,88,128]{3,2,1,0:T(8,128)(2,1)S(1)} %collective-permute-done.10.near_ref), channel_id=1, source_target_pairs={{0,4},{4,0},{1,5},{5,1},{2,6},{6,2},{3,7},{7,3},{8,12},{12,8},{9,1... | collective-permute-start | bytes 540680 | tf_op jit(solution)/shard_map/ppermute | solution.py:33
  102.8 1.6 %collective-permute-start.14 = (bf16[4,2,88,128]{3,2,1,0:T(8,128)(2,1)S(1)}, bf16[4,2,88,128]{3,2,1,0:T(8,128)(2,1)S(1)}, u32[]{:S(2)}, u32[]{:S(2)}) collective-permute-start(bf16[4,2,88,128]{3,2,1,0:T(8,128)(2,1)S(1)} %collective-permute-done.11.far_ref), channel_id=1, source_target_pairs={{0,4},{4,0},{1,5},{5,1},{2,6},{6,2},{3,7},{7,3},{8,12},{12,8},{9,1... | collective-permute-start | bytes 540680 | tf_op jit(solution)/shard_map/ppermute | solution.py:33
  102.8 12.1 %collective-permute-start.19 = (bf16[176,1408]{1,0:T(8,128)(2,1)}, bf16[176,1408]{1,0:T(8,128)(2,1)S(1)}, u32[]{:S(2)}, u32[]{:S(2)}) collective-permute-start(bf16[176,1408]{1,0:T(8,128)(2,1)} %collective-permute-done.16.m1_ref), channel_id=1, source_target_pairs={{0,4},{4,0},{1,5},{5,1},{2,6},{6,2},{3,7},{7,3},{8,12},{12,8},{9,1... | collective-permute-start | bytes 1486856 | tf_op jit(solution)/shard_map/ppermute | solution.py:33
  103.3 11.6 %collective-permute-start.20 = (bf16[176,1408]{1,0:T(8,128)(2,1)}, bf16[176,1408]{1,0:T(8,128)(2,1)}, u32[]{:S(2)}, u32[]{:S(2)}) collective-permute-start(bf16[176,1408]{1,0:T(8,128)(2,1)} %collective-permute-done.17.m3_ref), channel_id=1, source_target_pairs={{0,4},{4,0},{1,5},{5,1},{2,6},{6,2},{3,7},{7,3},{8,12},{12,8},{9,1... | collective-permute-start | bytes 1486856 | tf_op jit(solution)/shard_map/ppermute | solution.py:33
  103.4 18.8 %collective-permute-start.18 = (bf16[176,1408]{1,0:T(8,128)(2,1)S(1)}, bf16[176,1408]{1,0:T(8,128)(2,1)}, u32[]{:S(2)}, u32[]{:S(2)}) collective-permute-start(bf16[176,1408]{1,0:T(8,128)(2,1)S(1)} %collective-permute-done.15.m2_ref), channel_id=1, source_target_pairs={{0,4},{4,0},{1,5},{5,1},{2,6},{6,2},{3,7},{7,3},{8,12},{12,8},{9,1... | collective-permute-start | bytes 1486856 | tf_op jit(solution)/shard_map/ppermute | solution.py:33
  108.6 13.6 %all-to-all-start.3 = ((bf16[16,88,128]{2,1,0:T(8,128)(2,1)}), bf16[16,88,128]{2,1,0:T(8,128)(2,1)S(1)}, u32[]{:S(2)}, u32[]{:S(2)}) async-start(bf16[16,88,128]{2,1,0:T(8,128)(2,1)} %bitcast.17), calls=%async_computation.3 | async-start | bytes 720896 | tf_op jit(solution)/shard_map/all_to_all | solution.py:373
  (6 other events, 83.6 us)

commit v12 on v11

--- a/solution.py
+++ b/solution.py
@@ -33,7 +33,7 @@
     return lax.ppermute(x, axis, [(i, (i + by) % count) for i in range(count)])
 
 
-def call(kernel, out_shape, spaces, scratch=(), limit=8, flops=None):
+def call(kernel, out_shape, spaces, scratch=(), limit=8, flops=None, tail=()):
     single = not isinstance(out_shape, (list, tuple))
     outs = pl.BlockSpec(memory_space=VMEM)
     cost = flops and pl.CostEstimate(flops=flops, transcendentals=0, bytes_accessed=flops // 400)
@@ -41,7 +41,7 @@
         kernel,
         out_shape=out_shape,
         in_specs=[pl.BlockSpec(memory_space=s) for s in spaces],
-        out_specs=outs if single else [outs] * len(out_shape),
+        out_specs=outs if single else [outs] * (len(out_shape) - len(tail)) + [pl.BlockSpec(memory_space=x) for x in tail],
         scratch_shapes=scratch,
         compiler_params=pltpu.CompilerParams(vmem_limit_bytes=limit << 20),
         cost_estimate=cost,
@@ -129,7 +129,7 @@
     rows_ref[...] = total.astype(BF)
 
 
-def select_kernel(place_ref, mine_ref, other_ref, routed_ref):
+def select_kernel(place_ref, mine_ref, other_ref, routed_ref, same_ref):
     wide = mine_ref.shape[2]
     width = wide - FACTS
     rows = jnp.concatenate(
@@ -143,6 +143,8 @@
     chosen = (to == target // 16) & (source % 16 == target % 16)
     routed = dot(chosen.astype(BF), rows, (0, 0))
     routed_ref[...] = routed.astype(BF).reshape(8, 16, wide)
+    for index in range(3):
+        same_ref[index] = place_ref[index]
 
 
 def own_kernel(
@@ -326,7 +328,10 @@
         [SMEM] * 4 + [VMEM] * 2,
         flops=8 * 10**9,
     )(place, picture_grid, picture_block, picture_offset, picture, share[0])
-    own, merge_weight = lax.optimization_barrier((own, merge_weight))
+    own, text_early = lax.optimization_barrier((own, text_out))
+    half = local_width // 2
+    near_half = lax.dynamic_slice_in_dim(text_early, c * half, half, 0)
+    near_half, merge_weight = lax.optimization_barrier((near_half, merge_weight))
     merge_parts = jnp.split(merge_weight[0], [640, 1024], axis=0)
     routed = call(merge_kernel, shape((4, MERGED, wide)), [VMEM] * 8)(
         facts, own, *shares, *merge_parts
@@ -335,11 +340,11 @@
     got = lax.all_to_all(routed.reshape(16, 16, wide), ("y", "t"), 0, 0, tiled=True)
     got = call(sum_kernel, shape((4, 16, wide)), [VMEM])(got.reshape(4, 4, 16, wide))
     other = around(got, "c", 1)
-    routed = call(select_kernel, shape((8, 16, wide)), [SMEM, VMEM, VMEM])(place, got, other)
-    routed, text_out = lax.optimization_barrier((routed, text_out))
-    half = local_width // 2
-    near_half = lax.dynamic_slice_in_dim(text_out, c * half, half, 0)
-    near_half, tokens = lax.optimization_barrier((near_half, tokens))
+    routed, place = call(
+        select_kernel, [shape((8, 16, wide)), shape((3,), I32)], [SMEM, VMEM, VMEM], tail=(SMEM,)
+    )(place, got, other)
+    place = jnp.maximum(place, 0)
+    place, near_half, tokens = lax.optimization_barrier((place, near_half, tokens))
     halves = [None] + [around(near_half, "t", by) for by in (1, 3)]
     pieces = [tokens] + [around(tokens, "t", by) for by in range(1, 4)]
     got = lax.all_to_all(routed, "z", 0, 0, tiled=True)

time: 127 us -> 125 us (0.984)
  waiting for transfers between devices: 21.2 us -> 17.9 us
  starting transfers between devices: 38.8 us -> 41.4 us
    ppermute x19, waiting for transfers between devices: 7.5 us -> 4.55 us  [around(): return lax.ppermute(x, axis, [(i, (i + by) % count) for i in range(count)])]
    all_to_all x1, starting transfers between devices: 3.55 us -> 6.46 us  [local(): lax.all_to_all(sent.reshape(16, HEAD, BLOCK), ('t', 'y'), 0, 0, tiled=True)]
    ppermute x2, waiting for transfers between devices: 6.34 us -> 3.96 us  [ahead(): return lax.ppermute(x, axis, [(i, i + by) for i in range(count - by)])]
    split x2, local copies, waits for them, and re-layouts: 0.3 us -> 2.33 us  [local(): merge_parts = jnp.split(merge_weight[0], [640, 1024], axis=0)]
    all_to_all x1, waiting for transfers between devices: 0.01 us -> 2.01 us  [local(): got = lax.all_to_all(routed, 'z', 0, 0, tiled=True)]
  transfers between devices with their start and end apart: 23 -> 23, of which waited for: 8 -> 9; matrix products, arithmetic and copies ran while one was open for 8% -> 8% of each run, Pallas kernels for 7% -> 7%
where the time goes in v12:
time: 125 us; the launch traced here: 124 us
  starting transfers between devices  41.4 us (33%)
  blocking collectives  29.3 us (23%)
  Pallas kernels  21.7 us (17%)
  waiting for transfers between devices  17.9 us (14%)
  local copies, waits for them, and re-layouts  11.9 us (10%)
  between operations  1.62 us (1%)
    all_to_all x1, blocking collectives, local(): lax.all_to_all(routed.reshape(16, 16, wide), ('y', 't'), 0, 0, tiled=True)  20.2 us
    ppermute x19, starting transfers between devices, around(): return lax.ppermute(x, axis, [(i, (i + by) % count) for i in range(count)])  18.7 us
    all_to_all x1, blocking collectives, local(): mine = lax.all_to_all(heads, 'y', 0, 0, tiled=True)  9.1 us
    all_to_all x1, starting transfers between devices, local(): got = lax.all_to_all(routed, 'z', 0, 0, tiled=True)  8.12 us
    ppermute x2, starting transfers between devices, ahead(): return lax.ppermute(x, axis, [(i, i + by) for i in range(count - by)])  8.09 us
    all_to_all x1, waiting for transfers between devices, local(): lax.all_to_all(sent.reshape(16, HEAD, BLOCK), ('t', 'y'), 0, 0, tiled=True)  7.36 us
    pallas_call x1, Pallas kernels, local(): call(vision_kernel, [shape((MERGED, width))] * 4, [SMEM, HBM, HBM, HBM],...  7.21 us
    all_to_all x1, starting transfers between devices, local(): lax.all_to_all(sent.reshape(16, HEAD, BLOCK), ('t', 'y'), 0, 0, tiled=True)  6.46 us
  transfers between devices with their start and end apart: 23, of which 9 were waited for; matrix products, arithmetic and copies ran while one was open for 8% of the time, Pallas kernels for 7%

profile of v12, /device:TPU:64, one launch (start us, length us, event | category | flops | bytes accessed | tf_op | source)
XLA Modules:
  0.0 123.8 jit_solution(988063282009613796)
XLA Ops:
  0.0 7.2 %shard_map.109 = (bf16[64,1408]{1,0:T(8,128)(2,1)}, bf16[64,1408]{1,0:T(8,128)(2,1)}, bf16[64,1408]{1,0:T(8,128)(2,1)}, bf16[64,1408]{1,0:T(8,128)(2,1)}) custom-call(s32[1,2]{1,0:T(1,128)} %grid_ref.3, bf16[256,1408]{1,0:T(8,128)(2,1)} %bitcast.31, bf16[3,352,1408]{2,1,0:T(8,128)(2,1)} %bitcast.33, bf16[352,1408]{1,0:T(8,128)(2,1)} %out_hbm.1), custom_call_target="tpu_custom_call" | custom-call | tf_op jit(solution)/shard_map/pallas_call | solution.py:312
  7.2 1.6 %collective-permute-start = (bf16[64,1408]{1,0:T(8,128)(2,1)}, bf16[64,1408]{1,0:T(8,128)(2,1)S(1)}, u32[]{:S(2)}, u32[]{:S(2)}) collective-permute-start(bf16[64,1408]{1,0:T(8,128)(2,1)} %get-tuple-element.27), channel_id=1, source_target_pairs={{0,1},{1,2},{2,3},{3,0},{4,5},{5,6},{6,7},{7,4},{8,9},{9,10},{10,1... | collective-permute-start | bytes 540680 | tf_op jit(solution)/shard_map/ppermute | solution.py:33
  8.8 2.7 %collective-permute-start.1 = (bf16[64,1408]{1,0:T(8,128)(2,1)}, bf16[64,1408]{1,0:T(8,128)(2,1)S(1)}, u32[]{:S(2)}, u32[]{:S(2)}) collective-permute-start(bf16[64,1408]{1,0:T(8,128)(2,1)} %get-tuple-element.28), channel_id=1, source_target_pairs={{0,2},{1,3},{2,0},{3,1},{4,6},{5,7},{6,4},{7,5},{8,10},{9,11},{10,... | collective-permute-start | bytes 540680 | tf_op jit(solution)/shard_map/ppermute | solution.py:33
  11.5 1.4 %collective-permute-start.2 = (bf16[64,1408]{1,0:T(8,128)(2,1)}, bf16[64,1408]{1,0:T(8,128)(2,1)S(1)}, u32[]{:S(2)}, u32[]{:S(2)}) collective-permute-start(bf16[64,1408]{1,0:T(8,128)(2,1)} %get-tuple-element.29), channel_id=1, source_target_pairs={{0,3},{1,0},{2,1},{3,2},{4,7},{5,4},{6,5},{7,6},{8,11},{9,8},{10,9... | collective-permute-start | bytes 540680 | tf_op jit(solution)/shard_map/ppermute | solution.py:33
  17.3 2.2 %slice_bitcast_fusion.w0_ref = bf16[640,1408]{1,0:T(8,128)(2,1)S(1)} fusion(bf16[1,1408,1408]{2,1,0:T(8,128)(2,1)} %param.15), kind=kLoop, calls=%fused_computation | loop fusion | bytes 3604480 | tf_op jit(solution)/shard_map/split | solution.py:335
  20.9 20.2 %all_to_all.20 = bf16[16,16,1536]{2,1,0:T(8,128)(2,1)S(1)} all-to-all(bf16[16,16,1536]{2,1,0:T(8,128)(2,1)S(1)} %bitcast.27), channel_id=1, replica_groups=mesh['z'=8,'y'=4,'c'=2,'t'=4] {'y','t'}, dimensions={0} | all-to-all | bytes 1572864 | tf_op jit(solution)/shard_map/all_to_all | solution.py:340
  41.4 1.4 %collective-permute-done.3.other_ref = bf16[4,16,1536]{2,1,0:T(8,128)(2,1)S(1)} collective-permute-done((bf16[4,16,1536]{2,1,0:T(8,128)(2,1)S(1)}, bf16[4,16,1536]{2,1,0:T(8,128)(2,1)S(1)}, u32[]{:S(2)}, u32[]{:S(2)}) %collective-permute-start.3) | collective-permute-done | bytes 196640 | tf_op jit(solution)/shard_map/ppermute | solution.py:33
  44.8 8.1 %all-to-all-start.1 = ((bf16[8,16,1536]{2,1,0:T(8,128)(2,1)}), bf16[8,16,1536]{2,1,0:T(8,128)(2,1)S(1)}, u32[]{:S(2)}, u32[]{:S(2)}) async-start(bf16[8,16,1536]{2,1,0:T(8,128)(2,1)} %copy-done.4), calls=%async_computation.1 | async-start | bytes 786432 | tf_op jit(solution)/shard_map/all_to_all | solution.py:350
  53.6 1.7 %collective-permute-start.8 = (bf16[128,352]{0,1:T(8,128)(2,1)S(1)}, bf16[128,352]{0,1:T(8,128)(2,1)S(1)}, u32[]{:S(2)}, u32[]{:S(2)}) collective-permute-start(bf16[128,352]{0,1:T(8,128)(2,1)S(1)} %copy-done.10), channel_id=1, source_target_pairs={{0,2},{1,3},{2,0},{3,1},{4,6},{5,7},{6,4},{7,5},{8,10},{9,11},{10,... | collective-permute-start | bytes 270344 | tf_op jit(solution)/shard_map/ppermute | solution.py:33
  57.3 2.6 %collective-permute-start.17 = (bf16[176,1408]{1,0:T(8,128)(2,1)}, bf16[176,1408]{1,0:T(8,128)(2,1)}, u32[]{:S(2)}, u32[]{:S(2)}) collective-permute-start(bf16[176,1408]{1,0:T(8,128)(2,1)} %constant_dynamic-slice_fusion), channel_id=1, source_target_pairs={{0,3},{1,0},{2,1},{3,2},{4,7},{5,4},{6,5},{7,6},{8,11},{9,8},{10,9... | collective-permute-start | bytes 1486856 | tf_op jit(solution)/shard_map/ppermute | solution.py:33
  62.6 2.0 %all-to-all-done.1.parts_ref = bf16[8,16,1536]{2,1,0:T(8,128)(2,1)S(1)} async-done(((bf16[8,16,1536]{2,1,0:T(8,128)(2,1)}), bf16[8,16,1536]{2,1,0:T(8,128)(2,1)S(1)}, u32[]{:S(2)}, u32[]{:S(2)}) %all-to-all-start.1) | async-done | bytes 393248 | tf_op jit(solution)/shard_map/all_to_all | solution.py:350
  65.5 1.7 %collective-permute-start.5 = (bf16[16,1536]{1,0:T(8,128)(2,1)S(1)}, bf16[16,1536]{1,0:T(8,128)(2,1)S(1)}, u32[]{:S(2)}, u32[]{:S(2)}) collective-permute-start(bf16[16,1536]{1,0:T(8,128)(2,1)S(1)} %shard_map.114.r0_ref), channel_id=1, source_target_pairs={{0,2},{1,3},{2,0},{3,1},{4,6},{5,7},{6,4},{7,5},{8,10},{9,11},{10,... | collective-permute-start | bytes 147464 | tf_op jit(solution)/shard_map/ppermute | solution.py:33
  68.5 1.5 %bitcast_dynamic-update-slice_fusion = bf16[4,128,352]{1,2,0:T(8,128)(2,1)} fusion(bf16[4,128,352]{1,2,0:T(8,128)(2,1)} %bitcast_dynamic-update-slice_fusion.1, s32[]{:T(128)S(6)} %select_n.43, bf16[128,352]{0,1:T(8,128)(2,1)} %collective-permute-done.9), kind=kLoop, calls=%fused_computation.3 | loop fusion | bytes 180228 | tf_op jit(solution)/shard_map/jit(dynamic_update_index_in_dim)/dynamic_update_slice | solution.py:355
  71.2 1.8 %collective-permute-done.4.r1_ref = bf16[16,1536]{1,0:T(8,128)(2,1)S(1)} collective-permute-done((bf16[16,1536]{1,0:T(8,128)(2,1)S(1)}, bf16[16,1536]{1,0:T(8,128)(2,1)S(1)}, u32[]{:S(2)}, u32[]{:S(2)}) %collective-permute-start.4) | collective-permute-done | bytes 49184 | tf_op jit(solution)/shard_map/ppermute | solution.py:33
  73.6 2.4 %shard_map.115 = bf16[4,3,88,128]{3,2,1,0:T(8,128)(2,1)S(1)} custom-call(s32[3]{0:T(128)S(1)} %broadcast_maximum_fusion.place_ref.facts_ref, bf16[16,1536]{1,0:T(8,128)(2,1)S(1)} %shard_map.114.r0_ref, bf16[16,1536]{1,0:T(8,128)(2,1)S(1)} %collective-permute-done.4.r1_ref, bf16[16,1536]{1,0:T(8,128)(2,1)S(1)} %collective-permute-done.5.r2_ref, ...), custom_call_target="tpu_custom_call" | custom-call | tf_op jit(solution)/shard_map/pallas_call | solution.py:357
  77.1 9.1 %all_to_all.21.own_ref = bf16[4,3,88,128]{3,2,1,0:T(8,128)(2,1)S(1)} all-to-all(bf16[4,3,88,128]{3,2,1,0:T(8,128)(2,1)S(1)} %shard_map.115), channel_id=1, replica_groups=mesh['z'=8,'y'=4,'c'=2,'t'=4] {'y'}, dimensions={0} | all-to-all | bytes 540672 | tf_op jit(solution)/shard_map/all_to_all | solution.py:364
  86.2 3.5 %collective-permute-start.10 = (bf16[4,2,88,128]{3,2,1,0:T(8,128)(2,1)S(1)}, bf16[4,2,88,128]{3,2,1,0:T(8,128)(2,1)S(1)}, u32[]{:S(2)}, u32[]{:S(2)}) collective-permute-start(bf16[4,2,88,128]{3,2,1,0:T(8,128)(2,1)S(1)} %slice.7), channel_id=1, source_target_pairs={{0,32},{32,64},{64,96},{96,128},{128,160},{160,192},{192,224},{1,3... | collective-permute-start | bytes 540680 | tf_op jit(solution)/shard_map/ppermute | solution.py:28
  89.7 4.6 %collective-permute-start.11 = (bf16[4,2,88,128]{3,2,1,0:T(8,128)(2,1)S(1)}, bf16[4,2,88,128]{3,2,1,0:T(8,128)(2,1)S(1)}, u32[]{:S(2)}, u32[]{:S(2)}) collective-permute-start(bf16[4,2,88,128]{3,2,1,0:T(8,128)(2,1)S(1)} %slice.7), channel_id=1, source_target_pairs={{0,64},{32,96},{64,128},{96,160},{128,192},{160,224},{1,65},{33,97... | collective-permute-start | bytes 540680 | tf_op jit(solution)/shard_map/ppermute | solution.py:28
  94.4 1.8 %collective-permute-done.10.near_ref = bf16[4,2,88,128]{3,2,1,0:T(8,128)(2,1)S(1)} collective-permute-done((bf16[4,2,88,128]{3,2,1,0:T(8,128)(2,1)S(1)}, bf16[4,2,88,128]{3,2,1,0:T(8,128)(2,1)S(1)}, u32[]{:S(2)}, u32[]{:S(2)}) %collective-permute-start.10) | collective-permute-done | bytes 180256 | tf_op jit(solution)/shard_map/ppermute | solution.py:28
  96.2 2.1 %collective-permute-done.11.far_ref = bf16[4,2,88,128]{3,2,1,0:T(8,128)(2,1)S(1)} collective-permute-done((bf16[4,2,88,128]{3,2,1,0:T(8,128)(2,1)S(1)}, bf16[4,2,88,128]{3,2,1,0:T(8,128)(2,1)S(1)}, u32[]{:S(2)}, u32[]{:S(2)}) %collective-permute-start.11) | collective-permute-done | bytes 180256 | tf_op jit(solution)/shard_map/ppermute | solution.py:28
  100.0 4.3 %shard_map.116 = bf16[4,4,88,128]{3,2,1,0:T(8,128)(2,1)} custom-call(s32[3]{0:T(128)S(1)} %broadcast_maximum_fusion.place_ref.facts_ref, s32[16]{0:T(128)S(1)} %copy-done.6, bf16[4,3,88,128]{3,2,1,0:T(8,128)(2,1)S(1)} %all_to_all.21.own_ref, bf16[4,2,88,128]{3,2,1,0:T(8,128)(2,1)S(1)} %collective-permute-done.10.near_ref, ...), custom_call_target="tpu_custom_call" | custom-call | tf_op jit(solution)/shard_map/pallas_call | solution.py:372
  104.3 6.5 %all-to-all-start.3 = ((bf16[16,88,128]{2,1,0:T(8,128)(2,1)}), bf16[16,88,128]{2,1,0:T(8,128)(2,1)S(1)}, u32[]{:S(2)}, u32[]{:S(2)}) async-start(bf16[16,88,128]{2,1,0:T(8,128)(2,1)} %bitcast.17), calls=%async_computation.3 | async-start | bytes 720896 | tf_op jit(solution)/shard_map/all_to_all | solution.py:378
  113.2 7.4 %all-to-all-done.3 = bf16[16,88,128]{2,1,0:T(8,128)(2,1)S(1)} async-done(((bf16[16,88,128]{2,1,0:T(8,128)(2,1)}), bf16[16,88,128]{2,1,0:T(8,128)(2,1)S(1)}, u32[]{:S(2)}, u32[]{:S(2)}) %all-to-all-start.3) | async-done | bytes 360480 | tf_op jit(solution)/shard_map/all_to_all | solution.py:378
  120.5 3.3 %shard_map.118 = bf16[128,1408]{1,0:T(8,128)(2,1)} custom-call(s32[3]{0:T(128)S(1)} %broadcast_maximum_fusion.place_ref.facts_ref, bf16[4,2,176,128]{3,2,1,0:T(8,128)(2,1)S(1)} %bitcast.30, bf16[352,1408]{1,0:T(8,128)(2,1)S(1)} %copy-done.2, bf16[176,1408]{1,0:T(8,128)(2,1)S(1)} %collective-permute-done.15.m2_ref, ...), custom_call_target="tpu_custom_call" | custom-call | tf_op jit(solution)/shard_map/pallas_call | solution.py:379
  (69 shorter events, 21.2 us)
Async XLA Ops:
  7.2 12.4 %collective-permute-start = (bf16[64,1408]{1,0:T(8,128)(2,1)}, bf16[64,1408]{1,0:T(8,128)(2,1)S(1)}, u32[]{:S(2)}, u32[]{:S(2)}) collective-permute-start(bf16[64,1408]{1,0:T(8,128)(2,1)} %get-tuple-element.27), channel_id=1, source_target_pairs={{0,1},{1,2},{2,3},{3,0},{4,5},{5,6},{6,7},{7,4},{8,9},{9,10},{10,1... | collective-permute-start | bytes 540680 | tf_op jit(solution)/shard_map/ppermute | solution.py:33
  8.8 11.1 %collective-permute-start.1 = (bf16[64,1408]{1,0:T(8,128)(2,1)}, bf16[64,1408]{1,0:T(8,128)(2,1)S(1)}, u32[]{:S(2)}, u32[]{:S(2)}) collective-permute-start(bf16[64,1408]{1,0:T(8,128)(2,1)} %get-tuple-element.28), channel_id=1, source_target_pairs={{0,2},{1,3},{2,0},{3,1},{4,6},{5,7},{6,4},{7,5},{8,10},{9,11},{10,... | collective-permute-start | bytes 540680 | tf_op jit(solution)/shard_map/ppermute | solution.py:33
  11.5 8.3 %collective-permute-start.2 = (bf16[64,1408]{1,0:T(8,128)(2,1)}, bf16[64,1408]{1,0:T(8,128)(2,1)S(1)}, u32[]{:S(2)}, u32[]{:S(2)}) collective-permute-start(bf16[64,1408]{1,0:T(8,128)(2,1)} %get-tuple-element.29), channel_id=1, source_target_pairs={{0,3},{1,0},{2,1},{3,2},{4,7},{5,4},{6,5},{7,6},{8,11},{9,8},{10,9... | collective-permute-start | bytes 540680 | tf_op jit(solution)/shard_map/ppermute | solution.py:33
  41.2 1.5 %collective-permute-start.3 = (bf16[4,16,1536]{2,1,0:T(8,128)(2,1)S(1)}, bf16[4,16,1536]{2,1,0:T(8,128)(2,1)S(1)}, u32[]{:S(2)}, u32[]{:S(2)}) collective-permute-start(bf16[4,16,1536]{2,1,0:T(8,128)(2,1)S(1)} %shard_map.112.mine_ref), channel_id=1, source_target_pairs={{0,4},{4,0},{1,5},{5,1},{2,6},{6,2},{3,7},{7,3},{8,12},{12,8},{9,1... | collective-permute-start | bytes 589832 | tf_op jit(solution)/shard_map/ppermute | solution.py:33
  44.8 19.7 %all-to-all-start.1 = ((bf16[8,16,1536]{2,1,0:T(8,128)(2,1)}), bf16[8,16,1536]{2,1,0:T(8,128)(2,1)S(1)}, u32[]{:S(2)}, u32[]{:S(2)}) async-start(bf16[8,16,1536]{2,1,0:T(8,128)(2,1)} %copy-done.4), calls=%async_computation.1 | async-start | bytes 786432 | tf_op jit(solution)/shard_map/all_to_all | solution.py:350
  53.0 8.3 %collective-permute-start.7 = (bf16[128,352]{0,1:T(8,128)(2,1)S(1)}, bf16[128,352]{0,1:T(8,128)(2,1)S(1)}, u32[]{:S(2)}, u32[]{:S(2)}) collective-permute-start(bf16[128,352]{0,1:T(8,128)(2,1)S(1)} %copy-done.10), channel_id=1, source_target_pairs={{0,1},{1,2},{2,3},{3,0},{4,5},{5,6},{6,7},{7,4},{8,9},{9,10},{10,1... | collective-permute-start | bytes 270344 | tf_op jit(solution)/shard_map/ppermute | solution.py:33
  53.6 8.3 %collective-permute-start.8 = (bf16[128,352]{0,1:T(8,128)(2,1)S(1)}, bf16[128,352]{0,1:T(8,128)(2,1)S(1)}, u32[]{:S(2)}, u32[]{:S(2)}) collective-permute-start(bf16[128,352]{0,1:T(8,128)(2,1)S(1)} %copy-done.10), channel_id=1, source_target_pairs={{0,2},{1,3},{2,0},{3,1},{4,6},{5,7},{6,4},{7,5},{8,10},{9,11},{10,... | collective-permute-start | bytes 270344 | tf_op jit(solution)/shard_map/ppermute | solution.py:33
  55.3 11.9 %collective-permute-start.9 = (bf16[128,352]{0,1:T(8,128)(2,1)S(1)}, bf16[128,352]{0,1:T(8,128)(2,1)}, u32[]{:S(2)}, u32[]{:S(2)}) collective-permute-start(bf16[128,352]{0,1:T(8,128)(2,1)S(1)} %copy-done.10), channel_id=1, source_target_pairs={{0,3},{1,0},{2,1},{3,2},{4,7},{5,4},{6,5},{7,6},{8,11},{9,8},{10,9... | collective-permute-start | bytes 270344 | tf_op jit(solution)/shard_map/ppermute | solution.py:33
  56.6 37.7 %collective-permute-start.16 = (bf16[176,1408]{1,0:T(8,128)(2,1)}, bf16[176,1408]{1,0:T(8,128)(2,1)}, u32[]{:S(2)}, u32[]{:S(2)}) collective-permute-start(bf16[176,1408]{1,0:T(8,128)(2,1)} %constant_dynamic-slice_fusion), channel_id=1, source_target_pairs={{0,1},{1,2},{2,3},{3,0},{4,5},{5,6},{6,7},{7,4},{8,9},{9,10},{10,1... | collective-permute-start | bytes 1486856 | tf_op jit(solution)/shard_map/ppermute | solution.py:33
  57.3 41.1 %collective-permute-start.17 = (bf16[176,1408]{1,0:T(8,128)(2,1)}, bf16[176,1408]{1,0:T(8,128)(2,1)}, u32[]{:S(2)}, u32[]{:S(2)}) collective-permute-start(bf16[176,1408]{1,0:T(8,128)(2,1)} %constant_dynamic-slice_fusion), channel_id=1, source_target_pairs={{0,3},{1,0},{2,1},{3,2},{4,7},{5,4},{6,5},{7,6},{8,11},{9,8},{10,9... | collective-permute-start | bytes 1486856 | tf_op jit(solution)/shard_map/ppermute | solution.py:33
  64.6 8.4 %collective-permute-start.4 = (bf16[16,1536]{1,0:T(8,128)(2,1)S(1)}, bf16[16,1536]{1,0:T(8,128)(2,1)S(1)}, u32[]{:S(2)}, u32[]{:S(2)}) collective-permute-start(bf16[16,1536]{1,0:T(8,128)(2,1)S(1)} %shard_map.114.r0_ref), channel_id=1, source_target_pairs={{0,1},{1,2},{2,3},{3,0},{4,5},{5,6},{6,7},{7,4},{8,9},{9,10},{10,1... | collective-permute-start | bytes 147464 | tf_op jit(solution)/shard_map/ppermute | solution.py:33
  65.5 7.6 %collective-permute-start.5 = (bf16[16,1536]{1,0:T(8,128)(2,1)S(1)}, bf16[16,1536]{1,0:T(8,128)(2,1)S(1)}, u32[]{:S(2)}, u32[]{:S(2)}) collective-permute-start(bf16[16,1536]{1,0:T(8,128)(2,1)S(1)} %shard_map.114.r0_ref), channel_id=1, source_target_pairs={{0,2},{1,3},{2,0},{3,1},{4,6},{5,7},{6,4},{7,5},{8,10},{9,11},{10,... | collective-permute-start | bytes 147464 | tf_op jit(solution)/shard_map/ppermute | solution.py:33
  67.1 6.5 %collective-permute-start.6 = (bf16[16,1536]{1,0:T(8,128)(2,1)S(1)}, bf16[16,1536]{1,0:T(8,128)(2,1)S(1)}, u32[]{:S(2)}, u32[]{:S(2)}) collective-permute-start(bf16[16,1536]{1,0:T(8,128)(2,1)S(1)} %shard_map.114.r0_ref), channel_id=1, source_target_pairs={{0,3},{1,0},{2,1},{3,2},{4,7},{5,4},{6,5},{7,6},{8,11},{9,8},{10,9... | collective-permute-start | bytes 147464 | tf_op jit(solution)/shard_map/ppermute | solution.py:33
  76.0 23.0 %collective-permute-start.15 = (bf16[176,1408]{1,0:T(8,128)(2,1)S(1)}, bf16[176,1408]{1,0:T(8,128)(2,1)S(1)}, u32[]{:S(2)}, u32[]{:S(2)}) collective-permute-start(bf16[176,1408]{1,0:T(8,128)(2,1)S(1)} %copy-done.9), channel_id=1, source_target_pairs={{0,2},{1,3},{2,0},{3,1},{4,6},{5,7},{6,4},{7,5},{8,10},{9,11},{10,... | collective-permute-start | bytes 1486856 | tf_op jit(solution)/shard_map/ppermute | solution.py:33
  86.2 34.4 %copy-start.2 = (bf16[352,1408]{1,0:T(8,128)(2,1)S(1)}, bf16[352,1408]{1,0:T(8,128)(2,1)}, u32[]{:S(2)}) copy-start(bf16[352,1408]{1,0:T(8,128)(2,1)} %w0_ref.1) | copy-start | bytes 2973700
  86.2 10.0 %collective-permute-start.10 = (bf16[4,2,88,128]{3,2,1,0:T(8,128)(2,1)S(1)}, bf16[4,2,88,128]{3,2,1,0:T(8,128)(2,1)S(1)}, u32[]{:S(2)}, u32[]{:S(2)}) collective-permute-start(bf16[4,2,88,128]{3,2,1,0:T(8,128)(2,1)S(1)} %slice.7), channel_id=1, source_target_pairs={{0,32},{32,64},{64,96},{96,128},{128,160},{160,192},{192,224},{1,3... | collective-permute-start | bytes 540680 | tf_op jit(solution)/shard_map/ppermute | solution.py:28
  89.7 8.7 %collective-permute-start.11 = (bf16[4,2,88,128]{3,2,1,0:T(8,128)(2,1)S(1)}, bf16[4,2,88,128]{3,2,1,0:T(8,128)(2,1)S(1)}, u32[]{:S(2)}, u32[]{:S(2)}) collective-permute-start(bf16[4,2,88,128]{3,2,1,0:T(8,128)(2,1)S(1)} %slice.7), channel_id=1, source_target_pairs={{0,64},{32,96},{64,128},{96,160},{128,192},{160,224},{1,65},{33,97... | collective-permute-start | bytes 540680 | tf_op jit(solution)/shard_map/ppermute | solution.py:28
  94.3 4.6 %collective-permute-start.12 = (bf16[4,2,88,128]{3,2,1,0:T(8,128)(2,1)S(1)}, bf16[4,2,88,128]{3,2,1,0:T(8,128)(2,1)S(1)}, u32[]{:S(2)}, u32[]{:S(2)}) collective-permute-start(bf16[4,2,88,128]{3,2,1,0:T(8,128)(2,1)S(1)} %slice.7), channel_id=1, source_target_pairs={{0,4},{4,0},{1,5},{5,1},{2,6},{6,2},{3,7},{7,3},{8,12},{12,8},{9,1... | collective-permute-start | bytes 540680 | tf_op jit(solution)/shard_map/ppermute | solution.py:33
  96.2 3.2 %collective-permute-start.13 = (bf16[4,2,88,128]{3,2,1,0:T(8,128)(2,1)S(1)}, bf16[4,2,88,128]{3,2,1,0:T(8,128)(2,1)S(1)}, u32[]{:S(2)}, u32[]{:S(2)}) collective-permute-start(bf16[4,2,88,128]{3,2,1,0:T(8,128)(2,1)S(1)} %collective-permute-done.10.near_ref), channel_id=1, source_target_pairs={{0,4},{4,0},{1,5},{5,1},{2,6},{6,2},{3,7},{7,3},{8,12},{12,8},{9,1... | collective-permute-start | bytes 540680 | tf_op jit(solution)/shard_map/ppermute | solution.py:33
  98.4 1.6 %collective-permute-start.14 = (bf16[4,2,88,128]{3,2,1,0:T(8,128)(2,1)S(1)}, bf16[4,2,88,128]{3,2,1,0:T(8,128)(2,1)S(1)}, u32[]{:S(2)}, u32[]{:S(2)}) collective-permute-start(bf16[4,2,88,128]{3,2,1,0:T(8,128)(2,1)S(1)} %collective-permute-done.11.far_ref), channel_id=1, source_target_pairs={{0,4},{4,0},{1,5},{5,1},{2,6},{6,2},{3,7},{7,3},{8,12},{12,8},{9,1... | collective-permute-start | bytes 540680 | tf_op jit(solution)/shard_map/ppermute | solution.py:33
  98.4 14.8 %collective-permute-start.19 = (bf16[176,1408]{1,0:T(8,128)(2,1)}, bf16[176,1408]{1,0:T(8,128)(2,1)S(1)}, u32[]{:S(2)}, u32[]{:S(2)}) collective-permute-start(bf16[176,1408]{1,0:T(8,128)(2,1)} %collective-permute-done.16.m1_ref), channel_id=1, source_target_pairs={{0,4},{4,0},{1,5},{5,1},{2,6},{6,2},{3,7},{7,3},{8,12},{12,8},{9,1... | collective-permute-start | bytes 1486856 | tf_op jit(solution)/shard_map/ppermute | solution.py:33
  98.9 14.3 %collective-permute-start.20 = (bf16[176,1408]{1,0:T(8,128)(2,1)}, bf16[176,1408]{1,0:T(8,128)(2,1)}, u32[]{:S(2)}, u32[]{:S(2)}) collective-permute-start(bf16[176,1408]{1,0:T(8,128)(2,1)} %collective-permute-done.17.m3_ref), channel_id=1, source_target_pairs={{0,4},{4,0},{1,5},{5,1},{2,6},{6,2},{3,7},{7,3},{8,12},{12,8},{9,1... | collective-permute-start | bytes 1486856 | tf_op jit(solution)/shard_map/ppermute | solution.py:33
  99.0 21.6 %collective-permute-start.18 = (bf16[176,1408]{1,0:T(8,128)(2,1)S(1)}, bf16[176,1408]{1,0:T(8,128)(2,1)}, u32[]{:S(2)}, u32[]{:S(2)}) collective-permute-start(bf16[176,1408]{1,0:T(8,128)(2,1)S(1)} %collective-permute-done.15.m2_ref), channel_id=1, source_target_pairs={{0,4},{4,0},{1,5},{5,1},{2,6},{6,2},{3,7},{7,3},{8,12},{12,8},{9,1... | collective-permute-start | bytes 1486856 | tf_op jit(solution)/shard_map/ppermute | solution.py:33
  104.3 16.3 %all-to-all-start.3 = ((bf16[16,88,128]{2,1,0:T(8,128)(2,1)}), bf16[16,88,128]{2,1,0:T(8,128)(2,1)S(1)}, u32[]{:S(2)}, u32[]{:S(2)}) async-start(bf16[16,88,128]{2,1,0:T(8,128)(2,1)} %bitcast.17), calls=%async_computation.3 | async-start | bytes 720896 | tf_op jit(solution)/shard_map/all_to_all | solution.py:378
  (10 other events, 127.7 us)

commit v13 on v12

--- a/solution.py
+++ b/solution.py
@@ -122,11 +122,13 @@
         rows_ref[y] = total.astype(BF)
 
 
-def join_kernel(parts_ref, rows_ref):
+def join_kernel(place_ref, parts_ref, rows_ref, same_ref):
     total = parts_ref[0].astype(F32)
     for part in range(1, 8):
         total = total + parts_ref[part].astype(F32)
     rows_ref[...] = total.astype(BF)
+    for index in range(3):
+        same_ref[index] = place_ref[index]
 
 
 def select_kernel(place_ref, mine_ref, other_ref, routed_ref, same_ref):
@@ -348,8 +350,13 @@
     halves = [None] + [around(near_half, "t", by) for by in (1, 3)]
     pieces = [tokens] + [around(tokens, "t", by) for by in range(1, 4)]
     got = lax.all_to_all(routed, "z", 0, 0, tiled=True)
-    got = call(join_kernel, shape((16, wide)), [VMEM])(got)
+    got, place = call(
+        join_kernel, [shape((16, wide)), shape((3,), I32)], [SMEM, VMEM], tail=(SMEM,)
+    )(place, got)
     rows = [got] + [around(got, "t", by) for by in range(1, 4)]
+    place = jnp.maximum(place, 0)
+    place, near_half = lax.optimization_barrier((place, near_half))
+    halves[0] = around(near_half, "t", 2)
     own_tokens = jnp.zeros((4, BLOCK, local_width), BF)
     for by, piece in enumerate(pieces):
         own_tokens = lax.dynamic_update_index_in_dim(own_tokens, piece, (t - by) % 4, 0)
@@ -359,8 +366,7 @@
         shape((4, 3, HEAD, BLOCK)),
         [SMEM] + [VMEM] * 6,
     )(place, *rows, own_tokens, text_qkv.transpose(1, 2, 0))
-    heads, late_tokens, near_half = lax.optimization_barrier((heads, own_tokens, near_half))
-    halves[0] = around(near_half, "t", 2)
+    heads, late_tokens = lax.optimization_barrier((heads, own_tokens))
     mine = lax.all_to_all(heads, "y", 0, 0, tiled=True)
     prompt_in = call(place_kernel, shape((BLOCK, width)), [SMEM] + [VMEM] * 5)(
         place, *rows, late_tokens

time: 125 us -> 132 us (1.056)
  starting transfers between devices: 41.4 us -> 46.3 us
  Pallas kernels: 21.7 us -> 23.3 us
    all_to_all x1, starting transfers between devices: 6.46 us -> 11.6 us  [local(): lax.all_to_all(sent.reshape(16, HEAD, BLOCK), ('t', 'y'), 0, 0, tiled=True)]
  transfers between devices with their start and end apart: 23 -> 23, of which waited for: 9 -> 8; matrix products, arithmetic and copies ran while one was open for 8% -> 8% of each run, Pallas kernels for 7% -> 8%
where the time goes in v13:
time: 132 us; the launch traced here: 131 us
  starting transfers between devices  46.3 us (35%)
  blocking collectives  29.3 us (22%)
  Pallas kernels  23.3 us (18%)
  waiting for transfers between devices  18.9 us (14%)
  local copies, waits for them, and re-layouts  11.9 us (9%)
  between operations  1.65 us (1%)
    all_to_all x1, blocking collectives, local(): lax.all_to_all(routed.reshape(16, 16, wide), ('y', 't'), 0, 0, tiled=True)  20.2 us
    ppermute x19, starting transfers between devices, around(): return lax.ppermute(x, axis, [(i, (i + by) % count) for i in range(count)])  18.5 us
    all_to_all x1, starting transfers between devices, local(): lax.all_to_all(sent.reshape(16, HEAD, BLOCK), ('t', 'y'), 0, 0, tiled=True)  11.6 us
    all_to_all x1, blocking collectives, local(): mine = lax.all_to_all(heads, 'y', 0, 0, tiled=True)  9.11 us
    all_to_all x1, starting transfers between devices, local(): got = lax.all_to_all(routed, 'z', 0, 0, tiled=True)  8.12 us
    ppermute x2, starting transfers between devices, ahead(): return lax.ppermute(x, axis, [(i, i + by) for i in range(count - by)])  8.08 us
    pallas_call x1, Pallas kernels, local(): call(vision_kernel, [shape((MERGED, width))] * 4, [SMEM, HBM, HBM, HBM],...  7.21 us
    all_to_all x1, waiting for transfers between devices, local(): lax.all_to_all(sent.reshape(16, HEAD, BLOCK), ('t', 'y'), 0, 0, tiled=True)  7.1 us
  transfers between devices with their start and end apart: 23, of which 8 were waited for; matrix products, arithmetic and copies ran while one was open for 8% of the time, Pallas kernels for 8%

profile of v13, /device:TPU:64, one launch (start us, length us, event | category | flops | bytes accessed | tf_op | source)
XLA Modules:
  0.0 131.4 jit_solution(16523555550942586946)
XLA Ops:
  0.0 7.2 %shard_map.109 = (bf16[64,1408]{1,0:T(8,128)(2,1)}, bf16[64,1408]{1,0:T(8,128)(2,1)}, bf16[64,1408]{1,0:T(8,128)(2,1)}, bf16[64,1408]{1,0:T(8,128)(2,1)}) custom-call(s32[1,2]{1,0:T(1,128)} %grid_ref.3, bf16[256,1408]{1,0:T(8,128)(2,1)} %bitcast.31, bf16[3,352,1408]{2,1,0:T(8,128)(2,1)} %bitcast.33, bf16[352,1408]{1,0:T(8,128)(2,1)} %out_hbm.1), custom_call_target="tpu_custom_call" | custom-call | tf_op jit(solution)/shard_map/pallas_call | solution.py:314
  7.2 1.6 %collective-permute-start = (bf16[64,1408]{1,0:T(8,128)(2,1)}, bf16[64,1408]{1,0:T(8,128)(2,1)S(1)}, u32[]{:S(2)}, u32[]{:S(2)}) collective-permute-start(bf16[64,1408]{1,0:T(8,128)(2,1)} %get-tuple-element.30), channel_id=1, source_target_pairs={{0,1},{1,2},{2,3},{3,0},{4,5},{5,6},{6,7},{7,4},{8,9},{9,10},{10,1... | collective-permute-start | bytes 540680 | tf_op jit(solution)/shard_map/ppermute | solution.py:33
  8.8 2.7 %collective-permute-start.1 = (bf16[64,1408]{1,0:T(8,128)(2,1)}, bf16[64,1408]{1,0:T(8,128)(2,1)S(1)}, u32[]{:S(2)}, u32[]{:S(2)}) collective-permute-start(bf16[64,1408]{1,0:T(8,128)(2,1)} %get-tuple-element.31), channel_id=1, source_target_pairs={{0,2},{1,3},{2,0},{3,1},{4,6},{5,7},{6,4},{7,5},{8,10},{9,11},{10,... | collective-permute-start | bytes 540680 | tf_op jit(solution)/shard_map/ppermute | solution.py:33
  11.5 1.4 %collective-permute-start.2 = (bf16[64,1408]{1,0:T(8,128)(2,1)}, bf16[64,1408]{1,0:T(8,128)(2,1)S(1)}, u32[]{:S(2)}, u32[]{:S(2)}) collective-permute-start(bf16[64,1408]{1,0:T(8,128)(2,1)} %get-tuple-element.32), channel_id=1, source_target_pairs={{0,3},{1,0},{2,1},{3,2},{4,7},{5,4},{6,5},{7,6},{8,11},{9,8},{10,9... | collective-permute-start | bytes 540680 | tf_op jit(solution)/shard_map/ppermute | solution.py:33
  17.3 2.2 %slice_bitcast_fusion.w0_ref = bf16[640,1408]{1,0:T(8,128)(2,1)S(1)} fusion(bf16[1,1408,1408]{2,1,0:T(8,128)(2,1)} %param.15), kind=kLoop, calls=%fused_computation | loop fusion | bytes 3604480 | tf_op jit(solution)/shard_map/split | solution.py:337
  20.9 20.2 %all_to_all.20 = bf16[16,16,1536]{2,1,0:T(8,128)(2,1)S(1)} all-to-all(bf16[16,16,1536]{2,1,0:T(8,128)(2,1)S(1)} %bitcast.27), channel_id=1, replica_groups=mesh['z'=8,'y'=4,'c'=2,'t'=4] {'y','t'}, dimensions={0} | all-to-all | bytes 1572864 | tf_op jit(solution)/shard_map/all_to_all | solution.py:342
  41.4 1.4 %collective-permute-done.3.other_ref = bf16[4,16,1536]{2,1,0:T(8,128)(2,1)S(1)} collective-permute-done((bf16[4,16,1536]{2,1,0:T(8,128)(2,1)S(1)}, bf16[4,16,1536]{2,1,0:T(8,128)(2,1)S(1)}, u32[]{:S(2)}, u32[]{:S(2)}) %collective-permute-start.3) | collective-permute-done | bytes 196640 | tf_op jit(solution)/shard_map/ppermute | solution.py:33
  44.8 8.1 %all-to-all-start.1 = ((bf16[8,16,1536]{2,1,0:T(8,128)(2,1)}), bf16[8,16,1536]{2,1,0:T(8,128)(2,1)S(1)}, u32[]{:S(2)}, u32[]{:S(2)}) async-start(bf16[8,16,1536]{2,1,0:T(8,128)(2,1)} %copy-done.4), calls=%async_computation.1 | async-start | bytes 786432 | tf_op jit(solution)/shard_map/all_to_all | solution.py:352
  53.6 1.7 %collective-permute-start.8 = (bf16[128,352]{0,1:T(8,128)(2,1)S(1)}, bf16[128,352]{0,1:T(8,128)(2,1)S(1)}, u32[]{:S(2)}, u32[]{:S(2)}) collective-permute-start(bf16[128,352]{0,1:T(8,128)(2,1)S(1)} %copy-done.9), channel_id=1, source_target_pairs={{0,2},{1,3},{2,0},{3,1},{4,6},{5,7},{6,4},{7,5},{8,10},{9,11},{10,... | collective-permute-start | bytes 270344 | tf_op jit(solution)/shard_map/ppermute | solution.py:33
  57.3 2.6 %collective-permute-start.17 = (bf16[176,1408]{1,0:T(8,128)(2,1)}, bf16[176,1408]{1,0:T(8,128)(2,1)}, u32[]{:S(2)}, u32[]{:S(2)}) collective-permute-start(bf16[176,1408]{1,0:T(8,128)(2,1)} %constant_dynamic-slice_fusion), channel_id=1, source_target_pairs={{0,3},{1,0},{2,1},{3,2},{4,7},{5,4},{6,5},{7,6},{8,11},{9,8},{10,9... | collective-permute-start | bytes 1486856 | tf_op jit(solution)/shard_map/ppermute | solution.py:33
  62.6 2.0 %all-to-all-done.1.parts_ref = bf16[8,16,1536]{2,1,0:T(8,128)(2,1)S(1)} async-done(((bf16[8,16,1536]{2,1,0:T(8,128)(2,1)}), bf16[8,16,1536]{2,1,0:T(8,128)(2,1)S(1)}, u32[]{:S(2)}, u32[]{:S(2)}) %all-to-all-start.1) | async-done | bytes 393248 | tf_op jit(solution)/shard_map/all_to_all | solution.py:352
  66.6 1.7 %collective-permute-start.5 = (bf16[16,1536]{1,0:T(8,128)(2,1)S(1)}, bf16[16,1536]{1,0:T(8,128)(2,1)S(1)}, u32[]{:S(2)}, u32[]{:S(2)}) collective-permute-start(bf16[16,1536]{1,0:T(8,128)(2,1)S(1)} %get-tuple-element.42.r0_ref), channel_id=1, source_target_pairs={{0,2},{1,3},{2,0},{3,1},{4,6},{5,7},{6,4},{7,5},{8,10},{9,11},{10,... | collective-permute-start | bytes 147464 | tf_op jit(solution)/shard_map/ppermute | solution.py:33
  69.6 3.5 %collective-permute-done.4.r1_ref = bf16[16,1536]{1,0:T(8,128)(2,1)S(1)} collective-permute-done((bf16[16,1536]{1,0:T(8,128)(2,1)S(1)}, bf16[16,1536]{1,0:T(8,128)(2,1)S(1)}, u32[]{:S(2)}, u32[]{:S(2)}) %collective-permute-start.4) | collective-permute-done | bytes 49184 | tf_op jit(solution)/shard_map/ppermute | solution.py:33
  73.9 1.5 %bitcast_dynamic-update-slice_fusion = bf16[4,128,352]{1,2,0:T(8,128)(2,1)} fusion(bf16[4,128,352]{1,2,0:T(8,128)(2,1)} %bitcast_dynamic-update-slice_fusion.1, s32[]{:T(128)S(6)} %select_n.43, bf16[128,352]{0,1:T(8,128)(2,1)} %collective-permute-done.9), kind=kLoop, calls=%fused_computation.3 | loop fusion | bytes 180228 | tf_op jit(solution)/shard_map/jit(dynamic_update_index_in_dim)/dynamic_update_slice | solution.py:362
  76.6 2.6 %shard_map.115 = bf16[4,3,88,128]{3,2,1,0:T(8,128)(2,1)S(1)} custom-call(s32[3]{0:T(128)S(1)} %broadcast_maximum_fusion.place_ref.facts_ref, bf16[16,1536]{1,0:T(8,128)(2,1)S(1)} %get-tuple-element.42.r0_ref, bf16[16,1536]{1,0:T(8,128)(2,1)S(1)} %collective-permute-done.4.r1_ref, bf16[16,1536]{1,0:T(8,128)(2,1)S(1)} %collective-permute-done.5.r2_ref, ...), custom_call_target="tpu_custom_call" | custom-call | tf_op jit(solution)/shard_map/pallas_call | solution.py:364
  79.3 9.1 %all_to_all.21.own_ref = bf16[4,3,88,128]{3,2,1,0:T(8,128)(2,1)S(1)} all-to-all(bf16[4,3,88,128]{3,2,1,0:T(8,128)(2,1)S(1)} %shard_map.115), channel_id=1, replica_groups=mesh['z'=8,'y'=4,'c'=2,'t'=4] {'y'}, dimensions={0} | all-to-all | bytes 540672 | tf_op jit(solution)/shard_map/all_to_all | solution.py:370
  88.4 3.5 %collective-permute-start.10 = (bf16[4,2,88,128]{3,2,1,0:T(8,128)(2,1)S(1)}, bf16[4,2,88,128]{3,2,1,0:T(8,128)(2,1)S(1)}, u32[]{:S(2)}, u32[]{:S(2)}) collective-permute-start(bf16[4,2,88,128]{3,2,1,0:T(8,128)(2,1)S(1)} %slice.7), channel_id=1, source_target_pairs={{0,32},{32,64},{64,96},{96,128},{128,160},{160,192},{192,224},{1,3... | collective-permute-start | bytes 540680 | tf_op jit(solution)/shard_map/ppermute | solution.py:28
  91.9 4.6 %collective-permute-start.11 = (bf16[4,2,88,128]{3,2,1,0:T(8,128)(2,1)S(1)}, bf16[4,2,88,128]{3,2,1,0:T(8,128)(2,1)S(1)}, u32[]{:S(2)}, u32[]{:S(2)}) collective-permute-start(bf16[4,2,88,128]{3,2,1,0:T(8,128)(2,1)S(1)} %slice.7), channel_id=1, source_target_pairs={{0,64},{32,96},{64,128},{96,160},{128,192},{160,224},{1,65},{33,97... | collective-permute-start | bytes 540680 | tf_op jit(solution)/shard_map/ppermute | solution.py:28
  96.6 4.2 %collective-permute-done.10.near_ref = bf16[4,2,88,128]{3,2,1,0:T(8,128)(2,1)S(1)} collective-permute-done((bf16[4,2,88,128]{3,2,1,0:T(8,128)(2,1)S(1)}, bf16[4,2,88,128]{3,2,1,0:T(8,128)(2,1)S(1)}, u32[]{:S(2)}, u32[]{:S(2)}) %collective-permute-start.10) | collective-permute-done | bytes 180256 | tf_op jit(solution)/shard_map/ppermute | solution.py:28
  102.5 4.3 %shard_map.116 = bf16[4,4,88,128]{3,2,1,0:T(8,128)(2,1)} custom-call(s32[3]{0:T(128)S(1)} %broadcast_maximum_fusion.place_ref.facts_ref, s32[16]{0:T(128)S(1)} %copy-done.6, bf16[4,3,88,128]{3,2,1,0:T(8,128)(2,1)S(1)} %all_to_all.21.own_ref, bf16[4,2,88,128]{3,2,1,0:T(8,128)(2,1)S(1)} %collective-permute-done.10.near_ref, ...), custom_call_target="tpu_custom_call" | custom-call | tf_op jit(solution)/shard_map/pallas_call | solution.py:378
  106.8 11.6 %all-to-all-start.3 = ((bf16[16,88,128]{2,1,0:T(8,128)(2,1)}), bf16[16,88,128]{2,1,0:T(8,128)(2,1)S(1)}, u32[]{:S(2)}, u32[]{:S(2)}) async-start(bf16[16,88,128]{2,1,0:T(8,128)(2,1)} %bitcast.17), calls=%async_computation.3 | async-start | bytes 720896 | tf_op jit(solution)/shard_map/all_to_all | solution.py:384
  119.6 1.5 %shard_map.117.prompt_ref = bf16[128,1408]{1,0:T(8,128)(2,1)S(1)} custom-call(s32[3]{0:T(128)S(1)} %broadcast_maximum_fusion.place_ref.facts_ref, bf16[16,1536]{1,0:T(8,128)(2,1)S(1)} %get-tuple-element.42.r0_ref, bf16[16,1536]{1,0:T(8,128)(2,1)S(1)} %collective-permute-done.4.r1_ref, bf16[16,1536]{1,0:T(8,128)(2,1)S(1)} %collective-permute-done.5.r2_ref, ...), custom_call_target="tpu_custom_call" | custom-call | tf_op jit(solution)/shard_map/pallas_call | solution.py:371
  121.1 7.1 %all-to-all-done.3 = bf16[16,88,128]{2,1,0:T(8,128)(2,1)S(1)} async-done(((bf16[16,88,128]{2,1,0:T(8,128)(2,1)}), bf16[16,88,128]{2,1,0:T(8,128)(2,1)S(1)}, u32[]{:S(2)}, u32[]{:S(2)}) %all-to-all-start.3) | async-done | bytes 360480 | tf_op jit(solution)/shard_map/all_to_all | solution.py:384
  128.2 3.3 %shard_map.118 = bf16[128,1408]{1,0:T(8,128)(2,1)} custom-call(s32[3]{0:T(128)S(1)} %broadcast_maximum_fusion.place_ref.facts_ref, bf16[4,2,176,128]{3,2,1,0:T(8,128)(2,1)S(1)} %bitcast.30, bf16[352,1408]{1,0:T(8,128)(2,1)S(1)} %copy-done.2, bf16[176,1408]{1,0:T(8,128)(2,1)} %collective-permute-done.15.m2_ref, ...), custom_call_target="tpu_custom_call" | custom-call | tf_op jit(solution)/shard_map/pallas_call | solution.py:385
  (68 shorter events, 20.4 us)
Async XLA Ops:
  7.2 12.4 %collective-permute-start = (bf16[64,1408]{1,0:T(8,128)(2,1)}, bf16[64,1408]{1,0:T(8,128)(2,1)S(1)}, u32[]{:S(2)}, u32[]{:S(2)}) collective-permute-start(bf16[64,1408]{1,0:T(8,128)(2,1)} %get-tuple-element.30), channel_id=1, source_target_pairs={{0,1},{1,2},{2,3},{3,0},{4,5},{5,6},{6,7},{7,4},{8,9},{9,10},{10,1... | collective-permute-start | bytes 540680 | tf_op jit(solution)/shard_map/ppermute | solution.py:33
  8.8 11.1 %collective-permute-start.1 = (bf16[64,1408]{1,0:T(8,128)(2,1)}, bf16[64,1408]{1,0:T(8,128)(2,1)S(1)}, u32[]{:S(2)}, u32[]{:S(2)}) collective-permute-start(bf16[64,1408]{1,0:T(8,128)(2,1)} %get-tuple-element.31), channel_id=1, source_target_pairs={{0,2},{1,3},{2,0},{3,1},{4,6},{5,7},{6,4},{7,5},{8,10},{9,11},{10,... | collective-permute-start | bytes 540680 | tf_op jit(solution)/shard_map/ppermute | solution.py:33
  11.5 8.3 %collective-permute-start.2 = (bf16[64,1408]{1,0:T(8,128)(2,1)}, bf16[64,1408]{1,0:T(8,128)(2,1)S(1)}, u32[]{:S(2)}, u32[]{:S(2)}) collective-permute-start(bf16[64,1408]{1,0:T(8,128)(2,1)} %get-tuple-element.32), channel_id=1, source_target_pairs={{0,3},{1,0},{2,1},{3,2},{4,7},{5,4},{6,5},{7,6},{8,11},{9,8},{10,9... | collective-permute-start | bytes 540680 | tf_op jit(solution)/shard_map/ppermute | solution.py:33
  41.2 1.5 %collective-permute-start.3 = (bf16[4,16,1536]{2,1,0:T(8,128)(2,1)S(1)}, bf16[4,16,1536]{2,1,0:T(8,128)(2,1)S(1)}, u32[]{:S(2)}, u32[]{:S(2)}) collective-permute-start(bf16[4,16,1536]{2,1,0:T(8,128)(2,1)S(1)} %shard_map.112.mine_ref), channel_id=1, source_target_pairs={{0,4},{4,0},{1,5},{5,1},{2,6},{6,2},{3,7},{7,3},{8,12},{12,8},{9,1... | collective-permute-start | bytes 589832 | tf_op jit(solution)/shard_map/ppermute | solution.py:33
  44.8 19.7 %all-to-all-start.1 = ((bf16[8,16,1536]{2,1,0:T(8,128)(2,1)}), bf16[8,16,1536]{2,1,0:T(8,128)(2,1)S(1)}, u32[]{:S(2)}, u32[]{:S(2)}) async-start(bf16[8,16,1536]{2,1,0:T(8,128)(2,1)} %copy-done.4), calls=%async_computation.1 | async-start | bytes 786432 | tf_op jit(solution)/shard_map/all_to_all | solution.py:352
  53.0 8.3 %collective-permute-start.7 = (bf16[128,352]{0,1:T(8,128)(2,1)S(1)}, bf16[128,352]{0,1:T(8,128)(2,1)S(1)}, u32[]{:S(2)}, u32[]{:S(2)}) collective-permute-start(bf16[128,352]{0,1:T(8,128)(2,1)S(1)} %copy-done.9), channel_id=1, source_target_pairs={{0,1},{1,2},{2,3},{3,0},{4,5},{5,6},{6,7},{7,4},{8,9},{9,10},{10,1... | collective-permute-start | bytes 270344 | tf_op jit(solution)/shard_map/ppermute | solution.py:33
  53.6 8.3 %collective-permute-start.8 = (bf16[128,352]{0,1:T(8,128)(2,1)S(1)}, bf16[128,352]{0,1:T(8,128)(2,1)S(1)}, u32[]{:S(2)}, u32[]{:S(2)}) collective-permute-start(bf16[128,352]{0,1:T(8,128)(2,1)S(1)} %copy-done.9), channel_id=1, source_target_pairs={{0,2},{1,3},{2,0},{3,1},{4,6},{5,7},{6,4},{7,5},{8,10},{9,11},{10,... | collective-permute-start | bytes 270344 | tf_op jit(solution)/shard_map/ppermute | solution.py:33
  55.3 12.9 %collective-permute-start.9 = (bf16[128,352]{0,1:T(8,128)(2,1)S(1)}, bf16[128,352]{0,1:T(8,128)(2,1)}, u32[]{:S(2)}, u32[]{:S(2)}) collective-permute-start(bf16[128,352]{0,1:T(8,128)(2,1)S(1)} %copy-done.9), channel_id=1, source_target_pairs={{0,3},{1,0},{2,1},{3,2},{4,7},{5,4},{6,5},{7,6},{8,11},{9,8},{10,9... | collective-permute-start | bytes 270344 | tf_op jit(solution)/shard_map/ppermute | solution.py:33
  56.6 39.9 %collective-permute-start.16 = (bf16[176,1408]{1,0:T(8,128)(2,1)}, bf16[176,1408]{1,0:T(8,128)(2,1)}, u32[]{:S(2)}, u32[]{:S(2)}) collective-permute-start(bf16[176,1408]{1,0:T(8,128)(2,1)} %constant_dynamic-slice_fusion), channel_id=1, source_target_pairs={{0,1},{1,2},{2,3},{3,0},{4,5},{5,6},{6,7},{7,4},{8,9},{9,10},{10,1... | collective-permute-start | bytes 1486856 | tf_op jit(solution)/shard_map/ppermute | solution.py:33
  57.3 44.0 %collective-permute-start.17 = (bf16[176,1408]{1,0:T(8,128)(2,1)}, bf16[176,1408]{1,0:T(8,128)(2,1)}, u32[]{:S(2)}, u32[]{:S(2)}) collective-permute-start(bf16[176,1408]{1,0:T(8,128)(2,1)} %constant_dynamic-slice_fusion), channel_id=1, source_target_pairs={{0,3},{1,0},{2,1},{3,2},{4,7},{5,4},{6,5},{7,6},{8,11},{9,8},{10,9... | collective-permute-start | bytes 1486856 | tf_op jit(solution)/shard_map/ppermute | solution.py:33
  65.7 7.3 %collective-permute-start.4 = (bf16[16,1536]{1,0:T(8,128)(2,1)S(1)}, bf16[16,1536]{1,0:T(8,128)(2,1)S(1)}, u32[]{:S(2)}, u32[]{:S(2)}) collective-permute-start(bf16[16,1536]{1,0:T(8,128)(2,1)S(1)} %get-tuple-element.42.r0_ref), channel_id=1, source_target_pairs={{0,1},{1,2},{2,3},{3,0},{4,5},{5,6},{6,7},{7,4},{8,9},{9,10},{10,1... | collective-permute-start | bytes 147464 | tf_op jit(solution)/shard_map/ppermute | solution.py:33
  66.6 10.0 %collective-permute-start.5 = (bf16[16,1536]{1,0:T(8,128)(2,1)S(1)}, bf16[16,1536]{1,0:T(8,128)(2,1)S(1)}, u32[]{:S(2)}, u32[]{:S(2)}) collective-permute-start(bf16[16,1536]{1,0:T(8,128)(2,1)S(1)} %get-tuple-element.42.r0_ref), channel_id=1, source_target_pairs={{0,2},{1,3},{2,0},{3,1},{4,6},{5,7},{6,4},{7,5},{8,10},{9,11},{10,... | collective-permute-start | bytes 147464 | tf_op jit(solution)/shard_map/ppermute | solution.py:33
  68.2 8.4 %collective-permute-start.6 = (bf16[16,1536]{1,0:T(8,128)(2,1)S(1)}, bf16[16,1536]{1,0:T(8,128)(2,1)}, u32[]{:S(2)}, u32[]{:S(2)}) collective-permute-start(bf16[16,1536]{1,0:T(8,128)(2,1)S(1)} %get-tuple-element.42.r0_ref), channel_id=1, source_target_pairs={{0,3},{1,0},{2,1},{3,2},{4,7},{5,4},{6,5},{7,6},{8,11},{9,8},{10,9... | collective-permute-start | bytes 147464 | tf_op jit(solution)/shard_map/ppermute | solution.py:33
  73.0 28.8 %collective-permute-start.15 = (bf16[176,1408]{1,0:T(8,128)(2,1)}, bf16[176,1408]{1,0:T(8,128)(2,1)}, u32[]{:S(2)}, u32[]{:S(2)}) collective-permute-start(bf16[176,1408]{1,0:T(8,128)(2,1)} %constant_dynamic-slice_fusion), channel_id=1, source_target_pairs={{0,2},{1,3},{2,0},{3,1},{4,6},{5,7},{6,4},{7,5},{8,10},{9,11},{10,... | collective-permute-start | bytes 1486856 | tf_op jit(solution)/shard_map/ppermute | solution.py:33
  88.4 39.8 %copy-start.2 = (bf16[352,1408]{1,0:T(8,128)(2,1)S(1)}, bf16[352,1408]{1,0:T(8,128)(2,1)}, u32[]{:S(2)}) copy-start(bf16[352,1408]{1,0:T(8,128)(2,1)} %w0_ref.1) | copy-start | bytes 2973700
  88.4 12.4 %collective-permute-start.10 = (bf16[4,2,88,128]{3,2,1,0:T(8,128)(2,1)S(1)}, bf16[4,2,88,128]{3,2,1,0:T(8,128)(2,1)S(1)}, u32[]{:S(2)}, u32[]{:S(2)}) collective-permute-start(bf16[4,2,88,128]{3,2,1,0:T(8,128)(2,1)S(1)} %slice.7), channel_id=1, source_target_pairs={{0,32},{32,64},{64,96},{96,128},{128,160},{160,192},{192,224},{1,3... | collective-permute-start | bytes 540680 | tf_op jit(solution)/shard_map/ppermute | solution.py:28
  91.9 8.9 %collective-permute-start.11 = (bf16[4,2,88,128]{3,2,1,0:T(8,128)(2,1)S(1)}, bf16[4,2,88,128]{3,2,1,0:T(8,128)(2,1)S(1)}, u32[]{:S(2)}, u32[]{:S(2)}) collective-permute-start(bf16[4,2,88,128]{3,2,1,0:T(8,128)(2,1)S(1)} %slice.7), channel_id=1, source_target_pairs={{0,64},{32,96},{64,128},{96,160},{128,192},{160,224},{1,65},{33,97... | collective-permute-start | bytes 540680 | tf_op jit(solution)/shard_map/ppermute | solution.py:28
  96.5 4.9 %collective-permute-start.12 = (bf16[4,2,88,128]{3,2,1,0:T(8,128)(2,1)S(1)}, bf16[4,2,88,128]{3,2,1,0:T(8,128)(2,1)S(1)}, u32[]{:S(2)}, u32[]{:S(2)}) collective-permute-start(bf16[4,2,88,128]{3,2,1,0:T(8,128)(2,1)S(1)} %slice.7), channel_id=1, source_target_pairs={{0,4},{4,0},{1,5},{5,1},{2,6},{6,2},{3,7},{7,3},{8,12},{12,8},{9,1... | collective-permute-start | bytes 540680 | tf_op jit(solution)/shard_map/ppermute | solution.py:33
  100.8 1.4 %collective-permute-start.13 = (bf16[4,2,88,128]{3,2,1,0:T(8,128)(2,1)S(1)}, bf16[4,2,88,128]{3,2,1,0:T(8,128)(2,1)S(1)}, u32[]{:S(2)}, u32[]{:S(2)}) collective-permute-start(bf16[4,2,88,128]{3,2,1,0:T(8,128)(2,1)S(1)} %collective-permute-done.10.near_ref), channel_id=1, source_target_pairs={{0,4},{4,0},{1,5},{5,1},{2,6},{6,2},{3,7},{7,3},{8,12},{12,8},{9,1... | collective-permute-start | bytes 540680 | tf_op jit(solution)/shard_map/ppermute | solution.py:33
  100.8 1.7 %collective-permute-start.14 = (bf16[4,2,88,128]{3,2,1,0:T(8,128)(2,1)S(1)}, bf16[4,2,88,128]{3,2,1,0:T(8,128)(2,1)S(1)}, u32[]{:S(2)}, u32[]{:S(2)}) collective-permute-start(bf16[4,2,88,128]{3,2,1,0:T(8,128)(2,1)S(1)} %collective-permute-done.11.far_ref), channel_id=1, source_target_pairs={{0,4},{4,0},{1,5},{5,1},{2,6},{6,2},{3,7},{7,3},{8,12},{12,8},{9,1... | collective-permute-start | bytes 540680 | tf_op jit(solution)/shard_map/ppermute | solution.py:33
  101.3 19.7 %collective-permute-start.19 = (bf16[176,1408]{1,0:T(8,128)(2,1)}, bf16[176,1408]{1,0:T(8,128)(2,1)S(1)}, u32[]{:S(2)}, u32[]{:S(2)}) collective-permute-start(bf16[176,1408]{1,0:T(8,128)(2,1)} %collective-permute-done.16.m1_ref), channel_id=1, source_target_pairs={{0,4},{4,0},{1,5},{5,1},{2,6},{6,2},{3,7},{7,3},{8,12},{12,8},{9,1... | collective-permute-start | bytes 1486856 | tf_op jit(solution)/shard_map/ppermute | solution.py:33
  101.4 19.7 %collective-permute-start.20 = (bf16[176,1408]{1,0:T(8,128)(2,1)}, bf16[176,1408]{1,0:T(8,128)(2,1)S(1)}, u32[]{:S(2)}, u32[]{:S(2)}) collective-permute-start(bf16[176,1408]{1,0:T(8,128)(2,1)} %collective-permute-done.17.m3_ref), channel_id=1, source_target_pairs={{0,4},{4,0},{1,5},{5,1},{2,6},{6,2},{3,7},{7,3},{8,12},{12,8},{9,1... | collective-permute-start | bytes 1486856 | tf_op jit(solution)/shard_map/ppermute | solution.py:33
  101.8 26.3 %collective-permute-start.18 = (bf16[176,1408]{1,0:T(8,128)(2,1)}, bf16[176,1408]{1,0:T(8,128)(2,1)}, u32[]{:S(2)}, u32[]{:S(2)}) collective-permute-start(bf16[176,1408]{1,0:T(8,128)(2,1)} %collective-permute-done.15.m2_ref), channel_id=1, source_target_pairs={{0,4},{4,0},{1,5},{5,1},{2,6},{6,2},{3,7},{7,3},{8,12},{12,8},{9,1... | collective-permute-start | bytes 1486856 | tf_op jit(solution)/shard_map/ppermute | solution.py:33
  106.8 21.4 %all-to-all-start.3 = ((bf16[16,88,128]{2,1,0:T(8,128)(2,1)}), bf16[16,88,128]{2,1,0:T(8,128)(2,1)S(1)}, u32[]{:S(2)}, u32[]{:S(2)}) async-start(bf16[16,88,128]{2,1,0:T(8,128)(2,1)} %bitcast.17), calls=%async_computation.3 | async-start | bytes 720896 | tf_op jit(solution)/shard_map/all_to_all | solution.py:384
  (9 other events, 127.8 us)

commit v14 on v12

--- a/solution.py
+++ b/solution.py
@@ -116,9 +116,9 @@
 
 def sum_kernel(parts_ref, rows_ref):
     for y in range(4):
-        total = parts_ref[y, 0].astype(F32)
+        total = parts_ref[0, y].astype(F32)
         for t in range(1, 4):
-            total = total + parts_ref[y, t].astype(F32)
+            total = total + parts_ref[t, y].astype(F32)
         rows_ref[y] = total.astype(BF)
 
 
@@ -129,7 +129,12 @@
     rows_ref[...] = total.astype(BF)
 
 
-def select_kernel(place_ref, mine_ref, other_ref, routed_ref, same_ref):
+def order_kernel(place_ref, after_ref, same_ref):
+    for index in range(3):
+        same_ref[index] = place_ref[index]
+
+
+def select_kernel(place_ref, mine_ref, other_ref, routed_ref):
     wide = mine_ref.shape[2]
     width = wide - FACTS
     rows = jnp.concatenate(
@@ -143,8 +148,6 @@
     chosen = (to == target // 16) & (source % 16 == target % 16)
     routed = dot(chosen.astype(BF), rows, (0, 0))
     routed_ref[...] = routed.astype(BF).reshape(8, 16, wide)
-    for index in range(3):
-        same_ref[index] = place_ref[index]
 
 
 def own_kernel(
@@ -178,8 +181,11 @@
     to_y = facts_ref[1:2, 0:1]
     for y in range(4):
         here = to_y == float(y)
-        rows_ref[y, :, :width] = jnp.where(here, merged, jnp.zeros_like(merged))
-        rows_ref[y, :, width:] = jnp.where(here, facts, jnp.zeros_like(facts))
+        rows = jnp.where(here, merged, jnp.zeros_like(merged))
+        ends = jnp.where(here, facts, jnp.zeros_like(facts))
+        for t in range(4):
+            rows_ref[t, y, :, :width] = rows[t * 16 : (t + 1) * 16]
+            rows_ref[t, y, :, width:] = ends[t * 16 : (t + 1) * 16]
 
 
 def placed_rows(place_ref, pieces_refs, tokens_ref):
@@ -333,17 +339,15 @@
     near_half = lax.dynamic_slice_in_dim(text_early, c * half, half, 0)
     near_half, merge_weight = lax.optimization_barrier((near_half, merge_weight))
     merge_parts = jnp.split(merge_weight[0], [640, 1024], axis=0)
-    routed = call(merge_kernel, shape((4, MERGED, wide)), [VMEM] * 8)(
+    routed = call(merge_kernel, shape((4, 4, 16, wide)), [VMEM] * 8)(
         facts, own, *shares, *merge_parts
     )
 
-    got = lax.all_to_all(routed.reshape(16, 16, wide), ("y", "t"), 0, 0, tiled=True)
+    got = lax.all_to_all(routed.reshape(16, 16, wide), ("t", "y"), 0, 0, tiled=True)
     got = call(sum_kernel, shape((4, 16, wide)), [VMEM])(got.reshape(4, 4, 16, wide))
     other = around(got, "c", 1)
-    routed, place = call(
-        select_kernel, [shape((8, 16, wide)), shape((3,), I32)], [SMEM, VMEM, VMEM], tail=(SMEM,)
-    )(place, got, other)
-    place = jnp.maximum(place, 0)
+    routed = call(select_kernel, shape((8, 16, wide)), [SMEM, VMEM, VMEM])(place, got, other)
+    place, = call(order_kernel, [shape((3,), I32)], [SMEM, pl.ANY], tail=(SMEM,))(place, routed)
     place, near_half, tokens = lax.optimization_barrier((place, near_half, tokens))
     halves = [None] + [around(near_half, "t", by) for by in (1, 3)]
     pieces = [tokens] + [around(tokens, "t", by) for by in range(1, 4)]

time: 125 us -> 127 us (1.016)
  Pallas kernels: 21.7 us -> 23.8 us
  waiting for transfers between devices: 17.9 us -> 16.5 us
    all_to_all x1, waiting for transfers between devices: 2.01 us -> 0.01 us  [local(): got = lax.all_to_all(routed, 'z', 0, 0, tiled=True)]
    pallas_call x2 -> x3, Pallas kernels: 2.35 us -> 3.87 us  [the longest x1 1.72 us: local(): call(select_kernel, shape((8, 16, wide)), [SMEM, VMEM, VMEM])]
  transfers between devices with their start and end apart: 23 -> 23, of which waited for: 9 -> 8; matrix products, arithmetic and copies ran while one was open for 8% -> 9% of each run, Pallas kernels for 7% -> 8%
where the time goes in v14:
time: 127 us; the launch traced here: 125 us
  starting transfers between devices  42.2 us (33%)
  blocking collectives  29.1 us (23%)
  Pallas kernels  23.8 us (19%)
  waiting for transfers between devices  16.5 us (13%)
  local copies, waits for them, and re-layouts  12 us (9%)
  between operations  1.55 us (1%)
    all_to_all x1, blocking collectives, local(): lax.all_to_all(routed.reshape(16, 16, wide), ('t', 'y'), 0, 0, tiled=True)  19.8 us
    ppermute x19, starting transfers between devices, around(): return lax.ppermute(x, axis, [(i, (i + by) % count) for i in range(count)])  19.5 us
    all_to_all x1, blocking collectives, local(): mine = lax.all_to_all(heads, 'y', 0, 0, tiled=True)  9.3 us
    all_to_all x1, starting transfers between devices, local(): got = lax.all_to_all(routed, 'z', 0, 0, tiled=True)  8.38 us
    ppermute x2, starting transfers between devices, ahead(): return lax.ppermute(x, axis, [(i, i + by) for i in range(count - by)])  8.08 us
    pallas_call x1, Pallas kernels, local(): call(vision_kernel, [shape((MERGED, width))] * 4, [SMEM, HBM, HBM, HBM],...  7.22 us
    all_to_all x1, waiting for transfers between devices, local(): lax.all_to_all(sent.reshape(16, HEAD, BLOCK), ('t', 'y'), 0, 0, tiled=True)  7.1 us
    all_to_all x1, starting transfers between devices, local(): lax.all_to_all(sent.reshape(16, HEAD, BLOCK), ('t', 'y'), 0, 0, tiled=True)  6.19 us
  transfers between devices with their start and end apart: 23, of which 8 were waited for; matrix products, arithmetic and copies ran while one was open for 9% of the time, Pallas kernels for 8%

profile of v14, /device:TPU:64, one launch (start us, length us, event | category | flops | bytes accessed | tf_op | source)
XLA Modules:
  0.0 125.2 jit_solution(17588145721859174535)
XLA Ops:
  0.0 7.2 %shard_map.109 = (bf16[64,1408]{1,0:T(8,128)(2,1)}, bf16[64,1408]{1,0:T(8,128)(2,1)}, bf16[64,1408]{1,0:T(8,128)(2,1)}, bf16[64,1408]{1,0:T(8,128)(2,1)}) custom-call(s32[1,2]{1,0:T(1,128)} %grid_ref.3, bf16[256,1408]{1,0:T(8,128)(2,1)} %bitcast.31, bf16[3,352,1408]{2,1,0:T(8,128)(2,1)} %bitcast.33, bf16[352,1408]{1,0:T(8,128)(2,1)} %out_hbm.1), custom_call_target="tpu_custom_call" | custom-call | tf_op jit(solution)/shard_map/pallas_call | solution.py:318
  7.2 1.6 %collective-permute-start = (bf16[64,1408]{1,0:T(8,128)(2,1)}, bf16[64,1408]{1,0:T(8,128)(2,1)S(1)}, u32[]{:S(2)}, u32[]{:S(2)}) collective-permute-start(bf16[64,1408]{1,0:T(8,128)(2,1)} %get-tuple-element.25), channel_id=1, source_target_pairs={{0,1},{1,2},{2,3},{3,0},{4,5},{5,6},{6,7},{7,4},{8,9},{9,10},{10,1... | collective-permute-start | bytes 540680 | tf_op jit(solution)/shard_map/ppermute | solution.py:33
  8.8 2.7 %collective-permute-start.1 = (bf16[64,1408]{1,0:T(8,128)(2,1)}, bf16[64,1408]{1,0:T(8,128)(2,1)S(1)}, u32[]{:S(2)}, u32[]{:S(2)}) collective-permute-start(bf16[64,1408]{1,0:T(8,128)(2,1)} %get-tuple-element.26), channel_id=1, source_target_pairs={{0,2},{1,3},{2,0},{3,1},{4,6},{5,7},{6,4},{7,5},{8,10},{9,11},{10,... | collective-permute-start | bytes 540680 | tf_op jit(solution)/shard_map/ppermute | solution.py:33
  17.3 2.2 %slice_bitcast_fusion.w0_ref = bf16[640,1408]{1,0:T(8,128)(2,1)S(1)} fusion(bf16[1,1408,1408]{2,1,0:T(8,128)(2,1)} %param.15), kind=kLoop, calls=%fused_computation | loop fusion | bytes 3604480 | tf_op jit(solution)/shard_map/split | solution.py:341
  20.9 19.8 %all_to_all.20 = bf16[16,16,1536]{2,1,0:T(8,128)(2,1)S(1)} all-to-all(bf16[16,16,1536]{2,1,0:T(8,128)(2,1)S(1)} %bitcast.27), channel_id=1, replica_groups=mesh['z'=8,'y'=4,'c'=2,'t'=4] {'t','y'}, dimensions={0} | all-to-all | bytes 1572864 | tf_op jit(solution)/shard_map/all_to_all | solution.py:346
  42.3 1.7 %shard_map.113.after_ref = bf16[8,16,1536]{2,1,0:T(8,128)(2,1)} custom-call(s32[3]{0:T(128)S(1)} %pad_add_fusion.place_ref, bf16[4,16,1536]{2,1,0:T(8,128)(2,1)S(1)} %shard_map.112.mine_ref, bf16[4,16,1536]{2,1,0:T(8,128)(2,1)S(1)} %collective-permute-done.3.other_ref), custom_call_target="tpu_custom_call" | custom-call | tf_op jit(solution)/shard_map/pallas_call | solution.py:349
  44.1 8.4 %all-to-all-start.1 = ((bf16[8,16,1536]{2,1,0:T(8,128)(2,1)}), bf16[8,16,1536]{2,1,0:T(8,128)(2,1)S(1)}, u32[]{:S(2)}, u32[]{:S(2)}) async-start(bf16[8,16,1536]{2,1,0:T(8,128)(2,1)} %shard_map.113.after_ref), calls=%async_computation.1 | async-start | bytes 786432 | tf_op jit(solution)/shard_map/all_to_all | solution.py:354
  53.9 2.3 %collective-permute-start.8 = (bf16[128,352]{0,1:T(8,128)(2,1)}, bf16[128,352]{0,1:T(8,128)(2,1)S(1)}, u32[]{:S(2)}, u32[]{:S(2)}) collective-permute-start(bf16[128,352]{0,1:T(8,128)(2,1)} %param.18), channel_id=1, source_target_pairs={{0,2},{1,3},{2,0},{3,1},{4,6},{5,7},{6,4},{7,5},{8,10},{9,11},{10,... | collective-permute-start | bytes 270344 | tf_op jit(solution)/shard_map/ppermute | solution.py:33
  58.2 2.6 %collective-permute-start.17 = (bf16[176,1408]{1,0:T(8,128)(2,1)}, bf16[176,1408]{1,0:T(8,128)(2,1)}, u32[]{:S(2)}, u32[]{:S(2)}) collective-permute-start(bf16[176,1408]{1,0:T(8,128)(2,1)} %constant_dynamic-slice_fusion), channel_id=1, source_target_pairs={{0,3},{1,0},{2,1},{3,2},{4,7},{5,4},{6,5},{7,6},{8,11},{9,8},{10,9... | collective-permute-start | bytes 1486856 | tf_op jit(solution)/shard_map/ppermute | solution.py:33
  61.6 1.5 %bitcast_dynamic-update-slice_fusion.3 = bf16[4,128,352]{1,2,0:T(8,128)(2,1)} fusion(bf16[4,128,352]{1,2,0:T(8,128)(2,1)} %broadcast_in_dim.16, s32[]{:T(128)S(6)} %select_n.37, bf16[128,352]{0,1:T(8,128)(2,1)} %param.18), kind=kLoop, calls=%fused_computation.6 | loop fusion | bytes 180228 | tf_op jit(solution)/shard_map/jit(dynamic_update_index_in_dim)/dynamic_update_slice | solution.py:359
  64.8 2.1 %collective-permute-start.5 = (bf16[16,1536]{1,0:T(8,128)(2,1)S(1)}, bf16[16,1536]{1,0:T(8,128)(2,1)S(1)}, u32[]{:S(2)}, u32[]{:S(2)}) collective-permute-start(bf16[16,1536]{1,0:T(8,128)(2,1)S(1)} %shard_map.115.r0_ref), channel_id=1, source_target_pairs={{0,2},{1,3},{2,0},{3,1},{4,6},{5,7},{6,4},{7,5},{8,10},{9,11},{10,... | collective-permute-start | bytes 147464 | tf_op jit(solution)/shard_map/ppermute | solution.py:33
  66.9 1.5 %collective-permute-start.6 = (bf16[16,1536]{1,0:T(8,128)(2,1)S(1)}, bf16[16,1536]{1,0:T(8,128)(2,1)}, u32[]{:S(2)}, u32[]{:S(2)}) collective-permute-start(bf16[16,1536]{1,0:T(8,128)(2,1)S(1)} %shard_map.115.r0_ref), channel_id=1, source_target_pairs={{0,3},{1,0},{2,1},{3,2},{4,7},{5,4},{6,5},{7,6},{8,11},{9,8},{10,9... | collective-permute-start | bytes 147464 | tf_op jit(solution)/shard_map/ppermute | solution.py:33
  68.4 1.5 %bitcast_dynamic-update-slice_fusion = bf16[4,128,352]{1,2,0:T(8,128)(2,1)} fusion(bf16[4,128,352]{1,2,0:T(8,128)(2,1)} %bitcast_dynamic-update-slice_fusion.1, s32[]{:T(128)S(6)} %select_n.43, bf16[128,352]{0,1:T(8,128)(2,1)} %collective-permute-done.9), kind=kLoop, calls=%fused_computation.3 | loop fusion | bytes 180228 | tf_op jit(solution)/shard_map/jit(dynamic_update_index_in_dim)/dynamic_update_slice | solution.py:359
  71.1 2.7 %collective-permute-done.4.r1_ref = bf16[16,1536]{1,0:T(8,128)(2,1)S(1)} collective-permute-done((bf16[16,1536]{1,0:T(8,128)(2,1)S(1)}, bf16[16,1536]{1,0:T(8,128)(2,1)S(1)}, u32[]{:S(2)}, u32[]{:S(2)}) %collective-permute-start.4) | collective-permute-done | bytes 49184 | tf_op jit(solution)/shard_map/ppermute | solution.py:33
  74.5 2.7 %shard_map.116 = bf16[4,3,88,128]{3,2,1,0:T(8,128)(2,1)S(1)} custom-call(s32[3]{0:T(128)S(1)} %shard_map.114.place_ref.facts_ref, bf16[16,1536]{1,0:T(8,128)(2,1)S(1)} %shard_map.115.r0_ref, bf16[16,1536]{1,0:T(8,128)(2,1)S(1)} %collective-permute-done.4.r1_ref, bf16[16,1536]{1,0:T(8,128)(2,1)S(1)} %collective-permute-done.5.r2_ref, ...), custom_call_target="tpu_custom_call" | custom-call | tf_op jit(solution)/shard_map/pallas_call | solution.py:361
  78.6 9.3 %all_to_all.21.own_ref = bf16[4,3,88,128]{3,2,1,0:T(8,128)(2,1)S(1)} all-to-all(bf16[4,3,88,128]{3,2,1,0:T(8,128)(2,1)S(1)} %shard_map.116), channel_id=1, replica_groups=mesh['z'=8,'y'=4,'c'=2,'t'=4] {'y'}, dimensions={0} | all-to-all | bytes 540672 | tf_op jit(solution)/shard_map/all_to_all | solution.py:368
  87.9 3.5 %collective-permute-start.10 = (bf16[4,2,88,128]{3,2,1,0:T(8,128)(2,1)S(1)}, bf16[4,2,88,128]{3,2,1,0:T(8,128)(2,1)S(1)}, u32[]{:S(2)}, u32[]{:S(2)}) collective-permute-start(bf16[4,2,88,128]{3,2,1,0:T(8,128)(2,1)S(1)} %slice.7), channel_id=1, source_target_pairs={{0,32},{32,64},{64,96},{96,128},{128,160},{160,192},{192,224},{1,3... | collective-permute-start | bytes 540680 | tf_op jit(solution)/shard_map/ppermute | solution.py:28
  91.5 4.6 %collective-permute-start.11 = (bf16[4,2,88,128]{3,2,1,0:T(8,128)(2,1)S(1)}, bf16[4,2,88,128]{3,2,1,0:T(8,128)(2,1)S(1)}, u32[]{:S(2)}, u32[]{:S(2)}) collective-permute-start(bf16[4,2,88,128]{3,2,1,0:T(8,128)(2,1)S(1)} %slice.7), channel_id=1, source_target_pairs={{0,64},{32,96},{64,128},{96,160},{128,192},{160,224},{1,65},{33,97... | collective-permute-start | bytes 540680 | tf_op jit(solution)/shard_map/ppermute | solution.py:28
  96.2 3.8 %collective-permute-done.10.near_ref = bf16[4,2,88,128]{3,2,1,0:T(8,128)(2,1)S(1)} collective-permute-done((bf16[4,2,88,128]{3,2,1,0:T(8,128)(2,1)S(1)}, bf16[4,2,88,128]{3,2,1,0:T(8,128)(2,1)S(1)}, u32[]{:S(2)}, u32[]{:S(2)}) %collective-permute-start.10) | collective-permute-done | bytes 180256 | tf_op jit(solution)/shard_map/ppermute | solution.py:28
  101.6 4.3 %shard_map.117 = bf16[4,4,88,128]{3,2,1,0:T(8,128)(2,1)} custom-call(s32[3]{0:T(128)S(1)} %shard_map.114.place_ref.facts_ref, s32[16]{0:T(128)S(1)} %copy-done.5, bf16[4,3,88,128]{3,2,1,0:T(8,128)(2,1)S(1)} %all_to_all.21.own_ref, bf16[4,2,88,128]{3,2,1,0:T(8,128)(2,1)S(1)} %collective-permute-done.10.near_ref, ...), custom_call_target="tpu_custom_call" | custom-call | tf_op jit(solution)/shard_map/pallas_call | solution.py:376
  106.0 6.2 %all-to-all-start.3 = ((bf16[16,88,128]{2,1,0:T(8,128)(2,1)}), bf16[16,88,128]{2,1,0:T(8,128)(2,1)S(1)}, u32[]{:S(2)}, u32[]{:S(2)}) async-start(bf16[16,88,128]{2,1,0:T(8,128)(2,1)} %bitcast.17), calls=%async_computation.3 | async-start | bytes 720896 | tf_op jit(solution)/shard_map/all_to_all | solution.py:382
  113.4 1.5 %shard_map.118.prompt_ref = bf16[128,1408]{1,0:T(8,128)(2,1)S(1)} custom-call(s32[3]{0:T(128)S(1)} %shard_map.114.place_ref.facts_ref, bf16[16,1536]{1,0:T(8,128)(2,1)S(1)} %shard_map.115.r0_ref, bf16[16,1536]{1,0:T(8,128)(2,1)S(1)} %collective-permute-done.4.r1_ref, bf16[16,1536]{1,0:T(8,128)(2,1)S(1)} %collective-permute-done.5.r2_ref, ...), custom_call_target="tpu_custom_call" | custom-call | tf_op jit(solution)/shard_map/pallas_call | solution.py:369
  114.9 7.1 %all-to-all-done.3 = bf16[16,88,128]{2,1,0:T(8,128)(2,1)S(1)} async-done(((bf16[16,88,128]{2,1,0:T(8,128)(2,1)}), bf16[16,88,128]{2,1,0:T(8,128)(2,1)S(1)}, u32[]{:S(2)}, u32[]{:S(2)}) %all-to-all-start.3) | async-done | bytes 360480 | tf_op jit(solution)/shard_map/all_to_all | solution.py:382
  122.0 3.3 %shard_map.119 = bf16[128,1408]{1,0:T(8,128)(2,1)} custom-call(s32[3]{0:T(128)S(1)} %shard_map.114.place_ref.facts_ref, bf16[4,2,176,128]{3,2,1,0:T(8,128)(2,1)S(1)} %bitcast.30, bf16[352,1408]{1,0:T(8,128)(2,1)S(1)} %copy-done.2, bf16[176,1408]{1,0:T(8,128)(2,1)S(1)} %collective-permute-done.15.m2_ref, bf16[176,1408]{1,0:T(8,128)(2,1)} %collective-permute-done.16.m1_ref, ...), custom_call_target="tpu_custom_call" | custom-call | tf_op jit(solution)/shard_map/pallas_call | solution.py:383
  (65 shorter events, 19.5 us)
Async XLA Ops:
  7.2 12.4 %collective-permute-start = (bf16[64,1408]{1,0:T(8,128)(2,1)}, bf16[64,1408]{1,0:T(8,128)(2,1)S(1)}, u32[]{:S(2)}, u32[]{:S(2)}) collective-permute-start(bf16[64,1408]{1,0:T(8,128)(2,1)} %get-tuple-element.25), channel_id=1, source_target_pairs={{0,1},{1,2},{2,3},{3,0},{4,5},{5,6},{6,7},{7,4},{8,9},{9,10},{10,1... | collective-permute-start | bytes 540680 | tf_op jit(solution)/shard_map/ppermute | solution.py:33
  8.8 11.1 %collective-permute-start.1 = (bf16[64,1408]{1,0:T(8,128)(2,1)}, bf16[64,1408]{1,0:T(8,128)(2,1)S(1)}, u32[]{:S(2)}, u32[]{:S(2)}) collective-permute-start(bf16[64,1408]{1,0:T(8,128)(2,1)} %get-tuple-element.26), channel_id=1, source_target_pairs={{0,2},{1,3},{2,0},{3,1},{4,6},{5,7},{6,4},{7,5},{8,10},{9,11},{10,... | collective-permute-start | bytes 540680 | tf_op jit(solution)/shard_map/ppermute | solution.py:33
  11.5 8.3 %collective-permute-start.2 = (bf16[64,1408]{1,0:T(8,128)(2,1)}, bf16[64,1408]{1,0:T(8,128)(2,1)S(1)}, u32[]{:S(2)}, u32[]{:S(2)}) collective-permute-start(bf16[64,1408]{1,0:T(8,128)(2,1)} %get-tuple-element.27), channel_id=1, source_target_pairs={{0,3},{1,0},{2,1},{3,2},{4,7},{5,4},{6,5},{7,6},{8,11},{9,8},{10,9... | collective-permute-start | bytes 540680 | tf_op jit(solution)/shard_map/ppermute | solution.py:33
  40.8 1.5 %collective-permute-start.3 = (bf16[4,16,1536]{2,1,0:T(8,128)(2,1)S(1)}, bf16[4,16,1536]{2,1,0:T(8,128)(2,1)S(1)}, u32[]{:S(2)}, u32[]{:S(2)}) collective-permute-start(bf16[4,16,1536]{2,1,0:T(8,128)(2,1)S(1)} %shard_map.112.mine_ref), channel_id=1, source_target_pairs={{0,4},{4,0},{1,5},{5,1},{2,6},{6,2},{3,7},{7,3},{8,12},{12,8},{9,1... | collective-permute-start | bytes 589832 | tf_op jit(solution)/shard_map/ppermute | solution.py:33
  44.1 20.4 %all-to-all-start.1 = ((bf16[8,16,1536]{2,1,0:T(8,128)(2,1)}), bf16[8,16,1536]{2,1,0:T(8,128)(2,1)S(1)}, u32[]{:S(2)}, u32[]{:S(2)}) async-start(bf16[8,16,1536]{2,1,0:T(8,128)(2,1)} %shard_map.113.after_ref), calls=%async_computation.1 | async-start | bytes 786432 | tf_op jit(solution)/shard_map/all_to_all | solution.py:354
  53.6 9.6 %collective-permute-start.7 = (bf16[128,352]{0,1:T(8,128)(2,1)}, bf16[128,352]{0,1:T(8,128)(2,1)S(1)}, u32[]{:S(2)}, u32[]{:S(2)}) collective-permute-start(bf16[128,352]{0,1:T(8,128)(2,1)} %param.18), channel_id=1, source_target_pairs={{0,1},{1,2},{2,3},{3,0},{4,5},{5,6},{6,7},{7,4},{8,9},{9,10},{10,1... | collective-permute-start | bytes 270344 | tf_op jit(solution)/shard_map/ppermute | solution.py:33
  53.9 9.9 %collective-permute-start.8 = (bf16[128,352]{0,1:T(8,128)(2,1)}, bf16[128,352]{0,1:T(8,128)(2,1)S(1)}, u32[]{:S(2)}, u32[]{:S(2)}) collective-permute-start(bf16[128,352]{0,1:T(8,128)(2,1)} %param.18), channel_id=1, source_target_pairs={{0,2},{1,3},{2,0},{3,1},{4,6},{5,7},{6,4},{7,5},{8,10},{9,11},{10,... | collective-permute-start | bytes 270344 | tf_op jit(solution)/shard_map/ppermute | solution.py:33
  56.2 10.7 %collective-permute-start.9 = (bf16[128,352]{0,1:T(8,128)(2,1)}, bf16[128,352]{0,1:T(8,128)(2,1)}, u32[]{:S(2)}, u32[]{:S(2)}) collective-permute-start(bf16[128,352]{0,1:T(8,128)(2,1)} %param.18), channel_id=1, source_target_pairs={{0,3},{1,0},{2,1},{3,2},{4,7},{5,4},{6,5},{7,6},{8,11},{9,8},{10,9... | collective-permute-start | bytes 270344 | tf_op jit(solution)/shard_map/ppermute | solution.py:33
  57.6 38.5 %collective-permute-start.16 = (bf16[176,1408]{1,0:T(8,128)(2,1)}, bf16[176,1408]{1,0:T(8,128)(2,1)}, u32[]{:S(2)}, u32[]{:S(2)}) collective-permute-start(bf16[176,1408]{1,0:T(8,128)(2,1)} %constant_dynamic-slice_fusion), channel_id=1, source_target_pairs={{0,1},{1,2},{2,3},{3,0},{4,5},{5,6},{6,7},{7,4},{8,9},{9,10},{10,1... | collective-permute-start | bytes 1486856 | tf_op jit(solution)/shard_map/ppermute | solution.py:33
  58.2 42.3 %collective-permute-start.17 = (bf16[176,1408]{1,0:T(8,128)(2,1)}, bf16[176,1408]{1,0:T(8,128)(2,1)}, u32[]{:S(2)}, u32[]{:S(2)}) collective-permute-start(bf16[176,1408]{1,0:T(8,128)(2,1)} %constant_dynamic-slice_fusion), channel_id=1, source_target_pairs={{0,3},{1,0},{2,1},{3,2},{4,7},{5,4},{6,5},{7,6},{8,11},{9,8},{10,9... | collective-permute-start | bytes 1486856 | tf_op jit(solution)/shard_map/ppermute | solution.py:33
  64.5 9.4 %collective-permute-start.4 = (bf16[16,1536]{1,0:T(8,128)(2,1)S(1)}, bf16[16,1536]{1,0:T(8,128)(2,1)S(1)}, u32[]{:S(2)}, u32[]{:S(2)}) collective-permute-start(bf16[16,1536]{1,0:T(8,128)(2,1)S(1)} %shard_map.115.r0_ref), channel_id=1, source_target_pairs={{0,1},{1,2},{2,3},{3,0},{4,5},{5,6},{6,7},{7,4},{8,9},{9,10},{10,1... | collective-permute-start | bytes 147464 | tf_op jit(solution)/shard_map/ppermute | solution.py:33
  64.8 9.1 %collective-permute-start.5 = (bf16[16,1536]{1,0:T(8,128)(2,1)S(1)}, bf16[16,1536]{1,0:T(8,128)(2,1)S(1)}, u32[]{:S(2)}, u32[]{:S(2)}) collective-permute-start(bf16[16,1536]{1,0:T(8,128)(2,1)S(1)} %shard_map.115.r0_ref), channel_id=1, source_target_pairs={{0,2},{1,3},{2,0},{3,1},{4,6},{5,7},{6,4},{7,5},{8,10},{9,11},{10,... | collective-permute-start | bytes 147464 | tf_op jit(solution)/shard_map/ppermute | solution.py:33
  66.9 7.6 %collective-permute-start.6 = (bf16[16,1536]{1,0:T(8,128)(2,1)S(1)}, bf16[16,1536]{1,0:T(8,128)(2,1)}, u32[]{:S(2)}, u32[]{:S(2)}) collective-permute-start(bf16[16,1536]{1,0:T(8,128)(2,1)S(1)} %shard_map.115.r0_ref), channel_id=1, source_target_pairs={{0,3},{1,0},{2,1},{3,2},{4,7},{5,4},{6,5},{7,6},{8,11},{9,8},{10,9... | collective-permute-start | bytes 147464 | tf_op jit(solution)/shard_map/ppermute | solution.py:33
  77.2 23.7 %collective-permute-start.15 = (bf16[176,1408]{1,0:T(8,128)(2,1)S(1)}, bf16[176,1408]{1,0:T(8,128)(2,1)S(1)}, u32[]{:S(2)}, u32[]{:S(2)}) collective-permute-start(bf16[176,1408]{1,0:T(8,128)(2,1)S(1)} %copy-done.8), channel_id=1, source_target_pairs={{0,2},{1,3},{2,0},{3,1},{4,6},{5,7},{6,4},{7,5},{8,10},{9,11},{10,... | collective-permute-start | bytes 1486856 | tf_op jit(solution)/shard_map/ppermute | solution.py:33
  87.9 34.0 %copy-start.2 = (bf16[352,1408]{1,0:T(8,128)(2,1)S(1)}, bf16[352,1408]{1,0:T(8,128)(2,1)}, u32[]{:S(2)}) copy-start(bf16[352,1408]{1,0:T(8,128)(2,1)} %w0_ref.1) | copy-start | bytes 2973700
  87.9 12.0 %collective-permute-start.10 = (bf16[4,2,88,128]{3,2,1,0:T(8,128)(2,1)S(1)}, bf16[4,2,88,128]{3,2,1,0:T(8,128)(2,1)S(1)}, u32[]{:S(2)}, u32[]{:S(2)}) collective-permute-start(bf16[4,2,88,128]{3,2,1,0:T(8,128)(2,1)S(1)} %slice.7), channel_id=1, source_target_pairs={{0,32},{32,64},{64,96},{96,128},{128,160},{160,192},{192,224},{1,3... | collective-permute-start | bytes 540680 | tf_op jit(solution)/shard_map/ppermute | solution.py:28
  91.5 8.5 %collective-permute-start.11 = (bf16[4,2,88,128]{3,2,1,0:T(8,128)(2,1)S(1)}, bf16[4,2,88,128]{3,2,1,0:T(8,128)(2,1)S(1)}, u32[]{:S(2)}, u32[]{:S(2)}) collective-permute-start(bf16[4,2,88,128]{3,2,1,0:T(8,128)(2,1)S(1)} %slice.7), channel_id=1, source_target_pairs={{0,64},{32,96},{64,128},{96,160},{128,192},{160,224},{1,65},{33,97... | collective-permute-start | bytes 540680 | tf_op jit(solution)/shard_map/ppermute | solution.py:28
  96.1 4.5 %collective-permute-start.12 = (bf16[4,2,88,128]{3,2,1,0:T(8,128)(2,1)S(1)}, bf16[4,2,88,128]{3,2,1,0:T(8,128)(2,1)S(1)}, u32[]{:S(2)}, u32[]{:S(2)}) collective-permute-start(bf16[4,2,88,128]{3,2,1,0:T(8,128)(2,1)S(1)} %slice.7), channel_id=1, source_target_pairs={{0,4},{4,0},{1,5},{5,1},{2,6},{6,2},{3,7},{7,3},{8,12},{12,8},{9,1... | collective-permute-start | bytes 540680 | tf_op jit(solution)/shard_map/ppermute | solution.py:33
  100.0 1.4 %collective-permute-start.13 = (bf16[4,2,88,128]{3,2,1,0:T(8,128)(2,1)S(1)}, bf16[4,2,88,128]{3,2,1,0:T(8,128)(2,1)S(1)}, u32[]{:S(2)}, u32[]{:S(2)}) collective-permute-start(bf16[4,2,88,128]{3,2,1,0:T(8,128)(2,1)S(1)} %collective-permute-done.10.near_ref), channel_id=1, source_target_pairs={{0,4},{4,0},{1,5},{5,1},{2,6},{6,2},{3,7},{7,3},{8,12},{12,8},{9,1... | collective-permute-start | bytes 540680 | tf_op jit(solution)/shard_map/ppermute | solution.py:33
  100.0 1.7 %collective-permute-start.14 = (bf16[4,2,88,128]{3,2,1,0:T(8,128)(2,1)S(1)}, bf16[4,2,88,128]{3,2,1,0:T(8,128)(2,1)S(1)}, u32[]{:S(2)}, u32[]{:S(2)}) collective-permute-start(bf16[4,2,88,128]{3,2,1,0:T(8,128)(2,1)S(1)} %collective-permute-done.11.far_ref), channel_id=1, source_target_pairs={{0,4},{4,0},{1,5},{5,1},{2,6},{6,2},{3,7},{7,3},{8,12},{12,8},{9,1... | collective-permute-start | bytes 540680 | tf_op jit(solution)/shard_map/ppermute | solution.py:33
  100.5 14.4 %collective-permute-start.19 = (bf16[176,1408]{1,0:T(8,128)(2,1)}, bf16[176,1408]{1,0:T(8,128)(2,1)S(1)}, u32[]{:S(2)}, u32[]{:S(2)}) collective-permute-start(bf16[176,1408]{1,0:T(8,128)(2,1)} %collective-permute-done.16.m1_ref), channel_id=1, source_target_pairs={{0,4},{4,0},{1,5},{5,1},{2,6},{6,2},{3,7},{7,3},{8,12},{12,8},{9,1... | collective-permute-start | bytes 1486856 | tf_op jit(solution)/shard_map/ppermute | solution.py:33
  100.6 14.3 %collective-permute-start.20 = (bf16[176,1408]{1,0:T(8,128)(2,1)}, bf16[176,1408]{1,0:T(8,128)(2,1)}, u32[]{:S(2)}, u32[]{:S(2)}) collective-permute-start(bf16[176,1408]{1,0:T(8,128)(2,1)} %collective-permute-done.17.m3_ref), channel_id=1, source_target_pairs={{0,4},{4,0},{1,5},{5,1},{2,6},{6,2},{3,7},{7,3},{8,12},{12,8},{9,1... | collective-permute-start | bytes 1486856 | tf_op jit(solution)/shard_map/ppermute | solution.py:33
  101.0 21.0 %collective-permute-start.18 = (bf16[176,1408]{1,0:T(8,128)(2,1)S(1)}, bf16[176,1408]{1,0:T(8,128)(2,1)}, u32[]{:S(2)}, u32[]{:S(2)}) collective-permute-start(bf16[176,1408]{1,0:T(8,128)(2,1)S(1)} %collective-permute-done.15.m2_ref), channel_id=1, source_target_pairs={{0,4},{4,0},{1,5},{5,1},{2,6},{6,2},{3,7},{7,3},{8,12},{12,8},{9,1... | collective-permute-start | bytes 1486856 | tf_op jit(solution)/shard_map/ppermute | solution.py:33
  106.0 16.0 %all-to-all-start.3 = ((bf16[16,88,128]{2,1,0:T(8,128)(2,1)}), bf16[16,88,128]{2,1,0:T(8,128)(2,1)S(1)}, u32[]{:S(2)}, u32[]{:S(2)}) async-start(bf16[16,88,128]{2,1,0:T(8,128)(2,1)} %bitcast.17), calls=%async_computation.3 | async-start | bytes 720896 | tf_op jit(solution)/shard_map/all_to_all | solution.py:382
  (8 other events, 94.1 us)

commit v15 on v12

--- a/solution.py
+++ b/solution.py
@@ -129,7 +129,12 @@
     rows_ref[...] = total.astype(BF)
 
 
-def select_kernel(place_ref, mine_ref, other_ref, routed_ref, same_ref):
+def order_kernel(place_ref, after_ref, same_ref):
+    for index in range(3):
+        same_ref[index] = place_ref[index]
+
+
+def select_kernel(place_ref, mine_ref, other_ref, routed_ref):
     wide = mine_ref.shape[2]
     width = wide - FACTS
     rows = jnp.concatenate(
@@ -143,8 +148,6 @@
     chosen = (to == target // 16) & (source % 16 == target % 16)
     routed = dot(chosen.astype(BF), rows, (0, 0))
     routed_ref[...] = routed.astype(BF).reshape(8, 16, wide)
-    for index in range(3):
-        same_ref[index] = place_ref[index]
 
 
 def own_kernel(
@@ -340,10 +343,8 @@
     got = lax.all_to_all(routed.reshape(16, 16, wide), ("y", "t"), 0, 0, tiled=True)
     got = call(sum_kernel, shape((4, 16, wide)), [VMEM])(got.reshape(4, 4, 16, wide))
     other = around(got, "c", 1)
-    routed, place = call(
-        select_kernel, [shape((8, 16, wide)), shape((3,), I32)], [SMEM, VMEM, VMEM], tail=(SMEM,)
-    )(place, got, other)
-    place = jnp.maximum(place, 0)
+    routed = call(select_kernel, shape((8, 16, wide)), [SMEM, VMEM, VMEM])(place, got, other)
+    place, = call(order_kernel, [shape((3,), I32)], [SMEM, pl.ANY], tail=(SMEM,))(place, routed)
     place, near_half, tokens = lax.optimization_barrier((place, near_half, tokens))
     halves = [None] + [around(near_half, "t", by) for by in (1, 3)]
     pieces = [tokens] + [around(tokens, "t", by) for by in range(1, 4)]

time: 125 us -> 127 us (1.016)
  starting transfers between devices: 41.4 us -> 39.2 us
  Pallas kernels: 21.7 us -> 23.8 us
  waiting for transfers between devices: 17.9 us -> 19.3 us
    all_to_all x1, starting transfers between devices: 6.46 us -> 3.55 us  [local(): lax.all_to_all(sent.reshape(16, HEAD, BLOCK), ('t', 'y'), 0, 0, tiled=True)]
    ppermute x2, waiting for transfers between devices: 3.96 us -> 6.36 us  [ahead(): return lax.ppermute(x, axis, [(i, i + by) for i in range(count - by)])]
    all_to_all x1, waiting for transfers between devices: 2.01 us -> 0.01 us  [local(): got = lax.all_to_all(routed, 'z', 0, 0, tiled=True)]
    pallas_call x1 -> x2, Pallas kernels: 1.34 us -> 2.86 us  [the longest x1 1.73 us: local(): call(select_kernel, shape((8, 16, wide)), [SMEM, VMEM, VMEM])]
  transfers between devices with their start and end apart: 23 -> 23, of which waited for: 9 -> 8; matrix products, arithmetic and copies ran while one was open for 8% -> 9% of each run, Pallas kernels for 7% -> 8%
where the time goes in v15:
time: 127 us; the launch traced here: 125 us
  starting transfers between devices  39.2 us (31%)
  blocking collectives  29.2 us (23%)
  Pallas kernels  23.8 us (19%)
  waiting for transfers between devices  19.3 us (15%)
  local copies, waits for them, and re-layouts  12 us (9%)
  between operations  1.55 us (1%)
    all_to_all x1, blocking collectives, local(): lax.all_to_all(routed.reshape(16, 16, wide), ('y', 't'), 0, 0, tiled=True)  20.1 us
    ppermute x19, starting transfers between devices, around(): return lax.ppermute(x, axis, [(i, (i + by) % count) for i in range(count)])  19.2 us
    all_to_all x1, blocking collectives, local(): mine = lax.all_to_all(heads, 'y', 0, 0, tiled=True)  9.1 us
    all_to_all x1, starting transfers between devices, local(): got = lax.all_to_all(routed, 'z', 0, 0, tiled=True)  8.37 us
    ppermute x2, starting transfers between devices, ahead(): return lax.ppermute(x, axis, [(i, i + by) for i in range(count - by)])  8.08 us
    all_to_all x1, waiting for transfers between devices, local(): lax.all_to_all(sent.reshape(16, HEAD, BLOCK), ('t', 'y'), 0, 0, tiled=True)  7.33 us
    pallas_call x1, Pallas kernels, local(): call(vision_kernel, [shape((MERGED, width))] * 4, [SMEM, HBM, HBM, HBM],...  7.22 us
    ppermute x2, waiting for transfers between devices, ahead(): return lax.ppermute(x, axis, [(i, i + by) for i in range(count - by)])  6.36 us
  transfers between devices with their start and end apart: 23, of which 8 were waited for; matrix products, arithmetic and copies ran while one was open for 9% of the time, Pallas kernels for 8%

profile of v15, /device:TPU:64, one launch (start us, length us, event | category | flops | bytes accessed | tf_op | source)
XLA Modules:
  0.0 125.0 jit_solution(188108594536010074)
XLA Ops:
  0.0 7.2 %shard_map.109 = (bf16[64,1408]{1,0:T(8,128)(2,1)}, bf16[64,1408]{1,0:T(8,128)(2,1)}, bf16[64,1408]{1,0:T(8,128)(2,1)}, bf16[64,1408]{1,0:T(8,128)(2,1)}) custom-call(s32[1,2]{1,0:T(1,128)} %grid_ref.3, bf16[256,1408]{1,0:T(8,128)(2,1)} %bitcast.31, bf16[3,352,1408]{2,1,0:T(8,128)(2,1)} %bitcast.33, bf16[352,1408]{1,0:T(8,128)(2,1)} %out_hbm.1), custom_call_target="tpu_custom_call" | custom-call | tf_op jit(solution)/shard_map/pallas_call | solution.py:315
  7.2 1.6 %collective-permute-start = (bf16[64,1408]{1,0:T(8,128)(2,1)}, bf16[64,1408]{1,0:T(8,128)(2,1)S(1)}, u32[]{:S(2)}, u32[]{:S(2)}) collective-permute-start(bf16[64,1408]{1,0:T(8,128)(2,1)} %get-tuple-element.25), channel_id=1, source_target_pairs={{0,1},{1,2},{2,3},{3,0},{4,5},{5,6},{6,7},{7,4},{8,9},{9,10},{10,1... | collective-permute-start | bytes 540680 | tf_op jit(solution)/shard_map/ppermute | solution.py:33
  8.8 2.7 %collective-permute-start.1 = (bf16[64,1408]{1,0:T(8,128)(2,1)}, bf16[64,1408]{1,0:T(8,128)(2,1)S(1)}, u32[]{:S(2)}, u32[]{:S(2)}) collective-permute-start(bf16[64,1408]{1,0:T(8,128)(2,1)} %get-tuple-element.26), channel_id=1, source_target_pairs={{0,2},{1,3},{2,0},{3,1},{4,6},{5,7},{6,4},{7,5},{8,10},{9,11},{10,... | collective-permute-start | bytes 540680 | tf_op jit(solution)/shard_map/ppermute | solution.py:33
  17.3 2.2 %slice_bitcast_fusion.w0_ref = bf16[640,1408]{1,0:T(8,128)(2,1)S(1)} fusion(bf16[1,1408,1408]{2,1,0:T(8,128)(2,1)} %param.15), kind=kLoop, calls=%fused_computation | loop fusion | bytes 3604480 | tf_op jit(solution)/shard_map/split | solution.py:338
  20.9 20.1 %all_to_all.20 = bf16[16,16,1536]{2,1,0:T(8,128)(2,1)S(1)} all-to-all(bf16[16,16,1536]{2,1,0:T(8,128)(2,1)S(1)} %bitcast.27), channel_id=1, replica_groups=mesh['z'=8,'y'=4,'c'=2,'t'=4] {'y','t'}, dimensions={0} | all-to-all | bytes 1572864 | tf_op jit(solution)/shard_map/all_to_all | solution.py:343
  42.6 1.7 %shard_map.113.after_ref = bf16[8,16,1536]{2,1,0:T(8,128)(2,1)} custom-call(s32[3]{0:T(128)S(1)} %pad_add_fusion.place_ref, bf16[4,16,1536]{2,1,0:T(8,128)(2,1)S(1)} %shard_map.112.mine_ref, bf16[4,16,1536]{2,1,0:T(8,128)(2,1)S(1)} %collective-permute-done.3.other_ref), custom_call_target="tpu_custom_call" | custom-call | tf_op jit(solution)/shard_map/pallas_call | solution.py:346
  44.3 8.4 %all-to-all-start.1 = ((bf16[8,16,1536]{2,1,0:T(8,128)(2,1)}), bf16[8,16,1536]{2,1,0:T(8,128)(2,1)S(1)}, u32[]{:S(2)}, u32[]{:S(2)}) async-start(bf16[8,16,1536]{2,1,0:T(8,128)(2,1)} %shard_map.113.after_ref), calls=%async_computation.1 | async-start | bytes 786432 | tf_op jit(solution)/shard_map/all_to_all | solution.py:351
  54.5 1.7 %collective-permute-start.8 = (bf16[128,352]{0,1:T(8,128)(2,1)}, bf16[128,352]{0,1:T(8,128)(2,1)S(1)}, u32[]{:S(2)}, u32[]{:S(2)}) collective-permute-start(bf16[128,352]{0,1:T(8,128)(2,1)} %param.18), channel_id=1, source_target_pairs={{0,2},{1,3},{2,0},{3,1},{4,6},{5,7},{6,4},{7,5},{8,10},{9,11},{10,... | collective-permute-start | bytes 270344 | tf_op jit(solution)/shard_map/ppermute | solution.py:33
  58.2 2.6 %collective-permute-start.17 = (bf16[176,1408]{1,0:T(8,128)(2,1)}, bf16[176,1408]{1,0:T(8,128)(2,1)}, u32[]{:S(2)}, u32[]{:S(2)}) collective-permute-start(bf16[176,1408]{1,0:T(8,128)(2,1)} %constant_dynamic-slice_fusion), channel_id=1, source_target_pairs={{0,3},{1,0},{2,1},{3,2},{4,7},{5,4},{6,5},{7,6},{8,11},{9,8},{10,9... | collective-permute-start | bytes 1486856 | tf_op jit(solution)/shard_map/ppermute | solution.py:33
  61.5 1.5 %bitcast_dynamic-update-slice_fusion.3 = bf16[4,128,352]{1,2,0:T(8,128)(2,1)} fusion(bf16[4,128,352]{1,2,0:T(8,128)(2,1)} %broadcast_in_dim.16, s32[]{:T(128)S(6)} %select_n.37, bf16[128,352]{0,1:T(8,128)(2,1)} %param.18), kind=kLoop, calls=%fused_computation.6 | loop fusion | bytes 180228 | tf_op jit(solution)/shard_map/jit(dynamic_update_index_in_dim)/dynamic_update_slice | solution.py:356
  65.2 1.7 %collective-permute-start.5 = (bf16[16,1536]{1,0:T(8,128)(2,1)S(1)}, bf16[16,1536]{1,0:T(8,128)(2,1)S(1)}, u32[]{:S(2)}, u32[]{:S(2)}) collective-permute-start(bf16[16,1536]{1,0:T(8,128)(2,1)S(1)} %shard_map.115.r0_ref), channel_id=1, source_target_pairs={{0,2},{1,3},{2,0},{3,1},{4,6},{5,7},{6,4},{7,5},{8,10},{9,11},{10,... | collective-permute-start | bytes 147464 | tf_op jit(solution)/shard_map/ppermute | solution.py:33
  66.9 1.8 %collective-permute-start.6 = (bf16[16,1536]{1,0:T(8,128)(2,1)S(1)}, bf16[16,1536]{1,0:T(8,128)(2,1)}, u32[]{:S(2)}, u32[]{:S(2)}) collective-permute-start(bf16[16,1536]{1,0:T(8,128)(2,1)S(1)} %shard_map.115.r0_ref), channel_id=1, source_target_pairs={{0,3},{1,0},{2,1},{3,2},{4,7},{5,4},{6,5},{7,6},{8,11},{9,8},{10,9... | collective-permute-start | bytes 147464 | tf_op jit(solution)/shard_map/ppermute | solution.py:33
  68.7 1.5 %bitcast_dynamic-update-slice_fusion = bf16[4,128,352]{1,2,0:T(8,128)(2,1)} fusion(bf16[4,128,352]{1,2,0:T(8,128)(2,1)} %bitcast_dynamic-update-slice_fusion.1, s32[]{:T(128)S(6)} %select_n.43, bf16[128,352]{0,1:T(8,128)(2,1)} %collective-permute-done.9), kind=kLoop, calls=%fused_computation.3 | loop fusion | bytes 180228 | tf_op jit(solution)/shard_map/jit(dynamic_update_index_in_dim)/dynamic_update_slice | solution.py:356
  71.4 2.7 %collective-permute-done.4.r1_ref = bf16[16,1536]{1,0:T(8,128)(2,1)S(1)} collective-permute-done((bf16[16,1536]{1,0:T(8,128)(2,1)S(1)}, bf16[16,1536]{1,0:T(8,128)(2,1)S(1)}, u32[]{:S(2)}, u32[]{:S(2)}) %collective-permute-start.4) | collective-permute-done | bytes 49184 | tf_op jit(solution)/shard_map/ppermute | solution.py:33
  74.8 2.7 %shard_map.116 = bf16[4,3,88,128]{3,2,1,0:T(8,128)(2,1)S(1)} custom-call(s32[3]{0:T(128)S(1)} %shard_map.114.place_ref.facts_ref, bf16[16,1536]{1,0:T(8,128)(2,1)S(1)} %shard_map.115.r0_ref, bf16[16,1536]{1,0:T(8,128)(2,1)S(1)} %collective-permute-done.4.r1_ref, bf16[16,1536]{1,0:T(8,128)(2,1)S(1)} %collective-permute-done.5.r2_ref, ...), custom_call_target="tpu_custom_call" | custom-call | tf_op jit(solution)/shard_map/pallas_call | solution.py:358
  78.6 9.1 %all_to_all.21.own_ref = bf16[4,3,88,128]{3,2,1,0:T(8,128)(2,1)S(1)} all-to-all(bf16[4,3,88,128]{3,2,1,0:T(8,128)(2,1)S(1)} %shard_map.116), channel_id=1, replica_groups=mesh['z'=8,'y'=4,'c'=2,'t'=4] {'y'}, dimensions={0} | all-to-all | bytes 540672 | tf_op jit(solution)/shard_map/all_to_all | solution.py:365
  87.7 3.5 %collective-permute-start.10 = (bf16[4,2,88,128]{3,2,1,0:T(8,128)(2,1)S(1)}, bf16[4,2,88,128]{3,2,1,0:T(8,128)(2,1)S(1)}, u32[]{:S(2)}, u32[]{:S(2)}) collective-permute-start(bf16[4,2,88,128]{3,2,1,0:T(8,128)(2,1)S(1)} %slice.7), channel_id=1, source_target_pairs={{0,32},{32,64},{64,96},{96,128},{128,160},{160,192},{192,224},{1,3... | collective-permute-start | bytes 540680 | tf_op jit(solution)/shard_map/ppermute | solution.py:28
  91.2 4.6 %collective-permute-start.11 = (bf16[4,2,88,128]{3,2,1,0:T(8,128)(2,1)S(1)}, bf16[4,2,88,128]{3,2,1,0:T(8,128)(2,1)S(1)}, u32[]{:S(2)}, u32[]{:S(2)}) collective-permute-start(bf16[4,2,88,128]{3,2,1,0:T(8,128)(2,1)S(1)} %slice.7), channel_id=1, source_target_pairs={{0,64},{32,96},{64,128},{96,160},{128,192},{160,224},{1,65},{33,97... | collective-permute-start | bytes 540680 | tf_op jit(solution)/shard_map/ppermute | solution.py:28
  95.9 1.6 %collective-permute-done.10.near_ref = bf16[4,2,88,128]{3,2,1,0:T(8,128)(2,1)S(1)} collective-permute-done((bf16[4,2,88,128]{3,2,1,0:T(8,128)(2,1)S(1)}, bf16[4,2,88,128]{3,2,1,0:T(8,128)(2,1)S(1)}, u32[]{:S(2)}, u32[]{:S(2)}) %collective-permute-start.10) | collective-permute-done | bytes 180256 | tf_op jit(solution)/shard_map/ppermute | solution.py:28
  97.6 4.7 %collective-permute-done.11.far_ref = bf16[4,2,88,128]{3,2,1,0:T(8,128)(2,1)S(1)} collective-permute-done((bf16[4,2,88,128]{3,2,1,0:T(8,128)(2,1)S(1)}, bf16[4,2,88,128]{3,2,1,0:T(8,128)(2,1)S(1)}, u32[]{:S(2)}, u32[]{:S(2)}) %collective-permute-start.11) | collective-permute-done | bytes 180256 | tf_op jit(solution)/shard_map/ppermute | solution.py:28
  103.9 4.3 %shard_map.117 = bf16[4,4,88,128]{3,2,1,0:T(8,128)(2,1)} custom-call(s32[3]{0:T(128)S(1)} %shard_map.114.place_ref.facts_ref, s32[16]{0:T(128)S(1)} %copy-done.5, bf16[4,3,88,128]{3,2,1,0:T(8,128)(2,1)S(1)} %all_to_all.21.own_ref, bf16[4,2,88,128]{3,2,1,0:T(8,128)(2,1)S(1)} %collective-permute-done.10.near_ref, ...), custom_call_target="tpu_custom_call" | custom-call | tf_op jit(solution)/shard_map/pallas_call | solution.py:373
  108.2 3.5 %all-to-all-start.3 = ((bf16[16,88,128]{2,1,0:T(8,128)(2,1)}), bf16[16,88,128]{2,1,0:T(8,128)(2,1)S(1)}, u32[]{:S(2)}, u32[]{:S(2)}) async-start(bf16[16,88,128]{2,1,0:T(8,128)(2,1)} %bitcast.17), calls=%async_computation.3 | async-start | bytes 720896 | tf_op jit(solution)/shard_map/all_to_all | solution.py:379
  114.5 7.3 %all-to-all-done.3 = bf16[16,88,128]{2,1,0:T(8,128)(2,1)S(1)} async-done(((bf16[16,88,128]{2,1,0:T(8,128)(2,1)}), bf16[16,88,128]{2,1,0:T(8,128)(2,1)S(1)}, u32[]{:S(2)}, u32[]{:S(2)}) %all-to-all-start.3) | async-done | bytes 360480 | tf_op jit(solution)/shard_map/all_to_all | solution.py:379
  121.8 3.3 %shard_map.119 = bf16[128,1408]{1,0:T(8,128)(2,1)} custom-call(s32[3]{0:T(128)S(1)} %shard_map.114.place_ref.facts_ref, bf16[4,2,176,128]{3,2,1,0:T(8,128)(2,1)S(1)} %bitcast.30, bf16[352,1408]{1,0:T(8,128)(2,1)S(1)} %copy-done.2, bf16[176,1408]{1,0:T(8,128)(2,1)S(1)} %collective-permute-done.15.m2_ref, bf16[176,1408]{1,0:T(8,128)(2,1)} %collective-permute-done.16.m1_ref, ...), custom_call_target="tpu_custom_call" | custom-call | tf_op jit(solution)/shard_map/pallas_call | solution.py:380
  (65 shorter events, 21.5 us)
Async XLA Ops:
  7.2 12.4 %collective-permute-start = (bf16[64,1408]{1,0:T(8,128)(2,1)}, bf16[64,1408]{1,0:T(8,128)(2,1)S(1)}, u32[]{:S(2)}, u32[]{:S(2)}) collective-permute-start(bf16[64,1408]{1,0:T(8,128)(2,1)} %get-tuple-element.25), channel_id=1, source_target_pairs={{0,1},{1,2},{2,3},{3,0},{4,5},{5,6},{6,7},{7,4},{8,9},{9,10},{10,1... | collective-permute-start | bytes 540680 | tf_op jit(solution)/shard_map/ppermute | solution.py:33
  8.8 11.1 %collective-permute-start.1 = (bf16[64,1408]{1,0:T(8,128)(2,1)}, bf16[64,1408]{1,0:T(8,128)(2,1)S(1)}, u32[]{:S(2)}, u32[]{:S(2)}) collective-permute-start(bf16[64,1408]{1,0:T(8,128)(2,1)} %get-tuple-element.26), channel_id=1, source_target_pairs={{0,2},{1,3},{2,0},{3,1},{4,6},{5,7},{6,4},{7,5},{8,10},{9,11},{10,... | collective-permute-start | bytes 540680 | tf_op jit(solution)/shard_map/ppermute | solution.py:33
  11.5 8.3 %collective-permute-start.2 = (bf16[64,1408]{1,0:T(8,128)(2,1)}, bf16[64,1408]{1,0:T(8,128)(2,1)S(1)}, u32[]{:S(2)}, u32[]{:S(2)}) collective-permute-start(bf16[64,1408]{1,0:T(8,128)(2,1)} %get-tuple-element.27), channel_id=1, source_target_pairs={{0,3},{1,0},{2,1},{3,2},{4,7},{5,4},{6,5},{7,6},{8,11},{9,8},{10,9... | collective-permute-start | bytes 540680 | tf_op jit(solution)/shard_map/ppermute | solution.py:33
  41.1 1.5 %collective-permute-start.3 = (bf16[4,16,1536]{2,1,0:T(8,128)(2,1)S(1)}, bf16[4,16,1536]{2,1,0:T(8,128)(2,1)S(1)}, u32[]{:S(2)}, u32[]{:S(2)}) collective-permute-start(bf16[4,16,1536]{2,1,0:T(8,128)(2,1)S(1)} %shard_map.112.mine_ref), channel_id=1, source_target_pairs={{0,4},{4,0},{1,5},{5,1},{2,6},{6,2},{3,7},{7,3},{8,12},{12,8},{9,1... | collective-permute-start | bytes 589832 | tf_op jit(solution)/shard_map/ppermute | solution.py:33
  44.3 20.0 %all-to-all-start.1 = ((bf16[8,16,1536]{2,1,0:T(8,128)(2,1)}), bf16[8,16,1536]{2,1,0:T(8,128)(2,1)S(1)}, u32[]{:S(2)}, u32[]{:S(2)}) async-start(bf16[8,16,1536]{2,1,0:T(8,128)(2,1)} %shard_map.113.after_ref), calls=%async_computation.1 | async-start | bytes 786432 | tf_op jit(solution)/shard_map/all_to_all | solution.py:351
  53.8 9.2 %collective-permute-start.7 = (bf16[128,352]{0,1:T(8,128)(2,1)}, bf16[128,352]{0,1:T(8,128)(2,1)S(1)}, u32[]{:S(2)}, u32[]{:S(2)}) collective-permute-start(bf16[128,352]{0,1:T(8,128)(2,1)} %param.18), channel_id=1, source_target_pairs={{0,1},{1,2},{2,3},{3,0},{4,5},{5,6},{6,7},{7,4},{8,9},{9,10},{10,1... | collective-permute-start | bytes 270344 | tf_op jit(solution)/shard_map/ppermute | solution.py:33
  54.5 9.2 %collective-permute-start.8 = (bf16[128,352]{0,1:T(8,128)(2,1)}, bf16[128,352]{0,1:T(8,128)(2,1)S(1)}, u32[]{:S(2)}, u32[]{:S(2)}) collective-permute-start(bf16[128,352]{0,1:T(8,128)(2,1)} %param.18), channel_id=1, source_target_pairs={{0,2},{1,3},{2,0},{3,1},{4,6},{5,7},{6,4},{7,5},{8,10},{9,11},{10,... | collective-permute-start | bytes 270344 | tf_op jit(solution)/shard_map/ppermute | solution.py:33
  56.2 10.7 %collective-permute-start.9 = (bf16[128,352]{0,1:T(8,128)(2,1)}, bf16[128,352]{0,1:T(8,128)(2,1)}, u32[]{:S(2)}, u32[]{:S(2)}) collective-permute-start(bf16[128,352]{0,1:T(8,128)(2,1)} %param.18), channel_id=1, source_target_pairs={{0,3},{1,0},{2,1},{3,2},{4,7},{5,4},{6,5},{7,6},{8,11},{9,8},{10,9... | collective-permute-start | bytes 270344 | tf_op jit(solution)/shard_map/ppermute | solution.py:33
  57.5 38.3 %collective-permute-start.16 = (bf16[176,1408]{1,0:T(8,128)(2,1)}, bf16[176,1408]{1,0:T(8,128)(2,1)}, u32[]{:S(2)}, u32[]{:S(2)}) collective-permute-start(bf16[176,1408]{1,0:T(8,128)(2,1)} %constant_dynamic-slice_fusion), channel_id=1, source_target_pairs={{0,1},{1,2},{2,3},{3,0},{4,5},{5,6},{6,7},{7,4},{8,9},{9,10},{10,1... | collective-permute-start | bytes 1486856 | tf_op jit(solution)/shard_map/ppermute | solution.py:33
  58.2 44.1 %collective-permute-start.17 = (bf16[176,1408]{1,0:T(8,128)(2,1)}, bf16[176,1408]{1,0:T(8,128)(2,1)}, u32[]{:S(2)}, u32[]{:S(2)}) collective-permute-start(bf16[176,1408]{1,0:T(8,128)(2,1)} %constant_dynamic-slice_fusion), channel_id=1, source_target_pairs={{0,3},{1,0},{2,1},{3,2},{4,7},{5,4},{6,5},{7,6},{8,11},{9,8},{10,9... | collective-permute-start | bytes 1486856 | tf_op jit(solution)/shard_map/ppermute | solution.py:33
  64.4 9.7 %collective-permute-start.4 = (bf16[16,1536]{1,0:T(8,128)(2,1)S(1)}, bf16[16,1536]{1,0:T(8,128)(2,1)S(1)}, u32[]{:S(2)}, u32[]{:S(2)}) collective-permute-start(bf16[16,1536]{1,0:T(8,128)(2,1)S(1)} %shard_map.115.r0_ref), channel_id=1, source_target_pairs={{0,1},{1,2},{2,3},{3,0},{4,5},{5,6},{6,7},{7,4},{8,9},{9,10},{10,1... | collective-permute-start | bytes 147464 | tf_op jit(solution)/shard_map/ppermute | solution.py:33
  65.2 8.9 %collective-permute-start.5 = (bf16[16,1536]{1,0:T(8,128)(2,1)S(1)}, bf16[16,1536]{1,0:T(8,128)(2,1)S(1)}, u32[]{:S(2)}, u32[]{:S(2)}) collective-permute-start(bf16[16,1536]{1,0:T(8,128)(2,1)S(1)} %shard_map.115.r0_ref), channel_id=1, source_target_pairs={{0,2},{1,3},{2,0},{3,1},{4,6},{5,7},{6,4},{7,5},{8,10},{9,11},{10,... | collective-permute-start | bytes 147464 | tf_op jit(solution)/shard_map/ppermute | solution.py:33
  66.9 7.9 %collective-permute-start.6 = (bf16[16,1536]{1,0:T(8,128)(2,1)S(1)}, bf16[16,1536]{1,0:T(8,128)(2,1)}, u32[]{:S(2)}, u32[]{:S(2)}) collective-permute-start(bf16[16,1536]{1,0:T(8,128)(2,1)S(1)} %shard_map.115.r0_ref), channel_id=1, source_target_pairs={{0,3},{1,0},{2,1},{3,2},{4,7},{5,4},{6,5},{7,6},{8,11},{9,8},{10,9... | collective-permute-start | bytes 147464 | tf_op jit(solution)/shard_map/ppermute | solution.py:33
  77.5 25.4 %collective-permute-start.15 = (bf16[176,1408]{1,0:T(8,128)(2,1)S(1)}, bf16[176,1408]{1,0:T(8,128)(2,1)S(1)}, u32[]{:S(2)}, u32[]{:S(2)}) collective-permute-start(bf16[176,1408]{1,0:T(8,128)(2,1)S(1)} %copy-done.8), channel_id=1, source_target_pairs={{0,2},{1,3},{2,0},{3,1},{4,6},{5,7},{6,4},{7,5},{8,10},{9,11},{10,... | collective-permute-start | bytes 1486856 | tf_op jit(solution)/shard_map/ppermute | solution.py:33
  87.7 34.1 %copy-start.2 = (bf16[352,1408]{1,0:T(8,128)(2,1)S(1)}, bf16[352,1408]{1,0:T(8,128)(2,1)}, u32[]{:S(2)}) copy-start(bf16[352,1408]{1,0:T(8,128)(2,1)} %w0_ref.1) | copy-start | bytes 2973700
  87.7 9.9 %collective-permute-start.10 = (bf16[4,2,88,128]{3,2,1,0:T(8,128)(2,1)S(1)}, bf16[4,2,88,128]{3,2,1,0:T(8,128)(2,1)S(1)}, u32[]{:S(2)}, u32[]{:S(2)}) collective-permute-start(bf16[4,2,88,128]{3,2,1,0:T(8,128)(2,1)S(1)} %slice.7), channel_id=1, source_target_pairs={{0,32},{32,64},{64,96},{96,128},{128,160},{160,192},{192,224},{1,3... | collective-permute-start | bytes 540680 | tf_op jit(solution)/shard_map/ppermute | solution.py:28
  91.2 11.1 %collective-permute-start.11 = (bf16[4,2,88,128]{3,2,1,0:T(8,128)(2,1)S(1)}, bf16[4,2,88,128]{3,2,1,0:T(8,128)(2,1)S(1)}, u32[]{:S(2)}, u32[]{:S(2)}) collective-permute-start(bf16[4,2,88,128]{3,2,1,0:T(8,128)(2,1)S(1)} %slice.7), channel_id=1, source_target_pairs={{0,64},{32,96},{64,128},{96,160},{128,192},{160,224},{1,65},{33,97... | collective-permute-start | bytes 540680 | tf_op jit(solution)/shard_map/ppermute | solution.py:28
  95.8 7.0 %collective-permute-start.12 = (bf16[4,2,88,128]{3,2,1,0:T(8,128)(2,1)S(1)}, bf16[4,2,88,128]{3,2,1,0:T(8,128)(2,1)S(1)}, u32[]{:S(2)}, u32[]{:S(2)}) collective-permute-start(bf16[4,2,88,128]{3,2,1,0:T(8,128)(2,1)S(1)} %slice.7), channel_id=1, source_target_pairs={{0,4},{4,0},{1,5},{5,1},{2,6},{6,2},{3,7},{7,3},{8,12},{12,8},{9,1... | collective-permute-start | bytes 540680 | tf_op jit(solution)/shard_map/ppermute | solution.py:33
  97.6 5.8 %collective-permute-start.13 = (bf16[4,2,88,128]{3,2,1,0:T(8,128)(2,1)S(1)}, bf16[4,2,88,128]{3,2,1,0:T(8,128)(2,1)S(1)}, u32[]{:S(2)}, u32[]{:S(2)}) collective-permute-start(bf16[4,2,88,128]{3,2,1,0:T(8,128)(2,1)S(1)} %collective-permute-done.10.near_ref), channel_id=1, source_target_pairs={{0,4},{4,0},{1,5},{5,1},{2,6},{6,2},{3,7},{7,3},{8,12},{12,8},{9,1... | collective-permute-start | bytes 540680 | tf_op jit(solution)/shard_map/ppermute | solution.py:33
  102.3 1.6 %collective-permute-start.14 = (bf16[4,2,88,128]{3,2,1,0:T(8,128)(2,1)S(1)}, bf16[4,2,88,128]{3,2,1,0:T(8,128)(2,1)S(1)}, u32[]{:S(2)}, u32[]{:S(2)}) collective-permute-start(bf16[4,2,88,128]{3,2,1,0:T(8,128)(2,1)S(1)} %collective-permute-done.11.far_ref), channel_id=1, source_target_pairs={{0,4},{4,0},{1,5},{5,1},{2,6},{6,2},{3,7},{7,3},{8,12},{12,8},{9,1... | collective-permute-start | bytes 540680 | tf_op jit(solution)/shard_map/ppermute | solution.py:33
  102.3 12.1 %collective-permute-start.19 = (bf16[176,1408]{1,0:T(8,128)(2,1)}, bf16[176,1408]{1,0:T(8,128)(2,1)S(1)}, u32[]{:S(2)}, u32[]{:S(2)}) collective-permute-start(bf16[176,1408]{1,0:T(8,128)(2,1)} %collective-permute-done.16.m1_ref), channel_id=1, source_target_pairs={{0,4},{4,0},{1,5},{5,1},{2,6},{6,2},{3,7},{7,3},{8,12},{12,8},{9,1... | collective-permute-start | bytes 1486856 | tf_op jit(solution)/shard_map/ppermute | solution.py:33
  102.8 11.6 %collective-permute-start.20 = (bf16[176,1408]{1,0:T(8,128)(2,1)}, bf16[176,1408]{1,0:T(8,128)(2,1)}, u32[]{:S(2)}, u32[]{:S(2)}) collective-permute-start(bf16[176,1408]{1,0:T(8,128)(2,1)} %collective-permute-done.17.m3_ref), channel_id=1, source_target_pairs={{0,4},{4,0},{1,5},{5,1},{2,6},{6,2},{3,7},{7,3},{8,12},{12,8},{9,1... | collective-permute-start | bytes 1486856 | tf_op jit(solution)/shard_map/ppermute | solution.py:33
  102.9 18.9 %collective-permute-start.18 = (bf16[176,1408]{1,0:T(8,128)(2,1)S(1)}, bf16[176,1408]{1,0:T(8,128)(2,1)}, u32[]{:S(2)}, u32[]{:S(2)}) collective-permute-start(bf16[176,1408]{1,0:T(8,128)(2,1)S(1)} %collective-permute-done.15.m2_ref), channel_id=1, source_target_pairs={{0,4},{4,0},{1,5},{5,1},{2,6},{6,2},{3,7},{7,3},{8,12},{12,8},{9,1... | collective-permute-start | bytes 1486856 | tf_op jit(solution)/shard_map/ppermute | solution.py:33
  108.2 13.6 %all-to-all-start.3 = ((bf16[16,88,128]{2,1,0:T(8,128)(2,1)}), bf16[16,88,128]{2,1,0:T(8,128)(2,1)S(1)}, u32[]{:S(2)}, u32[]{:S(2)}) async-start(bf16[16,88,128]{2,1,0:T(8,128)(2,1)} %bitcast.17), calls=%async_computation.3 | async-start | bytes 720896 | tf_op jit(solution)/shard_map/all_to_all | solution.py:379
  (8 other events, 96.1 us)
